TPU v7x, 256 devices: a whole 4x4x8 slice. The times are simulated.
256 devices in a mesh: rows: 16 (over z, core), samp: 16 (over y, x).
Axes of the slice: x: 4, y: 4, z: 8, core: 2. Of those that a mesh axis runs over, the one named last changes fastest.
Arguments:
- right_sides: float32 [576, 128, 2048], P('rows', None, 'samp'), may hold values from -6 to 6
- factor_blocks: float32 [576, 6, 128, 128], P('rows', None, 'samp'), may hold values from -0.21875 to 0.21875
- block_columns: int32 [576, 6], P('rows'), may hold values from 0 to 8, as said below
- pivot_rows: int32 [8], replicated, may hold values from 0 to 575, as said below
- diag_inverse: float32 [8, 128, 128], replicated
Outputs:
- solved_blocks: float32 [8, 128, 2048], P(None, None, 'samp')
- updated_sides: float32 [576, 128, 2048], P('rows', None, 'samp')
Inputs may be any that keep to these rules, and one draw needn't show every extreme that they name: `block_columns`: in each block row the values below 8 are distinct; 8 marks an empty slot. `pivot_rows`: the 8 positions are distinct.
All inputs are finite; a program needn't handle non-finite values.
Results may differ from a plain program's by a relative error of at most 0.0001.
Values sent between devices are 32-bit elements; how exact they have to be, the bound alone decides.
No kernel may reach another device: no remote copies, remote signals or barrier semaphores. Data moves between devices by JAX's collectives and lax.ppermute only.
A program may use at most 128 MiB of HBM per device.

v0:
```python
import jax
import jax.numpy as jnp
from jax import lax
from jax.sharding import PartitionSpec as P


def spread(block, axis, source):
    block = jnp.where(lax.axis_index(axis) == source, block, jnp.zeros_like(block))
    return lax.psum(block, axis)


def local(right_sides, factor_blocks, block_columns, pivot_rows, diag_inverse):
    highest = lax.Precision.HIGHEST
    row_count = right_sides.shape[0]
    step_count = pivot_rows.shape[0]
    local_ids = lax.axis_index("rows") * row_count + jnp.arange(row_count, dtype=jnp.int32)
    matches = local_ids[:, None] == pivot_rows[None, :]
    targets = jnp.arange(step_count, dtype=jnp.int32)
    row_rank = step_count + jnp.sum(jnp.where(matches, targets[None, :] - step_count, 0), axis=1)
    selector = (
        (block_columns[:, :, None] == targets[None, None, :])
        & (targets[None, None, :] < row_rank[:, None, None])
    ).astype(jnp.float32)
    current = right_sides
    solved = []
    for column in range(step_count):
        owner_index = pivot_rows[column] // row_count
        slot_index = pivot_rows[column] % row_count
        pivot_side = lax.dynamic_index_in_dim(current, slot_index, 0, keepdims=False)
        candidate = jnp.dot(diag_inverse[column], pivot_side, precision=highest)
        solved_now = spread(candidate, "rows", owner_index)
        column_part = jnp.einsum(
            "rs,rsab->rab", selector[:, :, column], factor_blocks, precision=highest
        )

        def apply_block(piece, start, solved_now=solved_now):
            return jnp.einsum("rab,bn->ran", piece, solved_now, precision=highest)

        correction = apply_block(
            lax.all_gather(column_part, "samp", axis=1, tiled=True), jnp.int32(0)
        )
        current = current - correction
        solved.append(solved_now)
    return (jnp.stack(solved), current)


def solution(mesh):
    placed = (P("rows", None, "samp"), P("rows", None, "samp", None), P("rows", None), P(), P())
    return jax.shard_map(
        local,
        mesh=mesh,
        in_specs=placed,
        out_specs=(P(None, None, "samp"), P("rows", None, "samp")),
        check_vma=False,
    )
```

profile of v0, /device:TPU:1, one launch (start us, length us, event | category | flops | bytes accessed | tf_op | source)
XLA Modules:
  0.0 864.1 jit_solution(17479028503229165503)
XLA Ops:
  8.1 1.6 fusion.73
  11.7 1.8 fusion.23
  13.6 0.7 select_reduce_fusion
  14.3 0.7 fusion.64
  15.2 1.5 fusion.14
  16.9 1.5 fusion.12
  20.5 97.0 %all-reduce.9.cloned.1.call-done = f32[128,128]{0,1:T(8,128)} async-done(((f32[128,128]{0,1:T(8,128)}), f32[128,128]{0,1:T(8,128)}) %all-reduce.9.cloned.1.call-update) | async-done | bytes 65552 | tf_op jit(solution)/shard_map/psum | solution.py:9
  117.5 3.9 convolution_subtract_fusion.7
  121.4 1.4 copy-done.2
  122.8 1.7 fusion.22
  124.6 1.5 fusion.10
  128.0 0.8 all-gather.11.cloned.1.call-done
  128.8 93.2 %all-reduce.11.cloned.1.call-done = f32[128,128]{0,1:T(8,128)} async-done(((f32[128,128]{0,1:T(8,128)}), f32[128,128]{0,1:T(8,128)}) %all-reduce.11.cloned.1.call-update) | async-done | bytes 65552 | tf_op jit(solution)/shard_map/psum | solution.py:9
  222.0 4.4 convolution_subtract_fusion.6
  226.5 1.8 fusion.21
  228.3 1.5 fusion.8
  231.9 94.0 %all-reduce.13.cloned.1.call-done = f32[128,128]{0,1:T(8,128)} async-done(((f32[128,128]{0,1:T(8,128)}), f32[128,128]{0,1:T(8,128)}) %all-reduce.13.cloned.1.call-update) | async-done | bytes 65552 | tf_op jit(solution)/shard_map/psum | solution.py:9
  325.8 3.9 convolution_subtract_fusion.5
  329.7 1.4 copy-done.1
  331.1 1.7 fusion.20
  333.1 1.5 fusion.6
  336.6 94.2 %all-reduce.15.cloned.1.call-done = f32[128,128]{0,1:T(8,128)} async-done(((f32[128,128]{0,1:T(8,128)}), f32[128,128]{0,1:T(8,128)}) %all-reduce.15.cloned.1.call-update) | async-done | bytes 65552 | tf_op jit(solution)/shard_map/psum | solution.py:9
  430.8 4.4 convolution_subtract_fusion.4
  435.2 1.8 fusion.19
  437.0 1.5 fusion.4
  440.8 93.8 %all-reduce.17.cloned.1.call-done = f32[128,128]{0,1:T(8,128)} async-done(((f32[128,128]{0,1:T(8,128)}), f32[128,128]{0,1:T(8,128)}) %all-reduce.17.cloned.1.call-update) | async-done | bytes 65552 | tf_op jit(solution)/shard_map/psum | solution.py:9
  534.6 3.9 convolution_subtract_fusion.3
  538.5 1.4 copy-done.3
  539.9 1.7 fusion.18
  541.7 1.5 fusion.2
  545.0 94.6 %all-reduce.19.cloned.1.call-done = f32[128,128]{0,1:T(8,128)} async-done(((f32[128,128]{0,1:T(8,128)}), f32[128,128]{0,1:T(8,128)}) %all-reduce.19.cloned.1.call-update) | async-done | bytes 65552 | tf_op jit(solution)/shard_map/psum | solution.py:9
  639.6 4.4 convolution_subtract_fusion.2
  644.0 1.8 fusion.17
  648.4 95.0 %all-reduce.21.cloned.1.call-done = f32[128,128]{0,1:T(8,128)} async-done(((f32[128,128]{0,1:T(8,128)}), f32[128,128]{0,1:T(8,128)}) %all-reduce.21.cloned.1.call-update) | async-done | bytes 65552 | tf_op jit(solution)/shard_map/psum | solution.py:9
  743.4 3.9 convolution_subtract_fusion.1
  747.3 1.4 copy-done.4
  748.7 1.8 fusion.16
  750.5 1.5 fusion
  752.7 0.6 bitcast_dynamic-update-slice_fusion.6
  753.3 0.6 bitcast_dynamic-update-slice_fusion.5
  753.9 0.6 bitcast_dynamic-update-slice_fusion.4
  754.6 1.5 bitcast_dynamic-update-slice_fusion.3
  756.0 1.5 bitcast_dynamic-update-slice_fusion.2
  757.5 1.5 bitcast_dynamic-update-slice_fusion.1
  759.0 89.1 %all-reduce.23.cloned.1.call-done = f32[128,128]{0,1:T(8,128)} async-done(((f32[128,128]{0,1:T(8,128)}), f32[128,128]{0,1:T(8,128)}) %all-reduce.23.cloned.1.call-update) | async-done | bytes 65552 | tf_op jit(solution)/shard_map/psum | solution.py:9
  848.1 1.5 bitcast_dynamic-update-slice_fusion
  849.5 2.0 copy.34
  851.6 5.1 convolution_subtract_fusion
  (71 shorter events, 3.3 us)
Async XLA Ops:
  8.0 7.2 copy-start
  8.0 109.5 %copy-start.6 = (f32[36,128,128]{2,1,0:T(8,128)S(1)}, f32[36,128,128]{2,1,0:T(8,128)}, u32[]{:S(2)}) copy-start(f32[36,128,128]{2,1,0:T(8,128)} %param.5) | copy-start | bytes 7077892
  8.0 109.5 %all-reduce.9.cloned.1.call-start = ((), (), s32[]{:S(2)}) async-start(), calls=%async_computation | async-start | bytes 131072 | tf_op jit(solution)/shard_map/psum | solution.py:9
  13.5 104.0 %all-gather.9.cloned.1.call-start = ((), (), s32[]{:S(2)}) async-start(), calls=%async_computation.1 | async-start | bytes 2506752 | tf_op jit(solution)/shard_map/all_gather | solution.py:40
  16.7 112.2 %all-gather.11.cloned.1.call-start = ((), (), s32[]{:S(2)}) async-start(), calls=%async_computation.3 | async-start | bytes 2506752 | tf_op jit(solution)/shard_map/all_gather | solution.py:40
  18.4 203.7 %all-reduce.11.cloned.1.call-start = ((), (), s32[]{:S(2)}) async-start(), calls=%async_computation.2 | async-start | bytes 131072 | tf_op jit(solution)/shard_map/psum | solution.py:9
  121.4 1.4 copy-start.2
  124.6 107.3 %all-gather.13.cloned.1.call-start = ((), (), s32[]{:S(2)}) async-start(), calls=%async_computation.5 | async-start | bytes 2506752 | tf_op jit(solution)/shard_map/all_gather | solution.py:40
  126.1 199.7 %all-reduce.13.cloned.1.call-start = ((), (), s32[]{:S(2)}) async-start(), calls=%async_computation.4 | async-start | bytes 131072 | tf_op jit(solution)/shard_map/psum | solution.py:9
  228.2 108.3 %all-gather.15.cloned.1.call-start = ((), (), s32[]{:S(2)}) async-start(), calls=%async_computation.7 | async-start | bytes 2506752 | tf_op jit(solution)/shard_map/all_gather | solution.py:40
  229.8 201.0 %all-reduce.15.cloned.1.call-start = ((), (), s32[]{:S(2)}) async-start(), calls=%async_computation.6 | async-start | bytes 131072 | tf_op jit(solution)/shard_map/psum | solution.py:9
  329.7 1.4 copy-start.1
  332.9 107.9 %all-gather.17.cloned.1.call-start = ((), (), s32[]{:S(2)}) async-start(), calls=%async_computation.9 | async-start | bytes 2506752 | tf_op jit(solution)/shard_map/all_gather | solution.py:40
  334.6 200.0 %all-reduce.17.cloned.1.call-start = ((), (), s32[]{:S(2)}) async-start(), calls=%async_computation.8 | async-start | bytes 131072 | tf_op jit(solution)/shard_map/psum | solution.py:9
  437.0 108.0 %all-gather.19.cloned.1.call-start = ((), (), s32[]{:S(2)}) async-start(), calls=%async_computation.11 | async-start | bytes 2506752 | tf_op jit(solution)/shard_map/all_gather | solution.py:40
  438.5 201.1 %all-reduce.19.cloned.1.call-start = ((), (), s32[]{:S(2)}) async-start(), calls=%async_computation.10 | async-start | bytes 131072 | tf_op jit(solution)/shard_map/psum | solution.py:9
  538.5 1.4 copy-start.3
  541.7 106.7 %all-gather.21.cloned.1.call-start = ((), (), s32[]{:S(2)}) async-start(), calls=%async_computation.13 | async-start | bytes 2506752 | tf_op jit(solution)/shard_map/all_gather | solution.py:40
  543.2 200.2 %all-reduce.21.cloned.1.call-start = ((), (), s32[]{:S(2)}) async-start(), calls=%async_computation.12 | async-start | bytes 131072 | tf_op jit(solution)/shard_map/psum | solution.py:9
  645.8 202.2 %all-reduce.23.cloned.1.call-start = ((), (), s32[]{:S(2)}) async-start(), calls=%async_computation.14 | async-start | bytes 131072 | tf_op jit(solution)/shard_map/psum | solution.py:9
  648.3 103.7 %copy-start.7 = (f32[128,128]{0,1:T(8,128)S(1)}, f32[128,128]{0,1:T(8,128)}, u32[]{:S(2)}) copy-start(f32[128,128]{0,1:T(8,128)} %all-reduce.9.cloned.1.call-done) | copy-start | bytes 196612
  648.3 104.3 %copy-start.8 = (f32[128,128]{0,1:T(8,128)S(1)}, f32[128,128]{0,1:T(8,128)}, u32[]{:S(2)}) copy-start(f32[128,128]{0,1:T(8,128)} %all-reduce.11.cloned.1.call-done) | copy-start | bytes 196612
  648.3 105.0 %copy-start.9 = (f32[128,128]{0,1:T(8,128)S(1)}, f32[128,128]{0,1:T(8,128)}, u32[]{:S(2)}) copy-start(f32[128,128]{0,1:T(8,128)} %all-reduce.13.cloned.1.call-done) | copy-start | bytes 196612
  648.4 105.6 %copy-start.10 = (f32[128,128]{0,1:T(8,128)S(1)}, f32[128,128]{0,1:T(8,128)}, u32[]{:S(2)}) copy-start(f32[128,128]{0,1:T(8,128)} %all-reduce.15.cloned.1.call-done) | copy-start | bytes 196612
  747.3 1.4 copy-start.4
  750.4 101.1 %copy-start.5 = (f32[36,128,128]{2,1,0:T(8,128)S(1)}, f32[36,128,128]{2,1,0:T(8,128)}, u32[]{:S(2)}) copy-start(f32[36,128,128]{2,1,0:T(8,128)} %copy-done.4) | copy-start | bytes 7077892
  750.5 101.1 %all-gather.23.cloned.1.call-start = ((), (), s32[]{:S(2)}) async-start(), calls=%async_computation.15 | async-start | bytes 2506752 | tf_op jit(solution)/shard_map/all_gather | solution.py:40
Sparse Core Ops, SparseCore 0:
  13.6 103.8 all-reduce.8
  124.7 97.2 all-reduce.10
  228.4 97.4 all-reduce.12
  333.0 97.7 all-reduce.14
  437.1 97.4 all-reduce.16
  541.8 97.7 all-reduce.18
  645.9 97.4 all-reduce.20
  750.6 97.4 all-reduce.22
Sparse Core Ops, SparseCore 1:
  17.2 56.2 all-gather.8
  75.8 53.0 all-gather.10
  132.0 52.8 all-gather.12
  231.4 50.5 all-gather.14
  337.0 50.5 all-gather.16
  440.2 50.5 all-gather.18
  545.4 50.5 all-gather.20
  753.4 50.5 all-gather.22
where the time goes:
time: 865 us; the launch traced here: 864 us
  waiting for transfers between devices  752 us (87%)
  matrix products  59.6 us (7%)
  between operations  31.1 us (4%)
  local copies, waits for them, and re-layouts  18.8 us (2%)
    psum x8, waiting for transfers between devices, spread(): return lax.psum(block, axis)  751 us
    dot_general x8, matrix products, apply_block(): return jnp.einsum('rab,bn->ran', piece, solved_now, precision=highest)  33.8 us
  transfers between devices with their start and end apart: 16, of which 9 were waited for; matrix products, arithmetic and copies ran while one was open for 7% of the time, Pallas kernels for 0%

commit v1 on v0

v1 whole, which is shorter than its diff:
```python
import jax
import jax.numpy as jnp
from jax import lax
from jax.experimental import pallas as pl
from jax.experimental.pallas import tpu as pltpu
from jax.sharding import PartitionSpec as P

BLOCK = 128
STEPS = 8
SLOTS = 6
RANKS = 16
SLICE = BLOCK // RANKS
HALF = BLOCK // 2
TRI = 32
ROWS_PER_STEP = 4


def tri(k, i):
    return k * (k - 1) // 2 + i


TRI_PIVOT = [k for k in range(STEPS) for _ in range(k)] + [STEPS - 1] * (TRI - tri(STEPS, 0))


def split(x):
    hi = x.astype(jnp.bfloat16)
    lo = (x - hi.astype(jnp.float32)).astype(jnp.bfloat16)
    return hi, lo


def dot(a, b):
    return lax.dot_general(a, b, (((1,), (0,)), ((), ())), preferred_element_type=jnp.float32)


def dot3(a, b2):
    ah, al = split(a)
    full = dot(ah, b2)
    return full[:, :BLOCK] + full[:, BLOCK:] + dot(al, b2[:, :BLOCK])


def pair(x):
    return jnp.concatenate(split(x), axis=1)


def pack_kernel(place, columns, sides, factor, out, rows_buf, tri_buf, sem_f, sem_r, sem_o):
    copies = []
    for j in range(STEPS):
        at = place[j]
        f = pltpu.make_async_copy(factor.at[at], rows_buf.at[j], sem_f.at[j])
        f.start()
        copies.append(f)
    sides_copies = []
    for j in range(STEPS):
        at = place[j]
        for h in range(2):
            r = pltpu.make_async_copy(
                sides.at[at, pl.ds(h * HALF, HALF)], out.at[2 * j + h, pl.ds(0, HALF)], sem_r.at[2 * j + h]
            )
            r.start()
            sides_copies.append(r)
    for c in copies:
        c.wait()
    for j in range(STEPS):
        at = place[j]
        for i in range(j):
            piece = jnp.zeros((SLICE, BLOCK), jnp.float32)
            for s in range(SLOTS):
                piece = jnp.where(columns[at, s] == i, rows_buf[j, s], piece)
            b = tri(j, i)
            tri_buf[b // 2, pl.ds((b % 2) * SLICE, SLICE)] = piece
    for b in range(tri(STEPS, 0), TRI):
        tri_buf[b // 2, pl.ds((b % 2) * SLICE, SLICE)] = jnp.zeros((SLICE, BLOCK), jnp.float32)
    o = pltpu.make_async_copy(tri_buf, out.at[:, pl.ds(HALF, 2 * SLICE)], sem_o)
    o.start()
    for c in sides_copies:
        c.wait()
    o.wait()


def pack(place, columns, sides, factor):
    return pl.pallas_call(
        pack_kernel,
        out_shape=jax.ShapeDtypeStruct((RANKS, HALF + 2 * SLICE, BLOCK), jnp.float32),
        in_specs=[
            pl.BlockSpec(memory_space=pltpu.SMEM),
            pl.BlockSpec(memory_space=pltpu.SMEM),
            pl.BlockSpec(memory_space=pl.ANY),
            pl.BlockSpec(memory_space=pl.ANY),
        ],
        out_specs=pl.BlockSpec(memory_space=pl.ANY),
        scratch_shapes=[
            pltpu.VMEM((STEPS, SLOTS, SLICE, BLOCK), jnp.float32),
            pltpu.VMEM((RANKS, 2 * SLICE, BLOCK), jnp.float32),
            pltpu.SemaphoreType.DMA((STEPS,)),
            pltpu.SemaphoreType.DMA((2 * STEPS,)),
            pltpu.SemaphoreType.DMA,
        ],
        name="pack",
    )(place, columns, sides, factor)


def solve_kernel(core, gathered, mine, other, inverse, solved, pairs, side):
    flag = core[0]

    def factor(k, i):
        b = tri(k, i)
        h = b // RANKS
        own = mine[:, b % RANKS].reshape(BLOCK, BLOCK)
        far = other[:, b % RANKS].reshape(BLOCK, BLOCK)
        return jnp.where(flag == h, own, far)

    for j in range(STEPS):
        side[j] = gathered[2 * j : 2 * j + 2, :HALF].reshape(BLOCK, BLOCK)
    for j in range(STEPS):
        x = dot3(inverse[j], pair(side[j]))
        solved[j] = x
        x2 = pair(x)
        pairs[j] = x2
        for k in range(j + 1, STEPS):
            side[k] = side[k] - dot3(factor(k, j), x2)
    pairs[STEPS] = jnp.zeros((BLOCK, 2 * BLOCK), jnp.bfloat16)


def solve(core, gathered, mine, other, inverse):
    vmem = pl.BlockSpec(memory_space=pltpu.VMEM)
    return pl.pallas_call(
        solve_kernel,
        out_shape=(
            jax.ShapeDtypeStruct((STEPS, BLOCK, BLOCK), jnp.float32),
            jax.ShapeDtypeStruct((STEPS + 1, BLOCK, 2 * BLOCK), jnp.bfloat16),
        ),
        in_specs=[pl.BlockSpec(memory_space=pltpu.SMEM), vmem, vmem, vmem, vmem],
        out_specs=(vmem, vmem),
        scratch_shapes=[pltpu.VMEM((STEPS, BLOCK, BLOCK), jnp.float32)],
        name="solve",
    )(core, gathered, mine, other, inverse)


def update_kernel(picks, sides, factor, pairs, out):
    step = pl.program_id(0)
    for r in range(ROWS_PER_STEP):
        row = step * ROWS_PER_STEP + r
        hi, lo, x2 = [], [], []
        for s in range(SLOTS):
            fh, fl = split(factor[:, r, s].reshape(BLOCK, BLOCK))
            hi.append(fh)
            lo.append(fl)
            x2.append(pairs[picks[row, s]])
        hi = jnp.concatenate(hi, axis=1)
        lo = jnp.concatenate(lo, axis=1)
        x2 = jnp.concatenate(x2, axis=0)
        full = dot(hi, x2)
        out[r] = sides[r] - (full[:, :BLOCK] + full[:, BLOCK:] + dot(lo, x2[:, :BLOCK]))


def update(picks, sides, factor, pairs):
    rows = sides.shape[0]
    return pl.pallas_call(
        update_kernel,
        grid=(rows // ROWS_PER_STEP,),
        out_shape=jax.ShapeDtypeStruct(sides.shape, jnp.float32),
        in_specs=[
            pl.BlockSpec(memory_space=pltpu.SMEM),
            pl.BlockSpec((ROWS_PER_STEP, BLOCK, BLOCK), lambda g: (g, 0, 0)),
            pl.BlockSpec((RANKS, ROWS_PER_STEP, SLOTS, SLICE, BLOCK), lambda g: (0, g, 0, 0, 0)),
            pl.BlockSpec((STEPS + 1, BLOCK, 2 * BLOCK), lambda g: (0, 0, 0)),
        ],
        out_specs=pl.BlockSpec((ROWS_PER_STEP, BLOCK, BLOCK), lambda g: (g, 0, 0)),
        name="update",
    )(picks, sides, factor, pairs)


def local(right_sides, factor_blocks, block_columns, pivot_rows, diag_inverse):
    row_count = right_sides.shape[0]
    rank = lax.axis_index("rows")
    everything = lax.all_gather(factor_blocks, "samp", axis=0, tiled=False)

    owner = pivot_rows // row_count
    place = pivot_rows % row_count
    ids = rank * row_count + jnp.arange(row_count, dtype=jnp.int32)
    targets = jnp.arange(STEPS, dtype=jnp.int32)
    row_rank = STEPS + jnp.sum(jnp.where(ids[:, None] == pivot_rows[None, :], targets - STEPS, 0), axis=1)
    picks = jnp.where(block_columns < row_rank[:, None], block_columns, STEPS)

    payload = pack(place, block_columns, right_sides, factor_blocks)
    pieces = lax.all_to_all(payload, "rows", 0, 0)
    tri_owner = owner[jnp.array(TRI_PIVOT, jnp.int32)]
    part = jnp.concatenate(
        [
            lax.dynamic_slice(pieces, (owner[rank // 2], 0, 0), (1, HALF, BLOCK))[0],
            lax.dynamic_slice(pieces, (tri_owner[2 * rank], HALF, 0), (1, SLICE, BLOCK))[0],
            lax.dynamic_slice(pieces, (tri_owner[2 * rank + 1], HALF + SLICE, 0), (1, SLICE, BLOCK))[0],
        ]
    )
    gathered = lax.all_gather(part, "rows", axis=0, tiled=False)
    slices = gathered[:, HALF:].reshape(TRI, SLICE, BLOCK)
    core = rank % 2
    half = lax.dynamic_slice(slices, (core * RANKS, 0, 0), (RANKS, SLICE, BLOCK))
    mine = lax.all_to_all(jnp.broadcast_to(half, (RANKS,) + half.shape), "samp", 0, 0)
    other = lax.ppermute(mine, "rows", [(i, i ^ 1) for i in range(RANKS)])
    solved, pairs = solve(core.reshape(1), gathered, mine, other, diag_inverse)
    return solved, update(picks, right_sides, everything, pairs)


def solution(mesh):
    placed = (P("rows", None, "samp"), P("rows", None, "samp", None), P("rows", None), P(), P())
    return jax.shard_map(
        local,
        mesh=mesh,
        in_specs=placed,
        out_specs=(P(None, None, "samp"), P("rows", None, "samp")),
        check_vma=False,
    )
```

time: 865 us -> 148 us (0.17)
  waiting for transfers between devices: 752 us -> 22.7 us
  matrix products: 59.6 us -> 0 us
  blocking collectives: 0 us -> 51.4 us
  Pallas kernels: 0 us -> 35.6 us
  local copies, waits for them, and re-layouts: 18.8 us -> 4.43 us
  between operations: 31.1 us -> 19.7 us
  starting transfers between devices: 1.08 us -> 11.3 us
    psum x8 -> x0, waiting for transfers between devices: 751 us -> none  [spread(): return lax.psum(block, axis)]
    dot_general x24 -> x0, matrix products: 59.6 us -> none  [the longest x8 33.8 us: apply_block(): return jnp.einsum('rab,bn->ran', piece, solved_now, precision=highest)]
    pallas_call x0 -> x3, Pallas kernels: none -> 35.6 us  [the longest x1 18.4 us: pack(): pl.pallas_call(pack_kernel, out_shape=jax.ShapeDtypeStruct((RANKS, HALF +...]
    all_to_all x0 -> x1, blocking collectives: none -> 35.1 us  [local(): lax.all_to_all(jnp.broadcast_to(half, (RANKS,) + half.shape), 'samp', 0, 0)]
    all_gather x0 -> x1, blocking collectives: none -> 16.3 us  [local(): gathered = lax.all_gather(part, 'rows', axis=0, tiled=False)]
    all_to_all x0 -> x1, waiting for transfers between devices: none -> 12.4 us  [local(): pieces = lax.all_to_all(payload, 'rows', 0, 0)]
    unnamed x30 -> x13, local copies, waits for them, and re-layouts: 14.6 us -> 2.35 us
    all_to_all x0 -> x1, starting transfers between devices: none -> 9.99 us  [local(): pieces = lax.all_to_all(payload, 'rows', 0, 0)]
  transfers between devices with their start and end apart: 16 -> 3, of which waited for: 9 -> 3; matrix products, arithmetic and copies ran while one was open for 7% -> 4% of each run, Pallas kernels for 0% -> 16%
where the time goes in v1:
time: 148 us; the launch traced here: 147 us
  blocking collectives  51.4 us (35%)
  Pallas kernels  35.6 us (24%)
  waiting for transfers between devices  22.7 us (15%)
  between operations  19.7 us (13%)
  starting transfers between devices  11.3 us (8%)
  local copies, waits for them, and re-layouts  4.43 us (3%)
  other arithmetic  1.97 us (1%)
    all_to_all x1, blocking collectives, local(): lax.all_to_all(jnp.broadcast_to(half, (RANKS,) + half.shape), 'samp', 0, 0)  35.1 us
    pallas_call x1, Pallas kernels, pack(): pl.pallas_call(pack_kernel, out_shape=jax.ShapeDtypeStruct((RANKS, HALF +...  18.4 us
    all_gather x1, blocking collectives, local(): gathered = lax.all_gather(part, 'rows', axis=0, tiled=False)  16.3 us
    all_to_all x1, waiting for transfers between devices, local(): pieces = lax.all_to_all(payload, 'rows', 0, 0)  12.4 us
    pallas_call x1, Pallas kernels, update(): pl.pallas_call(update_kernel, grid=(rows // ROWS_PER_STEP,), out_shape=ja...  11.8 us
    all_to_all x1, starting transfers between devices, local(): pieces = lax.all_to_all(payload, 'rows', 0, 0)  9.99 us
    all_gather x1, waiting for transfers between devices, local(): everything = lax.all_gather(factor_blocks, 'samp', axis=0, tiled=False)  8.11 us
    pallas_call x1, Pallas kernels, solve(): pl.pallas_call(solve_kernel, out_shape=(jax.ShapeDtypeStruct((STEPS, BLOC...  5.41 us
  transfers between devices with their start and end apart: 3, of which 3 were waited for; matrix products, arithmetic and copies ran while one was open for 4% of the time, Pallas kernels for 16%

profile of v1, /device:TPU:1, one launch (start us, length us, event | category | flops | bytes accessed | tf_op | source)
XLA Modules:
  0.0 147.1 jit_solution(4054364209302834096)
XLA Ops:
  7.2 0.0 all-gather.4.cloned.1.call-start
  7.2 0.7 all-gather.4.cloned.1.call-update
  7.9 1.4 copy.17.columns
  9.3 1.2 and_select_fusion
  10.5 0.0 copy-start.4
  10.5 18.4 %pack.1 = f32[16,80,128]{2,1,0:T(8,128)} custom-call(s32[8]{0:T(128)} %get-tuple-element.11.place, s32[36,6]{1,0:T(8,128)} %copy.17.columns, f32[36,128,128]{2,1,0:T(8,128)} %sides.3, f32[36,6,8,128]{3,2,1,0:T(8,128)} %factor.1), custom_call_target="tpu_custom_call" | custom-call | tf_op jit(solution)/shard_map/pack/pallas_call | solution.py:81
  28.8 10.0 %all-to-all-start = ((f32[16,80,128]{2,1,0:T(8,128)}), f32[16,80,128]{2,1,0:T(8,128)S(1)}, u32[]{:S(2)}, u32[]{:S(2)}) async-start(f32[16,80,128]{2,1,0:T(8,128)} %pack.1), calls=%async_computation | async-start | bytes 1310720 | tf_op jit(solution)/shard_map/all_to_all | solution.py:186
  38.8 0.0 copy-done.4
  38.8 0.7 gather_fusion
  39.5 0.0 copy-start.5
  39.5 0.0 copy-start.3
  39.6 0.6 fusion
  42.6 0.7 dynamic_slice.21
  46.4 12.4 %all-to-all-done = f32[16,80,128]{2,1,0:T(8,128)S(1)} async-done(((f32[16,80,128]{2,1,0:T(8,128)}), f32[16,80,128]{2,1,0:T(8,128)S(1)}, u32[]{:S(2)}, u32[]{:S(2)}) %all-to-all-start) | async-done | bytes 655392 | tf_op jit(solution)/shard_map/all_to_all | solution.py:186
  58.9 16.3 %all-gather = f32[1280,128]{1,0:T(8,128)S(1)} all-gather(f32[80,128]{1,0:T(8,128)S(1)} %pad_maximum_fusion), channel_id=2, replica_groups=mesh['rows'=16,'samp'=16] {'rows'}, dimensions={0}, use_global_device_ids=true | all-gather | bytes 696320 | tf_op jit(solution)/shard_map/all_gather | solution.py:195
  75.1 0.0 copy-start.1
  75.2 0.1 broadcast_in_dim.22
  75.3 35.1 %all_to_all.10.mine = f32[16,16,8,128]{3,2,1,0:T(8,128)S(1)} all-to-all(f32[16,16,8,128]{3,2,1,0:T(8,128)S(1)} %broadcast_in_dim.22), channel_id=1, replica_groups=mesh['rows'=16,'samp'=16] {'samp'}, dimensions={0} | all-to-all | bytes 2097152 | tf_op jit(solution)/shard_map/all_to_all | solution.py:199
  110.4 0.0 copy-start
  110.4 1.3 collective-permute-start
  111.7 0.0 copy-done.5
  111.7 0.1 select_reduce_fusion
  111.8 0.0 copy-done.3
  111.8 0.7 compare_select_fusion.picks
  112.5 1.5 %collective-permute-done.other = f32[16,16,8,128]{3,2,1,0:T(8,128)S(1)} collective-permute-done((f32[16,16,8,128]{3,2,1,0:T(8,128)S(1)}, f32[16,16,8,128]{3,2,1,0:T(8,128)S(1)}, u32[]{:S(2)}, u32[]{:S(2)}) %collective-permute-start) | collective-permute-done | bytes 1048608 | tf_op jit(solution)/shard_map/ppermute | solution.py:200
  114.0 0.0 copy-start.2
  114.0 0.0 copy-done.1
  114.0 0.0 copy-done
  114.0 0.9 copy-done.2
  114.9 5.4 %solve.1 = (f32[8,128,128]{2,1,0:T(8,128)}, bf16[9,128,256]{2,1,0:T(8,128)(2,1)}) custom-call(s32[1]{0:T(128)} %bitcast.core, f32[16,80,128]{2,1,0:T(8,128)} %bitcast.15, f32[16,16,8,128]{3,2,1,0:T(8,128)} %copy-done, f32[16,16,8,128]{3,2,1,0:T(8,128)} %copy-done.2, f32[8,128,128]{2,1,0:T(8,128)} %inverse.1), custom_call_target="tpu_custom_call" | custom-call | tf_op jit(solution)/shard_map/solve/pallas_call | solution.py:126
  120.3 8.1 %all-gather.4.cloned.1.call-done = f32[576,6,8,128]{3,2,1,0:T(8,128)} async-done(((f32[36,6,8,128]{3,2,1,0:T(8,128)}), f32[576,6,8,128]{3,2,1,0:T(8,128)}) %all-gather.4.cloned.1.call-update) | async-done | bytes 14155792 | tf_op jit(solution)/shard_map/all_gather | solution.py:176
  128.4 11.8 %update.1 = f32[36,128,128]{2,1,0:T(8,128)} custom-call(s32[36,6]{1,0:T(8,128)} %compare_select_fusion.picks, f32[36,128,128]{2,1,0:T(8,128)} %sides.3, f32[16,36,6,8,128]{4,3,2,1,0:T(8,128)} %bitcast.13, bf16[9,128,256]{2,1,0:T(8,128)(2,1)} %get-tuple-element.5.pairs), custom_call_target="tpu_custom_call" | custom-call | tf_op jit(solution)/shard_map/update/pallas_call | solution.py:158
  (9 shorter events, 0.1 us)
Async XLA Ops:
  7.2 121.3 %all-gather.4.cloned.1.call-start = ((), (), s32[]{:S(2)}) async-start(), calls=%async_computation.2 | async-start | bytes 15040512 | tf_op jit(solution)/shard_map/all_gather | solution.py:176
  10.5 28.4 %copy-start.4 = (s32[32]{0:T(128)S(1)}, s32[32]{0:T(128)}, u32[]{:S(2)}) copy-start(s32[32]{0:T(128)} %constant.76) | copy-start | bytes 388
  28.8 30.0 %all-to-all-start = ((f32[16,80,128]{2,1,0:T(8,128)}), f32[16,80,128]{2,1,0:T(8,128)S(1)}, u32[]{:S(2)}, u32[]{:S(2)}) async-start(f32[16,80,128]{2,1,0:T(8,128)} %pack.1), calls=%async_computation | async-start | bytes 1310720 | tf_op jit(solution)/shard_map/all_to_all | solution.py:186
  39.5 72.2 %copy-start.5 = (s32[8]{0:T(128)S(1)}, s32[8]{0:T(128)}, u32[]{:S(2)}) copy-start(s32[8]{0:T(128)} %param.9) | copy-start | bytes 100
  39.5 72.3 %copy-start.3 = (s32[36,6]{1,0:T(8,128)S(1)}, s32[36,6]{1,0:T(8,128)}, u32[]{:S(2)}) copy-start(s32[36,6]{1,0:T(8,128)} %copy.17.columns) | copy-start | bytes 2596
  75.1 38.9 %copy-start.1 = (f32[1280,128]{1,0:T(8,128)}, f32[1280,128]{1,0:T(8,128)S(1)}, u32[]{:S(2)}) copy-start(f32[1280,128]{1,0:T(8,128)S(1)} %all-gather) | copy-start | bytes 1966084
  110.4 3.6 %copy-start = (f32[16,16,8,128]{3,2,1,0:T(8,128)}, f32[16,16,8,128]{3,2,1,0:T(8,128)S(1)}, u32[]{:S(2)}) copy-start(f32[16,16,8,128]{3,2,1,0:T(8,128)S(1)} %all_to_all.10.mine) | copy-start | bytes 3145732
  110.4 3.6 %collective-permute-start = (f32[16,16,8,128]{3,2,1,0:T(8,128)S(1)}, f32[16,16,8,128]{3,2,1,0:T(8,128)S(1)}, u32[]{:S(2)}, u32[]{:S(2)}) collective-permute-start(f32[16,16,8,128]{3,2,1,0:T(8,128)S(1)} %all_to_all.10.mine), channel_id=1, source_target_pairs={{0,16},{16,0},{32,48},{48,32},{64,80},{80,64},{96,112},{112,96},{1... | collective-permute-start | bytes 3145736 | tf_op jit(solution)/shard_map/ppermute | solution.py:200
  114.0 1.0 copy-start.2
Sparse Core Ops, SparseCore 0:
  10.4 117.9 all-gather.3

commit v2 on v1

--- a/solution.py
+++ b/solution.py
@@ -12,7 +12,7 @@
 SLICE = BLOCK // RANKS
 HALF = BLOCK // 2
 TRI = 32
-ROWS_PER_STEP = 4
+ROWS_PER_STEP = 12
 
 
 def tri(k, i):
@@ -42,24 +42,21 @@
     return jnp.concatenate(split(x), axis=1)
 
 
-def pack_kernel(place, columns, sides, factor, out, rows_buf, tri_buf, sem_f, sem_r, sem_o):
-    copies = []
-    for j in range(STEPS):
-        at = place[j]
-        f = pltpu.make_async_copy(factor.at[at], rows_buf.at[j], sem_f.at[j])
-        f.start()
-        copies.append(f)
-    sides_copies = []
-    for j in range(STEPS):
-        at = place[j]
+def pack_kernel(place, columns, sides, factor, out, rows_buf, sem_f, sem_r):
+    factor_copies, side_copies = [], []
+    for j in range(STEPS):
+        copy = pltpu.make_async_copy(factor.at[place[j]], rows_buf.at[j], sem_f.at[j])
+        copy.start()
+        factor_copies.append(copy)
+    for j in range(STEPS):
         for h in range(2):
-            r = pltpu.make_async_copy(
-                sides.at[at, pl.ds(h * HALF, HALF)], out.at[2 * j + h, pl.ds(0, HALF)], sem_r.at[2 * j + h]
+            copy = pltpu.make_async_copy(
+                sides.at[place[j], pl.ds(h * HALF, HALF)], out.at[2 * j + h, pl.ds(0, HALF)], sem_r.at[2 * j + h]
             )
-            r.start()
-            sides_copies.append(r)
-    for c in copies:
-        c.wait()
+            copy.start()
+            side_copies.append(copy)
+    for copy in factor_copies:
+        copy.wait()
     for j in range(STEPS):
         at = place[j]
         for i in range(j):
@@ -67,33 +64,25 @@
             for s in range(SLOTS):
                 piece = jnp.where(columns[at, s] == i, rows_buf[j, s], piece)
             b = tri(j, i)
-            tri_buf[b // 2, pl.ds((b % 2) * SLICE, SLICE)] = piece
+            out[b // 2, pl.ds(HALF + (b % 2) * SLICE, SLICE)] = piece
     for b in range(tri(STEPS, 0), TRI):
-        tri_buf[b // 2, pl.ds((b % 2) * SLICE, SLICE)] = jnp.zeros((SLICE, BLOCK), jnp.float32)
-    o = pltpu.make_async_copy(tri_buf, out.at[:, pl.ds(HALF, 2 * SLICE)], sem_o)
-    o.start()
-    for c in sides_copies:
-        c.wait()
-    o.wait()
+        out[b // 2, pl.ds(HALF + (b % 2) * SLICE, SLICE)] = jnp.zeros((SLICE, BLOCK), jnp.float32)
+    for copy in side_copies:
+        copy.wait()
 
 
 def pack(place, columns, sides, factor):
+    smem = pl.BlockSpec(memory_space=pltpu.SMEM)
+    hbm = pl.BlockSpec(memory_space=pl.ANY)
     return pl.pallas_call(
         pack_kernel,
         out_shape=jax.ShapeDtypeStruct((RANKS, HALF + 2 * SLICE, BLOCK), jnp.float32),
-        in_specs=[
-            pl.BlockSpec(memory_space=pltpu.SMEM),
-            pl.BlockSpec(memory_space=pltpu.SMEM),
-            pl.BlockSpec(memory_space=pl.ANY),
-            pl.BlockSpec(memory_space=pl.ANY),
-        ],
-        out_specs=pl.BlockSpec(memory_space=pl.ANY),
+        in_specs=[smem, smem, hbm, hbm],
+        out_specs=pl.BlockSpec(memory_space=pltpu.VMEM),
         scratch_shapes=[
             pltpu.VMEM((STEPS, SLOTS, SLICE, BLOCK), jnp.float32),
-            pltpu.VMEM((RANKS, 2 * SLICE, BLOCK), jnp.float32),
             pltpu.SemaphoreType.DMA((STEPS,)),
             pltpu.SemaphoreType.DMA((2 * STEPS,)),
-            pltpu.SemaphoreType.DMA,
         ],
         name="pack",
     )(place, columns, sides, factor)
@@ -166,6 +155,7 @@
             pl.BlockSpec((STEPS + 1, BLOCK, 2 * BLOCK), lambda g: (0, 0, 0)),
         ],
         out_specs=pl.BlockSpec((ROWS_PER_STEP, BLOCK, BLOCK), lambda g: (g, 0, 0)),
+        compiler_params=pltpu.CompilerParams(vmem_limit_bytes=48 * 2**20),
         name="update",
     )(picks, sides, factor, pairs)
 

time: 148 us -> 146 us (0.986)
  Pallas kernels: 35.6 us -> 17.9 us
  waiting for transfers between devices: 22.7 us -> 37.6 us
    pallas_call x1, Pallas kernels: 18.4 us -> 3.44 us  [pack(): pl.pallas_call(pack_kernel, out_shape=jax.ShapeDtypeStruct((RANKS, HALF +...]
    all_gather x1, waiting for transfers between devices: 8.11 us -> 22.7 us  [local(): everything = lax.all_gather(factor_blocks, 'samp', axis=0, tiled=False)]
    pallas_call x1, Pallas kernels: 11.8 us -> 8.94 us  [update(): pl.pallas_call(update_kernel, grid=(rows // ROWS_PER_STEP,), out_shape=ja...]
    unnamed x13 -> x15, local copies, waits for them, and re-layouts: 2.35 us -> 3.32 us
  transfers between devices with their start and end apart: 3 -> 3, of which waited for: 3 -> 3; matrix products, arithmetic and copies ran while one was open for 4% -> 3% of each run, Pallas kernels for 16% -> 6%
where the time goes in v2:
time: 146 us; the launch traced here: 145 us
  blocking collectives  51.5 us (35%)
  waiting for transfers between devices  37.6 us (26%)
  between operations  20.1 us (14%)
  Pallas kernels  17.9 us (12%)
  starting transfers between devices  11.3 us (8%)
  local copies, waits for them, and re-layouts  5.46 us (4%)
    all_to_all x1, blocking collectives, local(): lax.all_to_all(jnp.broadcast_to(half, (RANKS,) + half.shape), 'samp', 0, 0)  35.3 us
    all_gather x1, waiting for transfers between devices, local(): everything = lax.all_gather(factor_blocks, 'samp', axis=0, tiled=False)  22.7 us
    all_gather x1, blocking collectives, local(): gathered = lax.all_gather(part, 'rows', axis=0, tiled=False)  16.3 us
    all_to_all x1, waiting for transfers between devices, local(): pieces = lax.all_to_all(payload, 'rows', 0, 0)  12 us
    all_to_all x1, starting transfers between devices, local(): pieces = lax.all_to_all(payload, 'rows', 0, 0)  9.99 us
    pallas_call x1, Pallas kernels, update(): pl.pallas_call(update_kernel, grid=(rows // ROWS_PER_STEP,), out_shape=ja...  8.94 us
    pallas_call x1, Pallas kernels, solve(): pl.pallas_call(solve_kernel, out_shape=(jax.ShapeDtypeStruct((STEPS, BLOC...  5.55 us
    pallas_call x1, Pallas kernels, pack(): pl.pallas_call(pack_kernel, out_shape=jax.ShapeDtypeStruct((RANKS, HALF +...  3.44 us
  transfers between devices with their start and end apart: 3, of which 3 were waited for; matrix products, arithmetic and copies ran while one was open for 3% of the time, Pallas kernels for 6%

profile of v2, /device:TPU:1, one launch (start us, length us, event | category | flops | bytes accessed | tf_op | source)
XLA Modules:
  0.0 145.3 jit_solution(7417456808819108748)
XLA Ops:
  7.2 0.0 all-gather.4.cloned.1.call-start
  7.2 0.7 all-gather.4.cloned.1.call-update
  7.9 1.4 copy.17.columns
  9.3 1.2 and_select_fusion
  10.5 0.0 copy-start.5
  10.5 3.4 %pack.1 = f32[16,80,128]{2,1,0:T(8,128)} custom-call(s32[8]{0:T(128)} %get-tuple-element.11.place, s32[36,6]{1,0:T(8,128)} %copy.17.columns, f32[36,128,128]{2,1,0:T(8,128)} %sides.3, f32[36,6,8,128]{3,2,1,0:T(8,128)} %factor.1), custom_call_target="tpu_custom_call" | custom-call | tf_op jit(solution)/shard_map/pack/pallas_call | solution.py:77
  13.9 10.0 %all-to-all-start = ((f32[16,80,128]{2,1,0:T(8,128)}), f32[16,80,128]{2,1,0:T(8,128)S(1)}, u32[]{:S(2)}, u32[]{:S(2)}) async-start(f32[16,80,128]{2,1,0:T(8,128)} %pack.1), calls=%async_computation | async-start | bytes 1310720 | tf_op jit(solution)/shard_map/all_to_all | solution.py:176
  23.9 0.0 copy-done.5
  23.9 0.7 gather_fusion
  24.6 0.0 copy-start.6
  24.6 0.0 copy-start.4
  24.6 0.7 fusion
  27.9 0.7 dynamic_slice.21
  32.0 12.0 %all-to-all-done = f32[16,80,128]{2,1,0:T(8,128)S(1)} async-done(((f32[16,80,128]{2,1,0:T(8,128)}), f32[16,80,128]{2,1,0:T(8,128)S(1)}, u32[]{:S(2)}, u32[]{:S(2)}) %all-to-all-start) | async-done | bytes 655392 | tf_op jit(solution)/shard_map/all_to_all | solution.py:176
  43.9 16.3 %all-gather = f32[1280,128]{1,0:T(8,128)S(1)} all-gather(f32[80,128]{1,0:T(8,128)S(1)} %pad_maximum_fusion), channel_id=2, replica_groups=mesh['rows'=16,'samp'=16] {'rows'}, dimensions={0}, use_global_device_ids=true | all-gather | bytes 696320 | tf_op jit(solution)/shard_map/all_gather | solution.py:185
  60.2 0.0 copy-start.3
  60.2 0.8 copy-done.3
  61.1 0.1 broadcast_in_dim.22
  61.2 0.0 copy-start
  61.2 35.3 %all_to_all.10.mine = f32[16,16,8,128]{3,2,1,0:T(8,128)S(1)} all-to-all(f32[16,16,8,128]{3,2,1,0:T(8,128)S(1)} %broadcast_in_dim.22), channel_id=1, replica_groups=mesh['rows'=16,'samp'=16] {'samp'}, dimensions={0} | all-to-all | bytes 2097152 | tf_op jit(solution)/shard_map/all_to_all | solution.py:189
  96.5 0.0 copy-start.2
  96.5 1.3 collective-permute-start
  97.8 0.0 copy-done.6
  97.8 0.1 select_reduce_fusion
  97.9 0.0 copy-done.4
  97.9 0.1 compare_select_fusion.picks
  97.9 2.2 %collective-permute-done.other = f32[16,16,8,128]{3,2,1,0:T(8,128)} collective-permute-done((f32[16,16,8,128]{3,2,1,0:T(8,128)S(1)}, f32[16,16,8,128]{3,2,1,0:T(8,128)}, u32[]{:S(2)}, u32[]{:S(2)}) %collective-permute-start) | collective-permute-done | bytes 1048608 | tf_op jit(solution)/shard_map/ppermute | solution.py:190
  100.2 0.0 copy-done.2
  100.2 5.6 %solve.1 = (f32[8,128,128]{2,1,0:T(8,128)}, bf16[9,128,256]{2,1,0:T(8,128)(2,1)}) custom-call(s32[1]{0:T(128)} %bitcast.core, f32[16,80,128]{2,1,0:T(8,128)} %bitcast.15, f32[16,16,8,128]{3,2,1,0:T(8,128)} %copy-done.2, f32[16,16,8,128]{3,2,1,0:T(8,128)} %collective-permute-done.other, f32[8,128,128]{2,1,0:T(8,128)} %inverse.1), custom_call_target="tpu_custom_call" | custom-call | tf_op jit(solution)/shard_map/solve/pallas_call | solution.py:115
  105.7 22.7 %all-gather.4.cloned.1.call-done = f32[576,6,8,128]{3,2,1,0:T(8,128)} async-done(((f32[36,6,8,128]{3,2,1,0:T(8,128)}), f32[576,6,8,128]{3,2,1,0:T(8,128)}) %all-gather.4.cloned.1.call-update) | async-done | bytes 14155792 | tf_op jit(solution)/shard_map/all_gather | solution.py:166
  128.4 0.0 copy-done
  128.4 0.0 copy-start.1
  128.5 1.1 copy-done.1
  129.5 8.9 %update.1 = f32[36,128,128]{2,1,0:T(8,128)} custom-call(s32[36,6]{1,0:T(8,128)S(1)} %compare_select_fusion.picks, f32[36,128,128]{2,1,0:T(8,128)S(1)} %copy-done, f32[16,36,6,8,128]{4,3,2,1,0:T(8,128)} %bitcast.13, bf16[9,128,256]{2,1,0:T(8,128)(2,1)S(1)} %copy-done.1), custom_call_target="tpu_custom_call" | custom-call | tf_op jit(solution)/shard_map/update/pallas_call | solution.py:147
  (9 shorter events, 0.0 us)
Async XLA Ops:
  7.2 121.3 %all-gather.4.cloned.1.call-start = ((), (), s32[]{:S(2)}) async-start(), calls=%async_computation.2 | async-start | bytes 15040512 | tf_op jit(solution)/shard_map/all_gather | solution.py:166
  10.5 13.4 %copy-start.5 = (s32[32]{0:T(128)S(1)}, s32[32]{0:T(128)}, u32[]{:S(2)}) copy-start(s32[32]{0:T(128)} %constant.76) | copy-start | bytes 388
  13.9 30.0 %all-to-all-start = ((f32[16,80,128]{2,1,0:T(8,128)}), f32[16,80,128]{2,1,0:T(8,128)S(1)}, u32[]{:S(2)}, u32[]{:S(2)}) async-start(f32[16,80,128]{2,1,0:T(8,128)} %pack.1), calls=%async_computation | async-start | bytes 1310720 | tf_op jit(solution)/shard_map/all_to_all | solution.py:176
  24.6 73.1 %copy-start.6 = (s32[8]{0:T(128)S(1)}, s32[8]{0:T(128)}, u32[]{:S(2)}) copy-start(s32[8]{0:T(128)} %param.9) | copy-start | bytes 100
  24.6 73.2 %copy-start.4 = (s32[36,6]{1,0:T(8,128)S(1)}, s32[36,6]{1,0:T(8,128)}, u32[]{:S(2)}) copy-start(s32[36,6]{1,0:T(8,128)} %copy.17.columns) | copy-start | bytes 2596
  60.2 0.9 copy-start.3
  61.2 67.3 %copy-start = (f32[36,128,128]{2,1,0:T(8,128)S(1)}, f32[36,128,128]{2,1,0:T(8,128)}, u32[]{:S(2)}) copy-start(f32[36,128,128]{2,1,0:T(8,128)} %sides.3) | copy-start | bytes 7077892
  96.5 3.7 %copy-start.2 = (f32[16,16,8,128]{3,2,1,0:T(8,128)}, f32[16,16,8,128]{3,2,1,0:T(8,128)S(1)}, u32[]{:S(2)}) copy-start(f32[16,16,8,128]{3,2,1,0:T(8,128)S(1)} %all_to_all.10.mine) | copy-start | bytes 3145732
  96.5 3.7 %collective-permute-start = (f32[16,16,8,128]{3,2,1,0:T(8,128)S(1)}, f32[16,16,8,128]{3,2,1,0:T(8,128)}, u32[]{:S(2)}, u32[]{:S(2)}) collective-permute-start(f32[16,16,8,128]{3,2,1,0:T(8,128)S(1)} %all_to_all.10.mine), channel_id=1, source_target_pairs={{0,16},{16,0},{32,48},{48,32},{64,80},{80,64},{96,112},{112,96},{1... | collective-permute-start | bytes 3145736 | tf_op jit(solution)/shard_map/ppermute | solution.py:190
  128.4 1.1 copy-start.1
Sparse Core Ops, SparseCore 0:
  10.4 117.9 all-gather.3

commit v3 on v2

v3 whole, which is shorter than its diff:
```python
import jax
import jax.numpy as jnp
from jax import lax
from jax.experimental import pallas as pl
from jax.experimental.pallas import tpu as pltpu
from jax.sharding import PartitionSpec as P

BLOCK = 128
STEPS = 8
SLOTS = 6
RANKS = 16
SIDE = 4
SLICE = BLOCK // RANKS
HALF = BLOCK // 2
TRI = 32
SETS = 3
GROUP = 8
EPILOGUE_ROWS = 6


def tri(k, i):
    return k * (k - 1) // 2 + i


TRI_PIVOT = [k for k in range(STEPS) for _ in range(k)] + [STEPS - 1] * (TRI - tri(STEPS, 0))
COLUMNS_OF_Y = [[SIDE * y + x for y in range(SIDE)] for x in range(SIDE)]
ROWS_OF_X = [[SIDE * y + x for x in range(SIDE)] for y in range(SIDE)]
NEAR_X = [(i, i ^ 1) for i in range(RANKS)]
NEAR_Y = [(i, i ^ SIDE) for i in range(RANKS)]
FAR_X = [(i, i // SIDE * SIDE + SIDE - 1 - i % SIDE) for i in range(RANKS)]
FAR_Y = [(i, (SIDE - 1 - i // SIDE) * SIDE + i % SIDE) for i in range(RANKS)]
OTHER_CORE = [(i, i ^ 1) for i in range(RANKS)]


def split(x):
    hi = x.astype(jnp.bfloat16)
    lo = (x - hi.astype(jnp.float32)).astype(jnp.bfloat16)
    return hi, lo


def dot(a, b):
    return lax.dot_general(a, b, (((1,), (0,)), ((), ())), preferred_element_type=jnp.float32)


def pack_kernel(place, columns, sides, factor, out, rows_buf, sem_f, sem_r):
    factor_copies, side_copies = [], []
    for j in range(STEPS):
        copy = pltpu.make_async_copy(factor.at[place[j]], rows_buf.at[j], sem_f.at[j])
        copy.start()
        factor_copies.append(copy)
    for j in range(STEPS):
        for h in range(2):
            copy = pltpu.make_async_copy(
                sides.at[place[j], pl.ds(h * HALF, HALF)], out.at[2 * j + h, pl.ds(0, HALF)], sem_r.at[2 * j + h]
            )
            copy.start()
            side_copies.append(copy)
    for copy in factor_copies:
        copy.wait()
    for j in range(STEPS):
        at = place[j]
        for i in range(j):
            piece = jnp.zeros((SLICE, BLOCK), jnp.float32)
            for s in range(SLOTS):
                piece = jnp.where(columns[at, s] == i, rows_buf[j, s], piece)
            b = tri(j, i)
            out[b // 2, pl.ds(HALF + (b % 2) * SLICE, SLICE)] = piece
    for b in range(tri(STEPS, 0), TRI):
        out[b // 2, pl.ds(HALF + (b % 2) * SLICE, SLICE)] = jnp.zeros((SLICE, BLOCK), jnp.float32)
    for copy in side_copies:
        copy.wait()


def pack(place, columns, sides, factor):
    smem = pl.BlockSpec(memory_space=pltpu.SMEM)
    hbm = pl.BlockSpec(memory_space=pl.ANY)
    return pl.pallas_call(
        pack_kernel,
        out_shape=jax.ShapeDtypeStruct((RANKS, HALF + 2 * SLICE, BLOCK), jnp.float32),
        in_specs=[smem, smem, hbm, hbm],
        out_specs=pl.BlockSpec(memory_space=pltpu.VMEM),
        scratch_shapes=[
            pltpu.VMEM((STEPS, SLOTS, SLICE, BLOCK), jnp.float32),
            pltpu.SemaphoreType.DMA((STEPS,)),
            pltpu.SemaphoreType.DMA((2 * STEPS,)),
        ],
        name="pack",
    )(place, columns, sides, factor)


def solve_kernel(core, first, second, third, mine, other, inverse, solved, pairs, side):
    flag = core[0]

    def factor(k, i):
        b = tri(k, i)
        own = mine[:, b % RANKS].reshape(BLOCK, BLOCK)
        far = other[:, b % RANKS].reshape(BLOCK, BLOCK)
        return jnp.where(flag == b // RANKS, own, far)

    def product(a, hi, lo):
        ah, al = split(a)
        full = dot(ah, jnp.concatenate([hi, lo], axis=1))
        return full[:, : SETS * BLOCK] + full[:, SETS * BLOCK :] + dot(al, hi)

    for j in range(STEPS):
        for t, ref in enumerate((first, second, third)):
            side[j, :, t * BLOCK : (t + 1) * BLOCK] = ref[2 * j : 2 * j + 2, :HALF].reshape(BLOCK, BLOCK)
    for j in range(STEPS):
        hi, lo = split(side[j])
        x = product(inverse[j], hi, lo)
        solved[j] = x[:, :BLOCK]
        hi, lo = split(x)
        for t in range(SETS):
            pairs[t, j * BLOCK : (j + 1) * BLOCK, :BLOCK] = hi[:, t * BLOCK : (t + 1) * BLOCK]
            pairs[t, j * BLOCK : (j + 1) * BLOCK, BLOCK:] = lo[:, t * BLOCK : (t + 1) * BLOCK]
        for k in range(j + 1, STEPS):
            side[k] = side[k] - product(factor(k, j), hi, lo)


def solve(core, first, second, third, mine, other, inverse):
    vmem = pl.BlockSpec(memory_space=pltpu.VMEM)
    return pl.pallas_call(
        solve_kernel,
        out_shape=(
            jax.ShapeDtypeStruct((STEPS, BLOCK, BLOCK), jnp.float32),
            jax.ShapeDtypeStruct((SETS, STEPS * BLOCK, 2 * BLOCK), jnp.bfloat16),
        ),
        in_specs=[pl.BlockSpec(memory_space=pltpu.SMEM)] + [vmem] * 6,
        out_specs=(vmem, vmem),
        scratch_shapes=[pltpu.VMEM((STEPS, BLOCK, SETS * BLOCK), jnp.float32)],
        compiler_params=pltpu.CompilerParams(vmem_limit_bytes=48 * 2**20),
        name="solve",
    )(core, first, second, third, mine, other, inverse)


def product_kernel(partner, rows, slots, order, factor, pairs, near, far, buf, high, low, sems):
    copies = []
    for m in range(GROUP):
        copy = pltpu.make_async_copy(factor.at[order[m]], buf.at[m], sems.at[m])
        copy.start()
        copies.append(copy)
    for copy in copies:
        copy.wait()
    height = GROUP * SLICE

    def build(r, carry):
        at_row = pl.multiple_of(r * height, height)
        for c in range(STEPS):
            at = slots[r, c]
            block = buf[:, r, jnp.minimum(at, SLOTS - 1)].reshape(height, BLOCK)
            hi, lo = split(jnp.where(at < SLOTS, block, 0.0))
            high[pl.ds(at_row, height), c * BLOCK : (c + 1) * BLOCK] = hi
            low[pl.ds(at_row, height), c * BLOCK : (c + 1) * BLOCK] = lo
        return carry

    lax.fori_loop(0, rows, build, 0)
    own, theirs = pairs[0], pairs[partner]
    wide = jnp.concatenate([own, theirs], axis=1)
    tops = jnp.concatenate([own[:, :BLOCK], theirs[:, :BLOCK]], axis=1)
    chunk = rows * height // 3
    for g in range(3):
        full = dot(high[g * chunk : (g + 1) * chunk], wide)
        rest = dot(low[g * chunk : (g + 1) * chunk], tops)
        a = full[:, :BLOCK] + full[:, BLOCK : 2 * BLOCK] + rest[:, :BLOCK]
        b = full[:, 2 * BLOCK : 3 * BLOCK] + full[:, 3 * BLOCK :] + rest[:, BLOCK:]
        near[g * (rows // 3) : (g + 1) * (rows // 3)] = a.reshape(rows // 3, height, BLOCK)
        far[g * (rows // 3) : (g + 1) * (rows // 3)] = b.reshape(rows // 3, height, BLOCK)


def product(partner, slots, order, factor, pairs):
    rows = slots.shape[0]
    smem = pl.BlockSpec(memory_space=pltpu.SMEM)
    vmem = pl.BlockSpec(memory_space=pltpu.VMEM)
    height = GROUP * SLICE
    piece = jax.ShapeDtypeStruct((rows, height, BLOCK), jnp.float32)
    return pl.pallas_call(
        lambda *refs: product_kernel(partner, rows, *refs),
        out_shape=(piece, piece),
        in_specs=[smem, smem, pl.BlockSpec(memory_space=pl.ANY), vmem],
        out_specs=(vmem, vmem),
        scratch_shapes=[
            pltpu.VMEM((GROUP, rows, SLOTS, SLICE, BLOCK), jnp.float32),
            pltpu.VMEM((rows * height, STEPS * BLOCK), jnp.bfloat16),
            pltpu.VMEM((rows * height, STEPS * BLOCK), jnp.bfloat16),
            pltpu.SemaphoreType.DMA((GROUP,)),
        ],
        compiler_params=pltpu.CompilerParams(vmem_limit_bytes=48 * 2**20),
        name="product",
    )(slots, order, factor, pairs)


def finish_kernel(half_steps, spot, sides, near0, far0, near1, far1, out):
    step = pl.program_id(0)

    def place(near, far, parts, swap):
        height = BLOCK // (2 * parts)
        for r in range(EPILOGUE_ROWS):
            for q in range(parts):
                a, b = near[r, q * height : (q + 1) * height], far[r, q * height : (q + 1) * height]
                at = 2 * q * height
                out[r, at : at + height] = sides[r, at : at + height] - jnp.where(swap, b, a)
                at = at + height
                out[r, at : at + height] = sides[r, at : at + height] - jnp.where(swap, a, b)

    @pl.when(step < half_steps)
    def _():
        place(near0, far0, SIDE, spot[0] == 1)

    @pl.when(step >= half_steps)
    def _():
        place(near1, far1, 1, spot[1] == 1)


def finish(spot, sides, near0, far0, near1, far1):
    rows = sides.shape[0]
    half_steps = rows // 2 // EPILOGUE_ROWS
    height = GROUP * SLICE
    whole = pl.BlockSpec((EPILOGUE_ROWS, BLOCK, BLOCK), lambda g: (g, 0, 0))
    early = pl.BlockSpec((EPILOGUE_ROWS, height, BLOCK), lambda g: (jnp.minimum(g, half_steps - 1), 0, 0))
    late = pl.BlockSpec((EPILOGUE_ROWS, height, BLOCK), lambda g: (jnp.maximum(g - half_steps, 0), 0, 0))
    return pl.pallas_call(
        lambda *refs: finish_kernel(half_steps, *refs),
        grid=(rows // EPILOGUE_ROWS,),
        out_shape=jax.ShapeDtypeStruct(sides.shape, jnp.float32),
        in_specs=[pl.BlockSpec(memory_space=pltpu.SMEM), whole, early, early, late, late],
        out_specs=whole,
        name="finish",
    )(spot, sides, near0, far0, near1, far1)


def local(right_sides, factor_blocks, block_columns, pivot_rows, diag_inverse):
    row_count = right_sides.shape[0]
    half_rows = row_count // 2
    rank = lax.axis_index("rows")
    here = lax.axis_index("samp")
    y, x = here // SIDE, here % SIDE

    top, bottom = factor_blocks[:half_rows], factor_blocks[half_rows:]
    top = jnp.stack([top, lax.ppermute(top, "samp", NEAR_X)])
    bottom = jnp.stack([bottom, lax.ppermute(bottom, "samp", NEAR_Y)])
    shape = (GROUP, half_rows, SLOTS, SLICE, BLOCK)
    top = lax.all_gather(top, "samp", axis_index_groups=COLUMNS_OF_Y).reshape(shape)
    bottom = lax.all_gather(bottom, "samp", axis_index_groups=ROWS_OF_X).reshape(shape)
    group = jnp.arange(GROUP, dtype=jnp.int32)
    top_order = (group // 2) * 2 + ((group % 2) ^ (x % 2))
    bottom_order = (group % SIDE) * 2 + ((group // SIDE) ^ (y % 2))

    owner = pivot_rows // row_count
    place = pivot_rows % row_count
    ids = rank * row_count + jnp.arange(row_count, dtype=jnp.int32)
    targets = jnp.arange(STEPS, dtype=jnp.int32)
    row_rank = STEPS + jnp.sum(jnp.where(ids[:, None] == pivot_rows[None, :], targets - STEPS, 0), axis=1)
    picks = jnp.where(block_columns < row_rank[:, None], block_columns, STEPS)
    slots = jnp.min(
        jnp.where(picks[:, None, :] == targets[None, :, None], jnp.arange(SLOTS, dtype=jnp.int32), SLOTS), axis=2
    )

    payload = pack(place, block_columns, right_sides, factor_blocks)
    pieces = lax.all_to_all(payload, "rows", 0, 0)
    tri_owner = owner[jnp.array(TRI_PIVOT, jnp.int32)]
    part = jnp.concatenate(
        [
            lax.dynamic_slice(pieces, (owner[rank // 2], 0, 0), (1, HALF, BLOCK))[0],
            lax.dynamic_slice(pieces, (tri_owner[2 * rank], HALF, 0), (1, SLICE, BLOCK))[0],
            lax.dynamic_slice(pieces, (tri_owner[2 * rank + 1], HALF + SLICE, 0), (1, SLICE, BLOCK))[0],
        ]
    )
    gathered = lax.all_gather(part, "rows", axis=0, tiled=False)
    slices = gathered[:, HALF:].reshape(TRI, SLICE, BLOCK)
    core = rank % 2
    half = lax.dynamic_slice(slices, (core * RANKS, 0, 0), (RANKS, SLICE, BLOCK))
    mine = lax.all_to_all(jnp.broadcast_to(half, (RANKS,) + half.shape), "samp", 0, 0)
    other = lax.ppermute(mine, "rows", OTHER_CORE)
    own = gathered[:, :HALF]
    across_x = lax.ppermute(own, "samp", FAR_X)
    across_y = lax.ppermute(own, "samp", FAR_Y)
    solved, pairs = solve(core.reshape(1), own, across_x, across_y, mine, other, diag_inverse)
    near0, send0 = product(1, slots[:half_rows], top_order, top, pairs)
    far0 = lax.ppermute(send0, "samp", FAR_X)
    near1, send1 = product(2, slots[half_rows:], bottom_order, bottom, pairs)
    far1 = lax.ppermute(send1, "samp", FAR_Y)
    spot = jnp.stack([x // 2, y // 2])
    return solved, finish(spot, right_sides, near0, far0, near1, far1)


def solution(mesh):
    placed = (P("rows", None, "samp"), P("rows", None, "samp", None), P("rows", None), P(), P())
    return jax.shard_map(
        local,
        mesh=mesh,
        in_specs=placed,
        out_specs=(P(None, None, "samp"), P("rows", None, "samp")),
        check_vma=False,
    )
```

time: 146 us -> 195 us (1.34)
  waiting for transfers between devices: 37.6 us -> 83.5 us
  blocking collectives: 51.5 us -> 17.7 us
  starting transfers between devices: 11.3 us -> 27.1 us
  local copies, waits for them, and re-layouts: 5.46 us -> 14.9 us
  Pallas kernels: 17.9 us -> 26.4 us
  other arithmetic: 1.37 us -> 3.42 us
    ppermute x1 -> x7, waiting for transfers between devices: 2.24 us -> 42.9 us  [the longest x1 13.4 us: local(): across_y = lax.ppermute(own, 'samp', FAR_Y)]
    all_to_all x1 -> x0, blocking collectives: 35.3 us -> none  [local(): lax.all_to_all(jnp.broadcast_to(half, (RANKS,) + half.shape), 'samp', 0, 0)]
    all_to_all x0 -> x1, waiting for transfers between devices: none -> 28.5 us  [local(): lax.all_to_all(jnp.broadcast_to(half, (RANKS,) + half.shape), 'samp', 0, 0)]
    all_gather x1 -> x2, waiting for transfers between devices: 22.7 us -> 0.01 us  [the longest x1 0.01 us: local(): lax.all_gather(top, 'samp', axis_index_groups=COLUMNS_OF_Y).reshape(shape)]
    pallas_call x1 -> x3, Pallas kernels: 8.94 us -> 17 us  [the longest x2 11.4 us: product(): pl.pallas_call(lambda *refs: product_kernel(partner, rows, *refs), out_sh...]
    ppermute x1 -> x7, starting transfers between devices: 1.3 us -> 9.22 us  [the longest x1 2.66 us: local(): bottom = jnp.stack([bottom, lax.ppermute(bottom, 'samp', NEAR_Y)])]
    all_to_all x0 -> x1, starting transfers between devices: none -> 6.79 us  [local(): lax.all_to_all(jnp.broadcast_to(half, (RANKS,) + half.shape), 'samp', 0, 0)]
    unnamed x15 -> x25, local copies, waits for them, and re-layouts: 3.32 us -> 8.38 us
  transfers between devices with their start and end apart: 3 -> 11, of which waited for: 3 -> 7; matrix products, arithmetic and copies ran while one was open for 3% -> 4% of each run, Pallas kernels for 6% -> 11%
where the time goes in v3:
time: 195 us; the launch traced here: 193 us
  waiting for transfers between devices  83.5 us (43%)
  starting transfers between devices  27.1 us (14%)
  Pallas kernels  26.4 us (14%)
  between operations  20.1 us (10%)
  blocking collectives  17.7 us (9%)
  local copies, waits for them, and re-layouts  14.9 us (8%)
  other arithmetic  3.42 us (2%)
    all_to_all x1, waiting for transfers between devices, local(): lax.all_to_all(jnp.broadcast_to(half, (RANKS,) + half.shape), 'samp', 0, 0)  28.5 us
    all_gather x1, blocking collectives, local(): gathered = lax.all_gather(part, 'rows', axis=0, tiled=False)  17.7 us
    ppermute x1, waiting for transfers between devices, local(): across_y = lax.ppermute(own, 'samp', FAR_Y)  13.4 us
    all_to_all x1, waiting for transfers between devices, local(): pieces = lax.all_to_all(payload, 'rows', 0, 0)  12.1 us
    pallas_call x2, Pallas kernels, product(): pl.pallas_call(lambda *refs: product_kernel(partner, rows, *refs), out_sh...  11.4 us
    all_to_all x1, starting transfers between devices, local(): pieces = lax.all_to_all(payload, 'rows', 0, 0)  11.1 us
    ppermute x1, waiting for transfers between devices, local(): bottom = jnp.stack([bottom, lax.ppermute(bottom, 'samp', NEAR_Y)])  8.74 us
    ppermute x1, waiting for transfers between devices, local(): top = jnp.stack([top, lax.ppermute(top, 'samp', NEAR_X)])  8.55 us
  transfers between devices with their start and end apart: 11, of which 7 were waited for; matrix products, arithmetic and copies ran while one was open for 4% of the time, Pallas kernels for 11%

profile of v3, /device:TPU:1, one launch (start us, length us, event | category | flops | bytes accessed | tf_op | source)
XLA Modules:
  0.0 193.1 jit_solution(11211362682023642627)
XLA Ops:
  7.2 0.0 all-gather.6.cloned.1.call-start
  7.2 1.3 slice_bitcast_fusion
  8.5 2.1 %collective-permute-start.3 = (f32[18,6,8,128]{3,2,1,0:T(8,128)S(1)}, f32[18,6,8,128]{3,2,1,0:T(8,128)S(1)}, u32[]{:S(2)}, u32[]{:S(2)}) collective-permute-start(f32[18,6,8,128]{3,2,1,0:T(8,128)S(1)} %get-tuple-element.17), channel_id=1, source_target_pairs={{0,1},{1,0},{2,3},{3,2},{4,5},{5,4},{6,7},{7,6},{8,9},{9,8},{10,11... | collective-permute-start | bytes 1327112 | tf_op jit(solution)/shard_map/ppermute | solution.py:239
  10.6 8.6 %collective-permute-done.3 = f32[18,6,8,128]{3,2,1,0:T(8,128)S(1)} collective-permute-done((f32[18,6,8,128]{3,2,1,0:T(8,128)S(1)}, f32[18,6,8,128]{3,2,1,0:T(8,128)S(1)}, u32[]{:S(2)}, u32[]{:S(2)}) %collective-permute-start.3) | collective-permute-done | bytes 442400 | tf_op jit(solution)/shard_map/ppermute | solution.py:239
  19.2 1.0 pad_maximum_fusion
  20.2 0.0 all-gather.8.cloned.1.call-start
  20.3 2.7 %collective-permute-start.5 = (f32[18,6,8,128]{3,2,1,0:T(8,128)S(1)}, f32[18,6,8,128]{3,2,1,0:T(8,128)S(1)}, u32[]{:S(2)}, u32[]{:S(2)}) collective-permute-start(f32[18,6,8,128]{3,2,1,0:T(8,128)S(1)} %get-tuple-element.16), channel_id=1, source_target_pairs={{0,4},{1,5},{2,6},{3,7},{4,0},{5,1},{6,2},{7,3},{8,12},{9,13},{10,... | collective-permute-start | bytes 1327112 | tf_op jit(solution)/shard_map/ppermute | solution.py:240
  22.9 8.7 %collective-permute-done.5 = f32[18,6,8,128]{3,2,1,0:T(8,128)S(1)} collective-permute-done((f32[18,6,8,128]{3,2,1,0:T(8,128)S(1)}, f32[18,6,8,128]{3,2,1,0:T(8,128)S(1)}, u32[]{:S(2)}, u32[]{:S(2)}) %collective-permute-start.5) | collective-permute-done | bytes 442400 | tf_op jit(solution)/shard_map/ppermute | solution.py:240
  31.7 1.0 pad_maximum_fusion.1
  32.7 0.7 copy.14.columns
  33.4 0.6 and_select_fusion.4
  34.0 3.4 %pack.1 = f32[16,80,128]{2,1,0:T(8,128)} custom-call(s32[8]{0:T(128)} %get-tuple-element.25.place, s32[36,6]{1,0:T(8,128)} %copy.14.columns, f32[36,128,128]{2,1,0:T(8,128)} %refs_1_.1, f32[36,6,8,128]{3,2,1,0:T(8,128)} %factor.1), custom_call_target="tpu_custom_call" | custom-call | tf_op jit(solution)/shard_map/pack/pallas_call | solution.py:77
  37.5 11.1 %all-to-all-start = ((f32[16,80,128]{2,1,0:T(8,128)}), f32[16,80,128]{2,1,0:T(8,128)S(1)}, u32[]{:S(2)}, u32[]{:S(2)}) async-start(f32[16,80,128]{2,1,0:T(8,128)} %pack.1), calls=%async_computation | async-start | bytes 1310720 | tf_op jit(solution)/shard_map/all_to_all | solution.py:259
  48.5 0.6 dynamic_slice.21
  50.5 0.7 gather_fusion
  51.2 0.7 fusion.6
  56.5 12.1 %all-to-all-done = f32[16,80,128]{2,1,0:T(8,128)S(1)} async-done(((f32[16,80,128]{2,1,0:T(8,128)}), f32[16,80,128]{2,1,0:T(8,128)S(1)}, u32[]{:S(2)}, u32[]{:S(2)}) %all-to-all-start) | async-done | bytes 655392 | tf_op jit(solution)/shard_map/all_to_all | solution.py:259
  68.6 17.7 %all-gather = f32[1280,128]{1,0:T(8,128)} all-gather(f32[80,128]{1,0:T(8,128)S(1)} %pad_maximum_fusion.2), channel_id=2, replica_groups=mesh['rows'=16,'samp'=16] {'rows'}, dimensions={0}, use_global_device_ids=true | all-gather | bytes 696320 | tf_op jit(solution)/shard_map/all_gather | solution.py:268
  86.2 0.9 slice.27
  87.2 1.1 broadcast_in_dim.32
  88.2 6.8 %all-to-all-start.1 = ((f32[16,16,8,128]{3,2,1,0:T(8,128)}), f32[16,16,8,128]{3,2,1,0:T(8,128)S(1)}, u32[]{:S(2)}, u32[]{:S(2)}) async-start(f32[16,16,8,128]{3,2,1,0:T(8,128)} %broadcast_in_dim.32), calls=%async_computation.1 | async-start | bytes 2097152 | tf_op jit(solution)/shard_map/all_to_all | solution.py:272
  95.1 28.5 %all-to-all-done.1.mine = f32[16,16,8,128]{3,2,1,0:T(8,128)S(1)} async-done(((f32[16,16,8,128]{3,2,1,0:T(8,128)}), f32[16,16,8,128]{3,2,1,0:T(8,128)S(1)}, u32[]{:S(2)}, u32[]{:S(2)}) %all-to-all-start.1) | async-done | bytes 1048608 | tf_op jit(solution)/shard_map/all_to_all | solution.py:272
  123.6 1.3 collective-permute-start.2
  124.9 0.1 select_reduce_fusion.1
  125.0 1.1 slice.26.first
  126.1 0.7 collective-permute-start.1
  126.8 0.6 collective-permute-start
  127.4 0.1 fusion.5
  127.4 0.1 copy.18.refs_0_
  127.5 0.1 copy.17.refs_0_
  127.6 13.4 %collective-permute-done.1.third = f32[16,64,128]{2,1,0:T(8,128)S(1)} collective-permute-done((f32[16,64,128]{2,1,0:T(8,128)S(1)}, f32[16,64,128]{2,1,0:T(8,128)S(1)}, u32[]{:S(2)}, u32[]{:S(2)}) %collective-permute-start.1) | collective-permute-done | bytes 524320 | tf_op jit(solution)/shard_map/ppermute | solution.py:276
  141.1 0.8 copy-done.5
  141.9 1.0 copy-done
  142.8 1.2 copy-done.1
  144.1 1.0 copy-done.4
  145.1 1.0 copy-done.6
  146.1 6.0 %solve.1 = (f32[8,128,128]{2,1,0:T(8,128)}, bf16[3,1024,256]{2,1,0:T(8,128)(2,1)S(1)}) custom-call(s32[1]{0:T(128)} %bitcast.core, f32[16,64,128]{2,1,0:T(8,128)S(1)} %slice.26.first, f32[16,64,128]{2,1,0:T(8,128)} %collective-permute-done.second, f32[16,64,128]{2,1,0:T(8,128)S(1)} %copy-done.6, f32[16,16,8,128]{3,2,1,0:T(8,128)S(1)} %all-to-all-done.1.mine, ...), custom_call_target="tpu_custom_call" | custom-call | tf_op jit(solution)/shard_map/solve/pallas_call | solution.py:122
  152.1 5.7 %product.2 = (f32[18,64,128]{2,1,0:T(8,128)S(1)}, f32[18,64,128]{2,1,0:T(8,128)S(1)}) custom-call(s32[18,8]{1,0:T(8,128)S(1)} %copy.17.refs_0_, s32[8]{0:T(128)S(1)} %fusion.1.refs_1_, f32[8,18,6,8,128]{4,3,2,1,0:T(8,128)} %all-gather.6.cloned.1.call-done.refs_2_, bf16[3,1024,256]{2,1,0:T(8,128)(2,1)S(1)} %get-tuple-element.9.refs_3_), custom_call_target="tpu_custom_call" | custom-call | tf_op jit(solution)/shard_map/product/pallas_call | solution.py:176
  157.8 0.8 copy-done.2
  158.6 0.1 collective-permute-start.4
  158.7 5.7 %product.3 = (f32[18,64,128]{2,1,0:T(8,128)S(1)}, f32[18,64,128]{2,1,0:T(8,128)S(1)}) custom-call(s32[18,8]{1,0:T(8,128)S(1)} %copy.18.refs_0_, s32[8]{0:T(128)S(1)} %fusion.4.refs_1_, f32[8,18,6,8,128]{4,3,2,1,0:T(8,128)} %all-gather.8.cloned.1.call-done.refs_2_, bf16[3,1024,256]{2,1,0:T(8,128)(2,1)S(1)} %get-tuple-element.9.refs_3_), custom_call_target="tpu_custom_call" | custom-call | tf_op jit(solution)/shard_map/product/pallas_call | solution.py:176
  164.4 0.8 copy-done.3
  165.2 1.8 collective-permute-start.6
  167.0 0.6 pad_add_fusion.refs_0_
  167.7 6.4 %collective-permute-done.4.refs_3_ = f32[18,64,128]{2,1,0:T(8,128)} collective-permute-done((f32[18,64,128]{2,1,0:T(8,128)S(1)}, f32[18,64,128]{2,1,0:T(8,128)}, u32[]{:S(2)}, u32[]{:S(2)}) %collective-permute-start.4) | collective-permute-done | bytes 589856 | tf_op jit(solution)/shard_map/ppermute | solution.py:279
  174.1 5.7 %collective-permute-done.6.refs_5_ = f32[18,64,128]{2,1,0:T(8,128)S(1)} collective-permute-done((f32[18,64,128]{2,1,0:T(8,128)S(1)}, f32[18,64,128]{2,1,0:T(8,128)S(1)}, u32[]{:S(2)}, u32[]{:S(2)}) %collective-permute-start.6) | collective-permute-done | bytes 589856 | tf_op jit(solution)/shard_map/ppermute | solution.py:281
  179.9 0.8 copy-done.7
  180.7 5.6 %finish.1 = f32[36,128,128]{2,1,0:T(8,128)} custom-call(s32[2]{0:T(128)} %pad_add_fusion.refs_0_, f32[36,128,128]{2,1,0:T(8,128)} %refs_1_.1, f32[18,64,128]{2,1,0:T(8,128)} %copy-done.2, f32[18,64,128]{2,1,0:T(8,128)} %collective-permute-done.4.refs_3_, f32[18,64,128]{2,1,0:T(8,128)} %copy-done.3, f32[18,64,128]{2,1,0:T(8,128)} %copy-done.7), custom_call_target="tpu_custom_call" | custom-call | tf_op jit(solution)/shard_map/finish/pallas_call | solution.py:221
  (32 shorter events, 0.1 us)
Async XLA Ops:
  7.2 144.9 %all-gather.6.cloned.1.call-start = ((), (), s32[]{:S(2)}) async-start(), calls=%async_computation.2 | async-start | bytes 4423680 | tf_op jit(solution)/shard_map/all_gather | solution.py:242
  8.5 10.7 %collective-permute-start.3 = (f32[18,6,8,128]{3,2,1,0:T(8,128)S(1)}, f32[18,6,8,128]{3,2,1,0:T(8,128)S(1)}, u32[]{:S(2)}, u32[]{:S(2)}) collective-permute-start(f32[18,6,8,128]{3,2,1,0:T(8,128)S(1)} %get-tuple-element.17), channel_id=1, source_target_pairs={{0,1},{1,0},{2,3},{3,2},{4,5},{5,4},{6,7},{7,6},{8,9},{9,8},{10,11... | collective-permute-start | bytes 1327112 | tf_op jit(solution)/shard_map/ppermute | solution.py:239
  19.2 13.5 %copy-start.8 = (s32[36,6]{0,1:T(8,128)S(1)}, s32[36,6]{0,1:T(8,128)}, u32[]{:S(2)}) copy-start(s32[36,6]{0,1:T(8,128)} %param.8) | copy-start | bytes 2596
  19.2 14.2 %copy-start.10 = (s32[8]{0:T(128)S(1)}, s32[8]{0:T(128)}, u32[]{:S(2)}) copy-start(s32[8]{0:T(128)} %param.9) | copy-start | bytes 100
  20.2 138.4 %all-gather.8.cloned.1.call-start = ((), (), s32[]{:S(2)}) async-start(), calls=%async_computation.3 | async-start | bytes 4423680 | tf_op jit(solution)/shard_map/all_gather | solution.py:243
  20.3 11.4 %collective-permute-start.5 = (f32[18,6,8,128]{3,2,1,0:T(8,128)S(1)}, f32[18,6,8,128]{3,2,1,0:T(8,128)S(1)}, u32[]{:S(2)}, u32[]{:S(2)}) collective-permute-start(f32[18,6,8,128]{3,2,1,0:T(8,128)S(1)} %get-tuple-element.16), channel_id=1, source_target_pairs={{0,4},{1,5},{2,6},{3,7},{4,0},{5,1},{6,2},{7,3},{8,12},{9,13},{10,... | collective-permute-start | bytes 1327112 | tf_op jit(solution)/shard_map/ppermute | solution.py:240
  34.0 16.4 %copy-start.9 = (s32[32]{0:T(128)S(1)}, s32[32]{0:T(128)}, u32[]{:S(2)}) copy-start(s32[32]{0:T(128)} %constant.153) | copy-start | bytes 388
  37.5 31.1 %all-to-all-start = ((f32[16,80,128]{2,1,0:T(8,128)}), f32[16,80,128]{2,1,0:T(8,128)S(1)}, u32[]{:S(2)}, u32[]{:S(2)}) async-start(f32[16,80,128]{2,1,0:T(8,128)} %pack.1), calls=%async_computation | async-start | bytes 1310720 | tf_op jit(solution)/shard_map/all_to_all | solution.py:259
  88.2 35.4 %all-to-all-start.1 = ((f32[16,16,8,128]{3,2,1,0:T(8,128)}), f32[16,16,8,128]{3,2,1,0:T(8,128)S(1)}, u32[]{:S(2)}, u32[]{:S(2)}) async-start(f32[16,16,8,128]{3,2,1,0:T(8,128)} %broadcast_in_dim.32), calls=%async_computation.1 | async-start | bytes 2097152 | tf_op jit(solution)/shard_map/all_to_all | solution.py:272
  123.6 18.2 %collective-permute-start.2 = (f32[16,16,8,128]{3,2,1,0:T(8,128)S(1)}, f32[16,16,8,128]{3,2,1,0:T(8,128)S(1)}, u32[]{:S(2)}, u32[]{:S(2)}) collective-permute-start(f32[16,16,8,128]{3,2,1,0:T(8,128)S(1)} %all-to-all-done.1.mine), channel_id=1, source_target_pairs={{0,16},{16,0},{32,48},{48,32},{64,80},{80,64},{96,112},{112,96},{1... | collective-permute-start | bytes 3145736 | tf_op jit(solution)/shard_map/ppermute | solution.py:273
  126.1 15.0 %collective-permute-start.1 = (f32[16,64,128]{2,1,0:T(8,128)S(1)}, f32[16,64,128]{2,1,0:T(8,128)S(1)}, u32[]{:S(2)}, u32[]{:S(2)}) collective-permute-start(f32[16,64,128]{2,1,0:T(8,128)S(1)} %slice.26.first), channel_id=1, source_target_pairs={{0,12},{1,13},{2,14},{3,15},{4,8},{5,9},{6,10},{7,11},{8,4},{9,5},... | collective-permute-start | bytes 1572872 | tf_op jit(solution)/shard_map/ppermute | solution.py:276
  126.8 15.1 %collective-permute-start = (f32[16,64,128]{2,1,0:T(8,128)S(1)}, f32[16,64,128]{2,1,0:T(8,128)}, u32[]{:S(2)}, u32[]{:S(2)}) collective-permute-start(f32[16,64,128]{2,1,0:T(8,128)S(1)} %slice.26.first), channel_id=1, source_target_pairs={{0,3},{1,2},{2,1},{3,0},{4,7},{5,6},{6,5},{7,4},{8,11},{9,10},{10,... | collective-permute-start | bytes 1572872 | tf_op jit(solution)/shard_map/ppermute | solution.py:275
  141.1 0.8 copy-start.5
  141.9 1.0 copy-start
  142.8 1.2 copy-start.1
  144.0 1.0 copy-start.4
  145.1 1.0 copy-start.6
  157.8 0.8 copy-start.2
  158.6 15.5 %collective-permute-start.4 = (f32[18,64,128]{2,1,0:T(8,128)S(1)}, f32[18,64,128]{2,1,0:T(8,128)}, u32[]{:S(2)}, u32[]{:S(2)}) collective-permute-start(f32[18,64,128]{2,1,0:T(8,128)S(1)} %get-tuple-element.11), channel_id=1, source_target_pairs={{0,3},{1,2},{2,1},{3,0},{4,7},{5,6},{6,5},{7,4},{8,11},{9,10},{10,... | collective-permute-start | bytes 1769480 | tf_op jit(solution)/shard_map/ppermute | solution.py:279
  164.4 0.8 copy-start.3
  165.2 14.7 %collective-permute-start.6 = (f32[18,64,128]{2,1,0:T(8,128)S(1)}, f32[18,64,128]{2,1,0:T(8,128)S(1)}, u32[]{:S(2)}, u32[]{:S(2)}) collective-permute-start(f32[18,64,128]{2,1,0:T(8,128)S(1)} %get-tuple-element.13), channel_id=1, source_target_pairs={{0,12},{1,13},{2,14},{3,15},{4,8},{5,9},{6,10},{7,11},{8,4},{9,5},... | collective-permute-start | bytes 1769480 | tf_op jit(solution)/shard_map/ppermute | solution.py:281
  179.9 0.8 copy-start.7
Sparse Core Ops, SparseCore 0:
  20.4 50.5 all-gather.5
  72.7 56.8 all-gather.7

commit v4 on v3

--- a/solution.py
+++ b/solution.py
@@ -15,7 +15,7 @@
 TRI = 32
 SETS = 3
 GROUP = 8
-EPILOGUE_ROWS = 6
+EPILOGUE_ROWS = 9
 
 
 def tri(k, i):
@@ -29,6 +29,12 @@
 NEAR_Y = [(i, i ^ SIDE) for i in range(RANKS)]
 FAR_X = [(i, i // SIDE * SIDE + SIDE - 1 - i % SIDE) for i in range(RANKS)]
 FAR_Y = [(i, (SIDE - 1 - i // SIDE) * SIDE + i % SIDE) for i in range(RANKS)]
+
+
+def shift_y(d):
+    return [(i, (i // SIDE + d) % SIDE * SIDE + i % SIDE) for i in range(RANKS)]
+
+
 OTHER_CORE = [(i, i ^ 1) for i in range(RANKS)]
 
 
@@ -128,15 +134,15 @@
         in_specs=[pl.BlockSpec(memory_space=pltpu.SMEM)] + [vmem] * 6,
         out_specs=(vmem, vmem),
         scratch_shapes=[pltpu.VMEM((STEPS, BLOCK, SETS * BLOCK), jnp.float32)],
-        compiler_params=pltpu.CompilerParams(vmem_limit_bytes=48 * 2**20),
         name="solve",
     )(core, first, second, third, mine, other, inverse)
 
 
-def product_kernel(partner, rows, slots, order, factor, pairs, near, far, buf, high, low, sems):
+def product_kernel(partner, rows, slots, order, mine, pair, pairs, near, far, buf, high, low, sems):
     copies = []
     for m in range(GROUP):
-        copy = pltpu.make_async_copy(factor.at[order[m]], buf.at[m], sems.at[m])
+        source = (mine if m < SIDE else pair).at[m % SIDE]
+        copy = pltpu.make_async_copy(source, buf.at[order[m]], sems.at[m])
         copy.start()
         copies.append(copy)
     for copy in copies:
@@ -167,16 +173,17 @@
         far[g * (rows // 3) : (g + 1) * (rows // 3)] = b.reshape(rows // 3, height, BLOCK)
 
 
-def product(partner, slots, order, factor, pairs):
+def product(partner, slots, order, mine, pair, pairs):
     rows = slots.shape[0]
     smem = pl.BlockSpec(memory_space=pltpu.SMEM)
     vmem = pl.BlockSpec(memory_space=pltpu.VMEM)
+    hbm = pl.BlockSpec(memory_space=pl.ANY)
     height = GROUP * SLICE
     piece = jax.ShapeDtypeStruct((rows, height, BLOCK), jnp.float32)
     return pl.pallas_call(
         lambda *refs: product_kernel(partner, rows, *refs),
         out_shape=(piece, piece),
-        in_specs=[smem, smem, pl.BlockSpec(memory_space=pl.ANY), vmem],
+        in_specs=[smem, smem, hbm, hbm, vmem],
         out_specs=(vmem, vmem),
         scratch_shapes=[
             pltpu.VMEM((GROUP, rows, SLOTS, SLICE, BLOCK), jnp.float32),
@@ -184,9 +191,9 @@
             pltpu.VMEM((rows * height, STEPS * BLOCK), jnp.bfloat16),
             pltpu.SemaphoreType.DMA((GROUP,)),
         ],
-        compiler_params=pltpu.CompilerParams(vmem_limit_bytes=48 * 2**20),
+        compiler_params=pltpu.CompilerParams(vmem_limit_bytes=24 * 2**20),
         name="product",
-    )(slots, order, factor, pairs)
+    )(slots, order, mine, pair, pairs)
 
 
 def finish_kernel(half_steps, spot, sides, near0, far0, near1, far1, out):
@@ -236,14 +243,12 @@
     y, x = here // SIDE, here % SIDE
 
     top, bottom = factor_blocks[:half_rows], factor_blocks[half_rows:]
-    top = jnp.stack([top, lax.ppermute(top, "samp", NEAR_X)])
-    bottom = jnp.stack([bottom, lax.ppermute(bottom, "samp", NEAR_Y)])
-    shape = (GROUP, half_rows, SLOTS, SLICE, BLOCK)
-    top = lax.all_gather(top, "samp", axis_index_groups=COLUMNS_OF_Y).reshape(shape)
-    bottom = lax.all_gather(bottom, "samp", axis_index_groups=ROWS_OF_X).reshape(shape)
-    group = jnp.arange(GROUP, dtype=jnp.int32)
-    top_order = (group // 2) * 2 + ((group % 2) ^ (x % 2))
-    bottom_order = (group % SIDE) * 2 + ((group // SIDE) ^ (y % 2))
+    top_parts = [top] + [lax.ppermute(top, "samp", shift_y(d)) for d in (1, -1, 2)]
+    bottom = lax.all_gather(bottom, "samp", axis_index_groups=ROWS_OF_X)
+    seen_y = jnp.stack([y, (y + 3) % SIDE, (y + 1) % SIDE, (y + 2) % SIDE])
+    seen_x = jnp.arange(SIDE, dtype=jnp.int32)
+    top_order = jnp.concatenate([2 * seen_y + x % 2, 2 * seen_y + 1 - x % 2])
+    bottom_order = jnp.concatenate([SIDE * (y % 2) + seen_x, SIDE * (1 - y % 2) + seen_x])
 
     owner = pivot_rows // row_count
     place = pivot_rows % row_count
@@ -265,19 +270,26 @@
             lax.dynamic_slice(pieces, (tri_owner[2 * rank + 1], HALF + SLICE, 0), (1, SLICE, BLOCK))[0],
         ]
     )
+    part, bottom, *top_parts = lax.optimization_barrier((part, bottom, *top_parts))
+    top = jnp.stack(top_parts)
+    top_pair = lax.ppermute(top, "samp", NEAR_X)
+    bottom_pair = lax.ppermute(bottom, "samp", NEAR_Y)
     gathered = lax.all_gather(part, "rows", axis=0, tiled=False)
     slices = gathered[:, HALF:].reshape(TRI, SLICE, BLOCK)
     core = rank % 2
     half = lax.dynamic_slice(slices, (core * RANKS, 0, 0), (RANKS, SLICE, BLOCK))
-    mine = lax.all_to_all(jnp.broadcast_to(half, (RANKS,) + half.shape), "samp", 0, 0)
-    other = lax.ppermute(mine, "rows", OTHER_CORE)
     own = gathered[:, :HALF]
     across_x = lax.ppermute(own, "samp", FAR_X)
     across_y = lax.ppermute(own, "samp", FAR_Y)
+    mine = lax.all_to_all(jnp.broadcast_to(half, (RANKS,) + half.shape), "samp", 0, 0)
+    mine, across_x, across_y, top_pair, bottom_pair = lax.optimization_barrier(
+        (mine, across_x, across_y, top_pair, bottom_pair)
+    )
+    other = lax.ppermute(mine, "rows", OTHER_CORE)
     solved, pairs = solve(core.reshape(1), own, across_x, across_y, mine, other, diag_inverse)
-    near0, send0 = product(1, slots[:half_rows], top_order, top, pairs)
+    near0, send0 = product(1, slots[:half_rows], top_order, top, top_pair, pairs)
     far0 = lax.ppermute(send0, "samp", FAR_X)
-    near1, send1 = product(2, slots[half_rows:], bottom_order, bottom, pairs)
+    near1, send1 = product(2, slots[half_rows:], bottom_order, bottom, bottom_pair, pairs)
     far1 = lax.ppermute(send1, "samp", FAR_Y)
     spot = jnp.stack([x // 2, y // 2])
     return solved, finish(spot, right_sides, near0, far0, near1, far1)

time: 195 us -> 166 us (0.85)
  waiting for transfers between devices: 83.5 us -> 44.7 us
  starting transfers between devices: 27.1 us -> 31.4 us
  blocking collectives: 17.7 us -> 20.7 us
  Pallas kernels: 26.4 us -> 28.6 us
    all_to_all x1, waiting for transfers between devices: 28.5 us -> 0.01 us  [local(): lax.all_to_all(jnp.broadcast_to(half, (RANKS,) + half.shape), 'samp', 0, 0)]
    ppermute x1, waiting for transfers between devices: 0.01 us -> 19.5 us  [local(): across_x = lax.ppermute(own, 'samp', FAR_X)]
    ppermute x2 -> x5, waiting for transfers between devices: 17.3 us -> 2.87 us  [the longest x3 2.86 us: local(): lax.ppermute(top, 'samp', shift_y(d))]
    ppermute x1, waiting for transfers between devices: 13.4 us -> 0.61 us  [local(): across_y = lax.ppermute(own, 'samp', FAR_Y)]
    all_to_all x1, waiting for transfers between devices: 12.1 us -> 7.95 us  [local(): pieces = lax.all_to_all(payload, 'rows', 0, 0)]
    all_gather x1, blocking collectives: 17.7 us -> 20.7 us  [local(): gathered = lax.all_gather(part, 'rows', axis=0, tiled=False)]
    ppermute x1, waiting for transfers between devices: 5.74 us -> 7.9 us  [local(): far1 = lax.ppermute(send1, 'samp', FAR_Y)]
    ppermute x1, starting transfers between devices: 0.59 us -> 2.61 us  [local(): across_x = lax.ppermute(own, 'samp', FAR_X)]
  transfers between devices with their start and end apart: 11 -> 13, of which waited for: 7 -> 7; matrix products, arithmetic and copies ran while one was open for 4% -> 5% of each run, Pallas kernels for 11% -> 6%
where the time goes in v4:
time: 166 us; the launch traced here: 165 us
  waiting for transfers between devices  44.7 us (27%)
  starting transfers between devices  31.4 us (19%)
  Pallas kernels  28.6 us (17%)
  blocking collectives  20.7 us (12%)
  between operations  19.9 us (12%)
  local copies, waits for them, and re-layouts  15.4 us (9%)
  other arithmetic  4.38 us (3%)
    all_gather x1, blocking collectives, local(): gathered = lax.all_gather(part, 'rows', axis=0, tiled=False)  20.7 us
    ppermute x1, waiting for transfers between devices, local(): across_x = lax.ppermute(own, 'samp', FAR_X)  19.5 us
    pallas_call x2, Pallas kernels, product(): pl.pallas_call(lambda *refs: product_kernel(partner, rows, *refs), out_sh...  13.2 us
    all_to_all x1, starting transfers between devices, local(): pieces = lax.all_to_all(payload, 'rows', 0, 0)  9.99 us
    unnamed x39, local copies, waits for them, and re-layouts  9.2 us
    all_to_all x1, waiting for transfers between devices, local(): pieces = lax.all_to_all(payload, 'rows', 0, 0)  7.95 us
    ppermute x1, waiting for transfers between devices, local(): far1 = lax.ppermute(send1, 'samp', FAR_Y)  7.9 us
    pallas_call x1, Pallas kernels, solve(): pl.pallas_call(solve_kernel, out_shape=(jax.ShapeDtypeStruct((STEPS, BLOC...  7.55 us
  transfers between devices with their start and end apart: 13, of which 7 were waited for; matrix products, arithmetic and copies ran while one was open for 5% of the time, Pallas kernels for 6%

profile of v4, /device:TPU:1, one launch (start us, length us, event | category | flops | bytes accessed | tf_op | source)
XLA Modules:
  0.0 165.1 jit_solution(16959227557894989208)
XLA Ops:
  7.2 2.0 %fusion = (f32[18,6,8,128]{3,2,1,0:T(8,128)S(1)}, f32[18,6,8,128]{3,2,1,0:T(8,128)}) fusion(f32[36,6,8,128]{3,2,1,0:T(8,128)} %factor.1), kind=kLoop, calls=%fused_computation.25 | loop fusion | bytes 1769472 | tf_op jit(solution)/shard_map/slice | solution.py:245
  9.2 0.7 copy.14.columns
  10.0 0.6 and_select_fusion
  10.6 3.4 %pack.1 = f32[16,80,128]{2,1,0:T(8,128)} custom-call(s32[8]{0:T(128)} %get-tuple-element.47.place, s32[36,6]{1,0:T(8,128)} %copy.14.columns, f32[36,128,128]{2,1,0:T(8,128)} %refs_1_.1, f32[36,6,8,128]{3,2,1,0:T(8,128)} %factor.1), custom_call_target="tpu_custom_call" | custom-call | tf_op jit(solution)/shard_map/pack/pallas_call | solution.py:83
  14.0 10.0 %all-to-all-start = ((f32[16,80,128]{2,1,0:T(8,128)}), f32[16,80,128]{2,1,0:T(8,128)S(1)}, u32[]{:S(2)}, u32[]{:S(2)}) async-start(f32[16,80,128]{2,1,0:T(8,128)} %pack.1), calls=%async_computation | async-start | bytes 1310720 | tf_op jit(solution)/shard_map/all_to_all | solution.py:264
  24.0 1.3 collective-permute-start
  25.3 1.5 collective-permute-start.1
  26.8 1.6 collective-permute-start.2
  28.4 0.7 gather_fusion
  29.1 0.7 fusion.2
  32.2 0.7 dynamic_slice.21
  36.1 7.9 %all-to-all-done = f32[16,80,128]{2,1,0:T(8,128)S(1)} async-done(((f32[16,80,128]{2,1,0:T(8,128)}), f32[16,80,128]{2,1,0:T(8,128)S(1)}, u32[]{:S(2)}, u32[]{:S(2)}) %all-to-all-start) | async-done | bytes 655392 | tf_op jit(solution)/shard_map/all_to_all | solution.py:264
  44.0 0.6 pad_maximum_fusion.1
  44.7 2.9 %collective-permute-done.2 = f32[18,6,8,128]{3,2,1,0:T(8,128)S(1)} collective-permute-done((f32[18,6,8,128]{3,2,1,0:T(8,128)S(1)}, f32[18,6,8,128]{3,2,1,0:T(8,128)S(1)}, u32[]{:S(2)}, u32[]{:S(2)}) %collective-permute-start.2) | collective-permute-done | bytes 442400 | tf_op jit(solution)/shard_map/ppermute | solution.py:246
  47.6 0.7 copy-done.14
  48.3 1.7 %pad_maximum_fusion.refs_2_ = f32[4,18,6,8,128]{4,3,2,1,0:T(8,128)S(1)} fusion(f32[1,18,6,8,128]{4,3,2,1,0:T(8,128)} %bitcast.30, f32[1,18,6,8,128]{4,3,2,1,0:T(8,128)} %bitcast.29, f32[1,18,6,8,128]{4,3,2,1,0:T(8,128)} %bitcast.28, f32[1,18,6,8,128]{4,3,2,1,0:T(8,128)} %bitcast.27), kind=kLoop, calls=%fused_computation.1 | loop fusion | flops 1327104 | bytes 3538944 | tf_op jit(solution)/shard_map/stack | solution.py:274
  50.0 1.3 collective-permute-start.5
  51.3 0.5 collective-permute-start.6
  51.8 20.7 %all-gather.1 = f32[1280,128]{1,0:T(8,128)S(1)} all-gather(f32[80,128]{1,0:T(8,128)} %pad_maximum_fusion.1), channel_id=3, replica_groups=mesh['rows'=16,'samp'=16] {'rows'}, dimensions={0}, use_global_device_ids=true | all-gather | bytes 696320 | tf_op jit(solution)/shard_map/all_gather | solution.py:277
  72.5 0.9 copy-done.6
  73.4 1.1 broadcast_in_dim.32
  74.5 5.6 %all-to-all-start.1 = ((f32[16,16,8,128]{3,2,1,0:T(8,128)}), f32[16,16,8,128]{3,2,1,0:T(8,128)}, u32[]{:S(2)}, u32[]{:S(2)}) async-start(f32[16,16,8,128]{3,2,1,0:T(8,128)} %broadcast_in_dim.32), calls=%async_computation.1 | async-start | bytes 2097152 | tf_op jit(solution)/shard_map/all_to_all | solution.py:284
  80.1 1.1 slice.26.first
  81.2 2.6 %collective-permute-start.3 = (f32[16,64,128]{2,1,0:T(8,128)S(1)}, f32[16,64,128]{2,1,0:T(8,128)S(1)}, u32[]{:S(2)}, u32[]{:S(2)}) collective-permute-start(f32[16,64,128]{2,1,0:T(8,128)S(1)} %slice.26.first), channel_id=1, source_target_pairs={{0,3},{1,2},{2,1},{3,0},{4,7},{5,6},{6,5},{7,4},{8,11},{9,10},{10,... | collective-permute-start | bytes 1572872 | tf_op jit(solution)/shard_map/ppermute | solution.py:282
  83.9 2.4 %collective-permute-start.4 = (f32[16,64,128]{2,1,0:T(8,128)S(1)}, f32[16,64,128]{2,1,0:T(8,128)}, u32[]{:S(2)}, u32[]{:S(2)}) collective-permute-start(f32[16,64,128]{2,1,0:T(8,128)S(1)} %slice.26.first), channel_id=1, source_target_pairs={{0,12},{1,13},{2,14},{3,15},{4,8},{5,9},{6,10},{7,11},{8,4},{9,5},... | collective-permute-start | bytes 1572872 | tf_op jit(solution)/shard_map/ppermute | solution.py:283
  86.3 0.1 select_reduce_fusion.1
  86.4 19.5 %collective-permute-done.3.second = f32[16,64,128]{2,1,0:T(8,128)S(1)} collective-permute-done((f32[16,64,128]{2,1,0:T(8,128)S(1)}, f32[16,64,128]{2,1,0:T(8,128)S(1)}, u32[]{:S(2)}, u32[]{:S(2)}) %collective-permute-start.3) | collective-permute-done | bytes 524320 | tf_op jit(solution)/shard_map/ppermute | solution.py:282
  105.8 0.8 copy-done.11
  106.6 0.6 collective-permute-done.4.third
  107.3 1.1 collective-permute-start.7
  108.5 0.7 copy.17.refs_0_
  109.3 0.7 pad_add_fusion.1
  110.0 1.0 collective-permute-done.7.other
  111.0 7.5 %solve.1 = (f32[8,128,128]{2,1,0:T(8,128)}, bf16[3,1024,256]{2,1,0:T(8,128)(2,1)}) custom-call(s32[1]{0:T(128)} %bitcast.core, f32[16,64,128]{2,1,0:T(8,128)} %copy-done.7, f32[16,64,128]{2,1,0:T(8,128)} %copy-done.11, f32[16,64,128]{2,1,0:T(8,128)} %collective-permute-done.4.third, f32[16,16,8,128]{3,2,1,0:T(8,128)} %all-to-all-done.1.mine, ...), custom_call_target="tpu_custom_call" | custom-call | tf_op jit(solution)/shard_map/solve/pallas_call | solution.py:128
  118.6 1.4 copy-done
  120.0 0.7 copy-done.4
  120.7 0.7 copy-done.5
  121.3 7.0 %product.2 = (f32[18,64,128]{2,1,0:T(8,128)S(1)}, f32[18,64,128]{2,1,0:T(8,128)}) custom-call(s32[18,8]{1,0:T(8,128)S(1)} %copy-done.4, s32[8]{0:T(128)S(1)} %copy-done.5, f32[4,18,6,8,128]{4,3,2,1,0:T(8,128)S(1)} %pad_maximum_fusion.refs_2_, f32[4,18,6,8,128]{4,3,2,1,0:T(8,128)} %collective-permute-done.5.refs_3_, bf16[3,1024,256]{2,1,0:T(8,128)(2,1)S(1)} %copy-done), custom_call_target="tpu_custom_call" | custom-call | tf_op jit(solution)/shard_map/product/pallas_call | solution.py:183
  128.3 0.8 copy-done.2
  129.2 1.4 collective-permute-start.8
  130.6 6.2 %product.3 = (f32[18,64,128]{2,1,0:T(8,128)S(1)}, f32[18,64,128]{2,1,0:T(8,128)S(1)}) custom-call(s32[18,8]{1,0:T(8,128)S(1)} %copy.18.refs_0_, s32[8]{0:T(128)S(1)} %get-tuple-element.49.refs_1_, f32[4,18,6,8,128]{4,3,2,1,0:T(8,128)S(1)} %bitcast.24, f32[4,18,6,8,128]{4,3,2,1,0:T(8,128)} %collective-permute-done.6.refs_3_, bf16[3,1024,256]{2,1,0:T(8,128)(2,1)S(1)} %copy-done), custom_call_target="tpu_custom_call" | custom-call | tf_op jit(solution)/shard_map/product/pallas_call | solution.py:183
  136.8 0.8 copy-done.3
  137.6 2.0 %collective-permute-start.9 = (f32[18,64,128]{2,1,0:T(8,128)S(1)}, f32[18,64,128]{2,1,0:T(8,128)S(1)}, u32[]{:S(2)}, u32[]{:S(2)}) collective-permute-start(f32[18,64,128]{2,1,0:T(8,128)S(1)} %get-tuple-element.35), channel_id=1, source_target_pairs={{0,12},{1,13},{2,14},{3,15},{4,8},{5,9},{6,10},{7,11},{8,4},{9,5},... | collective-permute-start | bytes 1769480 | tf_op jit(solution)/shard_map/ppermute | solution.py:293
  139.6 0.6 pad_add_fusion.refs_0_
  140.2 4.9 %collective-permute-done.8.refs_3_ = f32[18,64,128]{2,1,0:T(8,128)S(1)} collective-permute-done((f32[18,64,128]{2,1,0:T(8,128)}, f32[18,64,128]{2,1,0:T(8,128)S(1)}, u32[]{:S(2)}, u32[]{:S(2)}) %collective-permute-start.8) | collective-permute-done | bytes 589856 | tf_op jit(solution)/shard_map/ppermute | solution.py:291
  145.1 7.9 %collective-permute-done.9.refs_5_ = f32[18,64,128]{2,1,0:T(8,128)S(1)} collective-permute-done((f32[18,64,128]{2,1,0:T(8,128)S(1)}, f32[18,64,128]{2,1,0:T(8,128)S(1)}, u32[]{:S(2)}, u32[]{:S(2)}) %collective-permute-start.9) | collective-permute-done | bytes 589856 | tf_op jit(solution)/shard_map/ppermute | solution.py:293
  153.0 0.8 copy-done.10
  153.8 4.5 %finish.1 = f32[36,128,128]{2,1,0:T(8,128)} custom-call(s32[2]{0:T(128)} %pad_add_fusion.refs_0_, f32[36,128,128]{2,1,0:T(8,128)} %refs_1_.1, f32[18,64,128]{2,1,0:T(8,128)} %copy-done.2, f32[18,64,128]{2,1,0:T(8,128)} %copy-done.9, f32[18,64,128]{2,1,0:T(8,128)} %copy-done.3, f32[18,64,128]{2,1,0:T(8,128)} %copy-done.10), custom_call_target="tpu_custom_call" | custom-call | tf_op jit(solution)/shard_map/finish/pallas_call | solution.py:228
  (51 shorter events, 0.4 us)
Async XLA Ops:
  7.2 2.1 %copy-start.15 = (s32[36,6]{0,1:T(8,128)S(1)}, s32[36,6]{0,1:T(8,128)}, u32[]{:S(2)}) copy-start(s32[36,6]{0,1:T(8,128)} %param.8) | copy-start | bytes 2596
  7.2 2.8 %copy-start.17 = (s32[8]{0:T(128)S(1)}, s32[8]{0:T(128)}, u32[]{:S(2)}) copy-start(s32[8]{0:T(128)} %param.9) | copy-start | bytes 100
  7.2 40.4 %all-gather.4.cloned.1.call-start = ((), (), s32[]{:S(2)}) async-start(), calls=%async_computation.2 | async-start | bytes 2211840 | tf_op jit(solution)/shard_map/all_gather | solution.py:247
  9.2 17.6 %copy-start.8 = (f32[18,6,8,128]{3,2,1,0:T(8,128)}, f32[18,6,8,128]{3,2,1,0:T(8,128)S(1)}, u32[]{:S(2)}) copy-start(f32[18,6,8,128]{3,2,1,0:T(8,128)S(1)} %get-tuple-element.20) | copy-start | bytes 1327108
  10.6 17.8 %copy-start.16 = (s32[32]{0:T(128)S(1)}, s32[32]{0:T(128)}, u32[]{:S(2)}) copy-start(s32[32]{0:T(128)} %constant.141) | copy-start | bytes 388
  14.0 30.0 %all-to-all-start = ((f32[16,80,128]{2,1,0:T(8,128)}), f32[16,80,128]{2,1,0:T(8,128)S(1)}, u32[]{:S(2)}, u32[]{:S(2)}) async-start(f32[16,80,128]{2,1,0:T(8,128)} %pack.1), calls=%async_computation | async-start | bytes 1310720 | tf_op jit(solution)/shard_map/all_to_all | solution.py:264
  24.0 20.7 %collective-permute-start = (f32[18,6,8,128]{3,2,1,0:T(8,128)S(1)}, f32[18,6,8,128]{3,2,1,0:T(8,128)S(1)}, u32[]{:S(2)}, u32[]{:S(2)}) collective-permute-start(f32[18,6,8,128]{3,2,1,0:T(8,128)S(1)} %get-tuple-element.20), channel_id=1, source_target_pairs={{0,4},{1,5},{2,6},{3,7},{4,8},{5,9},{6,10},{7,11},{8,12},{9,13},{1... | collective-permute-start | bytes 1327112 | tf_op jit(solution)/shard_map/ppermute | solution.py:246
  25.3 19.4 %collective-permute-start.1 = (f32[18,6,8,128]{3,2,1,0:T(8,128)S(1)}, f32[18,6,8,128]{3,2,1,0:T(8,128)S(1)}, u32[]{:S(2)}, u32[]{:S(2)}) collective-permute-start(f32[18,6,8,128]{3,2,1,0:T(8,128)S(1)} %get-tuple-element.20), channel_id=1, source_target_pairs={{0,12},{1,13},{2,14},{3,15},{4,0},{5,1},{6,2},{7,3},{8,4},{9,5},{1... | collective-permute-start | bytes 1327112 | tf_op jit(solution)/shard_map/ppermute | solution.py:246
  26.8 20.7 %collective-permute-start.2 = (f32[18,6,8,128]{3,2,1,0:T(8,128)S(1)}, f32[18,6,8,128]{3,2,1,0:T(8,128)S(1)}, u32[]{:S(2)}, u32[]{:S(2)}) collective-permute-start(f32[18,6,8,128]{3,2,1,0:T(8,128)S(1)} %get-tuple-element.20), channel_id=1, source_target_pairs={{0,8},{1,9},{2,10},{3,11},{4,12},{5,13},{6,14},{7,15},{8,0},{9,1},... | collective-permute-start | bytes 1327112 | tf_op jit(solution)/shard_map/ppermute | solution.py:246
  44.7 2.9 %copy-start.12 = (f32[18,6,8,128]{3,2,1,0:T(8,128)}, f32[18,6,8,128]{3,2,1,0:T(8,128)S(1)}, u32[]{:S(2)}) copy-start(f32[18,6,8,128]{3,2,1,0:T(8,128)S(1)} %collective-permute-done) | copy-start | bytes 1327108
  44.7 2.9 %copy-start.13 = (f32[18,6,8,128]{3,2,1,0:T(8,128)}, f32[18,6,8,128]{3,2,1,0:T(8,128)S(1)}, u32[]{:S(2)}) copy-start(f32[18,6,8,128]{3,2,1,0:T(8,128)S(1)} %collective-permute-done.1) | copy-start | bytes 1327108
  47.5 0.8 copy-start.14
  48.3 3.0 %copy-start.1 = (f32[72,6,8,128]{3,2,1,0:T(8,128)S(1)}, f32[72,6,8,128]{3,2,1,0:T(8,128)}, u32[]{:S(2)}) copy-start(f32[72,6,8,128]{3,2,1,0:T(8,128)} %all-gather.4.cloned.1.call-done) | copy-start | bytes 5308420
  50.0 57.3 %collective-permute-start.5 = (f32[4,18,6,8,128]{4,3,2,1,0:T(8,128)S(1)}, f32[4,18,6,8,128]{4,3,2,1,0:T(8,128)}, u32[]{:S(2)}, u32[]{:S(2)}) collective-permute-start(f32[4,18,6,8,128]{4,3,2,1,0:T(8,128)S(1)} %pad_maximum_fusion.refs_2_), channel_id=1, source_target_pairs={{0,1},{1,0},{2,3},{3,2},{4,5},{5,4},{6,7},{7,6},{8,9},{9,8},{10,11... | collective-permute-start | bytes 5308424 | tf_op jit(solution)/shard_map/ppermute | solution.py:275
  51.3 56.0 %collective-permute-start.6 = (f32[4,18,6,8,128]{4,3,2,1,0:T(8,128)S(1)}, f32[4,18,6,8,128]{4,3,2,1,0:T(8,128)}, u32[]{:S(2)}, u32[]{:S(2)}) collective-permute-start(f32[4,18,6,8,128]{4,3,2,1,0:T(8,128)S(1)} %bitcast.23), channel_id=1, source_target_pairs={{0,4},{1,5},{2,6},{3,7},{4,0},{5,1},{6,2},{7,3},{8,12},{9,13},{10,... | collective-permute-start | bytes 5308424 | tf_op jit(solution)/shard_map/ppermute | solution.py:276
  72.5 0.9 copy-start.6
  74.5 32.7 %all-to-all-start.1 = ((f32[16,16,8,128]{3,2,1,0:T(8,128)}), f32[16,16,8,128]{3,2,1,0:T(8,128)}, u32[]{:S(2)}, u32[]{:S(2)}) async-start(f32[16,16,8,128]{3,2,1,0:T(8,128)} %broadcast_in_dim.32), calls=%async_computation.1 | async-start | bytes 2097152 | tf_op jit(solution)/shard_map/all_to_all | solution.py:284
  81.2 2.6 %copy-start.7 = (f32[16,64,128]{2,1,0:T(8,128)}, f32[16,64,128]{2,1,0:T(8,128)S(1)}, u32[]{:S(2)}) copy-start(f32[16,64,128]{2,1,0:T(8,128)S(1)} %slice.26.first) | copy-start | bytes 1572868
  81.2 24.6 %collective-permute-start.3 = (f32[16,64,128]{2,1,0:T(8,128)S(1)}, f32[16,64,128]{2,1,0:T(8,128)S(1)}, u32[]{:S(2)}, u32[]{:S(2)}) collective-permute-start(f32[16,64,128]{2,1,0:T(8,128)S(1)} %slice.26.first), channel_id=1, source_target_pairs={{0,3},{1,2},{2,1},{3,0},{4,7},{5,6},{6,5},{7,4},{8,11},{9,10},{10,... | collective-permute-start | bytes 1572872 | tf_op jit(solution)/shard_map/ppermute | solution.py:282
  83.9 23.4 %collective-permute-start.4 = (f32[16,64,128]{2,1,0:T(8,128)S(1)}, f32[16,64,128]{2,1,0:T(8,128)}, u32[]{:S(2)}, u32[]{:S(2)}) collective-permute-start(f32[16,64,128]{2,1,0:T(8,128)S(1)} %slice.26.first), channel_id=1, source_target_pairs={{0,12},{1,13},{2,14},{3,15},{4,8},{5,9},{6,10},{7,11},{8,4},{9,5},... | collective-permute-start | bytes 1572872 | tf_op jit(solution)/shard_map/ppermute | solution.py:283
  105.8 0.8 copy-start.11
  107.3 3.8 %collective-permute-start.7 = (f32[16,16,8,128]{3,2,1,0:T(8,128)}, f32[16,16,8,128]{3,2,1,0:T(8,128)}, u32[]{:S(2)}, u32[]{:S(2)}) collective-permute-start(f32[16,16,8,128]{3,2,1,0:T(8,128)} %all-to-all-done.1.mine), channel_id=1, source_target_pairs={{0,16},{16,0},{32,48},{48,32},{64,80},{80,64},{96,112},{112,96},{1... | collective-permute-start | bytes 3145736 | tf_op jit(solution)/shard_map/ppermute | solution.py:288
  118.6 1.4 copy-start
  120.0 0.7 copy-start.4
  120.7 0.7 copy-start.5
  128.3 0.8 copy-start.2
  129.2 16.0 %collective-permute-start.8 = (f32[18,64,128]{2,1,0:T(8,128)}, f32[18,64,128]{2,1,0:T(8,128)S(1)}, u32[]{:S(2)}, u32[]{:S(2)}) collective-permute-start(f32[18,64,128]{2,1,0:T(8,128)} %get-tuple-element.32), channel_id=1, source_target_pairs={{0,3},{1,2},{2,1},{3,0},{4,7},{5,6},{6,5},{7,4},{8,11},{9,10},{10,... | collective-permute-start | bytes 1769480 | tf_op jit(solution)/shard_map/ppermute | solution.py:291
  136.7 0.9 copy-start.3
  137.6 15.4 %collective-permute-start.9 = (f32[18,64,128]{2,1,0:T(8,128)S(1)}, f32[18,64,128]{2,1,0:T(8,128)S(1)}, u32[]{:S(2)}, u32[]{:S(2)}) collective-permute-start(f32[18,64,128]{2,1,0:T(8,128)S(1)} %get-tuple-element.35), channel_id=1, source_target_pairs={{0,12},{1,13},{2,14},{3,15},{4,8},{5,9},{6,10},{7,11},{8,4},{9,5},... | collective-permute-start | bytes 1769480 | tf_op jit(solution)/shard_map/ppermute | solution.py:293
  145.1 7.9 %copy-start.9 = (f32[18,64,128]{2,1,0:T(8,128)}, f32[18,64,128]{2,1,0:T(8,128)S(1)}, u32[]{:S(2)}) copy-start(f32[18,64,128]{2,1,0:T(8,128)S(1)} %collective-permute-done.8.refs_3_) | copy-start | bytes 1769476
  153.0 0.8 copy-start.10
Sparse Core Ops, SparseCore 0:
  10.4 34.4 all-gather.3

commit v5 on v4

v5 whole, which is shorter than its diff:
```python
import jax
import jax.numpy as jnp
from jax import lax
from jax.experimental import pallas as pl
from jax.experimental.pallas import tpu as pltpu
from jax.sharding import PartitionSpec as P

BLOCK = 128
STEPS = 8
SLOTS = 6
RANKS = 16
SIDE = 4
SLICE = BLOCK // RANKS
HALF = BLOCK // 2
TRI = 32
SETS = 2
GATHERED_ROWS = 28
ROWS_PER_STEP = 14
GROUP = 8
EPILOGUE_ROWS = 4


def tri(k, i):
    return k * (k - 1) // 2 + i


TRI_PIVOT = [k for k in range(STEPS) for _ in range(k)] + [STEPS - 1] * (TRI - tri(STEPS, 0))
NEAR_X = [(i, i ^ 1) for i in range(RANKS)]
FAR_X = [(i, i // SIDE * SIDE + SIDE - 1 - i % SIDE) for i in range(RANKS)]


def shift_y(d):
    return [(i, (i // SIDE + d) % SIDE * SIDE + i % SIDE) for i in range(RANKS)]


OTHER_CORE = [(i, i ^ 1) for i in range(RANKS)]


def split(x):
    hi = x.astype(jnp.bfloat16)
    lo = (x - hi.astype(jnp.float32)).astype(jnp.bfloat16)
    return hi, lo


def dot(a, b):
    return lax.dot_general(a, b, (((1,), (0,)), ((), ())), preferred_element_type=jnp.float32)


def pack_kernel(pivots, columns, sides, factor, out, rows_buf, sem_f, sem_r):
    row_count = sides.shape[0]
    place = [lax.rem(pivots[j], row_count) for j in range(STEPS)]
    factor_copies, side_copies = [], []
    for j in range(STEPS):
        copy = pltpu.make_async_copy(factor.at[place[j]], rows_buf.at[j], sem_f.at[j])
        copy.start()
        factor_copies.append(copy)
    for j in range(STEPS):
        for h in range(2):
            copy = pltpu.make_async_copy(
                sides.at[place[j], pl.ds(h * HALF, HALF)], out.at[2 * j + h, pl.ds(0, HALF)], sem_r.at[2 * j + h]
            )
            copy.start()
            side_copies.append(copy)
    for copy in factor_copies:
        copy.wait()
    for j in range(STEPS):
        at = place[j]
        for i in range(j):
            piece = jnp.zeros((SLICE, BLOCK), jnp.float32)
            for s in range(SLOTS):
                piece = jnp.where(columns[s, at] == i, rows_buf[j, s], piece)
            b = tri(j, i)
            out[b // 2, pl.ds(HALF + (b % 2) * SLICE, SLICE)] = piece
    for b in range(tri(STEPS, 0), TRI):
        out[b // 2, pl.ds(HALF + (b % 2) * SLICE, SLICE)] = jnp.zeros((SLICE, BLOCK), jnp.float32)
    for copy in side_copies:
        copy.wait()


def pack(pivots, columns, sides, factor):
    smem = pl.BlockSpec(memory_space=pltpu.SMEM)
    hbm = pl.BlockSpec(memory_space=pl.ANY)
    return pl.pallas_call(
        pack_kernel,
        out_shape=jax.ShapeDtypeStruct((RANKS, HALF + 2 * SLICE, BLOCK), jnp.float32),
        in_specs=[smem, smem, hbm, hbm],
        out_specs=pl.BlockSpec(memory_space=pltpu.VMEM),
        scratch_shapes=[
            pltpu.VMEM((STEPS, SLOTS, SLICE, BLOCK), jnp.float32),
            pltpu.SemaphoreType.DMA((STEPS,)),
            pltpu.SemaphoreType.DMA((2 * STEPS,)),
        ],
        name="pack",
    )(pivots, columns, sides, factor)


def solve_kernel(core, first, second, mine, other, inverse, solved, pairs, side):
    flag = core[0]

    def factor(k, i):
        b = tri(k, i)
        own = mine[:, b % RANKS].reshape(BLOCK, BLOCK)
        far = other[:, b % RANKS].reshape(BLOCK, BLOCK)
        return jnp.where(flag == b // RANKS, own, far)

    def product(a, hi, lo):
        ah, al = split(a)
        full = dot(ah, jnp.concatenate([hi, lo], axis=1))
        return full[:, : SETS * BLOCK] + full[:, SETS * BLOCK :] + dot(al, hi)

    for j in range(STEPS):
        for t, ref in enumerate((first, second)):
            side[j, :, t * BLOCK : (t + 1) * BLOCK] = ref[2 * j : 2 * j + 2, :HALF].reshape(BLOCK, BLOCK)
    for j in range(STEPS):
        hi, lo = split(side[j])
        x = product(inverse[j], hi, lo)
        solved[j] = x[:, :BLOCK]
        hi, lo = split(x)
        for t in range(SETS):
            pairs[t, j * BLOCK : (j + 1) * BLOCK, :BLOCK] = hi[:, t * BLOCK : (t + 1) * BLOCK]
            pairs[t, j * BLOCK : (j + 1) * BLOCK, BLOCK:] = lo[:, t * BLOCK : (t + 1) * BLOCK]
        for k in range(j + 1, STEPS):
            side[k] = side[k] - product(factor(k, j), hi, lo)
    for t in range(SETS):
        pairs[t, STEPS * BLOCK :] = jnp.zeros((BLOCK, 2 * BLOCK), jnp.bfloat16)


def solve(core, first, second, mine, other, inverse):
    vmem = pl.BlockSpec(memory_space=pltpu.VMEM)
    return pl.pallas_call(
        solve_kernel,
        out_shape=(
            jax.ShapeDtypeStruct((STEPS, BLOCK, BLOCK), jnp.float32),
            jax.ShapeDtypeStruct((SETS, (STEPS + 1) * BLOCK, 2 * BLOCK), jnp.bfloat16),
        ),
        in_specs=[pl.BlockSpec(memory_space=pltpu.SMEM)] + [vmem] * 5,
        out_specs=(vmem, vmem),
        scratch_shapes=[pltpu.VMEM((STEPS, BLOCK, SETS * BLOCK), jnp.float32)],
        name="solve",
    )(core, first, second, mine, other, inverse)


def product_kernel(rows, slots, order, mine, pair, pairs, near, far, buf, high, low, sems):
    copies = []
    for m in range(GROUP):
        source = (mine if m < SIDE else pair).at[m % SIDE]
        copy = pltpu.make_async_copy(source, buf.at[order[m]], sems.at[m])
        copy.start()
        copies.append(copy)
    for copy in copies:
        copy.wait()
    height = GROUP * SLICE

    def build(r, carry):
        at_row = pl.multiple_of(r * height, height)
        for c in range(STEPS):
            at = slots[r, c]
            block = buf[:, r, jnp.minimum(at, SLOTS - 1)].reshape(height, BLOCK)
            hi, lo = split(jnp.where(at < SLOTS, block, 0.0))
            high[pl.ds(at_row, height), c * BLOCK : (c + 1) * BLOCK] = hi
            low[pl.ds(at_row, height), c * BLOCK : (c + 1) * BLOCK] = lo
        return carry

    lax.fori_loop(0, rows, build, 0)
    own, theirs = pairs[0, : STEPS * BLOCK], pairs[1, : STEPS * BLOCK]
    wide = jnp.concatenate([own, theirs], axis=1)
    tops = jnp.concatenate([own[:, :BLOCK], theirs[:, :BLOCK]], axis=1)
    full = dot(high[...], wide)
    rest = dot(low[...], tops)
    a = full[:, :BLOCK] + full[:, BLOCK : 2 * BLOCK] + rest[:, :BLOCK]
    b = full[:, 2 * BLOCK : 3 * BLOCK] + full[:, 3 * BLOCK :] + rest[:, BLOCK:]
    near[...] = a.reshape(rows, height, BLOCK)
    far[...] = b.reshape(rows, height, BLOCK)


def product(slots, order, mine, pair, pairs):
    rows = slots.shape[0]
    smem = pl.BlockSpec(memory_space=pltpu.SMEM)
    vmem = pl.BlockSpec(memory_space=pltpu.VMEM)
    hbm = pl.BlockSpec(memory_space=pl.ANY)
    height = GROUP * SLICE
    piece = jax.ShapeDtypeStruct((rows, height, BLOCK), jnp.float32)
    return pl.pallas_call(
        lambda *refs: product_kernel(rows, *refs),
        out_shape=(piece, piece),
        in_specs=[smem, smem, hbm, hbm, vmem],
        out_specs=(vmem, vmem),
        scratch_shapes=[
            pltpu.VMEM((GROUP, rows, SLOTS, SLICE, BLOCK), jnp.float32),
            pltpu.VMEM((rows * height, STEPS * BLOCK), jnp.bfloat16),
            pltpu.VMEM((rows * height, STEPS * BLOCK), jnp.bfloat16),
            pltpu.SemaphoreType.DMA((GROUP,)),
        ],
        name="product",
    )(slots, order, mine, pair, pairs)


def update_kernel(picks, sides, factor, pairs, out):
    step = pl.program_id(0)
    for r in range(ROWS_PER_STEP):
        row = step * ROWS_PER_STEP + r
        hi, lo, x2 = [], [], []
        for s in range(SLOTS):
            fh, fl = split(factor[:, r, s].reshape(BLOCK, BLOCK))
            hi.append(fh)
            lo.append(fl)
            at = pl.multiple_of(picks[row, s] * BLOCK, BLOCK)
            x2.append(pairs[0, pl.ds(at, BLOCK)])
        hi = jnp.concatenate(hi, axis=1)
        lo = jnp.concatenate(lo, axis=1)
        x2 = jnp.concatenate(x2, axis=0)
        full = dot(hi, x2)
        out[r] = sides[r] - (full[:, :BLOCK] + full[:, BLOCK:] + dot(lo, x2[:, :BLOCK]))


def update(picks, sides, factor, pairs):
    rows = factor.shape[1]
    return pl.pallas_call(
        update_kernel,
        grid=(rows // ROWS_PER_STEP,),
        out_shape=jax.ShapeDtypeStruct(sides.shape, jnp.float32),
        in_specs=[
            pl.BlockSpec(memory_space=pltpu.SMEM),
            pl.BlockSpec((ROWS_PER_STEP, BLOCK, BLOCK), lambda g: (g, 0, 0)),
            pl.BlockSpec((RANKS, ROWS_PER_STEP, SLOTS, SLICE, BLOCK), lambda g: (0, g, 0, 0, 0)),
            pl.BlockSpec((1, (STEPS + 1) * BLOCK, 2 * BLOCK), lambda g: (0, 0, 0)),
        ],
        out_specs=pl.BlockSpec((ROWS_PER_STEP, BLOCK, BLOCK), lambda g: (g, 0, 0)),
        compiler_params=pltpu.CompilerParams(vmem_limit_bytes=48 * 2**20),
        name="update",
    )(picks, sides, factor, pairs)


def finish_kernel(spot, sides, near, far, base, out):
    swap = spot[0] == 1
    height = BLOCK // (2 * SIDE)
    for r in range(EPILOGUE_ROWS):
        for q in range(SIDE):
            a, b = near[r, q * height : (q + 1) * height], far[r, q * height : (q + 1) * height]
            at = 2 * q * height
            out[r, at : at + height] = sides[r, at : at + height] - jnp.where(swap, b, a)
            at = at + height
            out[r, at : at + height] = sides[r, at : at + height] - jnp.where(swap, a, b)


def finish(spot, sides, near, far, base):
    first = GATHERED_ROWS // EPILOGUE_ROWS
    height = GROUP * SLICE
    whole = pl.BlockSpec((EPILOGUE_ROWS, BLOCK, BLOCK), lambda g: (g + first, 0, 0))
    piece = pl.BlockSpec((EPILOGUE_ROWS, height, BLOCK), lambda g: (g, 0, 0))
    return pl.pallas_call(
        finish_kernel,
        grid=(near.shape[0] // EPILOGUE_ROWS,),
        out_shape=jax.ShapeDtypeStruct(sides.shape, jnp.float32),
        in_specs=[pl.BlockSpec(memory_space=pltpu.SMEM), whole, piece, piece, pl.BlockSpec(memory_space=pl.ANY)],
        out_specs=whole,
        input_output_aliases={4: 0},
        name="finish",
    )(spot, sides, near, far, base)


def local(right_sides, factor_blocks, block_columns, pivot_rows, diag_inverse):
    row_count = right_sides.shape[0]
    rank = lax.axis_index("rows")
    here = lax.axis_index("samp")
    y, x = here // SIDE, here % SIDE

    everything = lax.all_gather(factor_blocks[:GATHERED_ROWS], "samp", axis=0, tiled=False)
    rest = factor_blocks[GATHERED_ROWS:]
    rest_parts = [rest] + [lax.ppermute(rest, "samp", shift_y(d)) for d in (1, -1, 2)]
    seen_y = jnp.stack([y, (y + 3) % SIDE, (y + 1) % SIDE, (y + 2) % SIDE])
    order = jnp.concatenate([2 * seen_y + x % 2, 2 * seen_y + 1 - x % 2])

    owner = pivot_rows // row_count
    ids = rank * row_count + jnp.arange(row_count, dtype=jnp.int32)
    targets = jnp.arange(STEPS, dtype=jnp.int32)
    row_rank = STEPS + jnp.sum(jnp.where(ids[:, None] == pivot_rows[None, :], targets - STEPS, 0), axis=1)
    picks = jnp.where(block_columns < row_rank[:, None], block_columns, STEPS)
    slots = jnp.min(
        jnp.where(picks[:, None, :] == targets[None, :, None], jnp.arange(SLOTS, dtype=jnp.int32), SLOTS), axis=2
    )

    payload = pack(pivot_rows, block_columns.T, right_sides, factor_blocks)
    pieces = lax.all_to_all(payload, "rows", 0, 0)
    tri_owner = owner[jnp.array(TRI_PIVOT, jnp.int32)]
    part = jnp.concatenate(
        [
            lax.dynamic_slice(pieces, (owner[rank // 2], 0, 0), (1, HALF, BLOCK))[0],
            lax.dynamic_slice(pieces, (tri_owner[2 * rank], HALF, 0), (1, SLICE, BLOCK))[0],
            lax.dynamic_slice(pieces, (tri_owner[2 * rank + 1], HALF + SLICE, 0), (1, SLICE, BLOCK))[0],
        ]
    )
    part, *rest_parts = lax.optimization_barrier((part, *rest_parts))
    rest = jnp.stack(rest_parts)
    rest_pair = lax.ppermute(rest, "samp", NEAR_X)
    gathered = lax.all_gather(part, "rows", axis=0, tiled=False)
    slices = gathered[:, HALF:].reshape(TRI, SLICE, BLOCK)
    core = rank % 2
    half = lax.dynamic_slice(slices, (core * RANKS, 0, 0), (RANKS, SLICE, BLOCK))
    own = gathered[:, :HALF]
    across = lax.ppermute(own, "samp", FAR_X)
    mine = lax.all_to_all(jnp.broadcast_to(half, (RANKS,) + half.shape), "samp", 0, 0)
    mine, across, rest_pair = lax.optimization_barrier((mine, across, rest_pair))
    other = lax.ppermute(mine, "rows", OTHER_CORE)
    solved, pairs = solve(core.reshape(1), own, across, mine, other, diag_inverse)
    near, send = product(slots[GATHERED_ROWS:], order, rest, rest_pair, pairs)
    far = lax.ppermute(send, "samp", FAR_X)
    updated = update(picks, right_sides, everything, pairs)
    return solved, finish((x // 2).reshape(1), right_sides, near, far, updated)


def solution(mesh):
    placed = (P("rows", None, "samp"), P("rows", None, "samp", None), P("rows", None), P(), P())
    return jax.shard_map(
        local,
        mesh=mesh,
        in_specs=placed,
        out_specs=(P(None, None, "samp"), P("rows", None, "samp")),
        check_vma=False,
    )
```

time: 166 us -> 162 us (0.976)
  waiting for transfers between devices: 44.7 us -> 62.6 us
  local copies, waits for them, and re-layouts: 15.4 us -> 7.77 us
  Pallas kernels: 28.6 us -> 23.9 us
  starting transfers between devices: 31.4 us -> 26.8 us
  other arithmetic: 4.38 us -> 0.93 us
    ppermute x9 -> x6, waiting for transfers between devices: 35.7 us -> 55.3 us  [the longest x1 39.7 us: local(): across = lax.ppermute(own, 'samp', FAR_X)]
    unnamed x39 -> x24, local copies, waits for them, and re-layouts: 9.2 us -> 1.53 us
    ppermute x9 -> x6, starting transfers between devices: 14.6 us -> 9.67 us  [the longest x3 4.48 us: local(): lax.ppermute(rest, 'samp', shift_y(d))]
    pallas_call x3, Pallas kernels: 17.6 us -> 13.8 us  [the longest x1 6.72 us: update(): pl.pallas_call(update_kernel, grid=(rows // ROWS_PER_STEP,), out_shape=ja...]
    another operation x2 -> x1, other arithmetic: 2.3 us -> 0.06 us  [local(): rest = jnp.stack(rest_parts)]
  transfers between devices with their start and end apart: 13 -> 10, of which waited for: 7 -> 4; matrix products, arithmetic and copies ran while one was open for 5% -> 4% of each run, Pallas kernels for 6% -> 14%
where the time goes in v5:
time: 162 us; the launch traced here: 161 us
  waiting for transfers between devices  62.6 us (39%)
  starting transfers between devices  26.8 us (17%)
  Pallas kernels  23.9 us (15%)
  between operations  20.1 us (12%)
  blocking collectives  19.1 us (12%)
  local copies, waits for them, and re-layouts  7.77 us (5%)
    ppermute x1, waiting for transfers between devices, local(): across = lax.ppermute(own, 'samp', FAR_X)  39.7 us
    all_gather x1, blocking collectives, local(): gathered = lax.all_gather(part, 'rows', axis=0, tiled=False)  19.1 us
    ppermute x1, waiting for transfers between devices, local(): rest_pair = lax.ppermute(rest, 'samp', NEAR_X)  15.6 us
    all_to_all x1, starting transfers between devices, local(): pieces = lax.all_to_all(payload, 'rows', 0, 0)  9.99 us
    pallas_call x1, Pallas kernels, solve(): pl.pallas_call(solve_kernel, out_shape=(jax.ShapeDtypeStruct((STEPS, BLOC...  6.93 us
    pallas_call x1, Pallas kernels, update(): pl.pallas_call(update_kernel, grid=(rows // ROWS_PER_STEP,), out_shape=ja...  6.72 us
    all_to_all x1, waiting for transfers between devices, local(): pieces = lax.all_to_all(payload, 'rows', 0, 0)  6.68 us
    all_to_all x1, starting transfers between devices, local(): lax.all_to_all(jnp.broadcast_to(half, (RANKS,) + half.shape), 'samp', 0, 0)  5.76 us
  transfers between devices with their start and end apart: 10, of which 4 were waited for; matrix products, arithmetic and copies ran while one was open for 4% of the time, Pallas kernels for 14%

profile of v5, /device:TPU:1, one launch (start us, length us, event | category | flops | bytes accessed | tf_op | source)
XLA Modules:
  0.0 161.2 jit_solution(17684637282129981356)
XLA Ops:
  7.2 0.0 all-gather.4.cloned.1.call-start
  7.2 2.0 %slice.19 = f32[28,6,8,128]{3,2,1,0:T(8,128)} slice(f32[36,6,8,128]{3,2,1,0:T(8,128)} %factor.1), slice={[0:28], [0:6], [0:8], [0:128]} | slice | bytes 1376256 | tf_op jit(solution)/shard_map/slice | solution.py:268
  9.2 0.0 all-gather.4.cloned.1.call-update
  9.3 0.0 copy-start.10
  9.3 0.0 copy-start.9
  9.3 3.2 %pack.1 = f32[16,80,128]{2,1,0:T(8,128)} custom-call(s32[8]{0:T(128)} %pivots.1, s32[6,36]{1,0:T(8,128)} %bitcast.31, f32[36,128,128]{2,1,0:T(8,128)} %sides.5, f32[36,6,8,128]{3,2,1,0:T(8,128)} %factor.1), custom_call_target="tpu_custom_call" | custom-call | tf_op jit(solution)/shard_map/pack/pallas_call | solution.py:83
  12.5 10.0 %all-to-all-start = ((f32[16,80,128]{2,1,0:T(8,128)}), f32[16,80,128]{2,1,0:T(8,128)S(1)}, u32[]{:S(2)}, u32[]{:S(2)}) async-start(f32[16,80,128]{2,1,0:T(8,128)} %pack.1), calls=%async_computation | async-start | bytes 1310720 | tf_op jit(solution)/shard_map/all_to_all | solution.py:284
  22.5 0.9 slice.15
  23.4 1.4 collective-permute-start
  24.8 1.5 collective-permute-start.1
  26.3 1.6 collective-permute-start.2
  27.9 0.0 copy-done.10
  27.9 0.7 gather_fusion
  28.6 0.6 fusion
  31.8 0.7 dynamic_slice.21
  35.8 6.7 %all-to-all-done = f32[16,80,128]{2,1,0:T(8,128)S(1)} async-done(((f32[16,80,128]{2,1,0:T(8,128)}), f32[16,80,128]{2,1,0:T(8,128)S(1)}, u32[]{:S(2)}, u32[]{:S(2)}) %all-to-all-start) | async-done | bytes 655392 | tf_op jit(solution)/shard_map/all_to_all | solution.py:284
  42.5 0.0 collective-permute-done
  42.5 0.0 collective-permute-done.1
  42.5 0.0 collective-permute-done.2
  42.5 19.1 %all-gather = f32[1280,128]{1,0:T(8,128)S(1)} all-gather(f32[80,128]{1,0:T(8,128)S(1)} %pad_maximum_fusion.1), channel_id=2, replica_groups=mesh['rows'=16,'samp'=16] {'rows'}, dimensions={0}, use_global_device_ids=true | all-gather | bytes 696320 | tf_op jit(solution)/shard_map/all_gather | solution.py:296
  61.6 1.1 broadcast_in_dim.32
  62.7 5.8 %all-to-all-start.1 = ((f32[16,16,8,128]{3,2,1,0:T(8,128)}), f32[16,16,8,128]{3,2,1,0:T(8,128)S(1)}, u32[]{:S(2)}, u32[]{:S(2)}) async-start(f32[16,16,8,128]{3,2,1,0:T(8,128)} %broadcast_in_dim.32), calls=%async_computation.1 | async-start | bytes 2097152 | tf_op jit(solution)/shard_map/all_to_all | solution.py:302
  68.5 0.1 pad_maximum_fusion.refs_2_
  68.6 1.4 collective-permute-start.4
  70.1 1.9 %collective-permute-start.3 = (f32[16,64,128]{2,1,0:T(8,128)S(1)}, f32[16,64,128]{2,1,0:T(8,128)S(1)}, u32[]{:S(2)}, u32[]{:S(2)}) collective-permute-start(f32[16,64,128]{2,1,0:T(8,128)S(1)} %slice.22.first), channel_id=1, source_target_pairs={{0,3},{1,2},{2,1},{3,0},{4,7},{5,6},{6,5},{7,4},{8,11},{9,10},{10,... | collective-permute-start | bytes 1572872 | tf_op jit(solution)/shard_map/ppermute | solution.py:301
  71.9 39.7 %collective-permute-done.3.second = f32[16,64,128]{2,1,0:T(8,128)S(1)} collective-permute-done((f32[16,64,128]{2,1,0:T(8,128)S(1)}, f32[16,64,128]{2,1,0:T(8,128)S(1)}, u32[]{:S(2)}, u32[]{:S(2)}) %collective-permute-start.3) | collective-permute-done | bytes 524320 | tf_op jit(solution)/shard_map/ppermute | solution.py:301
  111.7 15.6 %collective-permute-done.4.refs_3_ = f32[4,8,6,8,128]{4,3,2,1,0:T(8,128)} collective-permute-done((f32[4,8,6,8,128]{4,3,2,1,0:T(8,128)S(1)}, f32[4,8,6,8,128]{4,3,2,1,0:T(8,128)}, u32[]{:S(2)}, u32[]{:S(2)}) %collective-permute-start.4) | collective-permute-done | bytes 786464 | tf_op jit(solution)/shard_map/ppermute | solution.py:295
  127.2 0.0 all-to-all-done.1.mine
  127.2 1.3 collective-permute-start.5
  128.5 0.1 select_reduce_fusion.1
  128.6 0.1 copy.15
  128.7 0.1 compare_select_fusion.picks
  128.8 0.1 copy.17
  128.9 0.1 slice.18
  129.0 0.7 copy.19.refs_0_
  129.6 0.1 broadcast_add_fusion
  129.7 0.6 pad_add_fusion.refs_1_
  130.3 0.6 collective-permute-done.5.other
  131.0 0.0 copy-done.4
  131.0 0.0 copy-start
  131.0 6.9 %solve.1 = (f32[8,128,128]{2,1,0:T(8,128)}, bf16[2,1152,256]{2,1,0:T(8,128)(2,1)}) custom-call(s32[1]{0:T(128)} %bitcast.core, f32[16,64,128]{2,1,0:T(8,128)} %copy-done.6, f32[16,64,128]{2,1,0:T(8,128)} %copy-done.7, f32[16,16,8,128]{3,2,1,0:T(8,128)} %copy-done.4, f32[16,16,8,128]{3,2,1,0:T(8,128)} %collective-permute-done.5.other, f32[8,128,128]{2,1,0:T(8,128)} %inverse.1), custom_call_target="tpu_custom_call" | custom-call | tf_op jit(solution)/shard_map/solve/pallas_call | solution.py:130
  137.9 5.1 %product.1 = (f32[8,64,128]{2,1,0:T(8,128)}, f32[8,64,128]{2,1,0:T(8,128)}) custom-call(s32[8,8]{1,0:T(8,128)} %copy.19.refs_0_, s32[8]{0:T(128)} %pad_add_fusion.refs_1_, f32[4,8,6,8,128]{4,3,2,1,0:T(8,128)} %copy-done.5, f32[4,8,6,8,128]{4,3,2,1,0:T(8,128)} %collective-permute-done.4.refs_3_, bf16[2,1152,256]{2,1,0:T(8,128)(2,1)} %get-tuple-element.23.refs_4_.pairs), custom_call_target="tpu_custom_call" | custom-call | tf_op jit(solution)/shard_map/product/pallas_call | solution.py:183
  143.0 1.9 %collective-permute-start.6 = (f32[8,64,128]{2,1,0:T(8,128)}, f32[8,64,128]{2,1,0:T(8,128)}, u32[]{:S(2)}, u32[]{:S(2)}) collective-permute-start(f32[8,64,128]{2,1,0:T(8,128)} %get-tuple-element.25), channel_id=1, source_target_pairs={{0,3},{1,2},{2,1},{3,0},{4,7},{5,6},{6,5},{7,4},{8,11},{9,10},{10,... | collective-permute-start | bytes 786440 | tf_op jit(solution)/shard_map/ppermute | solution.py:307
  144.9 0.0 copy-done.1
  144.9 0.7 copy-done.3
  145.6 6.7 %update.1.base = f32[36,128,128]{2,1,0:T(8,128)} custom-call(s32[36,6]{1,0:T(8,128)S(1)} %copy-done.3, f32[36,128,128]{2,1,0:T(8,128)S(1)} %copy-done, f32[16,28,6,8,128]{4,3,2,1,0:T(8,128)} %bitcast.23, bf16[2,1152,256]{2,1,0:T(8,128)(2,1)S(1)} %copy-done.1), custom_call_target="tpu_custom_call" | custom-call | tf_op jit(solution)/shard_map/update/pallas_call | solution.py:218
  152.3 0.0 collective-permute-done.6.far
  152.3 2.0 %finish.1 = f32[36,128,128]{2,1,0:T(8,128)} custom-call(s32[1]{0:T(128)} %bitcast.14.spot, f32[36,128,128]{2,1,0:T(8,128)} %sides.5, f32[8,64,128]{2,1,0:T(8,128)} %get-tuple-element.24.near, f32[8,64,128]{2,1,0:T(8,128)} %collective-permute-done.6.far, f32[36,128,128]{2,1,0:T(8,128)} %update.1.base), custom_call_target="tpu_custom_call", output_to_operand_aliasing={{}: (4, {})} | custom-call | tf_op jit(solution)/shard_map/finish/pallas_call | solution.py:251
  (29 shorter events, 0.2 us)
Async XLA Ops:
  7.2 137.7 %all-gather.4.cloned.1.call-start = ((), (), s32[]{:S(2)}) async-start(), calls=%async_computation.2 | async-start | bytes 11698176 | tf_op jit(solution)/shard_map/all_gather | solution.py:268
  9.3 18.6 %copy-start.10 = (s32[32]{0:T(128)S(1)}, s32[32]{0:T(128)}, u32[]{:S(2)}) copy-start(s32[32]{0:T(128)} %constant.119) | copy-start | bytes 388
  9.3 18.6 %copy-start.9 = (s32[8]{0:T(128)S(1)}, s32[8]{0:T(128)}, u32[]{:S(2)}) copy-start(s32[8]{0:T(128)} %pivots.1) | copy-start | bytes 100
  12.5 30.0 %all-to-all-start = ((f32[16,80,128]{2,1,0:T(8,128)}), f32[16,80,128]{2,1,0:T(8,128)S(1)}, u32[]{:S(2)}, u32[]{:S(2)}) async-start(f32[16,80,128]{2,1,0:T(8,128)} %pack.1), calls=%async_computation | async-start | bytes 1310720 | tf_op jit(solution)/shard_map/all_to_all | solution.py:284
  23.4 19.1 %collective-permute-start = (f32[8,6,8,128]{3,2,1,0:T(8,128)S(1)}, f32[8,6,8,128]{3,2,1,0:T(8,128)S(1)}, u32[]{:S(2)}, u32[]{:S(2)}) collective-permute-start(f32[8,6,8,128]{3,2,1,0:T(8,128)S(1)} %slice.15), channel_id=1, source_target_pairs={{0,4},{1,5},{2,6},{3,7},{4,8},{5,9},{6,10},{7,11},{8,12},{9,13},{1... | collective-permute-start | bytes 589832 | tf_op jit(solution)/shard_map/ppermute | solution.py:270
  24.8 17.7 %collective-permute-start.1 = (f32[8,6,8,128]{3,2,1,0:T(8,128)S(1)}, f32[8,6,8,128]{3,2,1,0:T(8,128)S(1)}, u32[]{:S(2)}, u32[]{:S(2)}) collective-permute-start(f32[8,6,8,128]{3,2,1,0:T(8,128)S(1)} %slice.15), channel_id=1, source_target_pairs={{0,12},{1,13},{2,14},{3,15},{4,0},{5,1},{6,2},{7,3},{8,4},{9,5},{1... | collective-permute-start | bytes 589832 | tf_op jit(solution)/shard_map/ppermute | solution.py:270
  26.3 16.2 %collective-permute-start.2 = (f32[8,6,8,128]{3,2,1,0:T(8,128)S(1)}, f32[8,6,8,128]{3,2,1,0:T(8,128)S(1)}, u32[]{:S(2)}, u32[]{:S(2)}) collective-permute-start(f32[8,6,8,128]{3,2,1,0:T(8,128)S(1)} %slice.15), channel_id=1, source_target_pairs={{0,8},{1,9},{2,10},{3,11},{4,12},{5,13},{6,14},{7,15},{8,0},{9,1},... | collective-permute-start | bytes 589832 | tf_op jit(solution)/shard_map/ppermute | solution.py:270
  62.7 65.9 %copy-start.8 = (s32[36,6]{0,1:T(8,128)S(1)}, s32[36,6]{0,1:T(8,128)}, u32[]{:S(2)}) copy-start(s32[36,6]{0,1:T(8,128)} %param.8) | copy-start | bytes 2596
  62.7 64.5 %all-to-all-start.1 = ((f32[16,16,8,128]{3,2,1,0:T(8,128)}), f32[16,16,8,128]{3,2,1,0:T(8,128)S(1)}, u32[]{:S(2)}, u32[]{:S(2)}) async-start(f32[16,16,8,128]{3,2,1,0:T(8,128)} %broadcast_in_dim.32), calls=%async_computation.1 | async-start | bytes 2097152 | tf_op jit(solution)/shard_map/all_to_all | solution.py:302
  68.5 60.2 %copy-start.5 = (f32[4,8,6,8,128]{4,3,2,1,0:T(8,128)}, f32[4,8,6,8,128]{4,3,2,1,0:T(8,128)S(1)}, u32[]{:S(2)}) copy-start(f32[4,8,6,8,128]{4,3,2,1,0:T(8,128)S(1)} %pad_maximum_fusion.refs_2_) | copy-start | bytes 2359300
  68.6 58.7 %collective-permute-start.4 = (f32[4,8,6,8,128]{4,3,2,1,0:T(8,128)S(1)}, f32[4,8,6,8,128]{4,3,2,1,0:T(8,128)}, u32[]{:S(2)}, u32[]{:S(2)}) collective-permute-start(f32[4,8,6,8,128]{4,3,2,1,0:T(8,128)S(1)} %pad_maximum_fusion.refs_2_), channel_id=1, source_target_pairs={{0,1},{1,0},{2,3},{3,2},{4,5},{5,4},{6,7},{7,6},{8,9},{9,8},{10,11... | collective-permute-start | bytes 2359304 | tf_op jit(solution)/shard_map/ppermute | solution.py:295
  70.1 60.9 %copy-start.6 = (f32[16,64,128]{2,1,0:T(8,128)}, f32[16,64,128]{2,1,0:T(8,128)S(1)}, u32[]{:S(2)}) copy-start(f32[16,64,128]{2,1,0:T(8,128)S(1)} %slice.22.first) | copy-start | bytes 1572868
  70.1 41.6 %collective-permute-start.3 = (f32[16,64,128]{2,1,0:T(8,128)S(1)}, f32[16,64,128]{2,1,0:T(8,128)S(1)}, u32[]{:S(2)}, u32[]{:S(2)}) collective-permute-start(f32[16,64,128]{2,1,0:T(8,128)S(1)} %slice.22.first), channel_id=1, source_target_pairs={{0,3},{1,2},{2,1},{3,0},{4,7},{5,6},{6,5},{7,4},{8,11},{9,10},{10,... | collective-permute-start | bytes 1572872 | tf_op jit(solution)/shard_map/ppermute | solution.py:301
  111.7 19.3 %copy-start.7 = (f32[16,64,128]{2,1,0:T(8,128)}, f32[16,64,128]{2,1,0:T(8,128)S(1)}, u32[]{:S(2)}) copy-start(f32[16,64,128]{2,1,0:T(8,128)S(1)} %collective-permute-done.3.second) | copy-start | bytes 1572868
  127.2 3.7 %copy-start.4 = (f32[16,16,8,128]{3,2,1,0:T(8,128)}, f32[16,16,8,128]{3,2,1,0:T(8,128)S(1)}, u32[]{:S(2)}) copy-start(f32[16,16,8,128]{3,2,1,0:T(8,128)S(1)} %all-to-all-done.1.mine) | copy-start | bytes 3145732
  127.2 3.7 %collective-permute-start.5 = (f32[16,16,8,128]{3,2,1,0:T(8,128)S(1)}, f32[16,16,8,128]{3,2,1,0:T(8,128)}, u32[]{:S(2)}, u32[]{:S(2)}) collective-permute-start(f32[16,16,8,128]{3,2,1,0:T(8,128)S(1)} %all-to-all-done.1.mine), channel_id=1, source_target_pairs={{0,16},{16,0},{32,48},{48,32},{64,80},{80,64},{96,112},{112,96},{1... | collective-permute-start | bytes 3145736 | tf_op jit(solution)/shard_map/ppermute | solution.py:304
  128.8 2.2 %copy-start.2 = (s32[36,6]{1,0:T(8,128)}, s32[36,6]{1,0:T(8,128)S(1)}, u32[]{:S(2)}) copy-start(s32[36,6]{1,0:T(8,128)S(1)} %compare_select_fusion.picks) | copy-start | bytes 2596
  131.0 13.9 %copy-start = (f32[36,128,128]{2,1,0:T(8,128)S(1)}, f32[36,128,128]{2,1,0:T(8,128)}, u32[]{:S(2)}) copy-start(f32[36,128,128]{2,1,0:T(8,128)} %sides.5) | copy-start | bytes 7077892
  137.9 7.0 %copy-start.1 = (bf16[2,1152,256]{2,1,0:T(8,128)(2,1)S(1)}, bf16[2,1152,256]{2,1,0:T(8,128)(2,1)}, u32[]{:S(2)}) copy-start(bf16[2,1152,256]{2,1,0:T(8,128)(2,1)} %get-tuple-element.23.refs_4_.pairs) | copy-start | bytes 3538948
  143.0 9.3 %collective-permute-start.6 = (f32[8,64,128]{2,1,0:T(8,128)}, f32[8,64,128]{2,1,0:T(8,128)}, u32[]{:S(2)}, u32[]{:S(2)}) collective-permute-start(f32[8,64,128]{2,1,0:T(8,128)} %get-tuple-element.25), channel_id=1, source_target_pairs={{0,3},{1,2},{2,1},{3,0},{4,7},{5,6},{6,5},{7,4},{8,11},{9,10},{10,... | collective-permute-start | bytes 786440 | tf_op jit(solution)/shard_map/ppermute | solution.py:307
  144.9 0.7 copy-start.3
Sparse Core Ops, SparseCore 0:
  10.4 123.1 all-gather.3

commit v6 on v3

v6 whole, which is shorter than its diff:
```python
import jax
import jax.numpy as jnp
from jax import lax
from jax.experimental import pallas as pl
from jax.experimental.pallas import tpu as pltpu
from jax.sharding import PartitionSpec as P

BLOCK = 128
STEPS = 8
SLOTS = 6
RANKS = 16
SIDE = 4
SLICE = BLOCK // RANKS
HALF = BLOCK // 2
TRI = 32
MOVES = (1, -1, 2)
SETS = 1 + 2 * len(MOVES)
STRIP = SIDE * SLICE
EPILOGUE_ROWS = 9


def tri(k, i):
    return k * (k - 1) // 2 + i


def shift_y(d):
    return [(i, (i // SIDE + d) % SIDE * SIDE + i % SIDE) for i in range(RANKS)]


def shift_x(d):
    return [(i, i // SIDE * SIDE + (i % SIDE + d) % SIDE) for i in range(RANKS)]


TRI_PIVOT = [k for k in range(STEPS) for _ in range(k)] + [STEPS - 1] * (TRI - tri(STEPS, 0))
COLUMNS_OF_Y = [[SIDE * y + x for y in range(SIDE)] for x in range(SIDE)]
ROWS_OF_X = [[SIDE * y + x for x in range(SIDE)] for y in range(SIDE)]
OTHER_CORE = [(i, i ^ 1) for i in range(RANKS)]


def split(x):
    hi = x.astype(jnp.bfloat16)
    lo = (x - hi.astype(jnp.float32)).astype(jnp.bfloat16)
    return hi, lo


def dot(a, b):
    return lax.dot_general(a, b, (((1,), (0,)), ((), ())), preferred_element_type=jnp.float32)


def pack_kernel(pivots, columns, sides, factor, out, rows_buf, sem_f, sem_r):
    row_count = sides.shape[0]
    place = [lax.rem(pivots[j], row_count) for j in range(STEPS)]
    factor_copies, side_copies = [], []
    for j in range(STEPS):
        copy = pltpu.make_async_copy(factor.at[place[j]], rows_buf.at[j], sem_f.at[j])
        copy.start()
        factor_copies.append(copy)
    for j in range(STEPS):
        for h in range(2):
            copy = pltpu.make_async_copy(
                sides.at[place[j], pl.ds(h * HALF, HALF)], out.at[2 * j + h, pl.ds(0, HALF)], sem_r.at[2 * j + h]
            )
            copy.start()
            side_copies.append(copy)
    for copy in factor_copies:
        copy.wait()
    for j in range(STEPS):
        at = place[j]
        for i in range(j):
            piece = jnp.zeros((SLICE, BLOCK), jnp.float32)
            for s in range(SLOTS):
                piece = jnp.where(columns[s, at] == i, rows_buf[j, s], piece)
            b = tri(j, i)
            out[b // 2, pl.ds(HALF + (b % 2) * SLICE, SLICE)] = piece
    for b in range(tri(STEPS, 0), TRI):
        out[b // 2, pl.ds(HALF + (b % 2) * SLICE, SLICE)] = jnp.zeros((SLICE, BLOCK), jnp.float32)
    for copy in side_copies:
        copy.wait()


def pack(pivots, columns, sides, factor):
    smem = pl.BlockSpec(memory_space=pltpu.SMEM)
    hbm = pl.BlockSpec(memory_space=pl.ANY)
    return pl.pallas_call(
        pack_kernel,
        out_shape=jax.ShapeDtypeStruct((RANKS, HALF + 2 * SLICE, BLOCK), jnp.float32),
        in_specs=[smem, smem, hbm, hbm],
        out_specs=pl.BlockSpec(memory_space=pltpu.VMEM),
        scratch_shapes=[
            pltpu.VMEM((STEPS, SLOTS, SLICE, BLOCK), jnp.float32),
            pltpu.SemaphoreType.DMA((STEPS,)),
            pltpu.SemaphoreType.DMA((2 * STEPS,)),
        ],
        name="pack",
    )(pivots, columns, sides, factor)


def solve_kernel(core, own, sides_here, sides_there, mine, other, inverse, solved, pairs, side):
    flag = core[0]

    def factor(k, i):
        b = tri(k, i)
        near = mine[:, b % RANKS].reshape(BLOCK, BLOCK)
        far = other[:, b % RANKS].reshape(BLOCK, BLOCK)
        return jnp.where(flag == b // RANKS, near, far)

    def product(a, hi, lo):
        ah, al = split(a)
        return dot(ah, hi) + dot(ah, lo) + dot(al, hi)

    quarter = STEPS // 2
    for j in range(STEPS):
        side[j, :, :BLOCK] = own[2 * j : 2 * j + 2, :HALF].reshape(BLOCK, BLOCK)
        at = 2 * (j % quarter)
        for t in range(1, SETS):
            near = sides_here[t - 1, at : at + 2].reshape(BLOCK, BLOCK)
            far = sides_there[t - 1, at : at + 2].reshape(BLOCK, BLOCK)
            side[j, :, t * BLOCK : (t + 1) * BLOCK] = jnp.where(flag == j // quarter, near, far)
    for j in range(STEPS):
        hi, lo = split(side[j])
        x = product(inverse[j], hi, lo)
        solved[j] = x[:, :BLOCK]
        hi, lo = split(x)
        for t in range(SETS):
            pairs[t, j * BLOCK : (j + 1) * BLOCK, :BLOCK] = hi[:, t * BLOCK : (t + 1) * BLOCK]
            pairs[t, j * BLOCK : (j + 1) * BLOCK, BLOCK:] = lo[:, t * BLOCK : (t + 1) * BLOCK]
        for k in range(j + 1, STEPS):
            side[k] = side[k] - product(factor(k, j), hi, lo)


def solve(core, own, sides_here, sides_there, mine, other, inverse):
    vmem = pl.BlockSpec(memory_space=pltpu.VMEM)
    return pl.pallas_call(
        solve_kernel,
        out_shape=(
            jax.ShapeDtypeStruct((STEPS, BLOCK, BLOCK), jnp.float32),
            jax.ShapeDtypeStruct((SETS, STEPS * BLOCK, 2 * BLOCK), jnp.bfloat16),
        ),
        in_specs=[pl.BlockSpec(memory_space=pltpu.SMEM)] + [vmem] * 6,
        out_specs=(vmem, vmem),
        scratch_shapes=[pltpu.VMEM((STEPS, BLOCK, SETS * BLOCK), jnp.float32)],
        compiler_params=pltpu.CompilerParams(vmem_limit_bytes=28 * 2**20),
        name="solve",
    )(core, own, sides_here, sides_there, mine, other, inverse)


def product_kernel(first_set, rows, slots, factor, pairs, *rest):
    outs, (high, low) = rest[: 1 + len(MOVES)], rest[1 + len(MOVES) :]

    def build(r, carry):
        at_row = pl.multiple_of(r * STRIP, STRIP)
        for c in range(STEPS):
            at = slots[r, c]
            block = factor[:, r, jnp.minimum(at, SLOTS - 1)].reshape(STRIP, BLOCK)
            hi, lo = split(jnp.where(at < SLOTS, block, 0.0))
            high[pl.ds(at_row, STRIP), c * BLOCK : (c + 1) * BLOCK] = hi
            low[pl.ds(at_row, STRIP), c * BLOCK : (c + 1) * BLOCK] = lo
        return carry

    lax.fori_loop(0, rows, build, 0)
    sets = (0,) + tuple(range(first_set, first_set + len(MOVES)))
    for t, out in zip(sets, outs):
        full = dot(high[...], pairs[t])
        small = dot(low[...], pairs[t, :, :BLOCK])
        out[...] = (full[:, :BLOCK] + full[:, BLOCK:] + small).reshape(rows, STRIP, BLOCK)


def product(first_set, slots, factor, pairs):
    rows = slots.shape[0]
    vmem = pl.BlockSpec(memory_space=pltpu.VMEM)
    piece = jax.ShapeDtypeStruct((rows, STRIP, BLOCK), jnp.float32)
    return pl.pallas_call(
        lambda *refs: product_kernel(first_set, rows, *refs),
        out_shape=(piece,) * (1 + len(MOVES)),
        in_specs=[pl.BlockSpec(memory_space=pltpu.SMEM), vmem, vmem],
        out_specs=(vmem,) * (1 + len(MOVES)),
        scratch_shapes=[pltpu.VMEM((rows * STRIP, STEPS * BLOCK), jnp.bfloat16)] * 2,
        compiler_params=pltpu.CompilerParams(vmem_limit_bytes=24 * 2**20),
        name="product",
    )(slots, factor, pairs)


def finish_kernel(half_steps, spots, sides, *refs):
    step = pl.program_id(0)
    out = refs[-1]
    count = 1 + len(MOVES)
    tops, bottoms = refs[:count], refs[count : 2 * count]

    @pl.when(step < half_steps)
    def _():
        for t, ref in enumerate(tops):
            for r in range(EPILOGUE_ROWS):
                for q in range(SIDE):
                    at = pl.multiple_of(STRIP * q + SLICE * spots[0, t], SLICE)
                    out[r, pl.ds(at, SLICE)] = sides[r, pl.ds(at, SLICE)] - ref[r, SLICE * q : SLICE * (q + 1)]

    @pl.when(step >= half_steps)
    def _():
        for t, ref in enumerate(bottoms):
            at = pl.multiple_of(STRIP * spots[1, t], STRIP)
            out[:, pl.ds(at, STRIP)] = sides[:, pl.ds(at, STRIP)] - ref[...]


def finish(spots, sides, tops, bottoms):
    rows = sides.shape[0]
    half_steps = rows // 2 // EPILOGUE_ROWS
    whole = pl.BlockSpec((EPILOGUE_ROWS, BLOCK, BLOCK), lambda g: (g, 0, 0))
    early = pl.BlockSpec((EPILOGUE_ROWS, STRIP, BLOCK), lambda g: (jnp.minimum(g, half_steps - 1), 0, 0))
    late = pl.BlockSpec((EPILOGUE_ROWS, STRIP, BLOCK), lambda g: (jnp.maximum(g - half_steps, 0), 0, 0))
    return pl.pallas_call(
        lambda *refs: finish_kernel(half_steps, *refs),
        grid=(rows // EPILOGUE_ROWS,),
        out_shape=jax.ShapeDtypeStruct(sides.shape, jnp.float32),
        in_specs=[pl.BlockSpec(memory_space=pltpu.SMEM), whole] + [early] * len(tops) + [late] * len(bottoms),
        out_specs=whole,
        name="finish",
    )(spots, sides, *tops, *bottoms)


def local(right_sides, factor_blocks, block_columns, pivot_rows, diag_inverse):
    row_count = right_sides.shape[0]
    half_rows = row_count // 2
    rank = lax.axis_index("rows")
    here = lax.axis_index("samp")
    y, x = here // SIDE, here % SIDE

    top = lax.all_gather(factor_blocks[:half_rows], "samp", axis_index_groups=COLUMNS_OF_Y)
    bottom = lax.all_gather(factor_blocks[half_rows:], "samp", axis_index_groups=ROWS_OF_X)

    owner = pivot_rows // row_count
    ids = rank * row_count + jnp.arange(row_count, dtype=jnp.int32)
    targets = jnp.arange(STEPS, dtype=jnp.int32)
    row_rank = STEPS + jnp.sum(jnp.where(ids[:, None] == pivot_rows[None, :], targets - STEPS, 0), axis=1)
    picks = jnp.where(block_columns < row_rank[:, None], block_columns, STEPS)
    slots = jnp.min(
        jnp.where(picks[:, None, :] == targets[None, :, None], jnp.arange(SLOTS, dtype=jnp.int32), SLOTS), axis=2
    )

    payload = pack(pivot_rows, block_columns.T, right_sides, factor_blocks)
    pieces = lax.all_to_all(payload, "rows", 0, 0)
    tri_owner = owner[jnp.array(TRI_PIVOT, jnp.int32)]
    part = jnp.concatenate(
        [
            lax.dynamic_slice(pieces, (owner[rank // 2], 0, 0), (1, HALF, BLOCK))[0],
            lax.dynamic_slice(pieces, (tri_owner[2 * rank], HALF, 0), (1, SLICE, BLOCK))[0],
            lax.dynamic_slice(pieces, (tri_owner[2 * rank + 1], HALF + SLICE, 0), (1, SLICE, BLOCK))[0],
        ]
    )
    gathered = lax.all_gather(part, "rows", axis=0, tiled=False)
    gathered, top = lax.optimization_barrier((gathered, top))
    core = rank % 2
    slices = gathered[:, HALF:].reshape(TRI, SLICE, BLOCK)
    half = lax.dynamic_slice(slices, (core * RANKS, 0, 0), (RANKS, SLICE, BLOCK))
    own = gathered[:, :HALF]
    share = lax.dynamic_slice(own, (core * STEPS, 0, 0), (STEPS, HALF, BLOCK))
    shares = [lax.ppermute(share, "samp", shift(-d)) for shift in (shift_x, shift_y) for d in MOVES]
    mine = lax.all_to_all(jnp.broadcast_to(half, (RANKS,) + half.shape), "samp", 0, 0)
    mine, bottom, *shares = lax.optimization_barrier((mine, bottom, *shares))
    sides_here = jnp.stack(shares)
    sides_there = lax.ppermute(sides_here, "rows", OTHER_CORE)
    other = lax.ppermute(mine, "rows", OTHER_CORE)
    solved, pairs = solve(core.reshape(1), own, sides_here, sides_there, mine, other, diag_inverse)
    tops = list(product(1, slots[:half_rows], top, pairs))
    tops[1:] = [lax.ppermute(v, "samp", shift_x(d)) for v, d in zip(tops[1:], MOVES)]
    bottoms = list(product(1 + len(MOVES), slots[half_rows:], bottom, pairs))
    bottoms[1:] = [lax.ppermute(v, "samp", shift_y(d)) for v, d in zip(bottoms[1:], MOVES)]
    steps = jnp.array((0,) + MOVES, jnp.int32)
    spots = (jnp.stack([x, y])[:, None] - steps[None, :] + SIDE) % SIDE
    return solved, finish(spots, right_sides, tops, bottoms)


def solution(mesh):
    placed = (P("rows", None, "samp"), P("rows", None, "samp", None), P("rows", None), P(), P())
    return jax.shard_map(
        local,
        mesh=mesh,
        in_specs=placed,
        out_specs=(P(None, None, "samp"), P("rows", None, "samp")),
        check_vma=False,
    )
```

time: 195 us -> 168 us (0.86)
  waiting for transfers between devices: 83.5 us -> 52 us
  starting transfers between devices: 27.1 us -> 38.1 us
  other arithmetic: 3.42 us -> 0.88 us
    all_to_all x1, waiting for transfers between devices: 28.5 us -> 0.01 us  [local(): lax.all_to_all(jnp.broadcast_to(half, (RANKS,) + half.shape), 'samp', 0, 0)]
    ppermute x6 -> x13, starting transfers between devices: 7.92 us -> 21 us  [the longest x6 9.58 us: local(): lax.ppermute(share, 'samp', shift(-d))]
    ppermute x6 -> x13, waiting for transfers between devices: 42.9 us -> 35.7 us  [the longest x6 24.9 us: local(): lax.ppermute(share, 'samp', shift(-d))]
    pallas_call x1, Pallas kernels: 5.96 us -> 11.1 us  [solve(): pl.pallas_call(solve_kernel, out_shape=(jax.ShapeDtypeStruct((STEPS, BLOC...]
    ppermute x1, waiting for transfers between devices: 0.01 us -> 4.09 us  [local(): other = lax.ppermute(mine, 'rows', OTHER_CORE)]
    pallas_call x2, Pallas kernels: 11.4 us -> 7.96 us  [product(): pl.pallas_call(lambda *refs: product_kernel(first_set, rows, *refs), out_...]
    another operation x3 -> x1, other arithmetic: 2.68 us -> 0.07 us  [local(): spots = (jnp.stack([x, y])[:, None] - steps[None, :] + SIDE) % SIDE]
    slice x1 -> x2, local copies, waits for them, and re-layouts: 0.07 us -> 2.19 us  [the longest x1 2.12 us: local(): factor_blocks[half_rows:]]
  transfers between devices with their start and end apart: 11 -> 18, of which waited for: 7 -> 7; matrix products, arithmetic and copies ran while one was open for 4% -> 3% of each run, Pallas kernels for 11% -> 4%
where the time goes in v6:
time: 168 us
  waiting for transfers between devices  52 us (31%)
  starting transfers between devices  38.1 us (23%)
  Pallas kernels  26.7 us (16%)
  between operations  20.1 us (12%)
  blocking collectives  16.3 us (10%)
  local copies, waits for them, and re-layouts  13.7 us (8%)
    ppermute x6, waiting for transfers between devices, local(): lax.ppermute(share, 'samp', shift(-d))  24.9 us
    all_gather x1, blocking collectives, local(): gathered = lax.all_gather(part, 'rows', axis=0, tiled=False)  16.3 us
    all_to_all x1, waiting for transfers between devices, local(): pieces = lax.all_to_all(payload, 'rows', 0, 0)  11.5 us
    pallas_call x1, Pallas kernels, solve(): pl.pallas_call(solve_kernel, out_shape=(jax.ShapeDtypeStruct((STEPS, BLOC...  11.1 us
    ppermute x3, waiting for transfers between devices, local(): lax.ppermute(v, 'samp', shift_x(d))  10.8 us
    all_to_all x1, starting transfers between devices, local(): pieces = lax.all_to_all(payload, 'rows', 0, 0)  9.99 us
    ppermute x6, starting transfers between devices, local(): lax.ppermute(share, 'samp', shift(-d))  9.58 us
    unnamed x57, local copies, waits for them, and re-layouts  8.27 us
  transfers between devices with their start and end apart: 18, of which 7 were waited for; matrix products, arithmetic and copies ran while one was open for 3% of the time, Pallas kernels for 4%

profile of v6, /device:TPU:1, one launch (start us, length us, event | category | flops | bytes accessed | tf_op | source)
XLA Modules:
  0.0 167.7 jit_solution(15085735357960781920)
XLA Ops:
  7.2 0.0 all-gather.6.cloned.1.call-start
  7.2 2.1 %fusion.1 = (f32[18,6,8,128]{3,2,1,0:T(8,128)}, f32[18,6,8,128]{3,2,1,0:T(8,128)}) fusion(f32[36,6,8,128]{3,2,1,0:T(8,128)} %factor.1), kind=kLoop, calls=%fused_computation.28 | loop fusion | bytes 1769472 | tf_op jit(solution)/shard_map/slice | solution.py:228
  9.4 3.1 %pack.1 = f32[16,80,128]{2,1,0:T(8,128)} custom-call(s32[8]{0:T(128)} %pivots.1, s32[6,36]{1,0:T(8,128)} %bitcast.34, f32[36,128,128]{2,1,0:T(8,128)} %refs_1_.1, f32[36,6,8,128]{3,2,1,0:T(8,128)} %factor.1), custom_call_target="tpu_custom_call" | custom-call | tf_op jit(solution)/shard_map/pack/pallas_call | solution.py:84
  12.4 10.0 %all-to-all-start = ((f32[16,80,128]{2,1,0:T(8,128)}), f32[16,80,128]{2,1,0:T(8,128)S(1)}, u32[]{:S(2)}, u32[]{:S(2)}) async-start(f32[16,80,128]{2,1,0:T(8,128)} %pack.1), calls=%async_computation | async-start | bytes 1310720 | tf_op jit(solution)/shard_map/all_to_all | solution.py:240
  22.5 0.7 all-gather.8.cloned.1.call-update
  23.2 0.7 dynamic_slice.24
  25.2 0.7 gather_fusion
  25.9 0.7 fusion.3
  31.0 11.5 %all-to-all-done = f32[16,80,128]{2,1,0:T(8,128)S(1)} async-done(((f32[16,80,128]{2,1,0:T(8,128)}), f32[16,80,128]{2,1,0:T(8,128)S(1)}, u32[]{:S(2)}, u32[]{:S(2)}) %all-to-all-start) | async-done | bytes 655392 | tf_op jit(solution)/shard_map/all_to_all | solution.py:240
  42.5 16.3 %all-gather = f32[1280,128]{1,0:T(8,128)S(1)} all-gather(f32[80,128]{1,0:T(8,128)S(1)} %pad_maximum_fusion), channel_id=2, replica_groups=mesh['rows'=16,'samp'=16] {'rows'}, dimensions={0}, use_global_device_ids=true | all-gather | bytes 696320 | tf_op jit(solution)/shard_map/all_gather | solution.py:249
  58.8 1.1 broadcast_in_dim.34
  59.8 6.8 %all-to-all-start.1 = ((f32[16,16,8,128]{3,2,1,0:T(8,128)}), f32[16,16,8,128]{3,2,1,0:T(8,128)S(1)}, u32[]{:S(2)}, u32[]{:S(2)}) async-start(f32[16,16,8,128]{3,2,1,0:T(8,128)} %broadcast_in_dim.34), calls=%async_computation.1 | async-start | bytes 2097152 | tf_op jit(solution)/shard_map/all_to_all | solution.py:257
  66.7 2.6 %collective-permute-start = (f32[8,64,128]{2,1,0:T(8,128)S(1)}, f32[8,64,128]{2,1,0:T(8,128)S(1)}, u32[]{:S(2)}, u32[]{:S(2)}) collective-permute-start(f32[8,64,128]{2,1,0:T(8,128)S(1)} %constant_dynamic-slice_fusion), channel_id=1, source_target_pairs={{0,3},{1,0},{2,1},{3,2},{4,7},{5,4},{6,5},{7,6},{8,11},{9,8},{10,9... | collective-permute-start | bytes 786440 | tf_op jit(solution)/shard_map/ppermute | solution.py:256
  69.4 1.8 %collective-permute-start.2 = (f32[8,64,128]{2,1,0:T(8,128)S(1)}, f32[8,64,128]{2,1,0:T(8,128)S(1)}, u32[]{:S(2)}, u32[]{:S(2)}) collective-permute-start(f32[8,64,128]{2,1,0:T(8,128)S(1)} %constant_dynamic-slice_fusion), channel_id=1, source_target_pairs={{0,2},{1,3},{2,0},{3,1},{4,6},{5,7},{6,4},{7,5},{8,10},{9,11},{10,... | collective-permute-start | bytes 786440 | tf_op jit(solution)/shard_map/ppermute | solution.py:256
  71.1 2.4 %collective-permute-start.3 = (f32[8,64,128]{2,1,0:T(8,128)S(1)}, f32[8,64,128]{2,1,0:T(8,128)S(1)}, u32[]{:S(2)}, u32[]{:S(2)}) collective-permute-start(f32[8,64,128]{2,1,0:T(8,128)S(1)} %constant_dynamic-slice_fusion), channel_id=1, source_target_pairs={{0,12},{1,13},{2,14},{3,15},{4,0},{5,1},{6,2},{7,3},{8,4},{9,5},{1... | collective-permute-start | bytes 786440 | tf_op jit(solution)/shard_map/ppermute | solution.py:256
  73.5 19.3 %collective-permute-done = f32[8,64,128]{2,1,0:T(8,128)S(1)} collective-permute-done((f32[8,64,128]{2,1,0:T(8,128)S(1)}, f32[8,64,128]{2,1,0:T(8,128)S(1)}, u32[]{:S(2)}, u32[]{:S(2)}) %collective-permute-start) | collective-permute-done | bytes 262176 | tf_op jit(solution)/shard_map/ppermute | solution.py:256
  92.9 2.8 %collective-permute-start.5 = (f32[8,64,128]{2,1,0:T(8,128)S(1)}, f32[8,64,128]{2,1,0:T(8,128)S(1)}, u32[]{:S(2)}, u32[]{:S(2)}) collective-permute-start(f32[8,64,128]{2,1,0:T(8,128)S(1)} %constant_dynamic-slice_fusion), channel_id=1, source_target_pairs={{0,8},{1,9},{2,10},{3,11},{4,12},{5,13},{6,14},{7,15},{8,0},{9,1},... | collective-permute-start | bytes 786440 | tf_op jit(solution)/shard_map/ppermute | solution.py:256
  95.6 4.1 %collective-permute-done.2 = f32[8,64,128]{2,1,0:T(8,128)S(1)} collective-permute-done((f32[8,64,128]{2,1,0:T(8,128)S(1)}, f32[8,64,128]{2,1,0:T(8,128)S(1)}, u32[]{:S(2)}, u32[]{:S(2)}) %collective-permute-start.2) | collective-permute-done | bytes 262176 | tf_op jit(solution)/shard_map/ppermute | solution.py:256
  99.8 1.4 collective-permute-done.5
  101.2 0.7 copy-done.19
  101.9 1.0 bitcast_dynamic-update-slice_fusion.4
  103.0 1.0 bitcast_dynamic-update-slice_fusion.3
  104.0 2.0 %collective-permute-start.6 = (f32[6,8,64,128]{3,2,1,0:T(8,128)S(1)}, f32[6,8,64,128]{3,2,1,0:T(8,128)}, u32[]{:S(2)}, u32[]{:S(2)}) collective-permute-start(f32[6,8,64,128]{3,2,1,0:T(8,128)S(1)} %bitcast_dynamic-update-slice_fusion.sides_here), channel_id=1, source_target_pairs={{0,16},{16,0},{32,48},{48,32},{64,80},{80,64},{96,112},{112,96},{1... | collective-permute-start | bytes 4718600 | tf_op jit(solution)/shard_map/ppermute | solution.py:260
  106.0 0.3 collective-permute-start.7
  106.3 0.1 select_reduce_fusion.1
  106.5 0.1 fusion.2
  106.5 0.1 copy.15.refs_0_
  106.6 4.1 %collective-permute-done.7.other = f32[16,16,8,128]{3,2,1,0:T(8,128)} collective-permute-done((f32[16,16,8,128]{3,2,1,0:T(8,128)S(1)}, f32[16,16,8,128]{3,2,1,0:T(8,128)}, u32[]{:S(2)}, u32[]{:S(2)}) %collective-permute-start.7) | collective-permute-done | bytes 1048608 | tf_op jit(solution)/shard_map/ppermute | solution.py:261
  110.7 1.0 copy-done.4
  111.8 11.1 %solve.1 = (f32[8,128,128]{2,1,0:T(8,128)}, bf16[7,1024,256]{2,1,0:T(8,128)(2,1)S(1)}) custom-call(s32[1]{0:T(128)} %bitcast.core, f32[16,64,128]{2,1,0:T(8,128)S(1)} %slice.19.own, f32[6,8,64,128]{3,2,1,0:T(8,128)S(1)} %bitcast_dynamic-update-slice_fusion.sides_here, f32[6,8,64,128]{3,2,1,0:T(8,128)} %collective-permute-done.6.sides_there, ...), custom_call_target="tpu_custom_call" | custom-call | tf_op jit(solution)/shard_map/solve/pallas_call | solution.py:133
  122.9 4.0 %product.3 = (f32[18,32,128]{2,1,0:T(8,128)S(1)}, f32[18,32,128]{2,1,0:T(8,128)S(1)}, f32[18,32,128]{2,1,0:T(8,128)S(1)}, f32[18,32,128]{2,1,0:T(8,128)S(1)}) custom-call(s32[18,8]{1,0:T(8,128)S(1)} %copy.15.refs_0_, f32[4,18,6,8,128]{4,3,2,1,0:T(8,128)S(1)} %bitcast.30, bf16[7,1024,256]{2,1,0:T(8,128)(2,1)S(1)} %get-tuple-element.32.refs_2_), custom_call_target="tpu_custom_call" | custom-call | tf_op jit(solution)/shard_map/product/pallas_call | solution.py:172
  126.9 0.7 copy-done.5
  127.6 1.4 collective-permute-start.11
  128.9 0.1 copy.14.refs_0_
  129.0 1.3 collective-permute-start.12
  130.3 1.6 collective-permute-start.13
  131.9 2.0 %copy-done.1 = bf16[7,1024,256]{2,1,0:T(8,128)(2,1)S(1)} copy-done((bf16[7,1024,256]{2,1,0:T(8,128)(2,1)S(1)}, bf16[7,1024,256]{2,1,0:T(8,128)(2,1)}, u32[]{:S(2)}) %copy-start.1) | copy-done | bytes 3670040
  134.0 4.0 %product.2 = (f32[18,32,128]{2,1,0:T(8,128)S(1)}, f32[18,32,128]{2,1,0:T(8,128)S(1)}, f32[18,32,128]{2,1,0:T(8,128)S(1)}, f32[18,32,128]{2,1,0:T(8,128)S(1)}) custom-call(s32[18,8]{1,0:T(8,128)S(1)} %copy.14.refs_0_, f32[4,18,6,8,128]{4,3,2,1,0:T(8,128)S(1)} %bitcast.29, bf16[7,1024,256]{2,1,0:T(8,128)(2,1)S(1)} %copy-done.1), custom_call_target="tpu_custom_call" | custom-call | tf_op jit(solution)/shard_map/product/pallas_call | solution.py:172
  138.0 0.7 copy-done.6
  138.7 2.5 %collective-permute-start.10 = (f32[18,32,128]{2,1,0:T(8,128)S(1)}, f32[18,32,128]{2,1,0:T(8,128)S(1)}, u32[]{:S(2)}, u32[]{:S(2)}) collective-permute-start(f32[18,32,128]{2,1,0:T(8,128)S(1)} %get-tuple-element.36), channel_id=1, source_target_pairs={{0,2},{1,3},{2,0},{3,1},{4,6},{5,7},{6,4},{7,5},{8,10},{9,11},{10,... | collective-permute-start | bytes 884744 | tf_op jit(solution)/shard_map/ppermute | solution.py:264
  141.1 2.7 %collective-permute-start.9 = (f32[18,32,128]{2,1,0:T(8,128)S(1)}, f32[18,32,128]{2,1,0:T(8,128)S(1)}, u32[]{:S(2)}, u32[]{:S(2)}) collective-permute-start(f32[18,32,128]{2,1,0:T(8,128)S(1)} %get-tuple-element.35), channel_id=1, source_target_pairs={{0,3},{1,0},{2,1},{3,2},{4,7},{5,4},{6,5},{7,6},{8,11},{9,8},{10,9... | collective-permute-start | bytes 884744 | tf_op jit(solution)/shard_map/ppermute | solution.py:264
  143.8 0.1 pad_add_fusion
  143.9 0.7 and_select_fusion.refs_0_
  144.6 2.9 %collective-permute-done.10.refs_5_ = f32[18,32,128]{2,1,0:T(8,128)S(1)} collective-permute-done((f32[18,32,128]{2,1,0:T(8,128)S(1)}, f32[18,32,128]{2,1,0:T(8,128)S(1)}, u32[]{:S(2)}, u32[]{:S(2)}) %collective-permute-start.10) | collective-permute-done | bytes 294944 | tf_op jit(solution)/shard_map/ppermute | solution.py:264
  147.5 7.9 %collective-permute-done.8.refs_3_ = f32[18,32,128]{2,1,0:T(8,128)S(1)} collective-permute-done((f32[18,32,128]{2,1,0:T(8,128)S(1)}, f32[18,32,128]{2,1,0:T(8,128)S(1)}, u32[]{:S(2)}, u32[]{:S(2)}) %collective-permute-start.8) | collective-permute-done | bytes 294944 | tf_op jit(solution)/shard_map/ppermute | solution.py:264
  155.5 0.7 copy-done.11
  156.1 0.1 copy-done.12
  156.2 4.6 %finish.1 = f32[36,128,128]{2,1,0:T(8,128)} custom-call(s32[2,4]{1,0:T(2,128)} %and_select_fusion.refs_0_, f32[36,128,128]{2,1,0:T(8,128)} %refs_1_.1, f32[18,32,128]{2,1,0:T(8,128)} %copy-done.6, f32[18,32,128]{2,1,0:T(8,128)} %copy-done.11, f32[18,32,128]{2,1,0:T(8,128)} %copy-done.12, f32[18,32,128]{2,1,0:T(8,128)} %copy-done.10, ...), custom_call_target="tpu_custom_call" | custom-call | tf_op jit(solution)/shard_map/finish/pallas_call | solution.py:210
  (77 shorter events, 0.4 us)
Async XLA Ops:
  7.2 51.6 %all-gather.6.cloned.1.call-start = ((), (), s32[]{:S(2)}) async-start(), calls=%async_computation.2 | async-start | bytes 2211840 | tf_op jit(solution)/shard_map/all_gather | solution.py:227
  12.4 10.8 %copy-start.22 = (s32[8]{0:T(128)S(1)}, s32[8]{0:T(128)}, u32[]{:S(2)}) copy-start(s32[8]{0:T(128)} %pivots.1) | copy-start | bytes 100
  12.4 12.7 %copy-start.23 = (s32[32]{0:T(128)S(1)}, s32[32]{0:T(128)}, u32[]{:S(2)}) copy-start(s32[32]{0:T(128)} %constant.104) | copy-start | bytes 388
  12.4 30.0 %all-to-all-start = ((f32[16,80,128]{2,1,0:T(8,128)}), f32[16,80,128]{2,1,0:T(8,128)S(1)}, u32[]{:S(2)}, u32[]{:S(2)}) async-start(f32[16,80,128]{2,1,0:T(8,128)} %pack.1), calls=%async_computation | async-start | bytes 1310720 | tf_op jit(solution)/shard_map/all_to_all | solution.py:240
  22.4 73.2 %all-gather.8.cloned.1.call-start = ((), (), s32[]{:S(2)}) async-start(), calls=%async_computation.3 | async-start | bytes 2211840 | tf_op jit(solution)/shard_map/all_gather | solution.py:228
  59.8 41.3 %all-to-all-start.1 = ((f32[16,16,8,128]{3,2,1,0:T(8,128)}), f32[16,16,8,128]{3,2,1,0:T(8,128)S(1)}, u32[]{:S(2)}, u32[]{:S(2)}) async-start(f32[16,16,8,128]{3,2,1,0:T(8,128)} %broadcast_in_dim.34), calls=%async_computation.1 | async-start | bytes 2097152 | tf_op jit(solution)/shard_map/all_to_all | solution.py:257
  66.7 26.2 %collective-permute-start = (f32[8,64,128]{2,1,0:T(8,128)S(1)}, f32[8,64,128]{2,1,0:T(8,128)S(1)}, u32[]{:S(2)}, u32[]{:S(2)}) collective-permute-start(f32[8,64,128]{2,1,0:T(8,128)S(1)} %constant_dynamic-slice_fusion), channel_id=1, source_target_pairs={{0,3},{1,0},{2,1},{3,2},{4,7},{5,4},{6,5},{7,6},{8,11},{9,8},{10,9... | collective-permute-start | bytes 786440 | tf_op jit(solution)/shard_map/ppermute | solution.py:256
  69.3 26.3 %collective-permute-start.1 = (f32[8,64,128]{2,1,0:T(8,128)S(1)}, f32[8,64,128]{2,1,0:T(8,128)S(1)}, u32[]{:S(2)}, u32[]{:S(2)}) collective-permute-start(f32[8,64,128]{2,1,0:T(8,128)S(1)} %constant_dynamic-slice_fusion), channel_id=1, source_target_pairs={{0,1},{1,2},{2,3},{3,0},{4,5},{5,6},{6,7},{7,4},{8,9},{9,10},{10,1... | collective-permute-start | bytes 786440 | tf_op jit(solution)/shard_map/ppermute | solution.py:256
  69.4 30.4 %collective-permute-start.2 = (f32[8,64,128]{2,1,0:T(8,128)S(1)}, f32[8,64,128]{2,1,0:T(8,128)S(1)}, u32[]{:S(2)}, u32[]{:S(2)}) collective-permute-start(f32[8,64,128]{2,1,0:T(8,128)S(1)} %constant_dynamic-slice_fusion), channel_id=1, source_target_pairs={{0,2},{1,3},{2,0},{3,1},{4,6},{5,7},{6,4},{7,5},{8,10},{9,11},{10,... | collective-permute-start | bytes 786440 | tf_op jit(solution)/shard_map/ppermute | solution.py:256
  71.1 28.7 %collective-permute-start.3 = (f32[8,64,128]{2,1,0:T(8,128)S(1)}, f32[8,64,128]{2,1,0:T(8,128)S(1)}, u32[]{:S(2)}, u32[]{:S(2)}) collective-permute-start(f32[8,64,128]{2,1,0:T(8,128)S(1)} %constant_dynamic-slice_fusion), channel_id=1, source_target_pairs={{0,12},{1,13},{2,14},{3,15},{4,0},{5,1},{6,2},{7,3},{8,4},{9,5},{1... | collective-permute-start | bytes 786440 | tf_op jit(solution)/shard_map/ppermute | solution.py:256
  73.5 26.3 %collective-permute-start.4 = (f32[8,64,128]{2,1,0:T(8,128)S(1)}, f32[8,64,128]{2,1,0:T(8,128)S(1)}, u32[]{:S(2)}, u32[]{:S(2)}) collective-permute-start(f32[8,64,128]{2,1,0:T(8,128)S(1)} %constant_dynamic-slice_fusion), channel_id=1, source_target_pairs={{0,4},{1,5},{2,6},{3,7},{4,8},{5,9},{6,10},{7,11},{8,12},{9,13},{1... | collective-permute-start | bytes 786440 | tf_op jit(solution)/shard_map/ppermute | solution.py:256
  92.9 8.3 %collective-permute-start.5 = (f32[8,64,128]{2,1,0:T(8,128)S(1)}, f32[8,64,128]{2,1,0:T(8,128)S(1)}, u32[]{:S(2)}, u32[]{:S(2)}) collective-permute-start(f32[8,64,128]{2,1,0:T(8,128)S(1)} %constant_dynamic-slice_fusion), channel_id=1, source_target_pairs={{0,8},{1,9},{2,10},{3,11},{4,12},{5,13},{6,14},{7,15},{8,0},{9,1},... | collective-permute-start | bytes 786440 | tf_op jit(solution)/shard_map/ppermute | solution.py:256
  95.6 5.5 %copy-start.13 = (f32[8,64,128]{2,1,0:T(8,128)}, f32[8,64,128]{2,1,0:T(8,128)S(1)}, u32[]{:S(2)}) copy-start(f32[8,64,128]{2,1,0:T(8,128)S(1)} %collective-permute-done.1) | copy-start | bytes 786436
  99.8 1.4 copy-start.14
  99.8 1.4 copy-start.15
  99.8 1.4 copy-start.17
  101.2 0.7 copy-start.19
  101.9 2.1 %copy-start.16 = (f32[8,64,128]{2,1,0:T(8,128)S(1)}, f32[8,64,128]{2,1,0:T(8,128)}, u32[]{:S(2)}) copy-start(f32[8,64,128]{2,1,0:T(8,128)} %copy-done.15) | copy-start | bytes 786436
  101.9 2.1 %copy-start.18 = (f32[8,64,128]{2,1,0:T(8,128)S(1)}, f32[8,64,128]{2,1,0:T(8,128)}, u32[]{:S(2)}) copy-start(f32[8,64,128]{2,1,0:T(8,128)} %copy-done.17) | copy-start | bytes 786436
  101.9 2.1 %copy-start.20 = (f32[8,64,128]{2,1,0:T(8,128)S(1)}, f32[8,64,128]{2,1,0:T(8,128)}, u32[]{:S(2)}) copy-start(f32[8,64,128]{2,1,0:T(8,128)} %copy-done.19) | copy-start | bytes 786436
  101.9 4.5 %copy-start.21 = (s32[36,6]{0,1:T(8,128)S(1)}, s32[36,6]{0,1:T(8,128)}, u32[]{:S(2)}) copy-start(s32[36,6]{0,1:T(8,128)} %param.9) | copy-start | bytes 2596
  104.0 6.7 %collective-permute-start.6 = (f32[6,8,64,128]{3,2,1,0:T(8,128)S(1)}, f32[6,8,64,128]{3,2,1,0:T(8,128)}, u32[]{:S(2)}, u32[]{:S(2)}) collective-permute-start(f32[6,8,64,128]{3,2,1,0:T(8,128)S(1)} %bitcast_dynamic-update-slice_fusion.sides_here), channel_id=1, source_target_pairs={{0,16},{16,0},{32,48},{48,32},{64,80},{80,64},{96,112},{112,96},{1... | collective-permute-start | bytes 4718600 | tf_op jit(solution)/shard_map/ppermute | solution.py:260
  106.0 4.7 %collective-permute-start.7 = (f32[16,16,8,128]{3,2,1,0:T(8,128)S(1)}, f32[16,16,8,128]{3,2,1,0:T(8,128)}, u32[]{:S(2)}, u32[]{:S(2)}) collective-permute-start(f32[16,16,8,128]{3,2,1,0:T(8,128)S(1)} %all-to-all-done.1.mine), channel_id=1, source_target_pairs={{0,16},{16,0},{32,48},{48,32},{64,80},{80,64},{96,112},{112,96},{1... | collective-permute-start | bytes 3145736 | tf_op jit(solution)/shard_map/ppermute | solution.py:261
  110.7 1.0 copy-start.4
  111.8 11.1 %copy-start.3 = (f32[72,6,8,128]{3,2,1,0:T(8,128)S(1)}, f32[72,6,8,128]{3,2,1,0:T(8,128)}, u32[]{:S(2)}) copy-start(f32[72,6,8,128]{3,2,1,0:T(8,128)} %all-gather.8.cloned.1.call-done) | copy-start | bytes 5308420
  122.8 4.0 %copy-start = (bf16[7,1024,256]{2,1,0:T(8,128)(2,1)}, bf16[7,1024,256]{2,1,0:T(8,128)(2,1)S(1)}, u32[]{:S(2)}) copy-start(bf16[7,1024,256]{2,1,0:T(8,128)(2,1)S(1)} %get-tuple-element.32.refs_2_) | copy-start | bytes 11010052
  122.9 9.1 %copy-start.2 = (f32[72,6,8,128]{3,2,1,0:T(8,128)S(1)}, f32[72,6,8,128]{3,2,1,0:T(8,128)}, u32[]{:S(2)}) copy-start(f32[72,6,8,128]{3,2,1,0:T(8,128)} %all-gather.6.cloned.1.call-done) | copy-start | bytes 5308420
  126.9 0.7 copy-start.5
  127.6 13.6 %collective-permute-start.11 = (f32[18,32,128]{2,1,0:T(8,128)S(1)}, f32[18,32,128]{2,1,0:T(8,128)S(1)}, u32[]{:S(2)}, u32[]{:S(2)}) collective-permute-start(f32[18,32,128]{2,1,0:T(8,128)S(1)} %get-tuple-element.39), channel_id=1, source_target_pairs={{0,4},{1,5},{2,6},{3,7},{4,8},{5,9},{6,10},{7,11},{8,12},{9,13},{1... | collective-permute-start | bytes 884744 | tf_op jit(solution)/shard_map/ppermute | solution.py:266
  129.0 15.5 %collective-permute-start.12 = (f32[18,32,128]{2,1,0:T(8,128)S(1)}, f32[18,32,128]{2,1,0:T(8,128)S(1)}, u32[]{:S(2)}, u32[]{:S(2)}) collective-permute-start(f32[18,32,128]{2,1,0:T(8,128)S(1)} %get-tuple-element.40), channel_id=1, source_target_pairs={{0,12},{1,13},{2,14},{3,15},{4,0},{5,1},{6,2},{7,3},{8,4},{9,5},{1... | collective-permute-start | bytes 884744 | tf_op jit(solution)/shard_map/ppermute | solution.py:266
  130.3 14.2 %collective-permute-start.13 = (f32[18,32,128]{2,1,0:T(8,128)S(1)}, f32[18,32,128]{2,1,0:T(8,128)S(1)}, u32[]{:S(2)}, u32[]{:S(2)}) collective-permute-start(f32[18,32,128]{2,1,0:T(8,128)S(1)} %get-tuple-element.41), channel_id=1, source_target_pairs={{0,8},{1,9},{2,10},{3,11},{4,12},{5,13},{6,14},{7,15},{8,0},{9,1},... | collective-permute-start | bytes 884744 | tf_op jit(solution)/shard_map/ppermute | solution.py:266
  131.9 2.0 %copy-start.1 = (bf16[7,1024,256]{2,1,0:T(8,128)(2,1)S(1)}, bf16[7,1024,256]{2,1,0:T(8,128)(2,1)}, u32[]{:S(2)}) copy-start(bf16[7,1024,256]{2,1,0:T(8,128)(2,1)} %copy-done) | copy-start | bytes 11010052
  134.0 9.9 %copy-start.24 = (s32[4]{0:T(128)S(1)}, s32[4]{0:T(128)}, u32[]{:S(2)}) copy-start(s32[4]{0:T(128)} %constant.103) | copy-start | bytes 52
  137.9 0.7 copy-start.6
  138.7 8.8 %collective-permute-start.10 = (f32[18,32,128]{2,1,0:T(8,128)S(1)}, f32[18,32,128]{2,1,0:T(8,128)S(1)}, u32[]{:S(2)}, u32[]{:S(2)}) collective-permute-start(f32[18,32,128]{2,1,0:T(8,128)S(1)} %get-tuple-element.36), channel_id=1, source_target_pairs={{0,2},{1,3},{2,0},{3,1},{4,6},{5,7},{6,4},{7,5},{8,10},{9,11},{10,... | collective-permute-start | bytes 884744 | tf_op jit(solution)/shard_map/ppermute | solution.py:264
  141.1 14.3 %collective-permute-start.8 = (f32[18,32,128]{2,1,0:T(8,128)S(1)}, f32[18,32,128]{2,1,0:T(8,128)S(1)}, u32[]{:S(2)}, u32[]{:S(2)}) collective-permute-start(f32[18,32,128]{2,1,0:T(8,128)S(1)} %get-tuple-element.34), channel_id=1, source_target_pairs={{0,1},{1,2},{2,3},{3,0},{4,5},{5,6},{6,7},{7,4},{8,9},{9,10},{10,1... | collective-permute-start | bytes 884744 | tf_op jit(solution)/shard_map/ppermute | solution.py:264
  141.1 14.3 %copy-start.7 = (f32[18,32,128]{2,1,0:T(8,128)}, f32[18,32,128]{2,1,0:T(8,128)S(1)}, u32[]{:S(2)}) copy-start(f32[18,32,128]{2,1,0:T(8,128)S(1)} %collective-permute-done.11.refs_7_) | copy-start | bytes 884740
  141.1 14.3 %collective-permute-start.9 = (f32[18,32,128]{2,1,0:T(8,128)S(1)}, f32[18,32,128]{2,1,0:T(8,128)S(1)}, u32[]{:S(2)}, u32[]{:S(2)}) collective-permute-start(f32[18,32,128]{2,1,0:T(8,128)S(1)} %get-tuple-element.35), channel_id=1, source_target_pairs={{0,3},{1,0},{2,1},{3,2},{4,7},{5,4},{6,5},{7,6},{8,11},{9,8},{10,9... | collective-permute-start | bytes 884744 | tf_op jit(solution)/shard_map/ppermute | solution.py:264
  144.6 10.9 %copy-start.8 = (f32[18,32,128]{2,1,0:T(8,128)}, f32[18,32,128]{2,1,0:T(8,128)S(1)}, u32[]{:S(2)}) copy-start(f32[18,32,128]{2,1,0:T(8,128)S(1)} %collective-permute-done.12.refs_8_) | copy-start | bytes 884740
  144.6 10.9 %copy-start.9 = (f32[18,32,128]{2,1,0:T(8,128)}, f32[18,32,128]{2,1,0:T(8,128)S(1)}, u32[]{:S(2)}) copy-start(f32[18,32,128]{2,1,0:T(8,128)S(1)} %collective-permute-done.13.refs_9_) | copy-start | bytes 884740
  147.5 8.0 %copy-start.10 = (f32[18,32,128]{2,1,0:T(8,128)}, f32[18,32,128]{2,1,0:T(8,128)S(1)}, u32[]{:S(2)}) copy-start(f32[18,32,128]{2,1,0:T(8,128)S(1)} %collective-permute-done.10.refs_5_) | copy-start | bytes 884740
  155.4 0.7 copy-start.11
  155.4 0.8 copy-start.12
Sparse Core Ops, SparseCore 0:
  9.8 34.5 all-gather.5
  46.7 41.3 all-gather.7

commit v7 on v2

--- a/solution.py
+++ b/solution.py
@@ -12,7 +12,18 @@
 SLICE = BLOCK // RANKS
 HALF = BLOCK // 2
 TRI = 32
-ROWS_PER_STEP = 12
+ROWS_PER_STEP = 18
+SIDE = 4
+MOVES = (1, -1, 2)
+PART = 8
+
+
+def shift_y(d):
+    return [(i, (i // SIDE + d) % SIDE * SIDE + i % SIDE) for i in range(RANKS)]
+
+
+def shift_x(d):
+    return [(i, i // SIDE * SIDE + (i % SIDE + d) % SIDE) for i in range(RANKS)]
 
 
 def tri(k, i):
@@ -42,7 +53,9 @@
     return jnp.concatenate(split(x), axis=1)
 
 
-def pack_kernel(place, columns, sides, factor, out, rows_buf, sem_f, sem_r):
+def pack_kernel(pivots, columns, sides, factor, out, rows_buf, sem_f, sem_r):
+    row_count = sides.shape[0]
+    place = [lax.rem(pivots[j], row_count) for j in range(STEPS)]
     factor_copies, side_copies = [], []
     for j in range(STEPS):
         copy = pltpu.make_async_copy(factor.at[place[j]], rows_buf.at[j], sem_f.at[j])
@@ -62,7 +75,7 @@
         for i in range(j):
             piece = jnp.zeros((SLICE, BLOCK), jnp.float32)
             for s in range(SLOTS):
-                piece = jnp.where(columns[at, s] == i, rows_buf[j, s], piece)
+                piece = jnp.where(columns[s, at] == i, rows_buf[j, s], piece)
             b = tri(j, i)
             out[b // 2, pl.ds(HALF + (b % 2) * SLICE, SLICE)] = piece
     for b in range(tri(STEPS, 0), TRI):
@@ -71,7 +84,7 @@
         copy.wait()
 
 
-def pack(place, columns, sides, factor):
+def pack(pivots, columns, sides, factor):
     smem = pl.BlockSpec(memory_space=pltpu.SMEM)
     hbm = pl.BlockSpec(memory_space=pl.ANY)
     return pl.pallas_call(
@@ -85,18 +98,21 @@
             pltpu.SemaphoreType.DMA((2 * STEPS,)),
         ],
         name="pack",
-    )(place, columns, sides, factor)
-
-
-def solve_kernel(core, gathered, mine, other, inverse, solved, pairs, side):
+    )(pivots, columns, sides, factor)
+
+
+def solve_kernel(core, spots, gathered, mine, other, inverse, solved, pairs, side, blocks):
     flag = core[0]
+    for pieces, base in ((mine, 2 * PART * flag), (other, 2 * PART * (1 - flag))):
+        for p in range(2):
+            for e in range(SIDE):
+                for d in range(SIDE):
+                    at = pl.multiple_of(SLICE * spots[p, SIDE * e + d], SLICE)
+                    for i in range(PART):
+                        blocks[base + PART * p + i, pl.ds(at, SLICE)] = pieces[p, e, d, i]
 
     def factor(k, i):
-        b = tri(k, i)
-        h = b // RANKS
-        own = mine[:, b % RANKS].reshape(BLOCK, BLOCK)
-        far = other[:, b % RANKS].reshape(BLOCK, BLOCK)
-        return jnp.where(flag == h, own, far)
+        return blocks[tri(k, i)]
 
     for j in range(STEPS):
         side[j] = gathered[2 * j : 2 * j + 2, :HALF].reshape(BLOCK, BLOCK)
@@ -110,7 +126,7 @@
     pairs[STEPS] = jnp.zeros((BLOCK, 2 * BLOCK), jnp.bfloat16)
 
 
-def solve(core, gathered, mine, other, inverse):
+def solve(core, spots, gathered, mine, other, inverse):
     vmem = pl.BlockSpec(memory_space=pltpu.VMEM)
     return pl.pallas_call(
         solve_kernel,
@@ -118,11 +134,14 @@
             jax.ShapeDtypeStruct((STEPS, BLOCK, BLOCK), jnp.float32),
             jax.ShapeDtypeStruct((STEPS + 1, BLOCK, 2 * BLOCK), jnp.bfloat16),
         ),
-        in_specs=[pl.BlockSpec(memory_space=pltpu.SMEM), vmem, vmem, vmem, vmem],
+        in_specs=[pl.BlockSpec(memory_space=pltpu.SMEM)] * 2 + [vmem] * 4,
         out_specs=(vmem, vmem),
-        scratch_shapes=[pltpu.VMEM((STEPS, BLOCK, BLOCK), jnp.float32)],
+        scratch_shapes=[
+            pltpu.VMEM((STEPS, BLOCK, BLOCK), jnp.float32),
+            pltpu.VMEM((TRI, BLOCK, BLOCK), jnp.float32),
+        ],
         name="solve",
-    )(core, gathered, mine, other, inverse)
+    )(core, spots, gathered, mine, other, inverse)
 
 
 def update_kernel(picks, sides, factor, pairs, out):
@@ -166,13 +185,12 @@
     everything = lax.all_gather(factor_blocks, "samp", axis=0, tiled=False)
 
     owner = pivot_rows // row_count
-    place = pivot_rows % row_count
     ids = rank * row_count + jnp.arange(row_count, dtype=jnp.int32)
     targets = jnp.arange(STEPS, dtype=jnp.int32)
     row_rank = STEPS + jnp.sum(jnp.where(ids[:, None] == pivot_rows[None, :], targets - STEPS, 0), axis=1)
     picks = jnp.where(block_columns < row_rank[:, None], block_columns, STEPS)
 
-    payload = pack(place, block_columns, right_sides, factor_blocks)
+    payload = pack(pivot_rows, block_columns.T, right_sides, factor_blocks)
     pieces = lax.all_to_all(payload, "rows", 0, 0)
     tri_owner = owner[jnp.array(TRI_PIVOT, jnp.int32)]
     part = jnp.concatenate(
@@ -186,9 +204,19 @@
     slices = gathered[:, HALF:].reshape(TRI, SLICE, BLOCK)
     core = rank % 2
     half = lax.dynamic_slice(slices, (core * RANKS, 0, 0), (RANKS, SLICE, BLOCK))
-    mine = lax.all_to_all(jnp.broadcast_to(half, (RANKS,) + half.shape), "samp", 0, 0)
+    first, second = half[:PART], half[PART:]
+    first = [first] + [lax.ppermute(first, "samp", shift_y(d)) for d in MOVES]
+    second = [second] + [lax.ppermute(second, "samp", shift_x(d)) for d in MOVES]
+    first, second = jnp.stack(first), jnp.stack(second)
+    parts = [first] + [lax.ppermute(first, "samp", shift_x(d)) for d in MOVES]
+    parts += [second] + [lax.ppermute(second, "samp", shift_y(d)) for d in MOVES]
+    mine = jnp.stack(parts).reshape(2, SIDE, SIDE, PART, SLICE, BLOCK)
     other = lax.ppermute(mine, "rows", [(i, i ^ 1) for i in range(RANKS)])
-    solved, pairs = solve(core.reshape(1), gathered, mine, other, diag_inverse)
+    here = lax.axis_index("samp")
+    moves = jnp.array((0,) + MOVES, jnp.int32)
+    y, x = (here // SIDE - moves + SIDE) % SIDE, (here % SIDE - moves + SIDE) % SIDE
+    spots = jnp.stack([SIDE * y[None, :] + x[:, None], SIDE * y[:, None] + x[None, :]]).reshape(2, RANKS)
+    solved, pairs = solve(core.reshape(1), spots, gathered, mine, other, diag_inverse)
     return solved, update(picks, right_sides, everything, pairs)
 
 

time: 146 us -> 141 us (0.966)
  blocking collectives: 51.5 us -> 16.3 us
  starting transfers between devices: 11.3 us -> 29.7 us
  waiting for transfers between devices: 37.6 us -> 47.5 us
  local copies, waits for them, and re-layouts: 5.46 us -> 7.69 us
    all_to_all x1 -> x0, blocking collectives: 35.3 us -> none  [local(): lax.all_to_all(jnp.broadcast_to(half, (RANKS,) + half.shape), 'samp', 0, 0)]
    ppermute x0 -> x12, starting transfers between devices: none -> 16.6 us  [the longest x3 4.47 us: local(): first = [first] + [lax.ppermute(first, 'samp', shift_y(d)) for d in MOVES]]
    ppermute x0 -> x12, waiting for transfers between devices: none -> 6.97 us  [the longest x3 5.54 us: local(): parts = [first] + [lax.ppermute(first, 'samp', shift_x(d)) for d in MOVES]]
    all_gather x1, waiting for transfers between devices: 22.7 us -> 26.4 us  [local(): everything = lax.all_gather(factor_blocks, 'samp', axis=0, tiled=False)]
    ppermute x1, starting transfers between devices: 1.3 us -> 3.08 us  [local(): other = lax.ppermute(mine, 'rows', [(i, i ^ 1) for i in range(RANKS)])]
    unnamed x15 -> x20, local copies, waits for them, and re-layouts: 3.32 us -> 4.52 us
  transfers between devices with their start and end apart: 3 -> 15, of which waited for: 3 -> 7; matrix products, arithmetic and copies ran while one was open for 3% -> 6% of each run, Pallas kernels for 6% -> 6%
where the time goes in v7:
time: 141 us; the launch traced here: 140 us
  waiting for transfers between devices  47.5 us (34%)
  starting transfers between devices  29.7 us (21%)
  between operations  20.1 us (14%)
  Pallas kernels  16.9 us (12%)
  blocking collectives  16.3 us (12%)
  local copies, waits for them, and re-layouts  7.69 us (5%)
  other arithmetic  2.17 us (2%)
    all_gather x1, waiting for transfers between devices, local(): everything = lax.all_gather(factor_blocks, 'samp', axis=0, tiled=False)  26.4 us
    all_gather x1, blocking collectives, local(): gathered = lax.all_gather(part, 'rows', axis=0, tiled=False)  16.3 us
    all_to_all x1, waiting for transfers between devices, local(): pieces = lax.all_to_all(payload, 'rows', 0, 0)  12.1 us
    all_to_all x1, starting transfers between devices, local(): pieces = lax.all_to_all(payload, 'rows', 0, 0)  9.99 us
    pallas_call x1, Pallas kernels, update(): pl.pallas_call(update_kernel, grid=(rows // ROWS_PER_STEP,), out_shape=ja...  8.07 us
    pallas_call x1, Pallas kernels, solve(): pl.pallas_call(solve_kernel, out_shape=(jax.ShapeDtypeStruct((STEPS, BLOC...  5.64 us
    ppermute x3, waiting for transfers between devices, local(): parts = [first] + [lax.ppermute(first, 'samp', shift_x(d)) for d in MOVES]  5.54 us
    unnamed x20, local copies, waits for them, and re-layouts  4.52 us
  transfers between devices with their start and end apart: 15, of which 7 were waited for; matrix products, arithmetic and copies ran while one was open for 6% of the time, Pallas kernels for 6%

profile of v7, /device:TPU:1, one launch (start us, length us, event | category | flops | bytes accessed | tf_op | source)
XLA Modules:
  0.0 140.2 jit_solution(15270560197361724686)
XLA Ops:
  7.2 0.7 all-gather.4.cloned.1.call-update
  7.9 3.2 %pack.1 = f32[16,80,128]{2,1,0:T(8,128)} custom-call(s32[8]{0:T(128)} %pivots.1, s32[6,36]{1,0:T(8,128)} %bitcast.63, f32[36,128,128]{2,1,0:T(8,128)} %sides.3, f32[36,6,8,128]{3,2,1,0:T(8,128)} %factor.1), custom_call_target="tpu_custom_call" | custom-call | tf_op jit(solution)/shard_map/pack/pallas_call | solution.py:90
  11.1 10.0 %all-to-all-start = ((f32[16,80,128]{2,1,0:T(8,128)}), f32[16,80,128]{2,1,0:T(8,128)S(1)}, u32[]{:S(2)}, u32[]{:S(2)}) async-start(f32[16,80,128]{2,1,0:T(8,128)} %pack.1), calls=%async_computation | async-start | bytes 1310720 | tf_op jit(solution)/shard_map/all_to_all | solution.py:194
  21.2 0.7 gather_fusion
  21.9 0.6 fusion.3
  25.0 0.7 dynamic_slice.21
  29.1 12.1 %all-to-all-done = f32[16,80,128]{2,1,0:T(8,128)S(1)} async-done(((f32[16,80,128]{2,1,0:T(8,128)}), f32[16,80,128]{2,1,0:T(8,128)S(1)}, u32[]{:S(2)}, u32[]{:S(2)}) %all-to-all-start) | async-done | bytes 655392 | tf_op jit(solution)/shard_map/all_to_all | solution.py:194
  41.2 16.3 %all-gather = f32[1280,128]{1,0:T(8,128)S(1)} all-gather(f32[80,128]{1,0:T(8,128)S(1)} %pad_maximum_fusion.2), channel_id=2, replica_groups=mesh['rows'=16,'samp'=16] {'rows'}, dimensions={0}, use_global_device_ids=true | all-gather | bytes 696320 | tf_op jit(solution)/shard_map/all_gather | solution.py:203
  57.5 3.0 %collective-permute-start.2 = (f32[8,8,128]{2,1,0:T(8,128)S(1)}, f32[8,8,128]{2,1,0:T(8,128)S(1)}, u32[]{:S(2)}, u32[]{:S(2)}) collective-permute-start(f32[8,8,128]{2,1,0:T(8,128)S(1)} %get-tuple-element.9), channel_id=1, source_target_pairs={{0,8},{1,9},{2,10},{3,11},{4,12},{5,13},{6,14},{7,15},{8,0},{9,1},... | collective-permute-start | bytes 98312 | tf_op jit(solution)/shard_map/ppermute | solution.py:208
  60.5 0.8 collective-permute-start.1
  61.2 0.7 collective-permute-start
  61.9 0.1 copy.15
  62.0 2.8 %collective-permute-start.8 = (f32[8,8,128]{2,1,0:T(8,128)S(1)}, f32[8,8,128]{2,1,0:T(8,128)S(1)}, u32[]{:S(2)}, u32[]{:S(2)}) collective-permute-start(f32[8,8,128]{2,1,0:T(8,128)S(1)} %get-tuple-element.8), channel_id=1, source_target_pairs={{0,2},{1,3},{2,0},{3,1},{4,6},{5,7},{6,4},{7,5},{8,10},{9,11},{10,... | collective-permute-start | bytes 98312 | tf_op jit(solution)/shard_map/ppermute | solution.py:209
  64.8 0.9 collective-permute-start.7
  65.7 0.6 collective-permute-start.6
  66.3 1.3 collective-permute-start.3
  67.6 1.5 %collective-permute-start.4 = (f32[4,8,8,128]{3,2,1,0:T(8,128)S(1)}, f32[4,8,8,128]{3,2,1,0:T(8,128)S(1)}, u32[]{:S(2)}, u32[]{:S(2)}) collective-permute-start(f32[4,8,8,128]{3,2,1,0:T(8,128)S(1)} %pad_maximum_fusion), channel_id=1, source_target_pairs={{0,3},{1,0},{2,1},{3,2},{4,7},{5,4},{6,5},{7,6},{8,11},{9,8},{10,9... | collective-permute-start | bytes 393224 | tf_op jit(solution)/shard_map/ppermute | solution.py:211
  69.1 1.5 %collective-permute-start.5 = (f32[4,8,8,128]{3,2,1,0:T(8,128)S(1)}, f32[4,8,8,128]{3,2,1,0:T(8,128)S(1)}, u32[]{:S(2)}, u32[]{:S(2)}) collective-permute-start(f32[4,8,8,128]{3,2,1,0:T(8,128)S(1)} %pad_maximum_fusion), channel_id=1, source_target_pairs={{0,2},{1,3},{2,0},{3,1},{4,6},{5,7},{6,4},{7,5},{8,10},{9,11},{10,... | collective-permute-start | bytes 393224 | tf_op jit(solution)/shard_map/ppermute | solution.py:211
  70.6 0.1 collective-permute-done.6
  70.7 0.5 collective-permute-start.9
  71.2 2.3 %collective-permute-start.10 = (f32[4,8,8,128]{3,2,1,0:T(8,128)S(1)}, f32[4,8,8,128]{3,2,1,0:T(8,128)S(1)}, u32[]{:S(2)}, u32[]{:S(2)}) collective-permute-start(f32[4,8,8,128]{3,2,1,0:T(8,128)S(1)} %pad_maximum_fusion.1), channel_id=1, source_target_pairs={{0,12},{1,13},{2,14},{3,15},{4,0},{5,1},{6,2},{7,3},{8,4},{9,5},{1... | collective-permute-start | bytes 393224 | tf_op jit(solution)/shard_map/ppermute | solution.py:212
  73.5 0.7 bitcast_dynamic-update-slice_fusion.7
  74.1 1.9 %collective-permute-done.3 = f32[4,8,8,128]{3,2,1,0:T(8,128)S(1)} collective-permute-done((f32[4,8,8,128]{3,2,1,0:T(8,128)S(1)}, f32[4,8,8,128]{3,2,1,0:T(8,128)S(1)}, u32[]{:S(2)}, u32[]{:S(2)}) %collective-permute-start.3) | collective-permute-done | bytes 131104 | tf_op jit(solution)/shard_map/ppermute | solution.py:211
  76.0 0.8 collective-permute-start.11
  76.8 0.7 bitcast_dynamic-update-slice_fusion.6
  77.5 0.7 bitcast_dynamic-update-slice_fusion.5
  78.2 3.7 %collective-permute-done.5 = f32[4,8,8,128]{3,2,1,0:T(8,128)S(1)} collective-permute-done((f32[4,8,8,128]{3,2,1,0:T(8,128)S(1)}, f32[4,8,8,128]{3,2,1,0:T(8,128)S(1)}, u32[]{:S(2)}, u32[]{:S(2)}) %collective-permute-start.5) | collective-permute-done | bytes 131104 | tf_op jit(solution)/shard_map/ppermute | solution.py:211
  81.8 0.7 bitcast_dynamic-update-slice_fusion.4
  82.5 0.7 bitcast_dynamic-update-slice_fusion.3
  83.2 0.7 bitcast_dynamic-update-slice_fusion.2
  83.8 0.7 bitcast_dynamic-update-slice_fusion.1
  84.5 1.3 collective-permute-done.11
  85.8 0.7 bitcast_dynamic-update-slice_fusion
  86.5 3.1 %collective-permute-start.12 = (f32[2,4,4,8,8,128]{5,4,3,2,1,0:T(8,128)}, f32[2,4,4,8,8,128]{5,4,3,2,1,0:T(8,128)}, u32[]{:S(2)}, u32[]{:S(2)}) collective-permute-start(f32[2,4,4,8,8,128]{5,4,3,2,1,0:T(8,128)} %bitcast.26.mine), channel_id=1, source_target_pairs={{0,16},{16,0},{32,48},{48,32},{64,80},{80,64},{96,112},{112,96},{1... | collective-permute-start | bytes 3145736 | tf_op jit(solution)/shard_map/ppermute | solution.py:214
  89.6 0.1 add.140
  89.6 0.1 add.141
  89.7 0.1 add.143
  89.8 0.1 add.133
  89.9 0.1 add.137
  90.0 0.1 add.138
  90.1 0.6 pad_add_fusion.spots
  90.7 0.1 select_reduce_fusion
  90.8 0.1 compare_select_fusion.picks
  90.9 1.3 collective-permute-done.12.other
  92.2 5.6 %solve.1 = (f32[8,128,128]{2,1,0:T(8,128)}, bf16[9,128,256]{2,1,0:T(8,128)(2,1)}) custom-call(s32[1]{0:T(128)} %bitcast.core, s32[2,16]{1,0:T(2,128)} %pad_add_fusion.spots, f32[16,80,128]{2,1,0:T(8,128)} %bitcast.45, f32[2,4,4,8,8,128]{5,4,3,2,1,0:T(8,128)} %bitcast.26.mine, f32[2,4,4,8,8,128]{5,4,3,2,1,0:T(8,128)} %collective-permute-done.12.other, ...), custom_call_target="tpu_custom_call" | custom-call | tf_op jit(solution)/shard_map/solve/pallas_call | solution.py:131
  97.8 26.4 %all-gather.4.cloned.1.call-done = f32[576,6,8,128]{3,2,1,0:T(8,128)} async-done(((f32[36,6,8,128]{3,2,1,0:T(8,128)}), f32[576,6,8,128]{3,2,1,0:T(8,128)}) %all-gather.4.cloned.1.call-update) | async-done | bytes 14155792 | tf_op jit(solution)/shard_map/all_gather | solution.py:185
  124.2 1.1 copy-done.1
  125.3 8.1 %update.1 = f32[36,128,128]{2,1,0:T(8,128)} custom-call(s32[36,6]{1,0:T(8,128)S(1)} %compare_select_fusion.picks, f32[36,128,128]{2,1,0:T(8,128)S(1)} %copy-done, f32[16,36,6,8,128]{4,3,2,1,0:T(8,128)} %bitcast.43, bf16[9,128,256]{2,1,0:T(8,128)(2,1)S(1)} %copy-done.1), custom_call_target="tpu_custom_call" | custom-call | tf_op jit(solution)/shard_map/update/pallas_call | solution.py:166
  (39 shorter events, 0.2 us)
Async XLA Ops:
  7.2 117.1 %all-gather.4.cloned.1.call-start = ((), (), s32[]{:S(2)}) async-start(), calls=%async_computation.1 | async-start | bytes 15040512 | tf_op jit(solution)/shard_map/all_gather | solution.py:185
  7.9 13.2 %copy-start.6 = (s32[32]{0:T(128)S(1)}, s32[32]{0:T(128)}, u32[]{:S(2)}) copy-start(s32[32]{0:T(128)} %constant.107) | copy-start | bytes 388
  7.9 13.2 %copy-start.4 = (s32[8]{0:T(128)S(1)}, s32[8]{0:T(128)}, u32[]{:S(2)}) copy-start(s32[8]{0:T(128)} %pivots.1) | copy-start | bytes 100
  11.1 50.8 %copy-start.3 = (s32[36,6]{0,1:T(8,128)S(1)}, s32[36,6]{0,1:T(8,128)}, u32[]{:S(2)}) copy-start(s32[36,6]{0,1:T(8,128)} %param.9) | copy-start | bytes 2596
  11.1 30.0 %all-to-all-start = ((f32[16,80,128]{2,1,0:T(8,128)}), f32[16,80,128]{2,1,0:T(8,128)S(1)}, u32[]{:S(2)}, u32[]{:S(2)}) async-start(f32[16,80,128]{2,1,0:T(8,128)} %pack.1), calls=%async_computation | async-start | bytes 1310720 | tf_op jit(solution)/shard_map/all_to_all | solution.py:194
  21.1 68.4 %copy-start.5 = (s32[4]{0:T(128)S(1)}, s32[4]{0:T(128)}, u32[]{:S(2)}) copy-start(s32[4]{0:T(128)} %constant.102) | copy-start | bytes 52
  57.4 34.8 %copy-start.2 = (f32[1280,128]{1,0:T(8,128)}, f32[1280,128]{1,0:T(8,128)S(1)}, u32[]{:S(2)}) copy-start(f32[1280,128]{1,0:T(8,128)S(1)} %all-gather) | copy-start | bytes 1966084
  57.5 8.2 %collective-permute-start.2 = (f32[8,8,128]{2,1,0:T(8,128)S(1)}, f32[8,8,128]{2,1,0:T(8,128)S(1)}, u32[]{:S(2)}, u32[]{:S(2)}) collective-permute-start(f32[8,8,128]{2,1,0:T(8,128)S(1)} %get-tuple-element.9), channel_id=1, source_target_pairs={{0,8},{1,9},{2,10},{3,11},{4,12},{5,13},{6,14},{7,15},{8,0},{9,1},... | collective-permute-start | bytes 98312 | tf_op jit(solution)/shard_map/ppermute | solution.py:208
  60.5 5.8 %collective-permute-start.1 = (f32[8,8,128]{2,1,0:T(8,128)S(1)}, f32[8,8,128]{2,1,0:T(8,128)S(1)}, u32[]{:S(2)}, u32[]{:S(2)}) collective-permute-start(f32[8,8,128]{2,1,0:T(8,128)S(1)} %get-tuple-element.9), channel_id=1, source_target_pairs={{0,12},{1,13},{2,14},{3,15},{4,0},{5,1},{6,2},{7,3},{8,4},{9,5},{1... | collective-permute-start | bytes 98312 | tf_op jit(solution)/shard_map/ppermute | solution.py:208
  61.2 5.0 %collective-permute-start = (f32[8,8,128]{2,1,0:T(8,128)S(1)}, f32[8,8,128]{2,1,0:T(8,128)S(1)}, u32[]{:S(2)}, u32[]{:S(2)}) collective-permute-start(f32[8,8,128]{2,1,0:T(8,128)S(1)} %get-tuple-element.9), channel_id=1, source_target_pairs={{0,4},{1,5},{2,6},{3,7},{4,8},{5,9},{6,10},{7,11},{8,12},{9,13},{1... | collective-permute-start | bytes 98312 | tf_op jit(solution)/shard_map/ppermute | solution.py:208
  62.0 7.0 %collective-permute-start.8 = (f32[8,8,128]{2,1,0:T(8,128)S(1)}, f32[8,8,128]{2,1,0:T(8,128)S(1)}, u32[]{:S(2)}, u32[]{:S(2)}) collective-permute-start(f32[8,8,128]{2,1,0:T(8,128)S(1)} %get-tuple-element.8), channel_id=1, source_target_pairs={{0,2},{1,3},{2,0},{3,1},{4,6},{5,7},{6,4},{7,5},{8,10},{9,11},{10,... | collective-permute-start | bytes 98312 | tf_op jit(solution)/shard_map/ppermute | solution.py:209
  64.8 5.8 %collective-permute-start.7 = (f32[8,8,128]{2,1,0:T(8,128)S(1)}, f32[8,8,128]{2,1,0:T(8,128)S(1)}, u32[]{:S(2)}, u32[]{:S(2)}) collective-permute-start(f32[8,8,128]{2,1,0:T(8,128)S(1)} %get-tuple-element.8), channel_id=1, source_target_pairs={{0,3},{1,0},{2,1},{3,2},{4,7},{5,4},{6,5},{7,6},{8,11},{9,8},{10,9... | collective-permute-start | bytes 98312 | tf_op jit(solution)/shard_map/ppermute | solution.py:209
  65.7 5.0 %collective-permute-start.6 = (f32[8,8,128]{2,1,0:T(8,128)S(1)}, f32[8,8,128]{2,1,0:T(8,128)S(1)}, u32[]{:S(2)}, u32[]{:S(2)}) collective-permute-start(f32[8,8,128]{2,1,0:T(8,128)S(1)} %get-tuple-element.8), channel_id=1, source_target_pairs={{0,1},{1,2},{2,3},{3,0},{4,5},{5,6},{6,7},{7,4},{8,9},{9,10},{10,1... | collective-permute-start | bytes 98312 | tf_op jit(solution)/shard_map/ppermute | solution.py:209
  66.3 9.7 %collective-permute-start.3 = (f32[4,8,8,128]{3,2,1,0:T(8,128)S(1)}, f32[4,8,8,128]{3,2,1,0:T(8,128)S(1)}, u32[]{:S(2)}, u32[]{:S(2)}) collective-permute-start(f32[4,8,8,128]{3,2,1,0:T(8,128)S(1)} %pad_maximum_fusion), channel_id=1, source_target_pairs={{0,1},{1,2},{2,3},{3,0},{4,5},{5,6},{6,7},{7,4},{8,9},{9,10},{10,1... | collective-permute-start | bytes 393224 | tf_op jit(solution)/shard_map/ppermute | solution.py:211
  67.6 9.9 %collective-permute-start.4 = (f32[4,8,8,128]{3,2,1,0:T(8,128)S(1)}, f32[4,8,8,128]{3,2,1,0:T(8,128)S(1)}, u32[]{:S(2)}, u32[]{:S(2)}) collective-permute-start(f32[4,8,8,128]{3,2,1,0:T(8,128)S(1)} %pad_maximum_fusion), channel_id=1, source_target_pairs={{0,3},{1,0},{2,1},{3,2},{4,7},{5,4},{6,5},{7,6},{8,11},{9,8},{10,9... | collective-permute-start | bytes 393224 | tf_op jit(solution)/shard_map/ppermute | solution.py:211
  69.1 12.8 %collective-permute-start.5 = (f32[4,8,8,128]{3,2,1,0:T(8,128)S(1)}, f32[4,8,8,128]{3,2,1,0:T(8,128)S(1)}, u32[]{:S(2)}, u32[]{:S(2)}) collective-permute-start(f32[4,8,8,128]{3,2,1,0:T(8,128)S(1)} %pad_maximum_fusion), channel_id=1, source_target_pairs={{0,2},{1,3},{2,0},{3,1},{4,6},{5,7},{6,4},{7,5},{8,10},{9,11},{10,... | collective-permute-start | bytes 393224 | tf_op jit(solution)/shard_map/ppermute | solution.py:211
  70.7 12.4 %collective-permute-start.9 = (f32[4,8,8,128]{3,2,1,0:T(8,128)S(1)}, f32[4,8,8,128]{3,2,1,0:T(8,128)S(1)}, u32[]{:S(2)}, u32[]{:S(2)}) collective-permute-start(f32[4,8,8,128]{3,2,1,0:T(8,128)S(1)} %pad_maximum_fusion.1), channel_id=1, source_target_pairs={{0,4},{1,5},{2,6},{3,7},{4,8},{5,9},{6,10},{7,11},{8,12},{9,13},{1... | collective-permute-start | bytes 393224 | tf_op jit(solution)/shard_map/ppermute | solution.py:212
  71.2 12.6 %collective-permute-start.10 = (f32[4,8,8,128]{3,2,1,0:T(8,128)S(1)}, f32[4,8,8,128]{3,2,1,0:T(8,128)S(1)}, u32[]{:S(2)}, u32[]{:S(2)}) collective-permute-start(f32[4,8,8,128]{3,2,1,0:T(8,128)S(1)} %pad_maximum_fusion.1), channel_id=1, source_target_pairs={{0,12},{1,13},{2,14},{3,15},{4,0},{5,1},{6,2},{7,3},{8,4},{9,5},{1... | collective-permute-start | bytes 393224 | tf_op jit(solution)/shard_map/ppermute | solution.py:212
  76.0 9.8 %collective-permute-start.11 = (f32[4,8,8,128]{3,2,1,0:T(8,128)S(1)}, f32[4,8,8,128]{3,2,1,0:T(8,128)S(1)}, u32[]{:S(2)}, u32[]{:S(2)}) collective-permute-start(f32[4,8,8,128]{3,2,1,0:T(8,128)S(1)} %pad_maximum_fusion.1), channel_id=1, source_target_pairs={{0,8},{1,9},{2,10},{3,11},{4,12},{5,13},{6,14},{7,15},{8,0},{9,1},... | collective-permute-start | bytes 393224 | tf_op jit(solution)/shard_map/ppermute | solution.py:212
  78.2 46.1 %copy-start = (f32[36,128,128]{2,1,0:T(8,128)S(1)}, f32[36,128,128]{2,1,0:T(8,128)}, u32[]{:S(2)}) copy-start(f32[36,128,128]{2,1,0:T(8,128)} %sides.3) | copy-start | bytes 7077892
  86.5 5.7 %collective-permute-start.12 = (f32[2,4,4,8,8,128]{5,4,3,2,1,0:T(8,128)}, f32[2,4,4,8,8,128]{5,4,3,2,1,0:T(8,128)}, u32[]{:S(2)}, u32[]{:S(2)}) collective-permute-start(f32[2,4,4,8,8,128]{5,4,3,2,1,0:T(8,128)} %bitcast.26.mine), channel_id=1, source_target_pairs={{0,16},{16,0},{32,48},{48,32},{64,80},{80,64},{96,112},{112,96},{1... | collective-permute-start | bytes 3145736 | tf_op jit(solution)/shard_map/ppermute | solution.py:214
  124.2 1.1 copy-start.1
Sparse Core Ops, SparseCore 0:
  10.4 113.7 all-gather.3

commit v8 on v7

--- a/solution.py
+++ b/solution.py
@@ -12,10 +12,10 @@
 SLICE = BLOCK // RANKS
 HALF = BLOCK // 2
 TRI = 32
-ROWS_PER_STEP = 18
+CHUNK = 6
 SIDE = 4
 MOVES = (1, -1, 2)
-PART = 8
+PART = 7
 
 
 def shift_y(d):
@@ -144,37 +144,68 @@
     )(core, spots, gathered, mine, other, inverse)
 
 
-def update_kernel(picks, sides, factor, pairs, out):
-    step = pl.program_id(0)
-    for r in range(ROWS_PER_STEP):
-        row = step * ROWS_PER_STEP + r
-        hi, lo, x2 = [], [], []
-        for s in range(SLOTS):
-            fh, fl = split(factor[:, r, s].reshape(BLOCK, BLOCK))
-            hi.append(fh)
-            lo.append(fl)
-            x2.append(pairs[picks[row, s]])
-        hi = jnp.concatenate(hi, axis=1)
-        lo = jnp.concatenate(lo, axis=1)
-        x2 = jnp.concatenate(x2, axis=0)
-        full = dot(hi, x2)
-        out[r] = sides[r] - (full[:, :BLOCK] + full[:, BLOCK:] + dot(lo, x2[:, :BLOCK]))
+def update_kernel(picks, sides, factor, pairs, out, blocks, work, solved, sem_factor, sem_side, sem_pairs, sem_out):
+    count = sides.shape[0] // CHUNK
+
+    def fetch(g):
+        rows = pl.ds(g * CHUNK, CHUNK)
+        return pltpu.make_async_copy(factor.at[:, rows], blocks.at[:, rows], sem_factor.at[g])
+
+    def store(g):
+        rows = pl.ds(g * CHUNK, CHUNK)
+        return pltpu.make_async_copy(work.at[rows], out.at[rows], sem_out.at[g])
+
+    side_copy = pltpu.make_async_copy(sides, work, sem_side)
+    pairs_copy = pltpu.make_async_copy(pairs, solved, sem_pairs)
+    pairs_copy.start()
+    fetch(0).start()
+    side_copy.start()
+    for g in range(1, count):
+        fetch(g).start()
+    pairs_copy.wait()
+    side_copy.wait()
+
+    def step(g, carry):
+        fetch(g).wait()
+        for i in range(CHUNK):
+            row = g * CHUNK + i
+            hi, lo, x2 = [], [], []
+            for s in range(SLOTS):
+                fh, fl = split(blocks[:, row, s].reshape(BLOCK, BLOCK))
+                hi.append(fh)
+                lo.append(fl)
+                x2.append(solved[picks[row, s]])
+            hi = jnp.concatenate(hi, axis=1)
+            lo = jnp.concatenate(lo, axis=1)
+            x2 = jnp.concatenate(x2, axis=0)
+            full = dot(hi, x2)
+            work[row] = work[row] - (full[:, :BLOCK] + full[:, BLOCK:] + dot(lo, x2[:, :BLOCK]))
+        store(g).start()
+        return carry
+
+    lax.fori_loop(0, count, step, 0)
+    for g in range(count):
+        store(g).wait()
 
 
 def update(picks, sides, factor, pairs):
-    rows = sides.shape[0]
+    hbm = pl.BlockSpec(memory_space=pl.ANY)
+    count = sides.shape[0] // CHUNK
     return pl.pallas_call(
         update_kernel,
-        grid=(rows // ROWS_PER_STEP,),
         out_shape=jax.ShapeDtypeStruct(sides.shape, jnp.float32),
-        in_specs=[
-            pl.BlockSpec(memory_space=pltpu.SMEM),
-            pl.BlockSpec((ROWS_PER_STEP, BLOCK, BLOCK), lambda g: (g, 0, 0)),
-            pl.BlockSpec((RANKS, ROWS_PER_STEP, SLOTS, SLICE, BLOCK), lambda g: (0, g, 0, 0, 0)),
-            pl.BlockSpec((STEPS + 1, BLOCK, 2 * BLOCK), lambda g: (0, 0, 0)),
+        in_specs=[pl.BlockSpec(memory_space=pltpu.SMEM), hbm, hbm, hbm],
+        out_specs=hbm,
+        scratch_shapes=[
+            pltpu.VMEM(factor.shape, jnp.float32),
+            pltpu.VMEM(sides.shape, jnp.float32),
+            pltpu.VMEM(pairs.shape, jnp.bfloat16),
+            pltpu.SemaphoreType.DMA((count,)),
+            pltpu.SemaphoreType.DMA,
+            pltpu.SemaphoreType.DMA,
+            pltpu.SemaphoreType.DMA((count,)),
         ],
-        out_specs=pl.BlockSpec((ROWS_PER_STEP, BLOCK, BLOCK), lambda g: (g, 0, 0)),
-        compiler_params=pltpu.CompilerParams(vmem_limit_bytes=48 * 2**20),
+        compiler_params=pltpu.CompilerParams(vmem_limit_bytes=58 * 2**20),
         name="update",
     )(picks, sides, factor, pairs)
 
@@ -203,7 +234,7 @@
     gathered = lax.all_gather(part, "rows", axis=0, tiled=False)
     slices = gathered[:, HALF:].reshape(TRI, SLICE, BLOCK)
     core = rank % 2
-    half = lax.dynamic_slice(slices, (core * RANKS, 0, 0), (RANKS, SLICE, BLOCK))
+    half = lax.dynamic_slice(slices, (core * 2 * PART, 0, 0), (2 * PART, SLICE, BLOCK))
     first, second = half[:PART], half[PART:]
     first = [first] + [lax.ppermute(first, "samp", shift_y(d)) for d in MOVES]
     second = [second] + [lax.ppermute(second, "samp", shift_x(d)) for d in MOVES]

time: 141 us -> 143 us (1.014)
  local copies, waits for them, and re-layouts: 7.69 us -> 3.62 us
  Pallas kernels: 16.9 us -> 20.5 us
  waiting for transfers between devices: 47.5 us -> 50.1 us
    pallas_call x1, Pallas kernels: 8.07 us -> 11.8 us  [update(): pl.pallas_call(update_kernel, out_shape=jax.ShapeDtypeStruct(sides.shape,...]
    unnamed x20, local copies, waits for them, and re-layouts: 4.52 us -> 1.1 us
    ppermute x3, waiting for transfers between devices: 1.29 us -> 3.69 us  [local(): lax.ppermute(second, 'samp', shift_y(d))]
  transfers between devices with their start and end apart: 15 -> 15, of which waited for: 7 -> 6; matrix products, arithmetic and copies ran while one was open for 6% -> 3% of each run, Pallas kernels for 6% -> 6%
where the time goes in v8:
time: 143 us; the launch traced here: 142 us
  waiting for transfers between devices  50.1 us (35%)
  starting transfers between devices  29.9 us (21%)
  Pallas kernels  20.5 us (14%)
  between operations  20.2 us (14%)
  blocking collectives  16.3 us (11%)
  local copies, waits for them, and re-layouts  3.62 us (3%)
    all_gather x1, waiting for transfers between devices, local(): everything = lax.all_gather(factor_blocks, 'samp', axis=0, tiled=False)  27.3 us
    all_gather x1, blocking collectives, local(): gathered = lax.all_gather(part, 'rows', axis=0, tiled=False)  16.3 us
    all_to_all x1, waiting for transfers between devices, local(): pieces = lax.all_to_all(payload, 'rows', 0, 0)  12.1 us
    pallas_call x1, Pallas kernels, update(): pl.pallas_call(update_kernel, out_shape=jax.ShapeDtypeStruct(sides.shape,...  11.8 us
    all_to_all x1, starting transfers between devices, local(): pieces = lax.all_to_all(payload, 'rows', 0, 0)  9.99 us
    ppermute x3, waiting for transfers between devices, local(): parts = [first] + [lax.ppermute(first, 'samp', shift_x(d)) for d in MOVES]  6.2 us
    pallas_call x1, Pallas kernels, solve(): pl.pallas_call(solve_kernel, out_shape=(jax.ShapeDtypeStruct((STEPS, BLOC...  5.54 us
    ppermute x3, starting transfers between devices, local(): first = [first] + [lax.ppermute(first, 'samp', shift_y(d)) for d in MOVES]  4.47 us
  transfers between devices with their start and end apart: 15, of which 6 were waited for; matrix products, arithmetic and copies ran while one was open for 3% of the time, Pallas kernels for 6%

profile of v8, /device:TPU:1, one launch (start us, length us, event | category | flops | bytes accessed | tf_op | source)
XLA Modules:
  0.0 142.0 jit_solution(10482310649035269550)
XLA Ops:
  7.2 0.0 all-gather.4.cloned.1.call-start
  7.2 0.7 all-gather.4.cloned.1.call-update
  7.9 0.0 copy-start.6
  7.9 3.2 %pack.1 = f32[16,80,128]{2,1,0:T(8,128)} custom-call(s32[8]{0:T(128)} %pivots.1, s32[6,36]{1,0:T(8,128)} %bitcast.65, f32[36,128,128]{2,1,0:T(8,128)} %sides.3, f32[36,6,8,128]{3,2,1,0:T(8,128)} %factor.1), custom_call_target="tpu_custom_call" | custom-call | tf_op jit(solution)/shard_map/pack/pallas_call | solution.py:90
  11.1 10.0 %all-to-all-start = ((f32[16,80,128]{2,1,0:T(8,128)}), f32[16,80,128]{2,1,0:T(8,128)S(1)}, u32[]{:S(2)}, u32[]{:S(2)}) async-start(f32[16,80,128]{2,1,0:T(8,128)} %pack.1), calls=%async_computation | async-start | bytes 1310720 | tf_op jit(solution)/shard_map/all_to_all | solution.py:225
  21.1 0.0 copy-start.3
  21.2 0.7 gather_fusion
  21.9 0.6 fusion.3
  25.0 0.7 dynamic_slice.21
  29.1 12.1 %all-to-all-done = f32[16,80,128]{2,1,0:T(8,128)S(1)} async-done(((f32[16,80,128]{2,1,0:T(8,128)}), f32[16,80,128]{2,1,0:T(8,128)S(1)}, u32[]{:S(2)}, u32[]{:S(2)}) %all-to-all-start) | async-done | bytes 655392 | tf_op jit(solution)/shard_map/all_to_all | solution.py:225
  41.1 16.3 %all-gather = f32[1280,128]{1,0:T(8,128)S(1)} all-gather(f32[80,128]{1,0:T(8,128)S(1)} %pad_maximum_fusion.2), channel_id=2, replica_groups=mesh['rows'=16,'samp'=16] {'rows'}, dimensions={0}, use_global_device_ids=true | all-gather | bytes 696320 | tf_op jit(solution)/shard_map/all_gather | solution.py:234
  57.4 3.0 %collective-permute-start.2 = (f32[7,8,128]{2,1,0:T(8,128)S(1)}, f32[7,8,128]{2,1,0:T(8,128)S(1)}, u32[]{:S(2)}, u32[]{:S(2)}) collective-permute-start(f32[7,8,128]{2,1,0:T(8,128)S(1)} %get-tuple-element.9), channel_id=1, source_target_pairs={{0,8},{1,9},{2,10},{3,11},{4,12},{5,13},{6,14},{7,15},{8,0},{9,1},... | collective-permute-start | bytes 86024 | tf_op jit(solution)/shard_map/ppermute | solution.py:239
  60.4 0.8 collective-permute-start.1
  61.2 0.7 collective-permute-start
  61.9 2.7 %collective-permute-start.8 = (f32[7,8,128]{2,1,0:T(8,128)S(1)}, f32[7,8,128]{2,1,0:T(8,128)S(1)}, u32[]{:S(2)}, u32[]{:S(2)}) collective-permute-start(f32[7,8,128]{2,1,0:T(8,128)S(1)} %get-tuple-element.8), channel_id=1, source_target_pairs={{0,2},{1,3},{2,0},{3,1},{4,6},{5,7},{6,4},{7,5},{8,10},{9,11},{10,... | collective-permute-start | bytes 86024 | tf_op jit(solution)/shard_map/ppermute | solution.py:240
  64.7 0.9 collective-permute-start.7
  65.5 0.6 collective-permute-start.6
  66.1 0.0 collective-permute-done.1
  66.1 0.0 collective-permute-done
  66.1 1.3 collective-permute-start.3
  67.4 1.5 %collective-permute-start.4 = (f32[4,7,8,128]{3,2,1,0:T(8,128)S(1)}, f32[4,7,8,128]{3,2,1,0:T(8,128)S(1)}, u32[]{:S(2)}, u32[]{:S(2)}) collective-permute-start(f32[4,7,8,128]{3,2,1,0:T(8,128)S(1)} %pad_maximum_fusion), channel_id=1, source_target_pairs={{0,3},{1,0},{2,1},{3,2},{4,7},{5,4},{6,5},{7,6},{8,11},{9,8},{10,9... | collective-permute-start | bytes 344072 | tf_op jit(solution)/shard_map/ppermute | solution.py:242
  68.9 1.5 %collective-permute-start.5 = (f32[4,7,8,128]{3,2,1,0:T(8,128)S(1)}, f32[4,7,8,128]{3,2,1,0:T(8,128)S(1)}, u32[]{:S(2)}, u32[]{:S(2)}) collective-permute-start(f32[4,7,8,128]{3,2,1,0:T(8,128)S(1)} %pad_maximum_fusion), channel_id=1, source_target_pairs={{0,2},{1,3},{2,0},{3,1},{4,6},{5,7},{6,4},{7,5},{8,10},{9,11},{10,... | collective-permute-start | bytes 344072 | tf_op jit(solution)/shard_map/ppermute | solution.py:242
  70.4 0.0 collective-permute-done.7
  70.4 0.0 collective-permute-done.6
  70.5 0.5 collective-permute-start.9
  70.9 2.3 %collective-permute-start.10 = (f32[4,7,8,128]{3,2,1,0:T(8,128)S(1)}, f32[4,7,8,128]{3,2,1,0:T(8,128)S(1)}, u32[]{:S(2)}, u32[]{:S(2)}) collective-permute-start(f32[4,7,8,128]{3,2,1,0:T(8,128)S(1)} %pad_maximum_fusion.1), channel_id=1, source_target_pairs={{0,12},{1,13},{2,14},{3,15},{4,0},{5,1},{6,2},{7,3},{8,4},{9,5},{1... | collective-permute-start | bytes 344072 | tf_op jit(solution)/shard_map/ppermute | solution.py:243
  73.2 1.8 %collective-permute-done.3 = f32[4,7,8,128]{3,2,1,0:T(8,128)S(1)} collective-permute-done((f32[4,7,8,128]{3,2,1,0:T(8,128)S(1)}, f32[4,7,8,128]{3,2,1,0:T(8,128)S(1)}, u32[]{:S(2)}, u32[]{:S(2)}) %collective-permute-start.3) | collective-permute-done | bytes 114720 | tf_op jit(solution)/shard_map/ppermute | solution.py:242
  75.0 0.8 collective-permute-start.11
  75.8 4.5 %collective-permute-done.5 = f32[4,7,8,128]{3,2,1,0:T(8,128)S(1)} collective-permute-done((f32[4,7,8,128]{3,2,1,0:T(8,128)S(1)}, f32[4,7,8,128]{3,2,1,0:T(8,128)S(1)}, u32[]{:S(2)}, u32[]{:S(2)}) %collective-permute-start.5) | collective-permute-done | bytes 114720 | tf_op jit(solution)/shard_map/ppermute | solution.py:242
  80.4 0.0 collective-permute-done.10
  80.4 3.7 %collective-permute-done.11 = f32[4,7,8,128]{3,2,1,0:T(8,128)S(1)} collective-permute-done((f32[4,7,8,128]{3,2,1,0:T(8,128)S(1)}, f32[4,7,8,128]{3,2,1,0:T(8,128)S(1)}, u32[]{:S(2)}, u32[]{:S(2)}) %collective-permute-start.11) | collective-permute-done | bytes 114720 | tf_op jit(solution)/shard_map/ppermute | solution.py:243
  84.1 0.0 copy-start.1
  84.1 3.4 %collective-permute-start.12 = (f32[2,4,4,7,8,128]{5,4,3,2,1,0:T(8,128)S(1)}, f32[2,4,4,7,8,128]{5,4,3,2,1,0:T(8,128)S(1)}, u32[]{:S(2)}, u32[]{:S(2)}) collective-permute-start(f32[2,4,4,7,8,128]{5,4,3,2,1,0:T(8,128)S(1)} %bitcast.46), channel_id=1, source_target_pairs={{0,16},{16,0},{32,48},{48,32},{64,80},{80,64},{96,112},{112,96},{1... | collective-permute-start | bytes 2752520 | tf_op jit(solution)/shard_map/ppermute | solution.py:245
  87.5 0.1 copy.15
  87.6 0.1 add.140
  87.7 0.1 add.141
  87.8 0.1 add.143
  87.8 0.1 add.133
  87.9 0.1 add.137
  88.0 0.1 add.138
  88.1 0.6 pad_add_fusion.spots
  88.7 0.1 select_reduce_fusion
  88.8 0.7 compare_select_fusion.picks
  89.4 0.1 collective-permute-done.12.other
  89.6 0.9 copy-done.2
  90.5 5.5 %solve.1 = (f32[8,128,128]{2,1,0:T(8,128)}, bf16[9,128,256]{2,1,0:T(8,128)(2,1)}) custom-call(s32[1]{0:T(128)} %bitcast.core, s32[2,16]{1,0:T(2,128)} %pad_add_fusion.spots, f32[16,80,128]{2,1,0:T(8,128)} %bitcast.45, f32[2,4,4,7,8,128]{5,4,3,2,1,0:T(8,128)} %bitcast.47, f32[2,4,4,7,8,128]{5,4,3,2,1,0:T(8,128)} %copy-done.2, f32[8,128,128]{2,1,0:T(8,128)} %inverse.1), custom_call_target="tpu_custom_call" | custom-call | tf_op jit(solution)/shard_map/solve/pallas_call | solution.py:131
  96.0 27.3 %all-gather.4.cloned.1.call-done = f32[576,6,8,128]{3,2,1,0:T(8,128)} async-done(((f32[36,6,8,128]{3,2,1,0:T(8,128)}), f32[576,6,8,128]{3,2,1,0:T(8,128)}) %all-gather.4.cloned.1.call-update) | async-done | bytes 14155792 | tf_op jit(solution)/shard_map/all_gather | solution.py:216
  123.4 11.8 %update.1 = f32[36,128,128]{2,1,0:T(8,128)} custom-call(s32[36,6]{1,0:T(8,128)} %compare_select_fusion.picks, f32[36,128,128]{2,1,0:T(8,128)} %sides.3, f32[16,36,6,8,128]{4,3,2,1,0:T(8,128)} %bitcast.43, bf16[9,128,256]{2,1,0:T(8,128)(2,1)} %get-tuple-element.5.pairs), custom_call_target="tpu_custom_call" | custom-call | tf_op jit(solution)/shard_map/update/pallas_call | solution.py:194
  (39 shorter events, 0.2 us)
Async XLA Ops:
  7.2 116.2 %all-gather.4.cloned.1.call-start = ((), (), s32[]{:S(2)}) async-start(), calls=%async_computation.1 | async-start | bytes 15040512 | tf_op jit(solution)/shard_map/all_gather | solution.py:216
  7.9 13.2 %copy-start.6 = (s32[32]{0:T(128)S(1)}, s32[32]{0:T(128)}, u32[]{:S(2)}) copy-start(s32[32]{0:T(128)} %constant.110) | copy-start | bytes 388
  7.9 13.2 %copy-start.4 = (s32[8]{0:T(128)S(1)}, s32[8]{0:T(128)}, u32[]{:S(2)}) copy-start(s32[8]{0:T(128)} %pivots.1) | copy-start | bytes 100
  11.1 30.0 %all-to-all-start = ((f32[16,80,128]{2,1,0:T(8,128)}), f32[16,80,128]{2,1,0:T(8,128)S(1)}, u32[]{:S(2)}, u32[]{:S(2)}) async-start(f32[16,80,128]{2,1,0:T(8,128)} %pack.1), calls=%async_computation | async-start | bytes 1310720 | tf_op jit(solution)/shard_map/all_to_all | solution.py:225
  21.1 66.4 %copy-start.5 = (s32[4]{0:T(128)S(1)}, s32[4]{0:T(128)}, u32[]{:S(2)}) copy-start(s32[4]{0:T(128)} %constant.105) | copy-start | bytes 52
  21.1 66.4 %copy-start.3 = (s32[36,6]{0,1:T(8,128)S(1)}, s32[36,6]{0,1:T(8,128)}, u32[]{:S(2)}) copy-start(s32[36,6]{0,1:T(8,128)} %param.9) | copy-start | bytes 2596
  57.4 32.2 %copy-start = (f32[1280,128]{1,0:T(8,128)}, f32[1280,128]{1,0:T(8,128)S(1)}, u32[]{:S(2)}) copy-start(f32[1280,128]{1,0:T(8,128)S(1)} %all-gather) | copy-start | bytes 1966084
  57.4 8.1 %collective-permute-start.2 = (f32[7,8,128]{2,1,0:T(8,128)S(1)}, f32[7,8,128]{2,1,0:T(8,128)S(1)}, u32[]{:S(2)}, u32[]{:S(2)}) collective-permute-start(f32[7,8,128]{2,1,0:T(8,128)S(1)} %get-tuple-element.9), channel_id=1, source_target_pairs={{0,8},{1,9},{2,10},{3,11},{4,12},{5,13},{6,14},{7,15},{8,0},{9,1},... | collective-permute-start | bytes 86024 | tf_op jit(solution)/shard_map/ppermute | solution.py:239
  60.4 5.7 %collective-permute-start.1 = (f32[7,8,128]{2,1,0:T(8,128)S(1)}, f32[7,8,128]{2,1,0:T(8,128)S(1)}, u32[]{:S(2)}, u32[]{:S(2)}) collective-permute-start(f32[7,8,128]{2,1,0:T(8,128)S(1)} %get-tuple-element.9), channel_id=1, source_target_pairs={{0,12},{1,13},{2,14},{3,15},{4,0},{5,1},{6,2},{7,3},{8,4},{9,5},{1... | collective-permute-start | bytes 86024 | tf_op jit(solution)/shard_map/ppermute | solution.py:239
  61.2 4.9 %collective-permute-start = (f32[7,8,128]{2,1,0:T(8,128)S(1)}, f32[7,8,128]{2,1,0:T(8,128)S(1)}, u32[]{:S(2)}, u32[]{:S(2)}) collective-permute-start(f32[7,8,128]{2,1,0:T(8,128)S(1)} %get-tuple-element.9), channel_id=1, source_target_pairs={{0,4},{1,5},{2,6},{3,7},{4,8},{5,9},{6,10},{7,11},{8,12},{9,13},{1... | collective-permute-start | bytes 86024 | tf_op jit(solution)/shard_map/ppermute | solution.py:239
  61.9 7.0 %collective-permute-start.8 = (f32[7,8,128]{2,1,0:T(8,128)S(1)}, f32[7,8,128]{2,1,0:T(8,128)S(1)}, u32[]{:S(2)}, u32[]{:S(2)}) collective-permute-start(f32[7,8,128]{2,1,0:T(8,128)S(1)} %get-tuple-element.8), channel_id=1, source_target_pairs={{0,2},{1,3},{2,0},{3,1},{4,6},{5,7},{6,4},{7,5},{8,10},{9,11},{10,... | collective-permute-start | bytes 86024 | tf_op jit(solution)/shard_map/ppermute | solution.py:240
  64.7 5.8 %collective-permute-start.7 = (f32[7,8,128]{2,1,0:T(8,128)S(1)}, f32[7,8,128]{2,1,0:T(8,128)S(1)}, u32[]{:S(2)}, u32[]{:S(2)}) collective-permute-start(f32[7,8,128]{2,1,0:T(8,128)S(1)} %get-tuple-element.8), channel_id=1, source_target_pairs={{0,3},{1,0},{2,1},{3,2},{4,7},{5,4},{6,5},{7,6},{8,11},{9,8},{10,9... | collective-permute-start | bytes 86024 | tf_op jit(solution)/shard_map/ppermute | solution.py:240
  65.5 4.9 %collective-permute-start.6 = (f32[7,8,128]{2,1,0:T(8,128)S(1)}, f32[7,8,128]{2,1,0:T(8,128)S(1)}, u32[]{:S(2)}, u32[]{:S(2)}) collective-permute-start(f32[7,8,128]{2,1,0:T(8,128)S(1)} %get-tuple-element.8), channel_id=1, source_target_pairs={{0,1},{1,2},{2,3},{3,0},{4,5},{5,6},{6,7},{7,4},{8,9},{9,10},{10,1... | collective-permute-start | bytes 86024 | tf_op jit(solution)/shard_map/ppermute | solution.py:240
  66.1 8.8 %collective-permute-start.3 = (f32[4,7,8,128]{3,2,1,0:T(8,128)S(1)}, f32[4,7,8,128]{3,2,1,0:T(8,128)S(1)}, u32[]{:S(2)}, u32[]{:S(2)}) collective-permute-start(f32[4,7,8,128]{3,2,1,0:T(8,128)S(1)} %pad_maximum_fusion), channel_id=1, source_target_pairs={{0,1},{1,2},{2,3},{3,0},{4,5},{5,6},{6,7},{7,4},{8,9},{9,10},{10,1... | collective-permute-start | bytes 344072 | tf_op jit(solution)/shard_map/ppermute | solution.py:242
  67.4 8.4 %collective-permute-start.4 = (f32[4,7,8,128]{3,2,1,0:T(8,128)S(1)}, f32[4,7,8,128]{3,2,1,0:T(8,128)S(1)}, u32[]{:S(2)}, u32[]{:S(2)}) collective-permute-start(f32[4,7,8,128]{3,2,1,0:T(8,128)S(1)} %pad_maximum_fusion), channel_id=1, source_target_pairs={{0,3},{1,0},{2,1},{3,2},{4,7},{5,4},{6,5},{7,6},{8,11},{9,8},{10,9... | collective-permute-start | bytes 344072 | tf_op jit(solution)/shard_map/ppermute | solution.py:242
  68.9 11.4 %collective-permute-start.5 = (f32[4,7,8,128]{3,2,1,0:T(8,128)S(1)}, f32[4,7,8,128]{3,2,1,0:T(8,128)S(1)}, u32[]{:S(2)}, u32[]{:S(2)}) collective-permute-start(f32[4,7,8,128]{3,2,1,0:T(8,128)S(1)} %pad_maximum_fusion), channel_id=1, source_target_pairs={{0,2},{1,3},{2,0},{3,1},{4,6},{5,7},{6,4},{7,5},{8,10},{9,11},{10,... | collective-permute-start | bytes 344072 | tf_op jit(solution)/shard_map/ppermute | solution.py:242
  70.5 9.9 %collective-permute-start.9 = (f32[4,7,8,128]{3,2,1,0:T(8,128)S(1)}, f32[4,7,8,128]{3,2,1,0:T(8,128)S(1)}, u32[]{:S(2)}, u32[]{:S(2)}) collective-permute-start(f32[4,7,8,128]{3,2,1,0:T(8,128)S(1)} %pad_maximum_fusion.1), channel_id=1, source_target_pairs={{0,4},{1,5},{2,6},{3,7},{4,8},{5,9},{6,10},{7,11},{8,12},{9,13},{1... | collective-permute-start | bytes 344072 | tf_op jit(solution)/shard_map/ppermute | solution.py:243
  70.9 9.4 %collective-permute-start.10 = (f32[4,7,8,128]{3,2,1,0:T(8,128)S(1)}, f32[4,7,8,128]{3,2,1,0:T(8,128)S(1)}, u32[]{:S(2)}, u32[]{:S(2)}) collective-permute-start(f32[4,7,8,128]{3,2,1,0:T(8,128)S(1)} %pad_maximum_fusion.1), channel_id=1, source_target_pairs={{0,12},{1,13},{2,14},{3,15},{4,0},{5,1},{6,2},{7,3},{8,4},{9,5},{1... | collective-permute-start | bytes 344072 | tf_op jit(solution)/shard_map/ppermute | solution.py:243
  75.0 9.1 %collective-permute-start.11 = (f32[4,7,8,128]{3,2,1,0:T(8,128)S(1)}, f32[4,7,8,128]{3,2,1,0:T(8,128)S(1)}, u32[]{:S(2)}, u32[]{:S(2)}) collective-permute-start(f32[4,7,8,128]{3,2,1,0:T(8,128)S(1)} %pad_maximum_fusion.1), channel_id=1, source_target_pairs={{0,8},{1,9},{2,10},{3,11},{4,12},{5,13},{6,14},{7,15},{8,0},{9,1},... | collective-permute-start | bytes 344072 | tf_op jit(solution)/shard_map/ppermute | solution.py:243
  84.1 5.5 %copy-start.1 = (f32[8,4,7,8,128]{4,3,2,1,0:T(8,128)}, f32[8,4,7,8,128]{4,3,2,1,0:T(8,128)S(1)}, u32[]{:S(2)}) copy-start(f32[8,4,7,8,128]{4,3,2,1,0:T(8,128)S(1)} %bitcast_dynamic-update-slice_fusion) | copy-start | bytes 2752516
  84.1 5.5 %collective-permute-start.12 = (f32[2,4,4,7,8,128]{5,4,3,2,1,0:T(8,128)S(1)}, f32[2,4,4,7,8,128]{5,4,3,2,1,0:T(8,128)S(1)}, u32[]{:S(2)}, u32[]{:S(2)}) collective-permute-start(f32[2,4,4,7,8,128]{5,4,3,2,1,0:T(8,128)S(1)} %bitcast.46), channel_id=1, source_target_pairs={{0,16},{16,0},{32,48},{48,32},{64,80},{80,64},{96,112},{112,96},{1... | collective-permute-start | bytes 2752520 | tf_op jit(solution)/shard_map/ppermute | solution.py:245
  89.6 0.9 copy-start.2
Sparse Core Ops, SparseCore 0:
  10.4 112.8 all-gather.3

commit v9 on v7

--- a/solution.py
+++ b/solution.py
@@ -15,7 +15,7 @@
 ROWS_PER_STEP = 18
 SIDE = 4
 MOVES = (1, -1, 2)
-PART = 8
+PART = 7
 
 
 def shift_y(d):
@@ -174,7 +174,7 @@
             pl.BlockSpec((STEPS + 1, BLOCK, 2 * BLOCK), lambda g: (0, 0, 0)),
         ],
         out_specs=pl.BlockSpec((ROWS_PER_STEP, BLOCK, BLOCK), lambda g: (g, 0, 0)),
-        compiler_params=pltpu.CompilerParams(vmem_limit_bytes=48 * 2**20),
+        compiler_params=pltpu.CompilerParams(vmem_limit_bytes=58 * 2**20),
         name="update",
     )(picks, sides, factor, pairs)
 
@@ -203,7 +203,7 @@
     gathered = lax.all_gather(part, "rows", axis=0, tiled=False)
     slices = gathered[:, HALF:].reshape(TRI, SLICE, BLOCK)
     core = rank % 2
-    half = lax.dynamic_slice(slices, (core * RANKS, 0, 0), (RANKS, SLICE, BLOCK))
+    half = lax.dynamic_slice(slices, (core * 2 * PART, 0, 0), (2 * PART, SLICE, BLOCK))
     first, second = half[:PART], half[PART:]
     first = [first] + [lax.ppermute(first, "samp", shift_y(d)) for d in MOVES]
     second = [second] + [lax.ppermute(second, "samp", shift_x(d)) for d in MOVES]

time: 141 us -> 140 us (level)
  local copies, waits for them, and re-layouts: 7.69 us -> 3.62 us
  waiting for transfers between devices: 47.5 us -> 50.1 us
    unnamed x20, local copies, waits for them, and re-layouts: 4.52 us -> 1.1 us
    ppermute x3, waiting for transfers between devices: 1.29 us -> 3.69 us  [local(): lax.ppermute(second, 'samp', shift_y(d))]
  transfers between devices with their start and end apart: 15 -> 15, of which waited for: 7 -> 6; matrix products, arithmetic and copies ran while one was open for 6% -> 3% of each run, Pallas kernels for 6% -> 6%
where the time goes in v9:
time: 140 us; the launch traced here: 139 us
  waiting for transfers between devices  50.1 us (36%)
  starting transfers between devices  29.9 us (21%)
  between operations  20.1 us (14%)
  Pallas kernels  17.6 us (13%)
  blocking collectives  16.3 us (12%)
  local copies, waits for them, and re-layouts  3.62 us (3%)
  other arithmetic  1.42 us (1%)
    all_gather x1, waiting for transfers between devices, local(): everything = lax.all_gather(factor_blocks, 'samp', axis=0, tiled=False)  27.3 us
    all_gather x1, blocking collectives, local(): gathered = lax.all_gather(part, 'rows', axis=0, tiled=False)  16.3 us
    all_to_all x1, waiting for transfers between devices, local(): pieces = lax.all_to_all(payload, 'rows', 0, 0)  12.1 us
    all_to_all x1, starting transfers between devices, local(): pieces = lax.all_to_all(payload, 'rows', 0, 0)  9.99 us
    pallas_call x1, Pallas kernels, update(): pl.pallas_call(update_kernel, grid=(rows // ROWS_PER_STEP,), out_shape=ja...  8.93 us
    ppermute x3, waiting for transfers between devices, local(): parts = [first] + [lax.ppermute(first, 'samp', shift_x(d)) for d in MOVES]  6.2 us
    pallas_call x1, Pallas kernels, solve(): pl.pallas_call(solve_kernel, out_shape=(jax.ShapeDtypeStruct((STEPS, BLOC...  5.54 us
    ppermute x3, starting transfers between devices, local(): first = [first] + [lax.ppermute(first, 'samp', shift_y(d)) for d in MOVES]  4.47 us
  transfers between devices with their start and end apart: 15, of which 6 were waited for; matrix products, arithmetic and copies ran while one was open for 3% of the time, Pallas kernels for 6%

profile of v9, /device:TPU:1, one launch (start us, length us, event | category | flops | bytes accessed | tf_op | source)
XLA Modules:
  0.0 139.1 jit_solution(3244218687753180214)
XLA Ops:
  7.2 0.0 all-gather.4.cloned.1.call-start
  7.2 0.7 all-gather.4.cloned.1.call-update
  7.9 0.0 copy-start.6
  7.9 3.2 %pack.1 = f32[16,80,128]{2,1,0:T(8,128)} custom-call(s32[8]{0:T(128)} %pivots.1, s32[6,36]{1,0:T(8,128)} %bitcast.65, f32[36,128,128]{2,1,0:T(8,128)} %sides.3, f32[36,6,8,128]{3,2,1,0:T(8,128)} %factor.1), custom_call_target="tpu_custom_call" | custom-call | tf_op jit(solution)/shard_map/pack/pallas_call | solution.py:90
  11.1 10.0 %all-to-all-start = ((f32[16,80,128]{2,1,0:T(8,128)}), f32[16,80,128]{2,1,0:T(8,128)S(1)}, u32[]{:S(2)}, u32[]{:S(2)}) async-start(f32[16,80,128]{2,1,0:T(8,128)} %pack.1), calls=%async_computation | async-start | bytes 1310720 | tf_op jit(solution)/shard_map/all_to_all | solution.py:194
  21.1 0.0 copy-start.3
  21.2 0.7 gather_fusion
  21.9 0.6 fusion.3
  25.0 0.7 dynamic_slice.21
  29.1 12.1 %all-to-all-done = f32[16,80,128]{2,1,0:T(8,128)S(1)} async-done(((f32[16,80,128]{2,1,0:T(8,128)}), f32[16,80,128]{2,1,0:T(8,128)S(1)}, u32[]{:S(2)}, u32[]{:S(2)}) %all-to-all-start) | async-done | bytes 655392 | tf_op jit(solution)/shard_map/all_to_all | solution.py:194
  41.1 16.3 %all-gather = f32[1280,128]{1,0:T(8,128)S(1)} all-gather(f32[80,128]{1,0:T(8,128)S(1)} %pad_maximum_fusion.2), channel_id=2, replica_groups=mesh['rows'=16,'samp'=16] {'rows'}, dimensions={0}, use_global_device_ids=true | all-gather | bytes 696320 | tf_op jit(solution)/shard_map/all_gather | solution.py:203
  57.4 3.0 %collective-permute-start.2 = (f32[7,8,128]{2,1,0:T(8,128)S(1)}, f32[7,8,128]{2,1,0:T(8,128)S(1)}, u32[]{:S(2)}, u32[]{:S(2)}) collective-permute-start(f32[7,8,128]{2,1,0:T(8,128)S(1)} %get-tuple-element.9), channel_id=1, source_target_pairs={{0,8},{1,9},{2,10},{3,11},{4,12},{5,13},{6,14},{7,15},{8,0},{9,1},... | collective-permute-start | bytes 86024 | tf_op jit(solution)/shard_map/ppermute | solution.py:208
  60.4 0.8 collective-permute-start.1
  61.2 0.7 collective-permute-start
  61.9 2.7 %collective-permute-start.8 = (f32[7,8,128]{2,1,0:T(8,128)S(1)}, f32[7,8,128]{2,1,0:T(8,128)S(1)}, u32[]{:S(2)}, u32[]{:S(2)}) collective-permute-start(f32[7,8,128]{2,1,0:T(8,128)S(1)} %get-tuple-element.8), channel_id=1, source_target_pairs={{0,2},{1,3},{2,0},{3,1},{4,6},{5,7},{6,4},{7,5},{8,10},{9,11},{10,... | collective-permute-start | bytes 86024 | tf_op jit(solution)/shard_map/ppermute | solution.py:209
  64.7 0.9 collective-permute-start.7
  65.5 0.6 collective-permute-start.6
  66.1 0.0 collective-permute-done.1
  66.1 0.0 collective-permute-done
  66.1 1.3 collective-permute-start.3
  67.4 1.5 %collective-permute-start.4 = (f32[4,7,8,128]{3,2,1,0:T(8,128)S(1)}, f32[4,7,8,128]{3,2,1,0:T(8,128)S(1)}, u32[]{:S(2)}, u32[]{:S(2)}) collective-permute-start(f32[4,7,8,128]{3,2,1,0:T(8,128)S(1)} %pad_maximum_fusion), channel_id=1, source_target_pairs={{0,3},{1,0},{2,1},{3,2},{4,7},{5,4},{6,5},{7,6},{8,11},{9,8},{10,9... | collective-permute-start | bytes 344072 | tf_op jit(solution)/shard_map/ppermute | solution.py:211
  68.9 1.5 %collective-permute-start.5 = (f32[4,7,8,128]{3,2,1,0:T(8,128)S(1)}, f32[4,7,8,128]{3,2,1,0:T(8,128)S(1)}, u32[]{:S(2)}, u32[]{:S(2)}) collective-permute-start(f32[4,7,8,128]{3,2,1,0:T(8,128)S(1)} %pad_maximum_fusion), channel_id=1, source_target_pairs={{0,2},{1,3},{2,0},{3,1},{4,6},{5,7},{6,4},{7,5},{8,10},{9,11},{10,... | collective-permute-start | bytes 344072 | tf_op jit(solution)/shard_map/ppermute | solution.py:211
  70.4 0.0 collective-permute-done.7
  70.4 0.0 collective-permute-done.6
  70.5 0.5 collective-permute-start.9
  70.9 2.3 %collective-permute-start.10 = (f32[4,7,8,128]{3,2,1,0:T(8,128)S(1)}, f32[4,7,8,128]{3,2,1,0:T(8,128)S(1)}, u32[]{:S(2)}, u32[]{:S(2)}) collective-permute-start(f32[4,7,8,128]{3,2,1,0:T(8,128)S(1)} %pad_maximum_fusion.1), channel_id=1, source_target_pairs={{0,12},{1,13},{2,14},{3,15},{4,0},{5,1},{6,2},{7,3},{8,4},{9,5},{1... | collective-permute-start | bytes 344072 | tf_op jit(solution)/shard_map/ppermute | solution.py:212
  73.2 1.8 %collective-permute-done.3 = f32[4,7,8,128]{3,2,1,0:T(8,128)S(1)} collective-permute-done((f32[4,7,8,128]{3,2,1,0:T(8,128)S(1)}, f32[4,7,8,128]{3,2,1,0:T(8,128)S(1)}, u32[]{:S(2)}, u32[]{:S(2)}) %collective-permute-start.3) | collective-permute-done | bytes 114720 | tf_op jit(solution)/shard_map/ppermute | solution.py:211
  75.0 0.8 collective-permute-start.11
  75.8 4.5 %collective-permute-done.5 = f32[4,7,8,128]{3,2,1,0:T(8,128)S(1)} collective-permute-done((f32[4,7,8,128]{3,2,1,0:T(8,128)S(1)}, f32[4,7,8,128]{3,2,1,0:T(8,128)S(1)}, u32[]{:S(2)}, u32[]{:S(2)}) %collective-permute-start.5) | collective-permute-done | bytes 114720 | tf_op jit(solution)/shard_map/ppermute | solution.py:211
  80.4 0.0 collective-permute-done.10
  80.4 3.7 %collective-permute-done.11 = f32[4,7,8,128]{3,2,1,0:T(8,128)S(1)} collective-permute-done((f32[4,7,8,128]{3,2,1,0:T(8,128)S(1)}, f32[4,7,8,128]{3,2,1,0:T(8,128)S(1)}, u32[]{:S(2)}, u32[]{:S(2)}) %collective-permute-start.11) | collective-permute-done | bytes 114720 | tf_op jit(solution)/shard_map/ppermute | solution.py:212
  84.1 0.0 copy-start.1
  84.1 3.4 %collective-permute-start.12 = (f32[2,4,4,7,8,128]{5,4,3,2,1,0:T(8,128)S(1)}, f32[2,4,4,7,8,128]{5,4,3,2,1,0:T(8,128)S(1)}, u32[]{:S(2)}, u32[]{:S(2)}) collective-permute-start(f32[2,4,4,7,8,128]{5,4,3,2,1,0:T(8,128)S(1)} %bitcast.46), channel_id=1, source_target_pairs={{0,16},{16,0},{32,48},{48,32},{64,80},{80,64},{96,112},{112,96},{1... | collective-permute-start | bytes 2752520 | tf_op jit(solution)/shard_map/ppermute | solution.py:214
  87.5 0.1 copy.15
  87.6 0.1 add.140
  87.7 0.1 add.141
  87.8 0.1 add.143
  87.8 0.1 add.133
  87.9 0.1 add.137
  88.0 0.1 add.138
  88.1 0.6 pad_add_fusion.spots
  88.7 0.1 select_reduce_fusion
  88.8 0.7 compare_select_fusion.picks
  89.4 0.1 collective-permute-done.12.other
  89.6 0.9 copy-done.2
  90.5 5.5 %solve.1 = (f32[8,128,128]{2,1,0:T(8,128)}, bf16[9,128,256]{2,1,0:T(8,128)(2,1)}) custom-call(s32[1]{0:T(128)} %bitcast.core, s32[2,16]{1,0:T(2,128)} %pad_add_fusion.spots, f32[16,80,128]{2,1,0:T(8,128)} %bitcast.45, f32[2,4,4,7,8,128]{5,4,3,2,1,0:T(8,128)} %bitcast.47, f32[2,4,4,7,8,128]{5,4,3,2,1,0:T(8,128)} %copy-done.2, f32[8,128,128]{2,1,0:T(8,128)} %inverse.1), custom_call_target="tpu_custom_call" | custom-call | tf_op jit(solution)/shard_map/solve/pallas_call | solution.py:131
  96.0 27.3 %all-gather.4.cloned.1.call-done = f32[576,6,8,128]{3,2,1,0:T(8,128)} async-done(((f32[36,6,8,128]{3,2,1,0:T(8,128)}), f32[576,6,8,128]{3,2,1,0:T(8,128)}) %all-gather.4.cloned.1.call-update) | async-done | bytes 14155792 | tf_op jit(solution)/shard_map/all_gather | solution.py:185
  123.4 8.9 %update.1 = f32[36,128,128]{2,1,0:T(8,128)} custom-call(s32[36,6]{1,0:T(8,128)} %compare_select_fusion.picks, f32[36,128,128]{2,1,0:T(8,128)} %sides.3, f32[16,36,6,8,128]{4,3,2,1,0:T(8,128)} %bitcast.43, bf16[9,128,256]{2,1,0:T(8,128)(2,1)} %get-tuple-element.5.pairs), custom_call_target="tpu_custom_call" | custom-call | tf_op jit(solution)/shard_map/update/pallas_call | solution.py:166
  (39 shorter events, 0.2 us)
Async XLA Ops:
  7.2 116.2 %all-gather.4.cloned.1.call-start = ((), (), s32[]{:S(2)}) async-start(), calls=%async_computation.1 | async-start | bytes 15040512 | tf_op jit(solution)/shard_map/all_gather | solution.py:185
  7.9 13.2 %copy-start.6 = (s32[32]{0:T(128)S(1)}, s32[32]{0:T(128)}, u32[]{:S(2)}) copy-start(s32[32]{0:T(128)} %constant.110) | copy-start | bytes 388
  7.9 13.2 %copy-start.4 = (s32[8]{0:T(128)S(1)}, s32[8]{0:T(128)}, u32[]{:S(2)}) copy-start(s32[8]{0:T(128)} %pivots.1) | copy-start | bytes 100
  11.1 30.0 %all-to-all-start = ((f32[16,80,128]{2,1,0:T(8,128)}), f32[16,80,128]{2,1,0:T(8,128)S(1)}, u32[]{:S(2)}, u32[]{:S(2)}) async-start(f32[16,80,128]{2,1,0:T(8,128)} %pack.1), calls=%async_computation | async-start | bytes 1310720 | tf_op jit(solution)/shard_map/all_to_all | solution.py:194
  21.1 66.4 %copy-start.5 = (s32[4]{0:T(128)S(1)}, s32[4]{0:T(128)}, u32[]{:S(2)}) copy-start(s32[4]{0:T(128)} %constant.105) | copy-start | bytes 52
  21.1 66.4 %copy-start.3 = (s32[36,6]{0,1:T(8,128)S(1)}, s32[36,6]{0,1:T(8,128)}, u32[]{:S(2)}) copy-start(s32[36,6]{0,1:T(8,128)} %param.9) | copy-start | bytes 2596
  57.4 32.2 %copy-start = (f32[1280,128]{1,0:T(8,128)}, f32[1280,128]{1,0:T(8,128)S(1)}, u32[]{:S(2)}) copy-start(f32[1280,128]{1,0:T(8,128)S(1)} %all-gather) | copy-start | bytes 1966084
  57.4 8.1 %collective-permute-start.2 = (f32[7,8,128]{2,1,0:T(8,128)S(1)}, f32[7,8,128]{2,1,0:T(8,128)S(1)}, u32[]{:S(2)}, u32[]{:S(2)}) collective-permute-start(f32[7,8,128]{2,1,0:T(8,128)S(1)} %get-tuple-element.9), channel_id=1, source_target_pairs={{0,8},{1,9},{2,10},{3,11},{4,12},{5,13},{6,14},{7,15},{8,0},{9,1},... | collective-permute-start | bytes 86024 | tf_op jit(solution)/shard_map/ppermute | solution.py:208
  60.4 5.7 %collective-permute-start.1 = (f32[7,8,128]{2,1,0:T(8,128)S(1)}, f32[7,8,128]{2,1,0:T(8,128)S(1)}, u32[]{:S(2)}, u32[]{:S(2)}) collective-permute-start(f32[7,8,128]{2,1,0:T(8,128)S(1)} %get-tuple-element.9), channel_id=1, source_target_pairs={{0,12},{1,13},{2,14},{3,15},{4,0},{5,1},{6,2},{7,3},{8,4},{9,5},{1... | collective-permute-start | bytes 86024 | tf_op jit(solution)/shard_map/ppermute | solution.py:208
  61.2 4.9 %collective-permute-start = (f32[7,8,128]{2,1,0:T(8,128)S(1)}, f32[7,8,128]{2,1,0:T(8,128)S(1)}, u32[]{:S(2)}, u32[]{:S(2)}) collective-permute-start(f32[7,8,128]{2,1,0:T(8,128)S(1)} %get-tuple-element.9), channel_id=1, source_target_pairs={{0,4},{1,5},{2,6},{3,7},{4,8},{5,9},{6,10},{7,11},{8,12},{9,13},{1... | collective-permute-start | bytes 86024 | tf_op jit(solution)/shard_map/ppermute | solution.py:208
  61.9 7.0 %collective-permute-start.8 = (f32[7,8,128]{2,1,0:T(8,128)S(1)}, f32[7,8,128]{2,1,0:T(8,128)S(1)}, u32[]{:S(2)}, u32[]{:S(2)}) collective-permute-start(f32[7,8,128]{2,1,0:T(8,128)S(1)} %get-tuple-element.8), channel_id=1, source_target_pairs={{0,2},{1,3},{2,0},{3,1},{4,6},{5,7},{6,4},{7,5},{8,10},{9,11},{10,... | collective-permute-start | bytes 86024 | tf_op jit(solution)/shard_map/ppermute | solution.py:209
  64.7 5.8 %collective-permute-start.7 = (f32[7,8,128]{2,1,0:T(8,128)S(1)}, f32[7,8,128]{2,1,0:T(8,128)S(1)}, u32[]{:S(2)}, u32[]{:S(2)}) collective-permute-start(f32[7,8,128]{2,1,0:T(8,128)S(1)} %get-tuple-element.8), channel_id=1, source_target_pairs={{0,3},{1,0},{2,1},{3,2},{4,7},{5,4},{6,5},{7,6},{8,11},{9,8},{10,9... | collective-permute-start | bytes 86024 | tf_op jit(solution)/shard_map/ppermute | solution.py:209
  65.5 4.9 %collective-permute-start.6 = (f32[7,8,128]{2,1,0:T(8,128)S(1)}, f32[7,8,128]{2,1,0:T(8,128)S(1)}, u32[]{:S(2)}, u32[]{:S(2)}) collective-permute-start(f32[7,8,128]{2,1,0:T(8,128)S(1)} %get-tuple-element.8), channel_id=1, source_target_pairs={{0,1},{1,2},{2,3},{3,0},{4,5},{5,6},{6,7},{7,4},{8,9},{9,10},{10,1... | collective-permute-start | bytes 86024 | tf_op jit(solution)/shard_map/ppermute | solution.py:209
  66.1 8.8 %collective-permute-start.3 = (f32[4,7,8,128]{3,2,1,0:T(8,128)S(1)}, f32[4,7,8,128]{3,2,1,0:T(8,128)S(1)}, u32[]{:S(2)}, u32[]{:S(2)}) collective-permute-start(f32[4,7,8,128]{3,2,1,0:T(8,128)S(1)} %pad_maximum_fusion), channel_id=1, source_target_pairs={{0,1},{1,2},{2,3},{3,0},{4,5},{5,6},{6,7},{7,4},{8,9},{9,10},{10,1... | collective-permute-start | bytes 344072 | tf_op jit(solution)/shard_map/ppermute | solution.py:211
  67.4 8.4 %collective-permute-start.4 = (f32[4,7,8,128]{3,2,1,0:T(8,128)S(1)}, f32[4,7,8,128]{3,2,1,0:T(8,128)S(1)}, u32[]{:S(2)}, u32[]{:S(2)}) collective-permute-start(f32[4,7,8,128]{3,2,1,0:T(8,128)S(1)} %pad_maximum_fusion), channel_id=1, source_target_pairs={{0,3},{1,0},{2,1},{3,2},{4,7},{5,4},{6,5},{7,6},{8,11},{9,8},{10,9... | collective-permute-start | bytes 344072 | tf_op jit(solution)/shard_map/ppermute | solution.py:211
  68.9 11.4 %collective-permute-start.5 = (f32[4,7,8,128]{3,2,1,0:T(8,128)S(1)}, f32[4,7,8,128]{3,2,1,0:T(8,128)S(1)}, u32[]{:S(2)}, u32[]{:S(2)}) collective-permute-start(f32[4,7,8,128]{3,2,1,0:T(8,128)S(1)} %pad_maximum_fusion), channel_id=1, source_target_pairs={{0,2},{1,3},{2,0},{3,1},{4,6},{5,7},{6,4},{7,5},{8,10},{9,11},{10,... | collective-permute-start | bytes 344072 | tf_op jit(solution)/shard_map/ppermute | solution.py:211
  70.5 9.9 %collective-permute-start.9 = (f32[4,7,8,128]{3,2,1,0:T(8,128)S(1)}, f32[4,7,8,128]{3,2,1,0:T(8,128)S(1)}, u32[]{:S(2)}, u32[]{:S(2)}) collective-permute-start(f32[4,7,8,128]{3,2,1,0:T(8,128)S(1)} %pad_maximum_fusion.1), channel_id=1, source_target_pairs={{0,4},{1,5},{2,6},{3,7},{4,8},{5,9},{6,10},{7,11},{8,12},{9,13},{1... | collective-permute-start | bytes 344072 | tf_op jit(solution)/shard_map/ppermute | solution.py:212
  70.9 9.4 %collective-permute-start.10 = (f32[4,7,8,128]{3,2,1,0:T(8,128)S(1)}, f32[4,7,8,128]{3,2,1,0:T(8,128)S(1)}, u32[]{:S(2)}, u32[]{:S(2)}) collective-permute-start(f32[4,7,8,128]{3,2,1,0:T(8,128)S(1)} %pad_maximum_fusion.1), channel_id=1, source_target_pairs={{0,12},{1,13},{2,14},{3,15},{4,0},{5,1},{6,2},{7,3},{8,4},{9,5},{1... | collective-permute-start | bytes 344072 | tf_op jit(solution)/shard_map/ppermute | solution.py:212
  75.0 9.1 %collective-permute-start.11 = (f32[4,7,8,128]{3,2,1,0:T(8,128)S(1)}, f32[4,7,8,128]{3,2,1,0:T(8,128)S(1)}, u32[]{:S(2)}, u32[]{:S(2)}) collective-permute-start(f32[4,7,8,128]{3,2,1,0:T(8,128)S(1)} %pad_maximum_fusion.1), channel_id=1, source_target_pairs={{0,8},{1,9},{2,10},{3,11},{4,12},{5,13},{6,14},{7,15},{8,0},{9,1},... | collective-permute-start | bytes 344072 | tf_op jit(solution)/shard_map/ppermute | solution.py:212
  84.1 5.5 %copy-start.1 = (f32[8,4,7,8,128]{4,3,2,1,0:T(8,128)}, f32[8,4,7,8,128]{4,3,2,1,0:T(8,128)S(1)}, u32[]{:S(2)}) copy-start(f32[8,4,7,8,128]{4,3,2,1,0:T(8,128)S(1)} %bitcast_dynamic-update-slice_fusion) | copy-start | bytes 2752516
  84.1 5.5 %collective-permute-start.12 = (f32[2,4,4,7,8,128]{5,4,3,2,1,0:T(8,128)S(1)}, f32[2,4,4,7,8,128]{5,4,3,2,1,0:T(8,128)S(1)}, u32[]{:S(2)}, u32[]{:S(2)}) collective-permute-start(f32[2,4,4,7,8,128]{5,4,3,2,1,0:T(8,128)S(1)} %bitcast.46), channel_id=1, source_target_pairs={{0,16},{16,0},{32,48},{48,32},{64,80},{80,64},{96,112},{112,96},{1... | collective-permute-start | bytes 2752520 | tf_op jit(solution)/shard_map/ppermute | solution.py:214
  89.6 0.9 copy-start.2
Sparse Core Ops, SparseCore 0:
  10.4 112.8 all-gather.3

commit v10 on v9

--- a/solution.py
+++ b/solution.py
@@ -177,6 +177,15 @@
         compiler_params=pltpu.CompilerParams(vmem_limit_bytes=58 * 2**20),
         name="update",
     )(picks, sides, factor, pairs)
+
+
+def around(block, shift):
+    ahead = lax.ppermute(block, "samp", shift(1))
+    behind = lax.ppermute(block, "samp", shift(-1))
+    across = jnp.concatenate(
+        [lax.ppermute(ahead[: SIDE // 2], "samp", shift(1)), lax.ppermute(behind[SIDE // 2 :], "samp", shift(-1))]
+    )
+    return [block, ahead, behind, across]
 
 
 def local(right_sides, factor_blocks, block_columns, pivot_rows, diag_inverse):
@@ -208,8 +217,7 @@
     first = [first] + [lax.ppermute(first, "samp", shift_y(d)) for d in MOVES]
     second = [second] + [lax.ppermute(second, "samp", shift_x(d)) for d in MOVES]
     first, second = jnp.stack(first), jnp.stack(second)
-    parts = [first] + [lax.ppermute(first, "samp", shift_x(d)) for d in MOVES]
-    parts += [second] + [lax.ppermute(second, "samp", shift_y(d)) for d in MOVES]
+    parts = around(first, shift_x) + around(second, shift_y)
     mine = jnp.stack(parts).reshape(2, SIDE, SIDE, PART, SLICE, BLOCK)
     other = lax.ppermute(mine, "rows", [(i, i ^ 1) for i in range(RANKS)])
     here = lax.axis_index("samp")

time: 140 us -> 138 us (0.986)
  waiting for transfers between devices: 50.1 us -> 43.8 us
  starting transfers between devices: 29.9 us -> 35.4 us
    all_gather x1, waiting for transfers between devices: 27.3 us -> 21.7 us  [local(): everything = lax.all_gather(factor_blocks, 'samp', axis=0, tiled=False)]
    ppermute x6 -> x8, starting transfers between devices: 7.86 us -> 11.7 us  [the longest x2 6.05 us: around(): lax.ppermute(behind[SIDE // 2:], 'samp', shift(-1))]
    ppermute x6 -> x8, waiting for transfers between devices: 9.89 us -> 7.34 us  [the longest x2 5.34 us: around(): lax.ppermute(ahead[:SIDE // 2], 'samp', shift(1))]
    ppermute x1, starting transfers between devices: 3.38 us -> 4.92 us  [local(): other = lax.ppermute(mine, 'rows', [(i, i ^ 1) for i in range(RANKS)])]
    ppermute x3, waiting for transfers between devices: 0.01 us -> 1.53 us  [local(): lax.ppermute(second, 'samp', shift_x(d))]
  transfers between devices with their start and end apart: 15 -> 17, of which waited for: 6 -> 9; matrix products, arithmetic and copies ran while one was open for 3% -> 3% of each run, Pallas kernels for 6% -> 6%
where the time goes in v10:
time: 138 us
  waiting for transfers between devices  43.8 us (32%)
  starting transfers between devices  35.4 us (26%)
  between operations  19.8 us (14%)
  Pallas kernels  17.7 us (13%)
  blocking collectives  16.3 us (12%)
  local copies, waits for them, and re-layouts  3.53 us (3%)
  other arithmetic  1.46 us (1%)
    all_gather x1, waiting for transfers between devices, local(): everything = lax.all_gather(factor_blocks, 'samp', axis=0, tiled=False)  21.7 us
    all_gather x1, blocking collectives, local(): gathered = lax.all_gather(part, 'rows', axis=0, tiled=False)  16.3 us
    all_to_all x1, waiting for transfers between devices, local(): pieces = lax.all_to_all(payload, 'rows', 0, 0)  12.5 us
    all_to_all x1, starting transfers between devices, local(): pieces = lax.all_to_all(payload, 'rows', 0, 0)  9.99 us
    pallas_call x1, Pallas kernels, update(): pl.pallas_call(update_kernel, grid=(rows // ROWS_PER_STEP,), out_shape=ja...  8.93 us
    ppermute x2, starting transfers between devices, around(): lax.ppermute(behind[SIDE // 2:], 'samp', shift(-1))  6.05 us
    pallas_call x1, Pallas kernels, solve(): pl.pallas_call(solve_kernel, out_shape=(jax.ShapeDtypeStruct((STEPS, BLOC...  5.53 us
    ppermute x2, waiting for transfers between devices, around(): lax.ppermute(ahead[:SIDE // 2], 'samp', shift(1))  5.34 us
  transfers between devices with their start and end apart: 17, of which 9 were waited for; matrix products, arithmetic and copies ran while one was open for 3% of the time, Pallas kernels for 6%

profile of v10, /device:TPU:1, one launch (start us, length us, event | category | flops | bytes accessed | tf_op | source)
XLA Modules:
  0.0 137.9 jit_solution(8268967022894224670)
XLA Ops:
  7.2 0.0 all-gather.4.cloned.1.call-start
  7.2 0.7 all-gather.4.cloned.1.call-update
  7.9 0.0 copy-start.6
  7.9 3.2 %pack.1 = f32[16,80,128]{2,1,0:T(8,128)} custom-call(s32[8]{0:T(128)} %pivots.1, s32[6,36]{1,0:T(8,128)} %bitcast.69, f32[36,128,128]{2,1,0:T(8,128)} %sides.3, f32[36,6,8,128]{3,2,1,0:T(8,128)} %factor.1), custom_call_target="tpu_custom_call" | custom-call | tf_op jit(solution)/shard_map/pack/pallas_call | solution.py:90
  11.1 10.0 %all-to-all-start = ((f32[16,80,128]{2,1,0:T(8,128)}), f32[16,80,128]{2,1,0:T(8,128)S(1)}, u32[]{:S(2)}, u32[]{:S(2)}) async-start(f32[16,80,128]{2,1,0:T(8,128)} %pack.1), calls=%async_computation | async-start | bytes 1310720 | tf_op jit(solution)/shard_map/all_to_all | solution.py:203
  21.1 0.0 copy-start.3
  21.2 0.7 gather_fusion
  21.9 0.6 fusion.5
  24.9 0.6 dynamic_slice.21
  28.7 12.5 %all-to-all-done = f32[16,80,128]{2,1,0:T(8,128)S(1)} async-done(((f32[16,80,128]{2,1,0:T(8,128)}), f32[16,80,128]{2,1,0:T(8,128)S(1)}, u32[]{:S(2)}, u32[]{:S(2)}) %all-to-all-start) | async-done | bytes 655392 | tf_op jit(solution)/shard_map/all_to_all | solution.py:203
  41.2 16.3 %all-gather = f32[1280,128]{1,0:T(8,128)S(1)} all-gather(f32[80,128]{1,0:T(8,128)S(1)} %pad_maximum_fusion.2), channel_id=2, replica_groups=mesh['rows'=16,'samp'=16] {'rows'}, dimensions={0}, use_global_device_ids=true | all-gather | bytes 696320 | tf_op jit(solution)/shard_map/all_gather | solution.py:212
  57.5 3.0 %collective-permute-start.2 = (f32[7,8,128]{2,1,0:T(8,128)S(1)}, f32[7,8,128]{2,1,0:T(8,128)S(1)}, u32[]{:S(2)}, u32[]{:S(2)}) collective-permute-start(f32[7,8,128]{2,1,0:T(8,128)S(1)} %get-tuple-element.9), channel_id=1, source_target_pairs={{0,8},{1,9},{2,10},{3,11},{4,12},{5,13},{6,14},{7,15},{8,0},{9,1},... | collective-permute-start | bytes 86024 | tf_op jit(solution)/shard_map/ppermute | solution.py:217
  60.5 0.8 collective-permute-start.1
  61.2 0.7 collective-permute-start
  61.9 2.7 %collective-permute-start.9 = (f32[7,8,128]{2,1,0:T(8,128)S(1)}, f32[7,8,128]{2,1,0:T(8,128)S(1)}, u32[]{:S(2)}, u32[]{:S(2)}) collective-permute-start(f32[7,8,128]{2,1,0:T(8,128)S(1)} %get-tuple-element.8), channel_id=1, source_target_pairs={{0,2},{1,3},{2,0},{3,1},{4,6},{5,7},{6,4},{7,5},{8,10},{9,11},{10,... | collective-permute-start | bytes 86024 | tf_op jit(solution)/shard_map/ppermute | solution.py:218
  64.7 0.9 collective-permute-start.8
  65.5 0.6 collective-permute-start.7
  66.2 0.0 collective-permute-done
  66.2 1.3 collective-permute-start.3
  67.5 1.5 %collective-permute-start.4 = (f32[4,7,8,128]{3,2,1,0:T(8,128)S(1)}, f32[4,7,8,128]{3,2,1,0:T(8,128)S(1)}, u32[]{:S(2)}, u32[]{:S(2)}) collective-permute-start(f32[4,7,8,128]{3,2,1,0:T(8,128)S(1)} %pad_maximum_fusion), channel_id=1, source_target_pairs={{0,3},{1,0},{2,1},{3,2},{4,7},{5,4},{6,5},{7,6},{8,11},{9,8},{10,9... | collective-permute-start | bytes 344072 | tf_op jit(solution)/shard_map/ppermute | solution.py:184
  68.9 1.5 %collective-permute-done.7 = f32[7,8,128]{2,1,0:T(8,128)S(1)} collective-permute-done((f32[7,8,128]{2,1,0:T(8,128)S(1)}, f32[7,8,128]{2,1,0:T(8,128)S(1)}, u32[]{:S(2)}, u32[]{:S(2)}) %collective-permute-start.7) | collective-permute-done | bytes 28704 | tf_op jit(solution)/shard_map/ppermute | solution.py:218
  70.5 0.5 collective-permute-start.10
  70.9 2.3 %collective-permute-start.11 = (f32[4,7,8,128]{3,2,1,0:T(8,128)S(1)}, f32[4,7,8,128]{3,2,1,0:T(8,128)S(1)}, u32[]{:S(2)}, u32[]{:S(2)}) collective-permute-start(f32[4,7,8,128]{3,2,1,0:T(8,128)S(1)} %pad_maximum_fusion.1), channel_id=1, source_target_pairs={{0,12},{1,13},{2,14},{3,15},{4,0},{5,1},{6,2},{7,3},{8,4},{9,5},{1... | collective-permute-start | bytes 344072 | tf_op jit(solution)/shard_map/ppermute | solution.py:184
  73.2 1.2 collective-permute-done.4
  74.4 2.6 %collective-permute-start.6 = (f32[2,7,8,128]{3,2,1,0:T(8,128)S(1)}, f32[2,7,8,128]{3,2,1,0:T(8,128)S(1)}, u32[]{:S(2)}, u32[]{:S(2)}) collective-permute-start(f32[2,7,8,128]{3,2,1,0:T(8,128)S(1)} %slice.32), channel_id=1, source_target_pairs={{0,3},{1,0},{2,1},{3,2},{4,7},{5,4},{6,5},{7,6},{8,11},{9,8},{10,9... | collective-permute-start | bytes 172040 | tf_op jit(solution)/shard_map/ppermute | solution.py:186
  77.0 0.1 collective-permute-start.5
  77.1 0.4 collective-permute-done.11
  77.5 3.5 %collective-permute-start.13 = (f32[2,7,8,128]{3,2,1,0:T(8,128)S(1)}, f32[2,7,8,128]{3,2,1,0:T(8,128)S(1)}, u32[]{:S(2)}, u32[]{:S(2)}) collective-permute-start(f32[2,7,8,128]{3,2,1,0:T(8,128)S(1)} %slice.34), channel_id=1, source_target_pairs={{0,12},{1,13},{2,14},{3,15},{4,0},{5,1},{6,2},{7,3},{8,4},{9,5},{1... | collective-permute-start | bytes 172040 | tf_op jit(solution)/shard_map/ppermute | solution.py:186
  81.0 0.1 collective-permute-start.12
  81.2 1.7 %collective-permute-done.5 = f32[2,7,8,128]{3,2,1,0:T(8,128)S(1)} collective-permute-done((f32[2,7,8,128]{3,2,1,0:T(8,128)S(1)}, f32[2,7,8,128]{3,2,1,0:T(8,128)S(1)}, u32[]{:S(2)}, u32[]{:S(2)}) %collective-permute-start.5) | collective-permute-done | bytes 57376 | tf_op jit(solution)/shard_map/ppermute | solution.py:186
  83.0 0.4 collective-permute-done.13
  83.3 3.6 %collective-permute-done.12 = f32[2,7,8,128]{3,2,1,0:T(8,128)S(1)} collective-permute-done((f32[2,7,8,128]{3,2,1,0:T(8,128)S(1)}, f32[2,7,8,128]{3,2,1,0:T(8,128)S(1)}, u32[]{:S(2)}, u32[]{:S(2)}) %collective-permute-start.12) | collective-permute-done | bytes 57376 | tf_op jit(solution)/shard_map/ppermute | solution.py:186
  87.0 4.9 %collective-permute-start.14 = (f32[2,4,4,7,8,128]{5,4,3,2,1,0:T(8,128)S(1)}, f32[2,4,4,7,8,128]{5,4,3,2,1,0:T(8,128)S(1)}, u32[]{:S(2)}, u32[]{:S(2)}) collective-permute-start(f32[2,4,4,7,8,128]{5,4,3,2,1,0:T(8,128)S(1)} %bitcast.50), channel_id=1, source_target_pairs={{0,16},{16,0},{32,48},{48,32},{64,80},{80,64},{96,112},{112,96},{1... | collective-permute-start | bytes 2752520 | tf_op jit(solution)/shard_map/ppermute | solution.py:222
  91.9 0.1 copy.15
  92.0 0.1 add.140
  92.1 0.1 add.141
  92.2 0.1 add.143
  92.3 0.1 add.133
  92.4 0.1 add.137
  92.4 0.1 add.138
  92.5 0.6 pad_add_fusion.spots
  93.1 0.1 select_reduce_fusion
  93.2 0.7 compare_select_fusion.picks
  93.9 0.1 collective-permute-done.14.other
  94.0 0.9 copy-done.2
  94.9 5.5 %solve.1 = (f32[8,128,128]{2,1,0:T(8,128)}, bf16[9,128,256]{2,1,0:T(8,128)(2,1)}) custom-call(s32[1]{0:T(128)} %bitcast.core, s32[2,16]{1,0:T(2,128)} %pad_add_fusion.spots, f32[16,80,128]{2,1,0:T(8,128)} %bitcast.49, f32[2,4,4,7,8,128]{5,4,3,2,1,0:T(8,128)} %bitcast.51, f32[2,4,4,7,8,128]{5,4,3,2,1,0:T(8,128)} %copy-done.2, f32[8,128,128]{2,1,0:T(8,128)} %inverse.1), custom_call_target="tpu_custom_call" | custom-call | tf_op jit(solution)/shard_map/solve/pallas_call | solution.py:131
  100.5 21.7 %all-gather.4.cloned.1.call-done = f32[576,6,8,128]{3,2,1,0:T(8,128)} async-done(((f32[36,6,8,128]{3,2,1,0:T(8,128)}), f32[576,6,8,128]{3,2,1,0:T(8,128)}) %all-gather.4.cloned.1.call-update) | async-done | bytes 14155792 | tf_op jit(solution)/shard_map/all_gather | solution.py:194
  122.1 8.9 %update.1 = f32[36,128,128]{2,1,0:T(8,128)} custom-call(s32[36,6]{1,0:T(8,128)} %compare_select_fusion.picks, f32[36,128,128]{2,1,0:T(8,128)} %sides.3, f32[16,36,6,8,128]{4,3,2,1,0:T(8,128)} %bitcast.47, bf16[9,128,256]{2,1,0:T(8,128)(2,1)} %get-tuple-element.5.pairs), custom_call_target="tpu_custom_call" | custom-call | tf_op jit(solution)/shard_map/update/pallas_call | solution.py:166
  (47 shorter events, 0.3 us)
Async XLA Ops:
  7.2 115.0 %all-gather.4.cloned.1.call-start = ((), (), s32[]{:S(2)}) async-start(), calls=%async_computation.1 | async-start | bytes 15040512 | tf_op jit(solution)/shard_map/all_gather | solution.py:194
  7.9 13.3 %copy-start.6 = (s32[32]{0:T(128)S(1)}, s32[32]{0:T(128)}, u32[]{:S(2)}) copy-start(s32[32]{0:T(128)} %constant.110) | copy-start | bytes 388
  7.9 13.3 %copy-start.4 = (s32[8]{0:T(128)S(1)}, s32[8]{0:T(128)}, u32[]{:S(2)}) copy-start(s32[8]{0:T(128)} %pivots.1) | copy-start | bytes 100
  11.1 30.0 %all-to-all-start = ((f32[16,80,128]{2,1,0:T(8,128)}), f32[16,80,128]{2,1,0:T(8,128)S(1)}, u32[]{:S(2)}, u32[]{:S(2)}) async-start(f32[16,80,128]{2,1,0:T(8,128)} %pack.1), calls=%async_computation | async-start | bytes 1310720 | tf_op jit(solution)/shard_map/all_to_all | solution.py:203
  21.1 70.8 %copy-start.5 = (s32[4]{0:T(128)S(1)}, s32[4]{0:T(128)}, u32[]{:S(2)}) copy-start(s32[4]{0:T(128)} %constant.105) | copy-start | bytes 52
  21.1 70.8 %copy-start.3 = (s32[36,6]{0,1:T(8,128)S(1)}, s32[36,6]{0,1:T(8,128)}, u32[]{:S(2)}) copy-start(s32[36,6]{0,1:T(8,128)} %param.9) | copy-start | bytes 2596
  57.4 36.6 %copy-start = (f32[1280,128]{1,0:T(8,128)}, f32[1280,128]{1,0:T(8,128)S(1)}, u32[]{:S(2)}) copy-start(f32[1280,128]{1,0:T(8,128)S(1)} %all-gather) | copy-start | bytes 1966084
  57.5 8.1 %collective-permute-start.2 = (f32[7,8,128]{2,1,0:T(8,128)S(1)}, f32[7,8,128]{2,1,0:T(8,128)S(1)}, u32[]{:S(2)}, u32[]{:S(2)}) collective-permute-start(f32[7,8,128]{2,1,0:T(8,128)S(1)} %get-tuple-element.9), channel_id=1, source_target_pairs={{0,8},{1,9},{2,10},{3,11},{4,12},{5,13},{6,14},{7,15},{8,0},{9,1},... | collective-permute-start | bytes 86024 | tf_op jit(solution)/shard_map/ppermute | solution.py:217
  60.5 5.7 %collective-permute-start.1 = (f32[7,8,128]{2,1,0:T(8,128)S(1)}, f32[7,8,128]{2,1,0:T(8,128)S(1)}, u32[]{:S(2)}, u32[]{:S(2)}) collective-permute-start(f32[7,8,128]{2,1,0:T(8,128)S(1)} %get-tuple-element.9), channel_id=1, source_target_pairs={{0,12},{1,13},{2,14},{3,15},{4,0},{5,1},{6,2},{7,3},{8,4},{9,5},{1... | collective-permute-start | bytes 86024 | tf_op jit(solution)/shard_map/ppermute | solution.py:217
  61.2 4.9 %collective-permute-start = (f32[7,8,128]{2,1,0:T(8,128)S(1)}, f32[7,8,128]{2,1,0:T(8,128)S(1)}, u32[]{:S(2)}, u32[]{:S(2)}) collective-permute-start(f32[7,8,128]{2,1,0:T(8,128)S(1)} %get-tuple-element.9), channel_id=1, source_target_pairs={{0,4},{1,5},{2,6},{3,7},{4,8},{5,9},{6,10},{7,11},{8,12},{9,13},{1... | collective-permute-start | bytes 86024 | tf_op jit(solution)/shard_map/ppermute | solution.py:217
  61.9 7.0 %collective-permute-start.9 = (f32[7,8,128]{2,1,0:T(8,128)S(1)}, f32[7,8,128]{2,1,0:T(8,128)S(1)}, u32[]{:S(2)}, u32[]{:S(2)}) collective-permute-start(f32[7,8,128]{2,1,0:T(8,128)S(1)} %get-tuple-element.8), channel_id=1, source_target_pairs={{0,2},{1,3},{2,0},{3,1},{4,6},{5,7},{6,4},{7,5},{8,10},{9,11},{10,... | collective-permute-start | bytes 86024 | tf_op jit(solution)/shard_map/ppermute | solution.py:218
  64.7 4.3 %collective-permute-start.8 = (f32[7,8,128]{2,1,0:T(8,128)S(1)}, f32[7,8,128]{2,1,0:T(8,128)S(1)}, u32[]{:S(2)}, u32[]{:S(2)}) collective-permute-start(f32[7,8,128]{2,1,0:T(8,128)S(1)} %get-tuple-element.8), channel_id=1, source_target_pairs={{0,3},{1,0},{2,1},{3,2},{4,7},{5,4},{6,5},{7,6},{8,11},{9,8},{10,9... | collective-permute-start | bytes 86024 | tf_op jit(solution)/shard_map/ppermute | solution.py:218
  65.5 4.9 %collective-permute-start.7 = (f32[7,8,128]{2,1,0:T(8,128)S(1)}, f32[7,8,128]{2,1,0:T(8,128)S(1)}, u32[]{:S(2)}, u32[]{:S(2)}) collective-permute-start(f32[7,8,128]{2,1,0:T(8,128)S(1)} %get-tuple-element.8), channel_id=1, source_target_pairs={{0,1},{1,2},{2,3},{3,0},{4,5},{5,6},{6,7},{7,4},{8,9},{9,10},{10,1... | collective-permute-start | bytes 86024 | tf_op jit(solution)/shard_map/ppermute | solution.py:218
  66.2 10.8 %collective-permute-start.3 = (f32[4,7,8,128]{3,2,1,0:T(8,128)S(1)}, f32[4,7,8,128]{3,2,1,0:T(8,128)S(1)}, u32[]{:S(2)}, u32[]{:S(2)}) collective-permute-start(f32[4,7,8,128]{3,2,1,0:T(8,128)S(1)} %pad_maximum_fusion), channel_id=1, source_target_pairs={{0,1},{1,2},{2,3},{3,0},{4,5},{5,6},{6,7},{7,4},{8,9},{9,10},{10,1... | collective-permute-start | bytes 344072 | tf_op jit(solution)/shard_map/ppermute | solution.py:183
  67.5 7.0 %collective-permute-start.4 = (f32[4,7,8,128]{3,2,1,0:T(8,128)S(1)}, f32[4,7,8,128]{3,2,1,0:T(8,128)S(1)}, u32[]{:S(2)}, u32[]{:S(2)}) collective-permute-start(f32[4,7,8,128]{3,2,1,0:T(8,128)S(1)} %pad_maximum_fusion), channel_id=1, source_target_pairs={{0,3},{1,0},{2,1},{3,2},{4,7},{5,4},{6,5},{7,6},{8,11},{9,8},{10,9... | collective-permute-start | bytes 344072 | tf_op jit(solution)/shard_map/ppermute | solution.py:184
  70.5 10.6 %collective-permute-start.10 = (f32[4,7,8,128]{3,2,1,0:T(8,128)S(1)}, f32[4,7,8,128]{3,2,1,0:T(8,128)S(1)}, u32[]{:S(2)}, u32[]{:S(2)}) collective-permute-start(f32[4,7,8,128]{3,2,1,0:T(8,128)S(1)} %pad_maximum_fusion.1), channel_id=1, source_target_pairs={{0,4},{1,5},{2,6},{3,7},{4,8},{5,9},{6,10},{7,11},{8,12},{9,13},{1... | collective-permute-start | bytes 344072 | tf_op jit(solution)/shard_map/ppermute | solution.py:183
  70.9 6.6 %collective-permute-start.11 = (f32[4,7,8,128]{3,2,1,0:T(8,128)S(1)}, f32[4,7,8,128]{3,2,1,0:T(8,128)S(1)}, u32[]{:S(2)}, u32[]{:S(2)}) collective-permute-start(f32[4,7,8,128]{3,2,1,0:T(8,128)S(1)} %pad_maximum_fusion.1), channel_id=1, source_target_pairs={{0,12},{1,13},{2,14},{3,15},{4,0},{5,1},{6,2},{7,3},{8,4},{9,5},{1... | collective-permute-start | bytes 344072 | tf_op jit(solution)/shard_map/ppermute | solution.py:184
  74.4 6.7 %collective-permute-start.6 = (f32[2,7,8,128]{3,2,1,0:T(8,128)S(1)}, f32[2,7,8,128]{3,2,1,0:T(8,128)S(1)}, u32[]{:S(2)}, u32[]{:S(2)}) collective-permute-start(f32[2,7,8,128]{3,2,1,0:T(8,128)S(1)} %slice.32), channel_id=1, source_target_pairs={{0,3},{1,0},{2,1},{3,2},{4,7},{5,4},{6,5},{7,6},{8,11},{9,8},{10,9... | collective-permute-start | bytes 172040 | tf_op jit(solution)/shard_map/ppermute | solution.py:186
  77.0 5.9 %collective-permute-start.5 = (f32[2,7,8,128]{3,2,1,0:T(8,128)S(1)}, f32[2,7,8,128]{3,2,1,0:T(8,128)S(1)}, u32[]{:S(2)}, u32[]{:S(2)}) collective-permute-start(f32[2,7,8,128]{3,2,1,0:T(8,128)S(1)} %slice.31), channel_id=1, source_target_pairs={{0,1},{1,2},{2,3},{3,0},{4,5},{5,6},{6,7},{7,4},{8,9},{9,10},{10,1... | collective-permute-start | bytes 172040 | tf_op jit(solution)/shard_map/ppermute | solution.py:186
  77.5 5.8 %collective-permute-start.13 = (f32[2,7,8,128]{3,2,1,0:T(8,128)S(1)}, f32[2,7,8,128]{3,2,1,0:T(8,128)S(1)}, u32[]{:S(2)}, u32[]{:S(2)}) collective-permute-start(f32[2,7,8,128]{3,2,1,0:T(8,128)S(1)} %slice.34), channel_id=1, source_target_pairs={{0,12},{1,13},{2,14},{3,15},{4,0},{5,1},{6,2},{7,3},{8,4},{9,5},{1... | collective-permute-start | bytes 172040 | tf_op jit(solution)/shard_map/ppermute | solution.py:186
  81.0 5.9 %collective-permute-start.12 = (f32[2,7,8,128]{3,2,1,0:T(8,128)S(1)}, f32[2,7,8,128]{3,2,1,0:T(8,128)S(1)}, u32[]{:S(2)}, u32[]{:S(2)}) collective-permute-start(f32[2,7,8,128]{3,2,1,0:T(8,128)S(1)} %slice.33), channel_id=1, source_target_pairs={{0,4},{1,5},{2,6},{3,7},{4,8},{5,9},{6,10},{7,11},{8,12},{9,13},{1... | collective-permute-start | bytes 172040 | tf_op jit(solution)/shard_map/ppermute | solution.py:186
  87.0 7.0 %copy-start.1 = (f32[8,4,7,8,128]{4,3,2,1,0:T(8,128)}, f32[8,4,7,8,128]{4,3,2,1,0:T(8,128)S(1)}, u32[]{:S(2)}) copy-start(f32[8,4,7,8,128]{4,3,2,1,0:T(8,128)S(1)} %fusion.1) | copy-start | bytes 2752516
  87.0 7.0 %collective-permute-start.14 = (f32[2,4,4,7,8,128]{5,4,3,2,1,0:T(8,128)S(1)}, f32[2,4,4,7,8,128]{5,4,3,2,1,0:T(8,128)S(1)}, u32[]{:S(2)}, u32[]{:S(2)}) collective-permute-start(f32[2,4,4,7,8,128]{5,4,3,2,1,0:T(8,128)S(1)} %bitcast.50), channel_id=1, source_target_pairs={{0,16},{16,0},{32,48},{48,32},{64,80},{80,64},{96,112},{112,96},{1... | collective-permute-start | bytes 2752520 | tf_op jit(solution)/shard_map/ppermute | solution.py:222
  94.0 0.9 copy-start.2
Sparse Core Ops, SparseCore 0:
  10.4 111.6 all-gather.3

commit v11 on v10

--- a/solution.py
+++ b/solution.py
@@ -15,7 +15,7 @@
 ROWS_PER_STEP = 18
 SIDE = 4
 MOVES = (1, -1, 2)
-PART = 7
+PART = 4
 
 
 def shift_y(d):
@@ -101,9 +101,10 @@
     )(pivots, columns, sides, factor)
 
 
-def solve_kernel(core, spots, gathered, mine, other, inverse, solved, pairs, side, blocks):
-    flag = core[0]
-    for pieces, base in ((mine, 2 * PART * flag), (other, 2 * PART * (1 - flag))):
+def solve_kernel(starts, spots, gathered, mine, above, far, inverse, solved, pairs, side, blocks):
+    groups = (mine, above, far.at[0], far.at[1])
+    for q, pieces in enumerate(groups):
+        base = starts[q]
         for p in range(2):
             for e in range(SIDE):
                 for d in range(SIDE):
@@ -126,7 +127,7 @@
     pairs[STEPS] = jnp.zeros((BLOCK, 2 * BLOCK), jnp.bfloat16)
 
 
-def solve(core, spots, gathered, mine, other, inverse):
+def solve(starts, spots, gathered, mine, above, far, inverse):
     vmem = pl.BlockSpec(memory_space=pltpu.VMEM)
     return pl.pallas_call(
         solve_kernel,
@@ -134,14 +135,14 @@
             jax.ShapeDtypeStruct((STEPS, BLOCK, BLOCK), jnp.float32),
             jax.ShapeDtypeStruct((STEPS + 1, BLOCK, 2 * BLOCK), jnp.bfloat16),
         ),
-        in_specs=[pl.BlockSpec(memory_space=pltpu.SMEM)] * 2 + [vmem] * 4,
+        in_specs=[pl.BlockSpec(memory_space=pltpu.SMEM)] * 2 + [vmem] * 5,
         out_specs=(vmem, vmem),
         scratch_shapes=[
             pltpu.VMEM((STEPS, BLOCK, BLOCK), jnp.float32),
             pltpu.VMEM((TRI, BLOCK, BLOCK), jnp.float32),
         ],
         name="solve",
-    )(core, spots, gathered, mine, other, inverse)
+    )(starts, spots, gathered, mine, above, far, inverse)
 
 
 def update_kernel(picks, sides, factor, pairs, out):
@@ -211,20 +212,22 @@
     )
     gathered = lax.all_gather(part, "rows", axis=0, tiled=False)
     slices = gathered[:, HALF:].reshape(TRI, SLICE, BLOCK)
-    core = rank % 2
-    half = lax.dynamic_slice(slices, (core * 2 * PART, 0, 0), (2 * PART, SLICE, BLOCK))
+    quarter = rank % 4
+    half = lax.dynamic_slice(slices, (quarter * 2 * PART, 0, 0), (2 * PART, SLICE, BLOCK))
     first, second = half[:PART], half[PART:]
     first = [first] + [lax.ppermute(first, "samp", shift_y(d)) for d in MOVES]
     second = [second] + [lax.ppermute(second, "samp", shift_x(d)) for d in MOVES]
     first, second = jnp.stack(first), jnp.stack(second)
     parts = around(first, shift_x) + around(second, shift_y)
     mine = jnp.stack(parts).reshape(2, SIDE, SIDE, PART, SLICE, BLOCK)
-    other = lax.ppermute(mine, "rows", [(i, i ^ 1) for i in range(RANKS)])
+    above = lax.ppermute(mine, "rows", [(i, i ^ 2) for i in range(RANKS)])
+    far = lax.ppermute(jnp.stack([mine, above]), "rows", [(i, i ^ 1) for i in range(RANKS)])
+    starts = 2 * PART * (quarter ^ jnp.array([0, 2, 1, 3], jnp.int32))
     here = lax.axis_index("samp")
     moves = jnp.array((0,) + MOVES, jnp.int32)
     y, x = (here // SIDE - moves + SIDE) % SIDE, (here % SIDE - moves + SIDE) % SIDE
     spots = jnp.stack([SIDE * y[None, :] + x[:, None], SIDE * y[:, None] + x[None, :]]).reshape(2, RANKS)
-    solved, pairs = solve(core.reshape(1), spots, gathered, mine, other, diag_inverse)
+    solved, pairs = solve(starts, spots, gathered, mine, above, far, diag_inverse)
     return solved, update(picks, right_sides, everything, pairs)
 
 

time: 138 us -> 136 us (0.986)
  waiting for transfers between devices: 43.8 us -> 39.5 us
  other arithmetic: 1.46 us -> 3.08 us
    all_gather x1, waiting for transfers between devices: 21.7 us -> 11.4 us  [local(): everything = lax.all_gather(factor_blocks, 'samp', axis=0, tiled=False)]
    ppermute x1 -> x2, waiting for transfers between devices: 0.11 us -> 8.95 us  [the longest x1 8.94 us: local(): above = lax.ppermute(mine, 'rows', [(i, i ^ 2) for i in range(RANKS)])]
    ppermute x1 -> x2, starting transfers between devices: 4.92 us -> 5.62 us  [the longest x1 5.34 us: local(): lax.ppermute(jnp.stack([mine, above]), 'rows', [(i, i ^ 1) for i in range...]
  transfers between devices with their start and end apart: 17 -> 18, of which waited for: 9 -> 8; matrix products, arithmetic and copies ran while one was open for 3% -> 4% of each run, Pallas kernels for 6% -> 6%
where the time goes in v11:
time: 136 us
  waiting for transfers between devices  39.5 us (29%)
  starting transfers between devices  35.5 us (26%)
  between operations  20.2 us (15%)
  Pallas kernels  17.6 us (13%)
  blocking collectives  16.3 us (12%)
  local copies, waits for them, and re-layouts  3.64 us (3%)
  other arithmetic  3.08 us (2%)
    all_gather x1, blocking collectives, local(): gathered = lax.all_gather(part, 'rows', axis=0, tiled=False)  16.3 us
    all_to_all x1, waiting for transfers between devices, local(): pieces = lax.all_to_all(payload, 'rows', 0, 0)  12.1 us
    all_gather x1, waiting for transfers between devices, local(): everything = lax.all_gather(factor_blocks, 'samp', axis=0, tiled=False)  11.4 us
    all_to_all x1, starting transfers between devices, local(): pieces = lax.all_to_all(payload, 'rows', 0, 0)  9.99 us
    ppermute x1, waiting for transfers between devices, local(): above = lax.ppermute(mine, 'rows', [(i, i ^ 2) for i in range(RANKS)])  8.94 us
    pallas_call x1, Pallas kernels, update(): pl.pallas_call(update_kernel, grid=(rows // ROWS_PER_STEP,), out_shape=ja...  8.93 us
    ppermute x2, starting transfers between devices, around(): lax.ppermute(behind[SIDE // 2:], 'samp', shift(-1))  5.75 us
    pallas_call x1, Pallas kernels, solve(): pl.pallas_call(solve_kernel, out_shape=(jax.ShapeDtypeStruct((STEPS, BLOC...  5.5 us
  transfers between devices with their start and end apart: 18, of which 8 were waited for; matrix products, arithmetic and copies ran while one was open for 4% of the time, Pallas kernels for 6%

profile of v11, /device:TPU:1, one launch (start us, length us, event | category | flops | bytes accessed | tf_op | source)
XLA Modules:
  0.0 135.8 jit_solution(168344085430298390)
XLA Ops:
  7.2 0.0 all-gather.4.cloned.1.call-start
  7.2 0.7 all-gather.4.cloned.1.call-update
  7.9 0.0 copy-start.7
  7.9 3.2 %pack.1 = f32[16,80,128]{2,1,0:T(8,128)} custom-call(s32[8]{0:T(128)} %pivots.1, s32[6,36]{1,0:T(8,128)} %bitcast.72, f32[36,128,128]{2,1,0:T(8,128)} %sides.3, f32[36,6,8,128]{3,2,1,0:T(8,128)} %factor.1), custom_call_target="tpu_custom_call" | custom-call | tf_op jit(solution)/shard_map/pack/pallas_call | solution.py:90
  11.1 0.0 copy-start.6
  11.1 10.0 %all-to-all-start = ((f32[16,80,128]{2,1,0:T(8,128)}), f32[16,80,128]{2,1,0:T(8,128)S(1)}, u32[]{:S(2)}, u32[]{:S(2)}) async-start(f32[16,80,128]{2,1,0:T(8,128)} %pack.1), calls=%async_computation | async-start | bytes 1310720 | tf_op jit(solution)/shard_map/all_to_all | solution.py:204
  21.2 0.7 gather_fusion
  21.9 0.7 fusion.5
  25.2 0.6 dynamic_slice.21
  29.1 12.1 %all-to-all-done = f32[16,80,128]{2,1,0:T(8,128)S(1)} async-done(((f32[16,80,128]{2,1,0:T(8,128)}), f32[16,80,128]{2,1,0:T(8,128)S(1)}, u32[]{:S(2)}, u32[]{:S(2)}) %all-to-all-start) | async-done | bytes 655392 | tf_op jit(solution)/shard_map/all_to_all | solution.py:204
  41.2 16.3 %all-gather = f32[1280,128]{1,0:T(8,128)S(1)} all-gather(f32[80,128]{1,0:T(8,128)S(1)} %pad_maximum_fusion.3), channel_id=2, replica_groups=mesh['rows'=16,'samp'=16] {'rows'}, dimensions={0}, use_global_device_ids=true | all-gather | bytes 696320 | tf_op jit(solution)/shard_map/all_gather | solution.py:213
  57.5 3.0 %collective-permute-start.2 = (f32[4,8,128]{2,1,0:T(8,128)S(1)}, f32[4,8,128]{2,1,0:T(8,128)S(1)}, u32[]{:S(2)}, u32[]{:S(2)}) collective-permute-start(f32[4,8,128]{2,1,0:T(8,128)S(1)} %get-tuple-element.9), channel_id=1, source_target_pairs={{0,8},{1,9},{2,10},{3,11},{4,12},{5,13},{6,14},{7,15},{8,0},{9,1},... | collective-permute-start | bytes 49160 | tf_op jit(solution)/shard_map/ppermute | solution.py:218
  60.5 0.8 collective-permute-start.1
  61.3 0.7 collective-permute-start
  61.9 2.7 %collective-permute-start.9 = (f32[4,8,128]{2,1,0:T(8,128)S(1)}, f32[4,8,128]{2,1,0:T(8,128)S(1)}, u32[]{:S(2)}, u32[]{:S(2)}) collective-permute-start(f32[4,8,128]{2,1,0:T(8,128)S(1)} %get-tuple-element.8), channel_id=1, source_target_pairs={{0,2},{1,3},{2,0},{3,1},{4,6},{5,7},{6,4},{7,5},{8,10},{9,11},{10,... | collective-permute-start | bytes 49160 | tf_op jit(solution)/shard_map/ppermute | solution.py:219
  64.7 0.9 collective-permute-start.8
  65.6 0.6 collective-permute-start.7
  66.2 0.8 collective-permute-start.3
  67.0 1.9 %collective-permute-start.4 = (f32[4,4,8,128]{3,2,1,0:T(8,128)S(1)}, f32[4,4,8,128]{3,2,1,0:T(8,128)S(1)}, u32[]{:S(2)}, u32[]{:S(2)}) collective-permute-start(f32[4,4,8,128]{3,2,1,0:T(8,128)S(1)} %pad_maximum_fusion.1), channel_id=1, source_target_pairs={{0,3},{1,0},{2,1},{3,2},{4,7},{5,4},{6,5},{7,6},{8,11},{9,8},{10,9... | collective-permute-start | bytes 196616 | tf_op jit(solution)/shard_map/ppermute | solution.py:185
  68.9 1.1 collective-permute-done.7
  70.1 0.4 collective-permute-start.10
  70.5 2.3 %collective-permute-start.11 = (f32[4,4,8,128]{3,2,1,0:T(8,128)S(1)}, f32[4,4,8,128]{3,2,1,0:T(8,128)S(1)}, u32[]{:S(2)}, u32[]{:S(2)}) collective-permute-start(f32[4,4,8,128]{3,2,1,0:T(8,128)S(1)} %pad_maximum_fusion.2), channel_id=1, source_target_pairs={{0,12},{1,13},{2,14},{3,15},{4,0},{5,1},{6,2},{7,3},{8,4},{9,5},{1... | collective-permute-start | bytes 196616 | tf_op jit(solution)/shard_map/ppermute | solution.py:185
  72.8 2.3 %collective-permute-start.6 = (f32[2,4,8,128]{3,2,1,0:T(8,128)S(1)}, f32[2,4,8,128]{3,2,1,0:T(8,128)S(1)}, u32[]{:S(2)}, u32[]{:S(2)}) collective-permute-start(f32[2,4,8,128]{3,2,1,0:T(8,128)S(1)} %slice.32), channel_id=1, source_target_pairs={{0,3},{1,0},{2,1},{3,2},{4,7},{5,4},{6,5},{7,6},{8,11},{9,8},{10,9... | collective-permute-start | bytes 98312 | tf_op jit(solution)/shard_map/ppermute | solution.py:187
  75.1 0.3 collective-permute-done.11
  75.4 3.5 %collective-permute-start.13 = (f32[2,4,8,128]{3,2,1,0:T(8,128)S(1)}, f32[2,4,8,128]{3,2,1,0:T(8,128)S(1)}, u32[]{:S(2)}, u32[]{:S(2)}) collective-permute-start(f32[2,4,8,128]{3,2,1,0:T(8,128)S(1)} %slice.34), channel_id=1, source_target_pairs={{0,12},{1,13},{2,14},{3,15},{4,0},{5,1},{6,2},{7,3},{8,4},{9,5},{1... | collective-permute-start | bytes 98312 | tf_op jit(solution)/shard_map/ppermute | solution.py:187
  78.9 1.2 collective-permute-done.5
  80.1 0.3 collective-permute-done.13
  80.4 3.5 %collective-permute-done.12 = f32[2,4,8,128]{3,2,1,0:T(8,128)S(1)} collective-permute-done((f32[2,4,8,128]{3,2,1,0:T(8,128)S(1)}, f32[2,4,8,128]{3,2,1,0:T(8,128)S(1)}, u32[]{:S(2)}, u32[]{:S(2)}) %collective-permute-start.12) | collective-permute-done | bytes 32800 | tf_op jit(solution)/shard_map/ppermute | solution.py:187
  83.9 0.3 collective-permute-start.14
  84.3 8.9 %collective-permute-done.14.above = f32[2,4,4,4,8,128]{5,4,3,2,1,0:T(8,128)S(1)} collective-permute-done((f32[2,4,4,4,8,128]{5,4,3,2,1,0:T(8,128)S(1)}, f32[2,4,4,4,8,128]{5,4,3,2,1,0:T(8,128)S(1)}, u32[]{:S(2)}, u32[]{:S(2)}) %collective-permute-start.14) | collective-permute-done | bytes 524320 | tf_op jit(solution)/shard_map/ppermute | solution.py:223
  93.2 1.1 pad_maximum_fusion
  94.3 5.3 %collective-permute-start.15 = (f32[2,2,4,4,4,8,128]{6,5,4,3,2,1,0:T(8,128)}, f32[2,2,4,4,4,8,128]{6,5,4,3,2,1,0:T(8,128)S(1)}, u32[]{:S(2)}, u32[]{:S(2)}) collective-permute-start(f32[2,2,4,4,4,8,128]{6,5,4,3,2,1,0:T(8,128)} %pad_maximum_fusion), channel_id=1, source_target_pairs={{0,16},{16,0},{32,48},{48,32},{64,80},{80,64},{96,112},{112,96},{1... | collective-permute-start | bytes 3145736 | tf_op jit(solution)/shard_map/ppermute | solution.py:224
  99.7 0.1 copy.16
  99.8 0.1 add.140
  99.9 0.1 add.141
  99.9 0.1 add.143
  100.0 0.1 add.133
  100.1 0.1 add.137
  100.2 0.1 add.138
  100.3 0.6 pad_add_fusion.spots
  100.9 0.1 select_reduce_fusion
  100.9 0.5 xor_multiply_fusion.starts
  101.5 0.7 compare_select_fusion.picks
  102.2 0.0 collective-permute-done.15.far
  102.2 1.0 copy-done.3
  103.2 5.5 %solve.1 = (f32[8,128,128]{2,1,0:T(8,128)}, bf16[9,128,256]{2,1,0:T(8,128)(2,1)}) custom-call(s32[4]{0:T(128)} %xor_multiply_fusion.starts, s32[2,16]{1,0:T(2,128)} %pad_add_fusion.spots, f32[16,80,128]{2,1,0:T(8,128)} %bitcast.50, f32[2,4,4,4,8,128]{5,4,3,2,1,0:T(8,128)} %bitcast.53, f32[2,4,4,4,8,128]{5,4,3,2,1,0:T(8,128)} %copy-done.2, ...), custom_call_target="tpu_custom_call" | custom-call | tf_op jit(solution)/shard_map/solve/pallas_call | solution.py:132
  108.7 11.4 %all-gather.4.cloned.1.call-done = f32[576,6,8,128]{3,2,1,0:T(8,128)} async-done(((f32[36,6,8,128]{3,2,1,0:T(8,128)}), f32[576,6,8,128]{3,2,1,0:T(8,128)}) %all-gather.4.cloned.1.call-update) | async-done | bytes 14155792 | tf_op jit(solution)/shard_map/all_gather | solution.py:195
  120.0 8.9 %update.1 = f32[36,128,128]{2,1,0:T(8,128)} custom-call(s32[36,6]{1,0:T(8,128)} %compare_select_fusion.picks, f32[36,128,128]{2,1,0:T(8,128)} %sides.3, f32[16,36,6,8,128]{4,3,2,1,0:T(8,128)} %bitcast.48, bf16[9,128,256]{2,1,0:T(8,128)(2,1)} %get-tuple-element.5.pairs), custom_call_target="tpu_custom_call" | custom-call | tf_op jit(solution)/shard_map/update/pallas_call | solution.py:167
  (55 shorter events, 0.2 us)
Async XLA Ops:
  7.2 112.9 %all-gather.4.cloned.1.call-start = ((), (), s32[]{:S(2)}) async-start(), calls=%async_computation.1 | async-start | bytes 15040512 | tf_op jit(solution)/shard_map/all_gather | solution.py:195
  7.9 13.2 %copy-start.7 = (s32[32]{0:T(128)S(1)}, s32[32]{0:T(128)}, u32[]{:S(2)}) copy-start(s32[32]{0:T(128)} %constant.109) | copy-start | bytes 388
  7.9 13.2 %copy-start.5 = (s32[8]{0:T(128)S(1)}, s32[8]{0:T(128)}, u32[]{:S(2)}) copy-start(s32[8]{0:T(128)} %pivots.1) | copy-start | bytes 100
  11.1 73.1 %copy-start.6 = (s32[4]{0:T(128)S(1)}, s32[4]{0:T(128)}, u32[]{:S(2)}) copy-start(s32[4]{0:T(128)} %constant.104) | copy-start | bytes 52
  11.1 30.0 %all-to-all-start = ((f32[16,80,128]{2,1,0:T(8,128)}), f32[16,80,128]{2,1,0:T(8,128)S(1)}, u32[]{:S(2)}, u32[]{:S(2)}) async-start(f32[16,80,128]{2,1,0:T(8,128)} %pack.1), calls=%async_computation | async-start | bytes 1310720 | tf_op jit(solution)/shard_map/all_to_all | solution.py:204
  41.2 58.5 %copy-start.4 = (s32[36,6]{0,1:T(8,128)S(1)}, s32[36,6]{0,1:T(8,128)}, u32[]{:S(2)}) copy-start(s32[36,6]{0,1:T(8,128)} %param.10) | copy-start | bytes 2596
  41.2 59.8 %copy-start.8 = (s32[4]{0:T(128)S(1)}, s32[4]{0:T(128)}, u32[]{:S(2)}) copy-start(s32[4]{0:T(128)} %constant.99.clone) | copy-start | bytes 52
  57.4 44.7 %copy-start = (f32[1280,128]{1,0:T(8,128)}, f32[1280,128]{1,0:T(8,128)S(1)}, u32[]{:S(2)}) copy-start(f32[1280,128]{1,0:T(8,128)S(1)} %all-gather) | copy-start | bytes 1966084
  57.5 8.1 %collective-permute-start.2 = (f32[4,8,128]{2,1,0:T(8,128)S(1)}, f32[4,8,128]{2,1,0:T(8,128)S(1)}, u32[]{:S(2)}, u32[]{:S(2)}) collective-permute-start(f32[4,8,128]{2,1,0:T(8,128)S(1)} %get-tuple-element.9), channel_id=1, source_target_pairs={{0,8},{1,9},{2,10},{3,11},{4,12},{5,13},{6,14},{7,15},{8,0},{9,1},... | collective-permute-start | bytes 49160 | tf_op jit(solution)/shard_map/ppermute | solution.py:218
  60.5 5.7 %collective-permute-start.1 = (f32[4,8,128]{2,1,0:T(8,128)S(1)}, f32[4,8,128]{2,1,0:T(8,128)S(1)}, u32[]{:S(2)}, u32[]{:S(2)}) collective-permute-start(f32[4,8,128]{2,1,0:T(8,128)S(1)} %get-tuple-element.9), channel_id=1, source_target_pairs={{0,12},{1,13},{2,14},{3,15},{4,0},{5,1},{6,2},{7,3},{8,4},{9,5},{1... | collective-permute-start | bytes 49160 | tf_op jit(solution)/shard_map/ppermute | solution.py:218
  61.3 4.9 %collective-permute-start = (f32[4,8,128]{2,1,0:T(8,128)S(1)}, f32[4,8,128]{2,1,0:T(8,128)S(1)}, u32[]{:S(2)}, u32[]{:S(2)}) collective-permute-start(f32[4,8,128]{2,1,0:T(8,128)S(1)} %get-tuple-element.9), channel_id=1, source_target_pairs={{0,4},{1,5},{2,6},{3,7},{4,8},{5,9},{6,10},{7,11},{8,12},{9,13},{1... | collective-permute-start | bytes 49160 | tf_op jit(solution)/shard_map/ppermute | solution.py:218
  61.9 7.0 %collective-permute-start.9 = (f32[4,8,128]{2,1,0:T(8,128)S(1)}, f32[4,8,128]{2,1,0:T(8,128)S(1)}, u32[]{:S(2)}, u32[]{:S(2)}) collective-permute-start(f32[4,8,128]{2,1,0:T(8,128)S(1)} %get-tuple-element.8), channel_id=1, source_target_pairs={{0,2},{1,3},{2,0},{3,1},{4,6},{5,7},{6,4},{7,5},{8,10},{9,11},{10,... | collective-permute-start | bytes 49160 | tf_op jit(solution)/shard_map/ppermute | solution.py:219
  64.7 4.2 %collective-permute-start.8 = (f32[4,8,128]{2,1,0:T(8,128)S(1)}, f32[4,8,128]{2,1,0:T(8,128)S(1)}, u32[]{:S(2)}, u32[]{:S(2)}) collective-permute-start(f32[4,8,128]{2,1,0:T(8,128)S(1)} %get-tuple-element.8), channel_id=1, source_target_pairs={{0,3},{1,0},{2,1},{3,2},{4,7},{5,4},{6,5},{7,6},{8,11},{9,8},{10,9... | collective-permute-start | bytes 49160 | tf_op jit(solution)/shard_map/ppermute | solution.py:219
  65.6 4.5 %collective-permute-start.7 = (f32[4,8,128]{2,1,0:T(8,128)S(1)}, f32[4,8,128]{2,1,0:T(8,128)S(1)}, u32[]{:S(2)}, u32[]{:S(2)}) collective-permute-start(f32[4,8,128]{2,1,0:T(8,128)S(1)} %get-tuple-element.8), channel_id=1, source_target_pairs={{0,1},{1,2},{2,3},{3,0},{4,5},{5,6},{6,7},{7,4},{8,9},{9,10},{10,1... | collective-permute-start | bytes 49160 | tf_op jit(solution)/shard_map/ppermute | solution.py:219
  66.2 8.9 %collective-permute-start.3 = (f32[4,4,8,128]{3,2,1,0:T(8,128)S(1)}, f32[4,4,8,128]{3,2,1,0:T(8,128)S(1)}, u32[]{:S(2)}, u32[]{:S(2)}) collective-permute-start(f32[4,4,8,128]{3,2,1,0:T(8,128)S(1)} %pad_maximum_fusion.1), channel_id=1, source_target_pairs={{0,1},{1,2},{2,3},{3,0},{4,5},{5,6},{6,7},{7,4},{8,9},{9,10},{10,1... | collective-permute-start | bytes 196616 | tf_op jit(solution)/shard_map/ppermute | solution.py:184
  67.0 5.8 %collective-permute-start.4 = (f32[4,4,8,128]{3,2,1,0:T(8,128)S(1)}, f32[4,4,8,128]{3,2,1,0:T(8,128)S(1)}, u32[]{:S(2)}, u32[]{:S(2)}) collective-permute-start(f32[4,4,8,128]{3,2,1,0:T(8,128)S(1)} %pad_maximum_fusion.1), channel_id=1, source_target_pairs={{0,3},{1,0},{2,1},{3,2},{4,7},{5,4},{6,5},{7,6},{8,11},{9,8},{10,9... | collective-permute-start | bytes 196616 | tf_op jit(solution)/shard_map/ppermute | solution.py:185
  70.1 8.8 %collective-permute-start.10 = (f32[4,4,8,128]{3,2,1,0:T(8,128)S(1)}, f32[4,4,8,128]{3,2,1,0:T(8,128)S(1)}, u32[]{:S(2)}, u32[]{:S(2)}) collective-permute-start(f32[4,4,8,128]{3,2,1,0:T(8,128)S(1)} %pad_maximum_fusion.2), channel_id=1, source_target_pairs={{0,4},{1,5},{2,6},{3,7},{4,8},{5,9},{6,10},{7,11},{8,12},{9,13},{1... | collective-permute-start | bytes 196616 | tf_op jit(solution)/shard_map/ppermute | solution.py:184
  70.5 4.9 %collective-permute-start.11 = (f32[4,4,8,128]{3,2,1,0:T(8,128)S(1)}, f32[4,4,8,128]{3,2,1,0:T(8,128)S(1)}, u32[]{:S(2)}, u32[]{:S(2)}) collective-permute-start(f32[4,4,8,128]{3,2,1,0:T(8,128)S(1)} %pad_maximum_fusion.2), channel_id=1, source_target_pairs={{0,12},{1,13},{2,14},{3,15},{4,0},{5,1},{6,2},{7,3},{8,4},{9,5},{1... | collective-permute-start | bytes 196616 | tf_op jit(solution)/shard_map/ppermute | solution.py:185
  72.8 6.1 %collective-permute-start.6 = (f32[2,4,8,128]{3,2,1,0:T(8,128)S(1)}, f32[2,4,8,128]{3,2,1,0:T(8,128)S(1)}, u32[]{:S(2)}, u32[]{:S(2)}) collective-permute-start(f32[2,4,8,128]{3,2,1,0:T(8,128)S(1)} %slice.32), channel_id=1, source_target_pairs={{0,3},{1,0},{2,1},{3,2},{4,7},{5,4},{6,5},{7,6},{8,11},{9,8},{10,9... | collective-permute-start | bytes 98312 | tf_op jit(solution)/shard_map/ppermute | solution.py:187
  75.0 5.0 %collective-permute-start.5 = (f32[2,4,8,128]{3,2,1,0:T(8,128)S(1)}, f32[2,4,8,128]{3,2,1,0:T(8,128)S(1)}, u32[]{:S(2)}, u32[]{:S(2)}) collective-permute-start(f32[2,4,8,128]{3,2,1,0:T(8,128)S(1)} %slice.31), channel_id=1, source_target_pairs={{0,1},{1,2},{2,3},{3,0},{4,5},{5,6},{6,7},{7,4},{8,9},{9,10},{10,1... | collective-permute-start | bytes 98312 | tf_op jit(solution)/shard_map/ppermute | solution.py:187
  75.4 5.0 %collective-permute-start.13 = (f32[2,4,8,128]{3,2,1,0:T(8,128)S(1)}, f32[2,4,8,128]{3,2,1,0:T(8,128)S(1)}, u32[]{:S(2)}, u32[]{:S(2)}) collective-permute-start(f32[2,4,8,128]{3,2,1,0:T(8,128)S(1)} %slice.34), channel_id=1, source_target_pairs={{0,12},{1,13},{2,14},{3,15},{4,0},{5,1},{6,2},{7,3},{8,4},{9,5},{1... | collective-permute-start | bytes 98312 | tf_op jit(solution)/shard_map/ppermute | solution.py:187
  78.9 5.0 %collective-permute-start.12 = (f32[2,4,8,128]{3,2,1,0:T(8,128)S(1)}, f32[2,4,8,128]{3,2,1,0:T(8,128)S(1)}, u32[]{:S(2)}, u32[]{:S(2)}) collective-permute-start(f32[2,4,8,128]{3,2,1,0:T(8,128)S(1)} %slice.33), channel_id=1, source_target_pairs={{0,4},{1,5},{2,6},{3,7},{4,8},{5,9},{6,10},{7,11},{8,12},{9,13},{1... | collective-permute-start | bytes 98312 | tf_op jit(solution)/shard_map/ppermute | solution.py:187
  83.9 18.3 %copy-start.1 = (f32[8,4,4,8,128]{4,3,2,1,0:T(8,128)}, f32[8,4,4,8,128]{4,3,2,1,0:T(8,128)S(1)}, u32[]{:S(2)}) copy-start(f32[8,4,4,8,128]{4,3,2,1,0:T(8,128)S(1)} %fusion.1) | copy-start | bytes 1572868
  83.9 9.3 %collective-permute-start.14 = (f32[2,4,4,4,8,128]{5,4,3,2,1,0:T(8,128)S(1)}, f32[2,4,4,4,8,128]{5,4,3,2,1,0:T(8,128)S(1)}, u32[]{:S(2)}, u32[]{:S(2)}) collective-permute-start(f32[2,4,4,4,8,128]{5,4,3,2,1,0:T(8,128)S(1)} %bitcast.51), channel_id=1, source_target_pairs={{0,32},{16,48},{32,0},{48,16},{64,96},{80,112},{96,64},{112,80},{1... | collective-permute-start | bytes 1572872 | tf_op jit(solution)/shard_map/ppermute | solution.py:223
  93.2 9.0 %copy-start.2 = (f32[2,4,4,4,8,128]{5,4,3,2,1,0:T(8,128)}, f32[2,4,4,4,8,128]{5,4,3,2,1,0:T(8,128)S(1)}, u32[]{:S(2)}) copy-start(f32[2,4,4,4,8,128]{5,4,3,2,1,0:T(8,128)S(1)} %collective-permute-done.14.above) | copy-start | bytes 1572868
  94.3 7.8 %collective-permute-start.15 = (f32[2,2,4,4,4,8,128]{6,5,4,3,2,1,0:T(8,128)}, f32[2,2,4,4,4,8,128]{6,5,4,3,2,1,0:T(8,128)S(1)}, u32[]{:S(2)}, u32[]{:S(2)}) collective-permute-start(f32[2,2,4,4,4,8,128]{6,5,4,3,2,1,0:T(8,128)} %pad_maximum_fusion), channel_id=1, source_target_pairs={{0,16},{16,0},{32,48},{48,32},{64,80},{80,64},{96,112},{112,96},{1... | collective-permute-start | bytes 3145736 | tf_op jit(solution)/shard_map/ppermute | solution.py:224
  102.2 1.0 copy-start.3
Sparse Core Ops, SparseCore 0:
  10.4 109.5 all-gather.3

commit v12 on v11

--- a/solution.py
+++ b/solution.py
@@ -192,7 +192,8 @@
 def local(right_sides, factor_blocks, block_columns, pivot_rows, diag_inverse):
     row_count = right_sides.shape[0]
     rank = lax.axis_index("rows")
-    everything = lax.all_gather(factor_blocks, "samp", axis=0, tiled=False)
+    everything = lax.all_gather(factor_blocks.reshape(-1, BLOCK), "samp", axis=0, tiled=False)
+    everything = everything.reshape((RANKS,) + factor_blocks.shape)
 
     owner = pivot_rows // row_count
     ids = rank * row_count + jnp.arange(row_count, dtype=jnp.int32)

time: 136 us -> 136 us (level)
  no operation moved by 1% of the time
where the time goes in v12:
time: 136 us
  waiting for transfers between devices  39.5 us (29%)
  starting transfers between devices  35.5 us (26%)
  between operations  20.2 us (15%)
  Pallas kernels  17.6 us (13%)
  blocking collectives  16.3 us (12%)
  local copies, waits for them, and re-layouts  3.64 us (3%)
  other arithmetic  3.08 us (2%)
    all_gather x1, blocking collectives, local(): gathered = lax.all_gather(part, 'rows', axis=0, tiled=False)  16.3 us
    all_to_all x1, waiting for transfers between devices, local(): pieces = lax.all_to_all(payload, 'rows', 0, 0)  12.1 us
    all_gather x1, waiting for transfers between devices, local(): lax.all_gather(factor_blocks.reshape(-1, BLOCK), 'samp', axis=0, tiled=Fa...  11.4 us
    all_to_all x1, starting transfers between devices, local(): pieces = lax.all_to_all(payload, 'rows', 0, 0)  9.99 us
    ppermute x1, waiting for transfers between devices, local(): above = lax.ppermute(mine, 'rows', [(i, i ^ 2) for i in range(RANKS)])  8.94 us
    pallas_call x1, Pallas kernels, update(): pl.pallas_call(update_kernel, grid=(rows // ROWS_PER_STEP,), out_shape=ja...  8.93 us
    ppermute x2, starting transfers between devices, around(): lax.ppermute(behind[SIDE // 2:], 'samp', shift(-1))  5.75 us
    pallas_call x1, Pallas kernels, solve(): pl.pallas_call(solve_kernel, out_shape=(jax.ShapeDtypeStruct((STEPS, BLOC...  5.5 us
  transfers between devices with their start and end apart: 18, of which 8 were waited for; matrix products, arithmetic and copies ran while one was open for 4% of the time, Pallas kernels for 6%

profile of v12, /device:TPU:1, one launch (start us, length us, event | category | flops | bytes accessed | tf_op | source)
XLA Modules:
  0.0 135.8 jit_solution(168344085430298390)
XLA Ops:
  7.2 0.0 all-gather.3.cloned.1.call-start
  7.2 0.7 all-gather.3.cloned.1.call-update
  7.9 0.0 copy-start.7
  7.9 3.2 %pack.1 = f32[16,80,128]{2,1,0:T(8,128)} custom-call(s32[8]{0:T(128)} %pivots.1, s32[6,36]{1,0:T(8,128)} %bitcast.74, f32[36,128,128]{2,1,0:T(8,128)} %sides.3, f32[36,6,8,128]{3,2,1,0:T(8,128)} %factor.1), custom_call_target="tpu_custom_call" | custom-call | tf_op jit(solution)/shard_map/pack/pallas_call | solution.py:90
  11.1 0.0 copy-start.6
  11.1 10.0 %all-to-all-start = ((f32[16,80,128]{2,1,0:T(8,128)}), f32[16,80,128]{2,1,0:T(8,128)S(1)}, u32[]{:S(2)}, u32[]{:S(2)}) async-start(f32[16,80,128]{2,1,0:T(8,128)} %pack.1), calls=%async_computation | async-start | bytes 1310720 | tf_op jit(solution)/shard_map/all_to_all | solution.py:205
  21.2 0.7 gather_fusion
  21.9 0.7 fusion.5
  25.2 0.6 dynamic_slice.21
  29.1 12.1 %all-to-all-done = f32[16,80,128]{2,1,0:T(8,128)S(1)} async-done(((f32[16,80,128]{2,1,0:T(8,128)}), f32[16,80,128]{2,1,0:T(8,128)S(1)}, u32[]{:S(2)}, u32[]{:S(2)}) %all-to-all-start) | async-done | bytes 655392 | tf_op jit(solution)/shard_map/all_to_all | solution.py:205
  41.2 16.3 %all-gather = f32[1280,128]{1,0:T(8,128)S(1)} all-gather(f32[80,128]{1,0:T(8,128)S(1)} %pad_maximum_fusion.3), channel_id=2, replica_groups=mesh['rows'=16,'samp'=16] {'rows'}, dimensions={0}, use_global_device_ids=true | all-gather | bytes 696320 | tf_op jit(solution)/shard_map/all_gather | solution.py:214
  57.5 3.0 %collective-permute-start.2 = (f32[4,8,128]{2,1,0:T(8,128)S(1)}, f32[4,8,128]{2,1,0:T(8,128)S(1)}, u32[]{:S(2)}, u32[]{:S(2)}) collective-permute-start(f32[4,8,128]{2,1,0:T(8,128)S(1)} %get-tuple-element.9), channel_id=1, source_target_pairs={{0,8},{1,9},{2,10},{3,11},{4,12},{5,13},{6,14},{7,15},{8,0},{9,1},... | collective-permute-start | bytes 49160 | tf_op jit(solution)/shard_map/ppermute | solution.py:219
  60.5 0.8 collective-permute-start.1
  61.3 0.7 collective-permute-start
  61.9 2.7 %collective-permute-start.9 = (f32[4,8,128]{2,1,0:T(8,128)S(1)}, f32[4,8,128]{2,1,0:T(8,128)S(1)}, u32[]{:S(2)}, u32[]{:S(2)}) collective-permute-start(f32[4,8,128]{2,1,0:T(8,128)S(1)} %get-tuple-element.8), channel_id=1, source_target_pairs={{0,2},{1,3},{2,0},{3,1},{4,6},{5,7},{6,4},{7,5},{8,10},{9,11},{10,... | collective-permute-start | bytes 49160 | tf_op jit(solution)/shard_map/ppermute | solution.py:220
  64.7 0.9 collective-permute-start.8
  65.6 0.6 collective-permute-start.7
  66.2 0.8 collective-permute-start.3
  67.0 1.9 %collective-permute-start.4 = (f32[4,4,8,128]{3,2,1,0:T(8,128)S(1)}, f32[4,4,8,128]{3,2,1,0:T(8,128)S(1)}, u32[]{:S(2)}, u32[]{:S(2)}) collective-permute-start(f32[4,4,8,128]{3,2,1,0:T(8,128)S(1)} %pad_maximum_fusion.1), channel_id=1, source_target_pairs={{0,3},{1,0},{2,1},{3,2},{4,7},{5,4},{6,5},{7,6},{8,11},{9,8},{10,9... | collective-permute-start | bytes 196616 | tf_op jit(solution)/shard_map/ppermute | solution.py:185
  68.9 1.1 collective-permute-done.7
  70.1 0.4 collective-permute-start.10
  70.5 2.3 %collective-permute-start.11 = (f32[4,4,8,128]{3,2,1,0:T(8,128)S(1)}, f32[4,4,8,128]{3,2,1,0:T(8,128)S(1)}, u32[]{:S(2)}, u32[]{:S(2)}) collective-permute-start(f32[4,4,8,128]{3,2,1,0:T(8,128)S(1)} %pad_maximum_fusion.2), channel_id=1, source_target_pairs={{0,12},{1,13},{2,14},{3,15},{4,0},{5,1},{6,2},{7,3},{8,4},{9,5},{1... | collective-permute-start | bytes 196616 | tf_op jit(solution)/shard_map/ppermute | solution.py:185
  72.8 2.3 %collective-permute-start.6 = (f32[2,4,8,128]{3,2,1,0:T(8,128)S(1)}, f32[2,4,8,128]{3,2,1,0:T(8,128)S(1)}, u32[]{:S(2)}, u32[]{:S(2)}) collective-permute-start(f32[2,4,8,128]{3,2,1,0:T(8,128)S(1)} %slice.32), channel_id=1, source_target_pairs={{0,3},{1,0},{2,1},{3,2},{4,7},{5,4},{6,5},{7,6},{8,11},{9,8},{10,9... | collective-permute-start | bytes 98312 | tf_op jit(solution)/shard_map/ppermute | solution.py:187
  75.1 0.3 collective-permute-done.11
  75.4 3.5 %collective-permute-start.13 = (f32[2,4,8,128]{3,2,1,0:T(8,128)S(1)}, f32[2,4,8,128]{3,2,1,0:T(8,128)S(1)}, u32[]{:S(2)}, u32[]{:S(2)}) collective-permute-start(f32[2,4,8,128]{3,2,1,0:T(8,128)S(1)} %slice.34), channel_id=1, source_target_pairs={{0,12},{1,13},{2,14},{3,15},{4,0},{5,1},{6,2},{7,3},{8,4},{9,5},{1... | collective-permute-start | bytes 98312 | tf_op jit(solution)/shard_map/ppermute | solution.py:187
  78.9 1.2 collective-permute-done.5
  80.1 0.3 collective-permute-done.13
  80.4 3.5 %collective-permute-done.12 = f32[2,4,8,128]{3,2,1,0:T(8,128)S(1)} collective-permute-done((f32[2,4,8,128]{3,2,1,0:T(8,128)S(1)}, f32[2,4,8,128]{3,2,1,0:T(8,128)S(1)}, u32[]{:S(2)}, u32[]{:S(2)}) %collective-permute-start.12) | collective-permute-done | bytes 32800 | tf_op jit(solution)/shard_map/ppermute | solution.py:187
  83.9 0.3 collective-permute-start.14
  84.3 8.9 %collective-permute-done.14.above = f32[2,4,4,4,8,128]{5,4,3,2,1,0:T(8,128)S(1)} collective-permute-done((f32[2,4,4,4,8,128]{5,4,3,2,1,0:T(8,128)S(1)}, f32[2,4,4,4,8,128]{5,4,3,2,1,0:T(8,128)S(1)}, u32[]{:S(2)}, u32[]{:S(2)}) %collective-permute-start.14) | collective-permute-done | bytes 524320 | tf_op jit(solution)/shard_map/ppermute | solution.py:224
  93.2 1.1 pad_maximum_fusion
  94.3 5.3 %collective-permute-start.15 = (f32[2,2,4,4,4,8,128]{6,5,4,3,2,1,0:T(8,128)}, f32[2,2,4,4,4,8,128]{6,5,4,3,2,1,0:T(8,128)S(1)}, u32[]{:S(2)}, u32[]{:S(2)}) collective-permute-start(f32[2,2,4,4,4,8,128]{6,5,4,3,2,1,0:T(8,128)} %pad_maximum_fusion), channel_id=1, source_target_pairs={{0,16},{16,0},{32,48},{48,32},{64,80},{80,64},{96,112},{112,96},{1... | collective-permute-start | bytes 3145736 | tf_op jit(solution)/shard_map/ppermute | solution.py:225
  99.7 0.1 copy.16
  99.8 0.1 add.140
  99.9 0.1 add.141
  99.9 0.1 add.143
  100.0 0.1 add.133
  100.1 0.1 add.137
  100.2 0.1 add.138
  100.3 0.6 pad_add_fusion.spots
  100.9 0.1 select_reduce_fusion
  100.9 0.5 xor_multiply_fusion.starts
  101.5 0.7 compare_select_fusion.picks
  102.2 0.0 collective-permute-done.15.far
  102.2 1.0 copy-done.3
  103.2 5.5 %solve.1 = (f32[8,128,128]{2,1,0:T(8,128)}, bf16[9,128,256]{2,1,0:T(8,128)(2,1)}) custom-call(s32[4]{0:T(128)} %xor_multiply_fusion.starts, s32[2,16]{1,0:T(2,128)} %pad_add_fusion.spots, f32[16,80,128]{2,1,0:T(8,128)} %bitcast.52, f32[2,4,4,4,8,128]{5,4,3,2,1,0:T(8,128)} %bitcast.55, f32[2,4,4,4,8,128]{5,4,3,2,1,0:T(8,128)} %copy-done.2, ...), custom_call_target="tpu_custom_call" | custom-call | tf_op jit(solution)/shard_map/solve/pallas_call | solution.py:132
  108.7 11.4 %all-gather.3.cloned.1.call-done = f32[16,1728,128]{2,1,0:T(8,128)} async-done(((f32[1,1728,128]{2,1,0:T(8,128)}), f32[16,1728,128]{2,1,0:T(8,128)}) %all-gather.3.cloned.1.call-update) | async-done | bytes 14155792 | tf_op jit(solution)/shard_map/all_gather | solution.py:195
  120.0 8.9 %update.1 = f32[36,128,128]{2,1,0:T(8,128)} custom-call(s32[36,6]{1,0:T(8,128)} %compare_select_fusion.picks, f32[36,128,128]{2,1,0:T(8,128)} %sides.3, f32[16,36,6,8,128]{4,3,2,1,0:T(8,128)} %bitcast.49, bf16[9,128,256]{2,1,0:T(8,128)(2,1)} %get-tuple-element.5.pairs), custom_call_target="tpu_custom_call" | custom-call | tf_op jit(solution)/shard_map/update/pallas_call | solution.py:167
  (55 shorter events, 0.2 us)
Async XLA Ops:
  7.2 112.9 %all-gather.3.cloned.1.call-start = ((), (), s32[]{:S(2)}) async-start(), calls=%async_computation.1 | async-start | bytes 15040512 | tf_op jit(solution)/shard_map/all_gather | solution.py:195
  7.9 13.2 %copy-start.7 = (s32[32]{0:T(128)S(1)}, s32[32]{0:T(128)}, u32[]{:S(2)}) copy-start(s32[32]{0:T(128)} %constant.109) | copy-start | bytes 388
  7.9 13.2 %copy-start.5 = (s32[8]{0:T(128)S(1)}, s32[8]{0:T(128)}, u32[]{:S(2)}) copy-start(s32[8]{0:T(128)} %pivots.1) | copy-start | bytes 100
  11.1 73.1 %copy-start.6 = (s32[4]{0:T(128)S(1)}, s32[4]{0:T(128)}, u32[]{:S(2)}) copy-start(s32[4]{0:T(128)} %constant.104) | copy-start | bytes 52
  11.1 30.0 %all-to-all-start = ((f32[16,80,128]{2,1,0:T(8,128)}), f32[16,80,128]{2,1,0:T(8,128)S(1)}, u32[]{:S(2)}, u32[]{:S(2)}) async-start(f32[16,80,128]{2,1,0:T(8,128)} %pack.1), calls=%async_computation | async-start | bytes 1310720 | tf_op jit(solution)/shard_map/all_to_all | solution.py:205
  41.2 58.5 %copy-start.4 = (s32[36,6]{0,1:T(8,128)S(1)}, s32[36,6]{0,1:T(8,128)}, u32[]{:S(2)}) copy-start(s32[36,6]{0,1:T(8,128)} %param.10) | copy-start | bytes 2596
  41.2 59.8 %copy-start.8 = (s32[4]{0:T(128)S(1)}, s32[4]{0:T(128)}, u32[]{:S(2)}) copy-start(s32[4]{0:T(128)} %constant.99.clone) | copy-start | bytes 52
  57.4 44.7 %copy-start = (f32[1280,128]{1,0:T(8,128)}, f32[1280,128]{1,0:T(8,128)S(1)}, u32[]{:S(2)}) copy-start(f32[1280,128]{1,0:T(8,128)S(1)} %all-gather) | copy-start | bytes 1966084
  57.5 8.1 %collective-permute-start.2 = (f32[4,8,128]{2,1,0:T(8,128)S(1)}, f32[4,8,128]{2,1,0:T(8,128)S(1)}, u32[]{:S(2)}, u32[]{:S(2)}) collective-permute-start(f32[4,8,128]{2,1,0:T(8,128)S(1)} %get-tuple-element.9), channel_id=1, source_target_pairs={{0,8},{1,9},{2,10},{3,11},{4,12},{5,13},{6,14},{7,15},{8,0},{9,1},... | collective-permute-start | bytes 49160 | tf_op jit(solution)/shard_map/ppermute | solution.py:219
  60.5 5.7 %collective-permute-start.1 = (f32[4,8,128]{2,1,0:T(8,128)S(1)}, f32[4,8,128]{2,1,0:T(8,128)S(1)}, u32[]{:S(2)}, u32[]{:S(2)}) collective-permute-start(f32[4,8,128]{2,1,0:T(8,128)S(1)} %get-tuple-element.9), channel_id=1, source_target_pairs={{0,12},{1,13},{2,14},{3,15},{4,0},{5,1},{6,2},{7,3},{8,4},{9,5},{1... | collective-permute-start | bytes 49160 | tf_op jit(solution)/shard_map/ppermute | solution.py:219
  61.3 4.9 %collective-permute-start = (f32[4,8,128]{2,1,0:T(8,128)S(1)}, f32[4,8,128]{2,1,0:T(8,128)S(1)}, u32[]{:S(2)}, u32[]{:S(2)}) collective-permute-start(f32[4,8,128]{2,1,0:T(8,128)S(1)} %get-tuple-element.9), channel_id=1, source_target_pairs={{0,4},{1,5},{2,6},{3,7},{4,8},{5,9},{6,10},{7,11},{8,12},{9,13},{1... | collective-permute-start | bytes 49160 | tf_op jit(solution)/shard_map/ppermute | solution.py:219
  61.9 7.0 %collective-permute-start.9 = (f32[4,8,128]{2,1,0:T(8,128)S(1)}, f32[4,8,128]{2,1,0:T(8,128)S(1)}, u32[]{:S(2)}, u32[]{:S(2)}) collective-permute-start(f32[4,8,128]{2,1,0:T(8,128)S(1)} %get-tuple-element.8), channel_id=1, source_target_pairs={{0,2},{1,3},{2,0},{3,1},{4,6},{5,7},{6,4},{7,5},{8,10},{9,11},{10,... | collective-permute-start | bytes 49160 | tf_op jit(solution)/shard_map/ppermute | solution.py:220
  64.7 4.2 %collective-permute-start.8 = (f32[4,8,128]{2,1,0:T(8,128)S(1)}, f32[4,8,128]{2,1,0:T(8,128)S(1)}, u32[]{:S(2)}, u32[]{:S(2)}) collective-permute-start(f32[4,8,128]{2,1,0:T(8,128)S(1)} %get-tuple-element.8), channel_id=1, source_target_pairs={{0,3},{1,0},{2,1},{3,2},{4,7},{5,4},{6,5},{7,6},{8,11},{9,8},{10,9... | collective-permute-start | bytes 49160 | tf_op jit(solution)/shard_map/ppermute | solution.py:220
  65.6 4.5 %collective-permute-start.7 = (f32[4,8,128]{2,1,0:T(8,128)S(1)}, f32[4,8,128]{2,1,0:T(8,128)S(1)}, u32[]{:S(2)}, u32[]{:S(2)}) collective-permute-start(f32[4,8,128]{2,1,0:T(8,128)S(1)} %get-tuple-element.8), channel_id=1, source_target_pairs={{0,1},{1,2},{2,3},{3,0},{4,5},{5,6},{6,7},{7,4},{8,9},{9,10},{10,1... | collective-permute-start | bytes 49160 | tf_op jit(solution)/shard_map/ppermute | solution.py:220
  66.2 8.9 %collective-permute-start.3 = (f32[4,4,8,128]{3,2,1,0:T(8,128)S(1)}, f32[4,4,8,128]{3,2,1,0:T(8,128)S(1)}, u32[]{:S(2)}, u32[]{:S(2)}) collective-permute-start(f32[4,4,8,128]{3,2,1,0:T(8,128)S(1)} %pad_maximum_fusion.1), channel_id=1, source_target_pairs={{0,1},{1,2},{2,3},{3,0},{4,5},{5,6},{6,7},{7,4},{8,9},{9,10},{10,1... | collective-permute-start | bytes 196616 | tf_op jit(solution)/shard_map/ppermute | solution.py:184
  67.0 5.8 %collective-permute-start.4 = (f32[4,4,8,128]{3,2,1,0:T(8,128)S(1)}, f32[4,4,8,128]{3,2,1,0:T(8,128)S(1)}, u32[]{:S(2)}, u32[]{:S(2)}) collective-permute-start(f32[4,4,8,128]{3,2,1,0:T(8,128)S(1)} %pad_maximum_fusion.1), channel_id=1, source_target_pairs={{0,3},{1,0},{2,1},{3,2},{4,7},{5,4},{6,5},{7,6},{8,11},{9,8},{10,9... | collective-permute-start | bytes 196616 | tf_op jit(solution)/shard_map/ppermute | solution.py:185
  70.1 8.8 %collective-permute-start.10 = (f32[4,4,8,128]{3,2,1,0:T(8,128)S(1)}, f32[4,4,8,128]{3,2,1,0:T(8,128)S(1)}, u32[]{:S(2)}, u32[]{:S(2)}) collective-permute-start(f32[4,4,8,128]{3,2,1,0:T(8,128)S(1)} %pad_maximum_fusion.2), channel_id=1, source_target_pairs={{0,4},{1,5},{2,6},{3,7},{4,8},{5,9},{6,10},{7,11},{8,12},{9,13},{1... | collective-permute-start | bytes 196616 | tf_op jit(solution)/shard_map/ppermute | solution.py:184
  70.5 4.9 %collective-permute-start.11 = (f32[4,4,8,128]{3,2,1,0:T(8,128)S(1)}, f32[4,4,8,128]{3,2,1,0:T(8,128)S(1)}, u32[]{:S(2)}, u32[]{:S(2)}) collective-permute-start(f32[4,4,8,128]{3,2,1,0:T(8,128)S(1)} %pad_maximum_fusion.2), channel_id=1, source_target_pairs={{0,12},{1,13},{2,14},{3,15},{4,0},{5,1},{6,2},{7,3},{8,4},{9,5},{1... | collective-permute-start | bytes 196616 | tf_op jit(solution)/shard_map/ppermute | solution.py:185
  72.8 6.1 %collective-permute-start.6 = (f32[2,4,8,128]{3,2,1,0:T(8,128)S(1)}, f32[2,4,8,128]{3,2,1,0:T(8,128)S(1)}, u32[]{:S(2)}, u32[]{:S(2)}) collective-permute-start(f32[2,4,8,128]{3,2,1,0:T(8,128)S(1)} %slice.32), channel_id=1, source_target_pairs={{0,3},{1,0},{2,1},{3,2},{4,7},{5,4},{6,5},{7,6},{8,11},{9,8},{10,9... | collective-permute-start | bytes 98312 | tf_op jit(solution)/shard_map/ppermute | solution.py:187
  75.0 5.0 %collective-permute-start.5 = (f32[2,4,8,128]{3,2,1,0:T(8,128)S(1)}, f32[2,4,8,128]{3,2,1,0:T(8,128)S(1)}, u32[]{:S(2)}, u32[]{:S(2)}) collective-permute-start(f32[2,4,8,128]{3,2,1,0:T(8,128)S(1)} %slice.31), channel_id=1, source_target_pairs={{0,1},{1,2},{2,3},{3,0},{4,5},{5,6},{6,7},{7,4},{8,9},{9,10},{10,1... | collective-permute-start | bytes 98312 | tf_op jit(solution)/shard_map/ppermute | solution.py:187
  75.4 5.0 %collective-permute-start.13 = (f32[2,4,8,128]{3,2,1,0:T(8,128)S(1)}, f32[2,4,8,128]{3,2,1,0:T(8,128)S(1)}, u32[]{:S(2)}, u32[]{:S(2)}) collective-permute-start(f32[2,4,8,128]{3,2,1,0:T(8,128)S(1)} %slice.34), channel_id=1, source_target_pairs={{0,12},{1,13},{2,14},{3,15},{4,0},{5,1},{6,2},{7,3},{8,4},{9,5},{1... | collective-permute-start | bytes 98312 | tf_op jit(solution)/shard_map/ppermute | solution.py:187
  78.9 5.0 %collective-permute-start.12 = (f32[2,4,8,128]{3,2,1,0:T(8,128)S(1)}, f32[2,4,8,128]{3,2,1,0:T(8,128)S(1)}, u32[]{:S(2)}, u32[]{:S(2)}) collective-permute-start(f32[2,4,8,128]{3,2,1,0:T(8,128)S(1)} %slice.33), channel_id=1, source_target_pairs={{0,4},{1,5},{2,6},{3,7},{4,8},{5,9},{6,10},{7,11},{8,12},{9,13},{1... | collective-permute-start | bytes 98312 | tf_op jit(solution)/shard_map/ppermute | solution.py:187
  83.9 18.3 %copy-start.1 = (f32[8,4,4,8,128]{4,3,2,1,0:T(8,128)}, f32[8,4,4,8,128]{4,3,2,1,0:T(8,128)S(1)}, u32[]{:S(2)}) copy-start(f32[8,4,4,8,128]{4,3,2,1,0:T(8,128)S(1)} %fusion.1) | copy-start | bytes 1572868
  83.9 9.3 %collective-permute-start.14 = (f32[2,4,4,4,8,128]{5,4,3,2,1,0:T(8,128)S(1)}, f32[2,4,4,4,8,128]{5,4,3,2,1,0:T(8,128)S(1)}, u32[]{:S(2)}, u32[]{:S(2)}) collective-permute-start(f32[2,4,4,4,8,128]{5,4,3,2,1,0:T(8,128)S(1)} %bitcast.53), channel_id=1, source_target_pairs={{0,32},{16,48},{32,0},{48,16},{64,96},{80,112},{96,64},{112,80},{1... | collective-permute-start | bytes 1572872 | tf_op jit(solution)/shard_map/ppermute | solution.py:224
  93.2 9.0 %copy-start.2 = (f32[2,4,4,4,8,128]{5,4,3,2,1,0:T(8,128)}, f32[2,4,4,4,8,128]{5,4,3,2,1,0:T(8,128)S(1)}, u32[]{:S(2)}) copy-start(f32[2,4,4,4,8,128]{5,4,3,2,1,0:T(8,128)S(1)} %collective-permute-done.14.above) | copy-start | bytes 1572868
  94.3 7.8 %collective-permute-start.15 = (f32[2,2,4,4,4,8,128]{6,5,4,3,2,1,0:T(8,128)}, f32[2,2,4,4,4,8,128]{6,5,4,3,2,1,0:T(8,128)S(1)}, u32[]{:S(2)}, u32[]{:S(2)}) collective-permute-start(f32[2,2,4,4,4,8,128]{6,5,4,3,2,1,0:T(8,128)} %pad_maximum_fusion), channel_id=1, source_target_pairs={{0,16},{16,0},{32,48},{48,32},{64,80},{80,64},{96,112},{112,96},{1... | collective-permute-start | bytes 3145736 | tf_op jit(solution)/shard_map/ppermute | solution.py:225
  102.2 1.0 copy-start.3
Sparse Core Ops, SparseCore 0:
  10.4 109.5 all-gather.2

commit v13 on v12

--- a/solution.py
+++ b/solution.py
@@ -216,8 +216,7 @@
     quarter = rank % 4
     half = lax.dynamic_slice(slices, (quarter * 2 * PART, 0, 0), (2 * PART, SLICE, BLOCK))
     first, second = half[:PART], half[PART:]
-    first = [first] + [lax.ppermute(first, "samp", shift_y(d)) for d in MOVES]
-    second = [second] + [lax.ppermute(second, "samp", shift_x(d)) for d in MOVES]
+    first, second = around(first, shift_y), around(second, shift_x)
     first, second = jnp.stack(first), jnp.stack(second)
     parts = around(first, shift_x) + around(second, shift_y)
     mine = jnp.stack(parts).reshape(2, SIDE, SIDE, PART, SLICE, BLOCK)

time: 136 us -> 136 us (level)
  waiting for transfers between devices: 39.5 us -> 36.6 us
  starting transfers between devices: 35.5 us -> 37.9 us
    ppermute x6 -> x0, starting transfers between devices: 8.68 us -> none  [the longest x3 4.47 us: local(): first = [first] + [lax.ppermute(first, 'samp', shift_y(d)) for d in MOVES]]
    ppermute x2 -> x4, starting transfers between devices: 4.21 us -> 10.1 us  [around(): behind = lax.ppermute(block, 'samp', shift(-1))]
    ppermute x2 -> x4, starting transfers between devices: 5.75 us -> 11.5 us  [around(): lax.ppermute(behind[SIDE // 2:], 'samp', shift(-1))]
    all_gather x1, waiting for transfers between devices: 11.4 us -> 8.74 us  [local(): lax.all_gather(factor_blocks.reshape(-1, BLOCK), 'samp', axis=0, tiled=Fa...]
    ppermute x2 -> x4, waiting for transfers between devices: 4.69 us -> 6.48 us  [around(): lax.ppermute(ahead[:SIDE // 2], 'samp', shift(1))]
  transfers between devices with their start and end apart: 18 -> 20, of which waited for: 8 -> 6; matrix products, arithmetic and copies ran while one was open for 4% -> 4% of each run, Pallas kernels for 6% -> 6%
where the time goes in v13:
time: 136 us
  starting transfers between devices  37.9 us (28%)
  waiting for transfers between devices  36.6 us (27%)
  between operations  20.5 us (15%)
  Pallas kernels  17.6 us (13%)
  blocking collectives  16.3 us (12%)
  local copies, waits for them, and re-layouts  3.71 us (3%)
  other arithmetic  3.16 us (2%)
    all_gather x1, blocking collectives, local(): gathered = lax.all_gather(part, 'rows', axis=0, tiled=False)  16.3 us
    all_to_all x1, waiting for transfers between devices, local(): pieces = lax.all_to_all(payload, 'rows', 0, 0)  11.8 us
    ppermute x4, starting transfers between devices, around(): lax.ppermute(behind[SIDE // 2:], 'samp', shift(-1))  11.5 us
    ppermute x4, starting transfers between devices, around(): behind = lax.ppermute(block, 'samp', shift(-1))  10.1 us
    all_to_all x1, starting transfers between devices, local(): pieces = lax.all_to_all(payload, 'rows', 0, 0)  9.99 us
    pallas_call x1, Pallas kernels, update(): pl.pallas_call(update_kernel, grid=(rows // ROWS_PER_STEP,), out_shape=ja...  8.93 us
    ppermute x1, waiting for transfers between devices, local(): above = lax.ppermute(mine, 'rows', [(i, i ^ 2) for i in range(RANKS)])  8.8 us
    all_gather x1, waiting for transfers between devices, local(): lax.all_gather(factor_blocks.reshape(-1, BLOCK), 'samp', axis=0, tiled=Fa...  8.74 us
  transfers between devices with their start and end apart: 20, of which 6 were waited for; matrix products, arithmetic and copies ran while one was open for 4% of the time, Pallas kernels for 6%

profile of v13, /device:TPU:1, one launch (start us, length us, event | category | flops | bytes accessed | tf_op | source)
XLA Modules:
  0.0 135.6 jit_solution(6968065594621798696)
XLA Ops:
  7.2 0.0 all-gather.3.cloned.1.call-start
  7.2 0.7 all-gather.3.cloned.1.call-update
  7.9 0.0 copy-start.7
  7.9 3.2 %pack.1 = f32[16,80,128]{2,1,0:T(8,128)} custom-call(s32[8]{0:T(128)} %pivots.1, s32[6,36]{1,0:T(8,128)} %bitcast.72, f32[36,128,128]{2,1,0:T(8,128)} %sides.3, f32[36,6,8,128]{3,2,1,0:T(8,128)} %factor.1), custom_call_target="tpu_custom_call" | custom-call | tf_op jit(solution)/shard_map/pack/pallas_call | solution.py:90
  11.1 0.0 copy-start.6
  11.1 10.0 %all-to-all-start = ((f32[16,80,128]{2,1,0:T(8,128)}), f32[16,80,128]{2,1,0:T(8,128)S(1)}, u32[]{:S(2)}, u32[]{:S(2)}) async-start(f32[16,80,128]{2,1,0:T(8,128)} %pack.1), calls=%async_computation | async-start | bytes 1310720 | tf_op jit(solution)/shard_map/all_to_all | solution.py:205
  21.2 0.7 gather_fusion
  21.9 0.7 fusion.5
  25.2 0.7 dynamic_slice.21
  29.3 11.8 %all-to-all-done = f32[16,80,128]{2,1,0:T(8,128)S(1)} async-done(((f32[16,80,128]{2,1,0:T(8,128)}), f32[16,80,128]{2,1,0:T(8,128)S(1)}, u32[]{:S(2)}, u32[]{:S(2)}) %all-to-all-start) | async-done | bytes 655392 | tf_op jit(solution)/shard_map/all_to_all | solution.py:205
  41.2 0.0 copy-start.4
  41.2 0.0 copy-start.8
  41.2 16.3 %all-gather = f32[1280,128]{1,0:T(8,128)S(1)} all-gather(f32[80,128]{1,0:T(8,128)S(1)} %pad_maximum_fusion.3), channel_id=2, replica_groups=mesh['rows'=16,'samp'=16] {'rows'}, dimensions={0}, use_global_device_ids=true | all-gather | bytes 696320 | tf_op jit(solution)/shard_map/all_gather | solution.py:214
  57.5 2.8 %collective-permute-start.1 = (f32[4,8,128]{2,1,0:T(8,128)S(1)}, f32[4,8,128]{2,1,0:T(8,128)S(1)}, u32[]{:S(2)}, u32[]{:S(2)}) collective-permute-start(f32[4,8,128]{2,1,0:T(8,128)S(1)} %get-tuple-element.9), channel_id=1, source_target_pairs={{0,12},{1,13},{2,14},{3,15},{4,0},{5,1},{6,2},{7,3},{8,4},{9,5},{1... | collective-permute-start | bytes 49160 | tf_op jit(solution)/shard_map/ppermute | solution.py:185
  60.3 0.0 collective-permute-start
  60.3 2.5 %collective-permute-start.9 = (f32[4,8,128]{2,1,0:T(8,128)S(1)}, f32[4,8,128]{2,1,0:T(8,128)S(1)}, u32[]{:S(2)}, u32[]{:S(2)}) collective-permute-start(f32[4,8,128]{2,1,0:T(8,128)S(1)} %get-tuple-element.8), channel_id=1, source_target_pairs={{0,3},{1,0},{2,1},{3,2},{4,7},{5,4},{6,5},{7,6},{8,11},{9,8},{10,9... | collective-permute-start | bytes 49160 | tf_op jit(solution)/shard_map/ppermute | solution.py:185
  62.8 0.0 collective-permute-start.8
  62.8 2.8 %collective-permute-start.3 = (f32[2,8,128]{2,1,0:T(8,128)S(1)}, f32[2,8,128]{2,1,0:T(8,128)S(1)}, u32[]{:S(2)}, u32[]{:S(2)}) collective-permute-start(f32[2,8,128]{2,1,0:T(8,128)S(1)} %slice.48), channel_id=1, source_target_pairs={{0,12},{1,13},{2,14},{3,15},{4,0},{5,1},{6,2},{7,3},{8,4},{9,5},{1... | collective-permute-start | bytes 24584 | tf_op jit(solution)/shard_map/ppermute | solution.py:187
  65.6 2.7 %collective-permute-start.11 = (f32[2,8,128]{2,1,0:T(8,128)S(1)}, f32[2,8,128]{2,1,0:T(8,128)S(1)}, u32[]{:S(2)}, u32[]{:S(2)}) collective-permute-start(f32[2,8,128]{2,1,0:T(8,128)S(1)} %slice.52), channel_id=1, source_target_pairs={{0,3},{1,0},{2,1},{3,2},{4,7},{5,4},{6,5},{7,6},{8,11},{9,8},{10,9... | collective-permute-start | bytes 24584 | tf_op jit(solution)/shard_map/ppermute | solution.py:187
  68.3 1.5 %collective-permute-done.2 = f32[2,8,128]{2,1,0:T(8,128)S(1)} collective-permute-done((f32[2,8,128]{2,1,0:T(8,128)S(1)}, f32[2,8,128]{2,1,0:T(8,128)S(1)}, u32[]{:S(2)}, u32[]{:S(2)}) %collective-permute-start.2) | collective-permute-done | bytes 8224 | tf_op jit(solution)/shard_map/ppermute | solution.py:187
  69.8 0.6 collective-permute-start.4
  70.4 2.2 %collective-permute-start.5 = (f32[4,4,8,128]{3,2,1,0:T(8,128)S(1)}, f32[4,4,8,128]{3,2,1,0:T(8,128)S(1)}, u32[]{:S(2)}, u32[]{:S(2)}) collective-permute-start(f32[4,4,8,128]{3,2,1,0:T(8,128)S(1)} %pad_maximum_fusion.1), channel_id=1, source_target_pairs={{0,3},{1,0},{2,1},{3,2},{4,7},{5,4},{6,5},{7,6},{8,11},{9,8},{10,9... | collective-permute-start | bytes 196616 | tf_op jit(solution)/shard_map/ppermute | solution.py:185
  72.6 0.1 collective-permute-start.12
  72.7 2.7 %collective-permute-start.13 = (f32[4,4,8,128]{3,2,1,0:T(8,128)S(1)}, f32[4,4,8,128]{3,2,1,0:T(8,128)S(1)}, u32[]{:S(2)}, u32[]{:S(2)}) collective-permute-start(f32[4,4,8,128]{3,2,1,0:T(8,128)S(1)} %pad_maximum_fusion.2), channel_id=1, source_target_pairs={{0,12},{1,13},{2,14},{3,15},{4,0},{5,1},{6,2},{7,3},{8,4},{9,5},{1... | collective-permute-start | bytes 196616 | tf_op jit(solution)/shard_map/ppermute | solution.py:185
  75.4 3.3 %collective-permute-start.7 = (f32[2,4,8,128]{3,2,1,0:T(8,128)S(1)}, f32[2,4,8,128]{3,2,1,0:T(8,128)S(1)}, u32[]{:S(2)}, u32[]{:S(2)}) collective-permute-start(f32[2,4,8,128]{3,2,1,0:T(8,128)S(1)} %slice.50), channel_id=1, source_target_pairs={{0,3},{1,0},{2,1},{3,2},{4,7},{5,4},{6,5},{7,6},{8,11},{9,8},{10,9... | collective-permute-start | bytes 98312 | tf_op jit(solution)/shard_map/ppermute | solution.py:187
  78.7 2.7 %collective-permute-start.15 = (f32[2,4,8,128]{3,2,1,0:T(8,128)S(1)}, f32[2,4,8,128]{3,2,1,0:T(8,128)S(1)}, u32[]{:S(2)}, u32[]{:S(2)}) collective-permute-start(f32[2,4,8,128]{3,2,1,0:T(8,128)S(1)} %slice.54), channel_id=1, source_target_pairs={{0,12},{1,13},{2,14},{3,15},{4,0},{5,1},{6,2},{7,3},{8,4},{9,5},{1... | collective-permute-start | bytes 98312 | tf_op jit(solution)/shard_map/ppermute | solution.py:187
  81.5 2.2 %collective-permute-done.6 = f32[2,4,8,128]{3,2,1,0:T(8,128)S(1)} collective-permute-done((f32[2,4,8,128]{3,2,1,0:T(8,128)S(1)}, f32[2,4,8,128]{3,2,1,0:T(8,128)S(1)}, u32[]{:S(2)}, u32[]{:S(2)}) %collective-permute-start.6) | collective-permute-done | bytes 32800 | tf_op jit(solution)/shard_map/ppermute | solution.py:187
  83.8 2.7 %collective-permute-done.14 = f32[2,4,8,128]{3,2,1,0:T(8,128)S(1)} collective-permute-done((f32[2,4,8,128]{3,2,1,0:T(8,128)S(1)}, f32[2,4,8,128]{3,2,1,0:T(8,128)S(1)}, u32[]{:S(2)}, u32[]{:S(2)}) %collective-permute-start.14) | collective-permute-done | bytes 32800 | tf_op jit(solution)/shard_map/ppermute | solution.py:187
  86.5 0.1 collective-permute-start.16
  86.7 8.8 %collective-permute-done.16.above = f32[2,4,4,4,8,128]{5,4,3,2,1,0:T(8,128)S(1)} collective-permute-done((f32[2,4,4,4,8,128]{5,4,3,2,1,0:T(8,128)S(1)}, f32[2,4,4,4,8,128]{5,4,3,2,1,0:T(8,128)S(1)}, u32[]{:S(2)}, u32[]{:S(2)}) %collective-permute-start.16) | collective-permute-done | bytes 524320 | tf_op jit(solution)/shard_map/ppermute | solution.py:223
  95.5 1.1 pad_maximum_fusion
  96.6 5.5 %collective-permute-start.17 = (f32[2,2,4,4,4,8,128]{6,5,4,3,2,1,0:T(8,128)}, f32[2,2,4,4,4,8,128]{6,5,4,3,2,1,0:T(8,128)S(1)}, u32[]{:S(2)}, u32[]{:S(2)}) collective-permute-start(f32[2,2,4,4,4,8,128]{6,5,4,3,2,1,0:T(8,128)} %pad_maximum_fusion), channel_id=1, source_target_pairs={{0,16},{16,0},{32,48},{48,32},{64,80},{80,64},{96,112},{112,96},{1... | collective-permute-start | bytes 3145736 | tf_op jit(solution)/shard_map/ppermute | solution.py:224
  102.1 0.1 copy.16
  102.2 0.1 add.140
  102.3 0.1 add.141
  102.4 0.1 add.143
  102.4 0.1 add.133
  102.5 0.1 add.137
  102.6 0.1 add.138
  102.7 0.6 pad_add_fusion.spots
  103.3 0.1 select_reduce_fusion
  103.4 0.6 xor_multiply_fusion.starts
  104.0 0.7 compare_select_fusion.picks
  104.7 0.0 copy-start.3
  104.7 1.0 copy-done.3
  105.6 5.5 %solve.1 = (f32[8,128,128]{2,1,0:T(8,128)}, bf16[9,128,256]{2,1,0:T(8,128)(2,1)}) custom-call(s32[4]{0:T(128)} %xor_multiply_fusion.starts, s32[2,16]{1,0:T(2,128)} %pad_add_fusion.spots, f32[16,80,128]{2,1,0:T(8,128)} %bitcast.54, f32[2,4,4,4,8,128]{5,4,3,2,1,0:T(8,128)} %bitcast.57, f32[2,4,4,4,8,128]{5,4,3,2,1,0:T(8,128)} %copy-done.2, ...), custom_call_target="tpu_custom_call" | custom-call | tf_op jit(solution)/shard_map/solve/pallas_call | solution.py:132
  111.1 8.7 %all-gather.3.cloned.1.call-done = f32[16,1728,128]{2,1,0:T(8,128)} async-done(((f32[1,1728,128]{2,1,0:T(8,128)}), f32[16,1728,128]{2,1,0:T(8,128)}) %all-gather.3.cloned.1.call-update) | async-done | bytes 14155792 | tf_op jit(solution)/shard_map/all_gather | solution.py:195
  119.8 8.9 %update.1 = f32[36,128,128]{2,1,0:T(8,128)} custom-call(s32[36,6]{1,0:T(8,128)} %compare_select_fusion.picks, f32[36,128,128]{2,1,0:T(8,128)} %sides.3, f32[16,36,6,8,128]{4,3,2,1,0:T(8,128)} %bitcast.51, bf16[9,128,256]{2,1,0:T(8,128)(2,1)} %get-tuple-element.5.pairs), custom_call_target="tpu_custom_call" | custom-call | tf_op jit(solution)/shard_map/update/pallas_call | solution.py:167
  (65 shorter events, 0.3 us)
Async XLA Ops:
  7.2 112.7 %all-gather.3.cloned.1.call-start = ((), (), s32[]{:S(2)}) async-start(), calls=%async_computation.1 | async-start | bytes 15040512 | tf_op jit(solution)/shard_map/all_gather | solution.py:195
  7.9 13.2 %copy-start.7 = (s32[32]{0:T(128)S(1)}, s32[32]{0:T(128)}, u32[]{:S(2)}) copy-start(s32[32]{0:T(128)} %constant.109) | copy-start | bytes 388
  7.9 13.2 %copy-start.5 = (s32[8]{0:T(128)S(1)}, s32[8]{0:T(128)}, u32[]{:S(2)}) copy-start(s32[8]{0:T(128)} %pivots.1) | copy-start | bytes 100
  11.1 75.5 %copy-start.6 = (s32[4]{0:T(128)S(1)}, s32[4]{0:T(128)}, u32[]{:S(2)}) copy-start(s32[4]{0:T(128)} %constant.104) | copy-start | bytes 52
  11.1 30.0 %all-to-all-start = ((f32[16,80,128]{2,1,0:T(8,128)}), f32[16,80,128]{2,1,0:T(8,128)S(1)}, u32[]{:S(2)}, u32[]{:S(2)}) async-start(f32[16,80,128]{2,1,0:T(8,128)} %pack.1), calls=%async_computation | async-start | bytes 1310720 | tf_op jit(solution)/shard_map/all_to_all | solution.py:205
  41.2 60.9 %copy-start.4 = (s32[36,6]{0,1:T(8,128)S(1)}, s32[36,6]{0,1:T(8,128)}, u32[]{:S(2)}) copy-start(s32[36,6]{0,1:T(8,128)} %param.10) | copy-start | bytes 2596
  41.2 62.2 %copy-start.8 = (s32[4]{0:T(128)S(1)}, s32[4]{0:T(128)}, u32[]{:S(2)}) copy-start(s32[4]{0:T(128)} %constant.99.clone) | copy-start | bytes 52
  57.4 47.2 %copy-start = (f32[1280,128]{1,0:T(8,128)}, f32[1280,128]{1,0:T(8,128)S(1)}, u32[]{:S(2)}) copy-start(f32[1280,128]{1,0:T(8,128)S(1)} %all-gather) | copy-start | bytes 1966084
  57.5 5.3 %collective-permute-start.1 = (f32[4,8,128]{2,1,0:T(8,128)S(1)}, f32[4,8,128]{2,1,0:T(8,128)S(1)}, u32[]{:S(2)}, u32[]{:S(2)}) collective-permute-start(f32[4,8,128]{2,1,0:T(8,128)S(1)} %get-tuple-element.9), channel_id=1, source_target_pairs={{0,12},{1,13},{2,14},{3,15},{4,0},{5,1},{6,2},{7,3},{8,4},{9,5},{1... | collective-permute-start | bytes 49160 | tf_op jit(solution)/shard_map/ppermute | solution.py:185
  60.3 5.2 %collective-permute-start = (f32[4,8,128]{2,1,0:T(8,128)S(1)}, f32[4,8,128]{2,1,0:T(8,128)S(1)}, u32[]{:S(2)}, u32[]{:S(2)}) collective-permute-start(f32[4,8,128]{2,1,0:T(8,128)S(1)} %get-tuple-element.9), channel_id=1, source_target_pairs={{0,4},{1,5},{2,6},{3,7},{4,8},{5,9},{6,10},{7,11},{8,12},{9,13},{1... | collective-permute-start | bytes 49160 | tf_op jit(solution)/shard_map/ppermute | solution.py:184
  60.3 5.3 %collective-permute-start.9 = (f32[4,8,128]{2,1,0:T(8,128)S(1)}, f32[4,8,128]{2,1,0:T(8,128)S(1)}, u32[]{:S(2)}, u32[]{:S(2)}) collective-permute-start(f32[4,8,128]{2,1,0:T(8,128)S(1)} %get-tuple-element.8), channel_id=1, source_target_pairs={{0,3},{1,0},{2,1},{3,2},{4,7},{5,4},{6,5},{7,6},{8,11},{9,8},{10,9... | collective-permute-start | bytes 49160 | tf_op jit(solution)/shard_map/ppermute | solution.py:185
  62.8 5.5 %collective-permute-start.8 = (f32[4,8,128]{2,1,0:T(8,128)S(1)}, f32[4,8,128]{2,1,0:T(8,128)S(1)}, u32[]{:S(2)}, u32[]{:S(2)}) collective-permute-start(f32[4,8,128]{2,1,0:T(8,128)S(1)} %get-tuple-element.8), channel_id=1, source_target_pairs={{0,1},{1,2},{2,3},{3,0},{4,5},{5,6},{6,7},{7,4},{8,9},{9,10},{10,1... | collective-permute-start | bytes 49160 | tf_op jit(solution)/shard_map/ppermute | solution.py:184
  62.8 5.5 %collective-permute-start.3 = (f32[2,8,128]{2,1,0:T(8,128)S(1)}, f32[2,8,128]{2,1,0:T(8,128)S(1)}, u32[]{:S(2)}, u32[]{:S(2)}) collective-permute-start(f32[2,8,128]{2,1,0:T(8,128)S(1)} %slice.48), channel_id=1, source_target_pairs={{0,12},{1,13},{2,14},{3,15},{4,0},{5,1},{6,2},{7,3},{8,4},{9,5},{1... | collective-permute-start | bytes 24584 | tf_op jit(solution)/shard_map/ppermute | solution.py:187
  65.5 4.3 %collective-permute-start.2 = (f32[2,8,128]{2,1,0:T(8,128)S(1)}, f32[2,8,128]{2,1,0:T(8,128)S(1)}, u32[]{:S(2)}, u32[]{:S(2)}) collective-permute-start(f32[2,8,128]{2,1,0:T(8,128)S(1)} %slice.47), channel_id=1, source_target_pairs={{0,4},{1,5},{2,6},{3,7},{4,8},{5,9},{6,10},{7,11},{8,12},{9,13},{1... | collective-permute-start | bytes 24584 | tf_op jit(solution)/shard_map/ppermute | solution.py:187
  65.6 7.0 %collective-permute-start.11 = (f32[2,8,128]{2,1,0:T(8,128)S(1)}, f32[2,8,128]{2,1,0:T(8,128)S(1)}, u32[]{:S(2)}, u32[]{:S(2)}) collective-permute-start(f32[2,8,128]{2,1,0:T(8,128)S(1)} %slice.52), channel_id=1, source_target_pairs={{0,3},{1,0},{2,1},{3,2},{4,7},{5,4},{6,5},{7,6},{8,11},{9,8},{10,9... | collective-permute-start | bytes 24584 | tf_op jit(solution)/shard_map/ppermute | solution.py:187
  68.2 4.3 %collective-permute-start.10 = (f32[2,8,128]{2,1,0:T(8,128)S(1)}, f32[2,8,128]{2,1,0:T(8,128)S(1)}, u32[]{:S(2)}, u32[]{:S(2)}) collective-permute-start(f32[2,8,128]{2,1,0:T(8,128)S(1)} %slice.51), channel_id=1, source_target_pairs={{0,1},{1,2},{2,3},{3,0},{4,5},{5,6},{6,7},{7,4},{8,9},{9,10},{10,1... | collective-permute-start | bytes 24584 | tf_op jit(solution)/shard_map/ppermute | solution.py:187
  69.8 8.9 %collective-permute-start.4 = (f32[4,4,8,128]{3,2,1,0:T(8,128)S(1)}, f32[4,4,8,128]{3,2,1,0:T(8,128)S(1)}, u32[]{:S(2)}, u32[]{:S(2)}) collective-permute-start(f32[4,4,8,128]{3,2,1,0:T(8,128)S(1)} %pad_maximum_fusion.1), channel_id=1, source_target_pairs={{0,1},{1,2},{2,3},{3,0},{4,5},{5,6},{6,7},{7,4},{8,9},{9,10},{10,1... | collective-permute-start | bytes 196616 | tf_op jit(solution)/shard_map/ppermute | solution.py:184
  70.4 5.0 %collective-permute-start.5 = (f32[4,4,8,128]{3,2,1,0:T(8,128)S(1)}, f32[4,4,8,128]{3,2,1,0:T(8,128)S(1)}, u32[]{:S(2)}, u32[]{:S(2)}) collective-permute-start(f32[4,4,8,128]{3,2,1,0:T(8,128)S(1)} %pad_maximum_fusion.1), channel_id=1, source_target_pairs={{0,3},{1,0},{2,1},{3,2},{4,7},{5,4},{6,5},{7,6},{8,11},{9,8},{10,9... | collective-permute-start | bytes 196616 | tf_op jit(solution)/shard_map/ppermute | solution.py:185
  72.6 8.9 %collective-permute-start.12 = (f32[4,4,8,128]{3,2,1,0:T(8,128)S(1)}, f32[4,4,8,128]{3,2,1,0:T(8,128)S(1)}, u32[]{:S(2)}, u32[]{:S(2)}) collective-permute-start(f32[4,4,8,128]{3,2,1,0:T(8,128)S(1)} %pad_maximum_fusion.2), channel_id=1, source_target_pairs={{0,4},{1,5},{2,6},{3,7},{4,8},{5,9},{6,10},{7,11},{8,12},{9,13},{1... | collective-permute-start | bytes 196616 | tf_op jit(solution)/shard_map/ppermute | solution.py:184
  72.7 6.0 %collective-permute-start.13 = (f32[4,4,8,128]{3,2,1,0:T(8,128)S(1)}, f32[4,4,8,128]{3,2,1,0:T(8,128)S(1)}, u32[]{:S(2)}, u32[]{:S(2)}) collective-permute-start(f32[4,4,8,128]{3,2,1,0:T(8,128)S(1)} %pad_maximum_fusion.2), channel_id=1, source_target_pairs={{0,12},{1,13},{2,14},{3,15},{4,0},{5,1},{6,2},{7,3},{8,4},{9,5},{1... | collective-permute-start | bytes 196616 | tf_op jit(solution)/shard_map/ppermute | solution.py:185
  75.4 6.1 %collective-permute-start.7 = (f32[2,4,8,128]{3,2,1,0:T(8,128)S(1)}, f32[2,4,8,128]{3,2,1,0:T(8,128)S(1)}, u32[]{:S(2)}, u32[]{:S(2)}) collective-permute-start(f32[2,4,8,128]{3,2,1,0:T(8,128)S(1)} %slice.50), channel_id=1, source_target_pairs={{0,3},{1,0},{2,1},{3,2},{4,7},{5,4},{6,5},{7,6},{8,11},{9,8},{10,9... | collective-permute-start | bytes 98312 | tf_op jit(solution)/shard_map/ppermute | solution.py:187
  78.7 5.0 %collective-permute-start.6 = (f32[2,4,8,128]{3,2,1,0:T(8,128)S(1)}, f32[2,4,8,128]{3,2,1,0:T(8,128)S(1)}, u32[]{:S(2)}, u32[]{:S(2)}) collective-permute-start(f32[2,4,8,128]{3,2,1,0:T(8,128)S(1)} %slice.49), channel_id=1, source_target_pairs={{0,1},{1,2},{2,3},{3,0},{4,5},{5,6},{6,7},{7,4},{8,9},{9,10},{10,1... | collective-permute-start | bytes 98312 | tf_op jit(solution)/shard_map/ppermute | solution.py:187
  78.7 5.1 %collective-permute-start.15 = (f32[2,4,8,128]{3,2,1,0:T(8,128)S(1)}, f32[2,4,8,128]{3,2,1,0:T(8,128)S(1)}, u32[]{:S(2)}, u32[]{:S(2)}) collective-permute-start(f32[2,4,8,128]{3,2,1,0:T(8,128)S(1)} %slice.54), channel_id=1, source_target_pairs={{0,12},{1,13},{2,14},{3,15},{4,0},{5,1},{6,2},{7,3},{8,4},{9,5},{1... | collective-permute-start | bytes 98312 | tf_op jit(solution)/shard_map/ppermute | solution.py:187
  81.5 5.0 %collective-permute-start.14 = (f32[2,4,8,128]{3,2,1,0:T(8,128)S(1)}, f32[2,4,8,128]{3,2,1,0:T(8,128)S(1)}, u32[]{:S(2)}, u32[]{:S(2)}) collective-permute-start(f32[2,4,8,128]{3,2,1,0:T(8,128)S(1)} %slice.53), channel_id=1, source_target_pairs={{0,4},{1,5},{2,6},{3,7},{4,8},{5,9},{6,10},{7,11},{8,12},{9,13},{1... | collective-permute-start | bytes 98312 | tf_op jit(solution)/shard_map/ppermute | solution.py:187
  86.5 18.1 %copy-start.1 = (f32[8,4,4,8,128]{4,3,2,1,0:T(8,128)}, f32[8,4,4,8,128]{4,3,2,1,0:T(8,128)S(1)}, u32[]{:S(2)}) copy-start(f32[8,4,4,8,128]{4,3,2,1,0:T(8,128)S(1)} %fusion.1) | copy-start | bytes 1572868
  86.5 9.0 %collective-permute-start.16 = (f32[2,4,4,4,8,128]{5,4,3,2,1,0:T(8,128)S(1)}, f32[2,4,4,4,8,128]{5,4,3,2,1,0:T(8,128)S(1)}, u32[]{:S(2)}, u32[]{:S(2)}) collective-permute-start(f32[2,4,4,4,8,128]{5,4,3,2,1,0:T(8,128)S(1)} %bitcast.55), channel_id=1, source_target_pairs={{0,32},{16,48},{32,0},{48,16},{64,96},{80,112},{96,64},{112,80},{1... | collective-permute-start | bytes 1572872 | tf_op jit(solution)/shard_map/ppermute | solution.py:223
  95.5 9.2 %copy-start.2 = (f32[2,4,4,4,8,128]{5,4,3,2,1,0:T(8,128)}, f32[2,4,4,4,8,128]{5,4,3,2,1,0:T(8,128)S(1)}, u32[]{:S(2)}) copy-start(f32[2,4,4,4,8,128]{5,4,3,2,1,0:T(8,128)S(1)} %collective-permute-done.16.above) | copy-start | bytes 1572868
  96.6 8.0 %collective-permute-start.17 = (f32[2,2,4,4,4,8,128]{6,5,4,3,2,1,0:T(8,128)}, f32[2,2,4,4,4,8,128]{6,5,4,3,2,1,0:T(8,128)S(1)}, u32[]{:S(2)}, u32[]{:S(2)}) collective-permute-start(f32[2,2,4,4,4,8,128]{6,5,4,3,2,1,0:T(8,128)} %pad_maximum_fusion), channel_id=1, source_target_pairs={{0,16},{16,0},{32,48},{48,32},{64,80},{80,64},{96,112},{112,96},{1... | collective-permute-start | bytes 3145736 | tf_op jit(solution)/shard_map/ppermute | solution.py:224
  104.7 1.0 copy-start.3
Sparse Core Ops, SparseCore 0:
  10.4 109.3 all-gather.2
